TPU v7x, 32 devices: a whole 2x2x4 slice. The times are simulated.
32 devices in a mesh: dp: 2 (over x), col: 4 (over y, core), row: 4 (over z).
Axes of the slice: x: 2, y: 2, z: 4, core: 2. Of those that a mesh axis runs over, the one named last changes fastest.
Arguments:
- tokens: bfloat16 [16, 2048, 512], P(('dp', 'row'), 'col'), may hold values from -6 to 6
- doc_lengths: int32 [16, 8], P(('dp', 'row')), may hold values from 1 to 1024, 2048 in all within a row
- norm_gain: float32 [512], replicated, may hold values from 0.25 to 1.75
- norm_shift: float32 [512], replicated, may hold values from -1 to 1
- qkv_weight: float32 [512, 1536], P('row', 'col'), may hold values from -0.25 to 0.25
- query_bias: float32 [512], replicated, may hold values from -2.5 to 2.5
- value_bias: float32 [512], replicated, may hold values from -0.5 to 0.5
- mix_weight: float32 [512, 512], P('row', 'col'), may hold values from -1 to 1
- mix_bias: float32 [512], replicated, may hold values from -1 to 1
- ffn_gain: float32 [512], replicated, may hold values from 0.25 to 1.75
- ffn_shift: float32 [512], replicated, may hold values from -1 to 1
- up_weight: float32 [512, 2048], P('row', 'col'), may hold values from -0.25 to 0.25
- up_bias: float32 [2048], replicated, may hold values from -2.5 to 2.5
- down_weight: float32 [2048, 512], P('row', 'col'), may hold values from -0.125 to 0.125
- down_bias: float32 [512], replicated, may hold values from -1 to 1
- cotangent: bfloat16 [16, 2048, 512], P(('dp', 'row'), 'col'), may hold values from -6 to 6
Outputs:
- layer_out: bfloat16 [16, 2048, 512], P(('dp', 'row'), 'col')
- tokens_grad: bfloat16 [16, 2048, 512], P(('dp', 'row'), 'col')
- qkv_grad: float32 [512, 1536], P('row', 'col')
- mix_grad: float32 [512, 512], P('row', 'col')
- up_grad: float32 [512, 2048], P('row', 'col')
- down_grad: float32 [2048, 512], P('row', 'col')
- vector_grads: float32 [8, 512], replicated
- hidden_grad: float32 [2048], replicated
Inputs may be any that keep to these rules, and one draw needn't show every extreme that they name: `doc_lengths`: the 8 document lengths of a sequence sum to 2048; in every sequence the longest is 1024 tokens.
All inputs are finite; a program needn't handle non-finite values.
Results may differ from a plain program's by a relative error of at most 0.017.
Values may be sent and summed in bfloat16 or wider, within the bound.
No kernel may reach another device: no remote copies, remote signals or barrier semaphores. Data moves between devices by JAX's collectives and lax.ppermute only.
A program may use at most 128 MiB of HBM per device.

v0:
```python
import jax
import jax.numpy as jnp
from jax import lax
from jax.sharding import PartitionSpec as P

HEAD_DIM = 64


epsilon = 1e-05
masked_out = -1e30


def norm_layer(values, scale_vec, shift_vec):
    center = values - jnp.mean(values, axis=-1, keepdims=True)
    spread = jnp.mean(center * center, axis=-1, keepdims=True)
    return center * lax.rsqrt(spread + epsilon) * scale_vec + shift_vec


def exact_gelu(values):
    return jax.nn.gelu(values, approximate=False)


def segment_ids(lengths, full_len):
    doc_ends = jnp.cumsum(lengths, axis=-1)
    places = jnp.arange(full_len, dtype=jnp.int32)
    passed = places[None, :, None] >= doc_ends[:, None, :]
    return jnp.sum(passed.astype(jnp.int32), axis=-1)


def blocked_matmul(left_rows, blocks, col_count, row_count):
    tok_count = left_rows.shape[0]
    inner_len = blocks.shape[1]
    narrow = blocks.shape[2]
    weight_grid = blocks.reshape(col_count, row_count, inner_len, narrow)
    left_parts = left_rows.reshape(tok_count, row_count, inner_len)
    product = jnp.einsum(
        "trk,crkn->tcn", left_parts, weight_grid, preferred_element_type=jnp.float32
    )
    return product.reshape(tok_count, col_count * narrow)


def blocked_back(grad_rows, blocks, col_count, row_count):
    tok_count = grad_rows.shape[0]
    inner_len = blocks.shape[1]
    narrow = blocks.shape[2]
    weight_grid = blocks.reshape(col_count, row_count, inner_len, narrow)
    grad_parts = grad_rows.reshape(tok_count, col_count, narrow)
    product = jnp.einsum(
        "tcn,crkn->trk", grad_parts, weight_grid, preferred_element_type=jnp.float32
    )
    return product.reshape(tok_count, row_count * inner_len)


def weight_grad(left_rows, grad_rows, col_count, row_count, pieces):
    tok_count = left_rows.shape[0]
    inner_len = left_rows.shape[1] // (row_count * pieces)
    narrow = grad_rows.shape[1] // col_count
    left_parts = left_rows.reshape(tok_count, row_count, pieces, inner_len)
    others = grad_rows.reshape(tok_count, col_count, narrow)
    product = jnp.einsum("trpk,tcn->pcrkn", left_parts, others, preferred_element_type=jnp.float32)
    return product.reshape(pieces * col_count * row_count, inner_len, narrow)


def whole_block(share):
    return share.reshape(share.shape[0] * share.shape[1], share.shape[2])


def attend_forward(head_rows, seg_all, heads_local, block_rows):
    seq_count, full_len = seg_all.shape
    local_width = head_rows.shape[3]
    scale = HEAD_DIM ** (-0.5)
    blocks = full_len // block_rows
    mixed_list = []
    lse_list = []
    for position in range(seq_count):
        queries = head_rows[position, :, 0].reshape(full_len, heads_local, HEAD_DIM)
        key_rows = head_rows[position, :, 1].reshape(full_len, heads_local, HEAD_DIM)
        values = head_rows[position, :, 2].reshape(full_len, heads_local, HEAD_DIM)
        seg_seq = seg_all[position]

        def attend_block(number):
            start = number * block_rows
            query_rows = lax.dynamic_slice_in_dim(queries, start, block_rows, 0)
            seg_rows = lax.dynamic_slice_in_dim(seg_seq, start, block_rows, 0)
            scores = (
                jnp.einsum("qhd,khd->hqk", query_rows, key_rows, preferred_element_type=jnp.float32)
                * scale
            )
            same_doc = (seg_rows[:, None] == seg_seq[None, :])[None]
            masked = jnp.where(same_doc, scores, masked_out)
            largest = jnp.max(masked, axis=-1, keepdims=True)
            weights = jnp.exp(masked - largest)
            totals = jnp.sum(weights, axis=-1, keepdims=True)
            probs_low = (weights / totals).astype(jnp.bfloat16)
            mixed_rows = jnp.einsum(
                "hqk,khd->qhd", probs_low, values, preferred_element_type=jnp.float32
            )
            return (mixed_rows.astype(jnp.bfloat16), (largest + jnp.log(totals))[..., 0])

        mixed_seq, lse_seq = lax.map(attend_block, jnp.arange(blocks, dtype=jnp.int32))
        mixed_list.append(mixed_seq.reshape(full_len, local_width))
        lse_list.append(lse_seq)
    return (jnp.stack(mixed_list), jnp.stack(lse_list))


def attend_backward(head_rows, seg_all, lse_all, grad_heads, heads_local, block_rows):
    seq_count, full_len = seg_all.shape
    local_width = head_rows.shape[3]
    scale = HEAD_DIM ** (-0.5)
    blocks = full_len // block_rows
    grad_list = []
    for position in range(seq_count):
        queries = head_rows[position, :, 0].reshape(full_len, heads_local, HEAD_DIM)
        key_rows = head_rows[position, :, 1].reshape(full_len, heads_local, HEAD_DIM)
        values = head_rows[position, :, 2].reshape(full_len, heads_local, HEAD_DIM)
        seg_seq = seg_all[position]
        grad_mix = grad_heads[position].reshape(full_len, heads_local, HEAD_DIM)
        lse_seq = lse_all[position]

        def back_block(carry, number):
            key_grad, value_grad = carry
            start = number * block_rows
            query_rows = lax.dynamic_slice_in_dim(queries, start, block_rows, 0)
            seg_rows = lax.dynamic_slice_in_dim(seg_seq, start, block_rows, 0)
            grad_rows = lax.dynamic_slice_in_dim(grad_mix, start, block_rows, 0)
            lse_rows = lax.dynamic_index_in_dim(lse_seq, number, 0, keepdims=False)
            scores = (
                jnp.einsum("qhd,khd->hqk", query_rows, key_rows, preferred_element_type=jnp.float32)
                * scale
            )
            same_doc = (seg_rows[:, None] == seg_seq[None, :])[None]
            probs = jnp.where(same_doc, jnp.exp(scores - lse_rows[..., None]), 0.0)
            grad_probs = jnp.einsum(
                "qhd,khd->hqk", grad_rows, values, preferred_element_type=jnp.float32
            )
            inner = jnp.sum(probs * grad_probs, axis=-1, keepdims=True)
            grad_scores = (probs * (grad_probs - inner)).astype(jnp.bfloat16)
            probs_low = probs.astype(jnp.bfloat16)
            query_grad = (
                jnp.einsum(
                    "hqk,khd->qhd", grad_scores, key_rows, preferred_element_type=jnp.float32
                )
                * scale
            )
            key_grad = (
                key_grad
                + jnp.einsum(
                    "hqk,qhd->khd", grad_scores, query_rows, preferred_element_type=jnp.float32
                )
                * scale
            )
            value_grad = value_grad + jnp.einsum(
                "hqk,qhd->khd", probs_low, grad_rows, preferred_element_type=jnp.float32
            )
            return ((key_grad, value_grad), query_grad.astype(jnp.bfloat16))

        zero_grads = jnp.zeros((full_len, heads_local, HEAD_DIM), jnp.float32)
        (key_grad, value_grad), query_grads = lax.scan(
            back_block, (zero_grads, zero_grads), jnp.arange(blocks, dtype=jnp.int32)
        )
        stacked = jnp.stack(
            [
                query_grads.reshape(full_len, local_width),
                key_grad.reshape(full_len, local_width).astype(jnp.bfloat16),
                value_grad.reshape(full_len, local_width).astype(jnp.bfloat16),
            ],
            axis=1,
        )
        grad_list.append(stacked)
    return jnp.stack(grad_list)


def body(
    tokens,
    doc_lengths,
    norm_gain,
    norm_shift,
    qkv_weight,
    query_bias,
    value_bias,
    mix_weight,
    mix_bias,
    ffn_gain,
    ffn_shift,
    up_weight,
    up_bias,
    down_weight,
    down_bias,
    cotangent,
):
    col_count = lax.axis_size("col")
    row_count = lax.axis_size("row")
    seq_count, block_len, model_width = tokens.shape
    full_len = block_len * col_count
    tok_count = seq_count * block_len
    local_width = model_width // col_count
    heads_local = local_width // HEAD_DIM
    block_rows = min(512, full_len)
    pieces = 1
    qkv_shard = qkv_weight.astype(jnp.bfloat16)[None]
    mix_shard = mix_weight.astype(jnp.bfloat16)[None]
    up_shard = up_weight.astype(jnp.bfloat16)[None]
    down_shard = down_weight.astype(jnp.bfloat16)[None]
    qkv_blocks, mix_blocks = (
        lax.all_gather(qkv_shard, ("col", "row"), axis=0, tiled=True),
        lax.all_gather(mix_shard, ("col", "row"), axis=0, tiled=True),
    )
    flat_tokens = tokens.reshape(tok_count, model_width).astype(jnp.float32)
    normed_one, first_pull = jax.vjp(norm_layer, flat_tokens, norm_gain, norm_shift)
    first_low = normed_one.astype(jnp.bfloat16)
    shifts = jnp.concatenate([query_bias, jnp.zeros_like(query_bias), value_bias])
    qkv_rows = (blocked_matmul(first_low, qkv_blocks, col_count, row_count) + shifts).astype(
        jnp.bfloat16
    )
    head_rows = lax.all_to_all(
        qkv_rows.reshape(seq_count, block_len, 3, model_width),
        "col",
        split_axis=3,
        concat_axis=1,
        tiled=True,
    )
    seg_all = segment_ids(doc_lengths, full_len)
    mixed_heads, lse_all = attend_forward(head_rows, seg_all, heads_local, block_rows)
    up_blocks, down_blocks = (
        lax.all_gather(up_shard, ("col", "row"), axis=0, tiled=True),
        lax.all_gather(down_shard, ("col", "row"), axis=0, tiled=True),
    )
    mixed_tokens = lax.all_to_all(
        mixed_heads, "col", split_axis=1, concat_axis=2, tiled=True
    ).reshape(tok_count, model_width)
    residual = (
        flat_tokens + blocked_matmul(mixed_tokens, mix_blocks, col_count, row_count) + mix_bias
    )
    normed_two, second_pull = jax.vjp(norm_layer, residual, ffn_gain, ffn_shift)
    second_low = normed_two.astype(jnp.bfloat16)
    hidden = blocked_matmul(second_low, up_blocks, col_count, row_count) + up_bias
    active_f, gelu_pull = jax.vjp(exact_gelu, hidden)
    active = active_f.astype(jnp.bfloat16)
    ffn_out = blocked_matmul(active, down_blocks, col_count, row_count) + down_bias
    layer_out = (residual + ffn_out).astype(jnp.bfloat16).reshape(seq_count, block_len, model_width)
    qkv_back, mix_back, up_back, down_back = (
        lax.all_gather(qkv_shard, ("col", "row"), axis=0, tiled=True),
        lax.all_gather(mix_shard, ("col", "row"), axis=0, tiled=True),
        lax.all_gather(up_shard, ("col", "row"), axis=0, tiled=True),
        lax.all_gather(down_shard, ("col", "row"), axis=0, tiled=True),
    )
    grad_ffn = cotangent.reshape(tok_count, model_width)
    grad_ffn_f = grad_ffn.astype(jnp.float32)
    down_part = weight_grad(active, grad_ffn, col_count, row_count, pieces)
    down_bias_grad = jnp.sum(grad_ffn_f, axis=0)
    grad_active = blocked_back(grad_ffn, down_back, col_count, row_count)
    grad_hidden = gelu_pull(grad_active)[0].astype(jnp.bfloat16)
    up_part = weight_grad(second_low, grad_hidden, col_count, row_count, pieces)
    up_bias_grad = jnp.sum(grad_hidden, axis=0, dtype=jnp.float32)
    up_share, down_share = (
        lax.psum_scatter(
            up_part.astype(jnp.bfloat16), ("col", "row"), scatter_dimension=0, tiled=True
        ).astype(jnp.float32),
        lax.psum_scatter(
            down_part.astype(jnp.bfloat16), ("col", "row"), scatter_dimension=0, tiled=True
        ).astype(jnp.float32),
    )
    grad_second = blocked_back(grad_hidden, up_back, col_count, row_count)
    grad_norm_two, ffn_gain_grad, ffn_shift_grad = second_pull(grad_second)
    grad_resid = grad_ffn_f + grad_norm_two
    grad_attn = grad_resid.astype(jnp.bfloat16)
    mix_part = weight_grad(mixed_tokens, grad_attn, col_count, row_count, pieces)
    mix_bias_grad = jnp.sum(grad_attn, axis=0, dtype=jnp.float32)
    grad_mixed = blocked_back(grad_attn, mix_back, col_count, row_count).astype(jnp.bfloat16)
    grad_mix_heads = lax.all_to_all(
        grad_mixed.reshape(seq_count, block_len, model_width),
        "col",
        split_axis=2,
        concat_axis=1,
        tiled=True,
    )
    grad_heads = attend_backward(
        head_rows, seg_all, lse_all, grad_mix_heads, heads_local, block_rows
    )
    grad_qkv = lax.all_to_all(grad_heads, "col", split_axis=1, concat_axis=3, tiled=True).reshape(
        tok_count, 3 * model_width
    )
    qkv_part = weight_grad(first_low, grad_qkv, col_count, row_count, pieces)
    query_grad = jnp.sum(grad_qkv[:, :model_width], axis=0, dtype=jnp.float32)
    value_grad = jnp.sum(grad_qkv[:, 2 * model_width :], axis=0, dtype=jnp.float32)
    grad_first = blocked_back(grad_qkv, qkv_back, col_count, row_count)
    grad_norm_one, norm_gain_grad, norm_shift_grad = first_pull(grad_first)
    tokens_grad = (
        (grad_resid + grad_norm_one).astype(jnp.bfloat16).reshape(seq_count, block_len, model_width)
    )
    qkv_share, mix_share = (
        lax.psum_scatter(
            qkv_part.astype(jnp.bfloat16), ("col", "row"), scatter_dimension=0, tiled=True
        ).astype(jnp.float32),
        lax.psum_scatter(
            mix_part.astype(jnp.bfloat16), ("col", "row"), scatter_dimension=0, tiled=True
        ).astype(jnp.float32),
    )
    finals = (
        lax.psum(qkv_share.astype(jnp.bfloat16), "dp").astype(jnp.float32),
        lax.psum(mix_share.astype(jnp.bfloat16), "dp").astype(jnp.float32),
        lax.psum(up_share.astype(jnp.bfloat16), "dp").astype(jnp.float32),
        lax.psum(down_share.astype(jnp.bfloat16), "dp").astype(jnp.float32),
    )
    vector_local = jnp.stack(
        [
            norm_gain_grad,
            norm_shift_grad,
            query_grad,
            value_grad,
            mix_bias_grad,
            ffn_gain_grad,
            ffn_shift_grad,
            down_bias_grad,
        ]
    )
    vector_grads, hidden_grad = lax.psum((vector_local, up_bias_grad), ("dp", "col", "row"))
    return (
        layer_out,
        tokens_grad,
        whole_block(finals[0]),
        whole_block(finals[1]),
        whole_block(finals[2]),
        whole_block(finals[3]),
        vector_grads,
        hidden_grad,
    )


def solution(mesh):
    return jax.shard_map(
        body,
        mesh=mesh,
        in_specs=(
            P(("dp", "row"), "col", None),
            P(("dp", "row"), None),
            P(),
            P(),
            P("row", "col"),
            P(),
            P(),
            P("row", "col"),
            P(),
            P(),
            P(),
            P("row", "col"),
            P(),
            P("row", "col"),
            P(),
            P(("dp", "row"), "col", None),
        ),
        out_specs=(
            P(("dp", "row"), "col", None),
            P(("dp", "row"), "col", None),
            P("row", "col"),
            P("row", "col"),
            P("row", "col"),
            P("row", "col"),
            P(),
            P(),
        ),
        check_vma=False,
    )
```

profile of v0, /device:TPU:0, one launch (start us, length us, event | category | flops | bytes accessed | tf_op | source)
XLA Modules:
  0.0 833.0 jit_solution(5345084864977231863)
XLA Ops:
  13.7 39.6 %all-gather.8.cloned.1.call-done = bf16[2048,384]{1,0:T(8,128)(2,1)} async-done(((bf16[128,384]{1,0:T(8,128)(2,1)}), bf16[2048,384]{1,0:T(8,128)(2,1)}) %all-gather.8.cloned.1.call-update) | async-done | bytes 1572880 | tf_op jit(solution)/shard_map/all_gather | solution.py:205
  64.3 11.4 %copy.302 = bf16[2,512,3,512]{1,0,2,3:T(2,128)(2,1)} copy(bf16[2,512,3,512]{3,2,1,0:T(4,128)(2,1)} %reshape.573) | data formatting | bytes 6291456 | tf_op jit(solution)/shard_map/reshape | solution.py:216
  80.7 42.8 %all-to-all-done = bf16[2,512,3,512]{1,0,2,3:T(2,128)(2,1)S(1)} async-done(((bf16[2,512,3,512]{1,0,2,3:T(2,128)(2,1)}), bf16[2,512,3,512]{1,0,2,3:T(2,128)(2,1)S(1)}, u32[]{:S(2)}, u32[]{:S(2)}) %all-to-all-start) | async-done | bytes 3145760 | tf_op jit(solution)/shard_map/all_to_all | solution.py:215
  135.0 36.8 %while.55 = (s32[]{:T(128)}, bf16[4,512,2,64]{1,3,2,0:T(8,128)(2,1)S(1)}, f32[4,2,512]{2,1,0:T(2,128)S(1)}, s32[4]{0:T(128)S(1)}, s32[2048]{0:T(1024)S(1)}, /*in...) while((s32[]{:T(128)}, ...), condition=%wide.region_11.12_spmd, body=%wide.region_8.11_spmd.sunk | while | flops 563149824 | bytes 30718160 | solution.py:100
  174.8 37.2 %while.54 = (s32[]{:T(128)}, bf16[4,512,2,64]{1,3,2,0:T(8,128)(2,1)S(1)}, f32[4,2,512]{2,1,0:T(2,128)S(1)}, s32[4]{0:T(128)S(1)}, s32[2048]{0:T(1024)S(1)}, /*in...) while((s32[]{:T(128)}, ...), condition=%wide.region_7.8_spmd, body=%wide.region_4.7_spmd.sunk | while | flops 563149824 | bytes 30718160 | solution.py:100
  227.3 41.7 %all-gather.1 = bf16[2048,128]{1,0:T(8,128)(2,1)} all-gather(bf16[128,128]{1,0:T(8,128)(2,1)S(1)} %convert_element_type.264), channel_id=3, replica_groups=mesh['dp'=2,'col'=4,'row'=4] {'col','row'}, dimensions={0}, use_global_device_ids=true | all-gather | bytes 557056 | tf_op jit(solution)/shard_map/all_gather | solution.py:206
  283.4 21.8 %multiply_convert_fusion.2 = (bf16[1024,2048]{1,0:T(8,128)(2,1)}, f32[1024,2048]{1,0:T(8,128)}, f32[1024,2048,1]{1,0,2:T(8,128)}) fusion(f32[2048]{0:T(1024)S(1)} %copy-done.76, bf16[1024,4,128]{0,2,1:T(8,128)(2,1)S(1)} %bitcast.423, bf16[2048,128,4]{1,0,2:T(8,128)(2,1)S(1)} %bitcast.396), kind=kOutput, calls=%fused_computation.103 | convolution fusion | flops 2285895680 | bytes 24125440 | tf_op jit(solution)/shard_map/trk,crkn->tcn/dot_general | solution.py:36
  305.2 10.0 %convert_reduce_fusion = (f32[2048]{0:T(1024)}, bf16[1024,2048]{1,0:T(8,128)(2,1)S(1)}) fusion(f32[1024,2048]{1,0:T(8,128)} %get-tuple-element.518, bf16[2048,4,128]{2,0,1:T(8,128)(2,1)} %bitcast.392, bf16[1024,4,128]{2,1,0:T(4,128)(2,1)S(1)} %copy-done.44, f32[2048]{0:T(1024)S(1)} %copy-done.76, f32[1024,2048,1]{1,0,2:T(8,128)} %get-tuple-element.543), kind=kOutput, calls=%fused_computation.102 | convolution fusion | flops 2183133184 | bytes 24133632 | tf_op jit(solution)/shard_map/tcn,crkn->trk/dot_general | solution.py:48
  330.1 8.1 reshape.529
  338.2 5.3 fusion.112
  354.6 7.8 reshape.526
  362.5 5.2 convert_bitcast_fusion
  377.1 130.4 %while.56 = (s32[]{:T(128)}, f32[2048,2,64]{0,2,1:T(8,128)S(1)}, f32[2048,2,64]{0,2,1:T(8,128)}, bf16[4,512,2,64]{1,3,2,0:T(8,128)(2,1)}, s32[4]{0:T(128)S(1)}, ...) while((s32[]{:T(128)}, f32[2048,2,64]{0,2,1:T(8,128)S(1)}, ...), condition=%wide.region_18.19_spmd.clone, body=%wide.region_16.18_spmd.clone.sunk | while | flops 1376123904 | bytes 128100840 | solution.py:158
  378.8 5.5 fusion.236
  387.1 6.8 multiply_reduce_fusion.10
  401.2 5.3 fusion.238
  411.5 5.5 fusion.236
  419.8 6.8 multiply_reduce_fusion.10
  433.8 5.0 fusion.238
  443.9 5.5 fusion.236
  452.2 6.8 multiply_reduce_fusion.10
  466.3 5.2 fusion.238
  476.5 5.5 fusion.236
  484.9 6.8 multiply_reduce_fusion.10
  498.9 5.1 fusion.238
  516.3 126.9 %while.57 = (s32[]{:T(128)}, f32[2048,2,64]{0,2,1:T(8,128)S(1)}, f32[2048,2,64]{0,2,1:T(8,128)}, bf16[4,512,2,64]{1,3,2,0:T(8,128)(2,1)}, s32[4]{0:T(128)S(1)}, ...) while((s32[]{:T(128)}, f32[2048,2,64]{0,2,1:T(8,128)S(1)}, ...), condition=%wide.region_21.22_spmd.clone, body=%wide.region_19.21_spmd.clone.sunk | while | flops 1376123904 | bytes 128100848 | solution.py:158
  518.0 5.5 fusion.249
  526.9 5.7 multiply_reduce_fusion.11
  540.0 4.8 fusion.251
  549.6 5.5 fusion.249
  558.6 5.7 multiply_reduce_fusion.11
  571.6 4.8 fusion.251
  581.3 5.5 fusion.249
  590.2 5.7 multiply_reduce_fusion.11
  603.3 4.8 fusion.251
  612.9 5.5 fusion.249
  621.8 5.7 multiply_reduce_fusion.11
  634.9 4.8 fusion.251
  648.3 5.8 copy.332
  654.1 4.8 all-to-all-start.3
  660.7 35.1 %all-to-all-done.3 = bf16[2,2048,3,128]{3,0,2,1:T(2,128)(2,1)} async-done(((bf16[2,2048,3,128]{3,0,2,1:T(2,128)(2,1)}), bf16[2,2048,3,128]{3,0,2,1:T(2,128)(2,1)}, u32[]{:S(2)}, u32[]{:S(2)}) %all-to-all-start.3) | async-done | bytes 3145760 | tf_op jit(solution)/shard_map/all_to_all | solution.py:280
  703.6 5.2 fusion.117
  716.1 5.4 fusion.106
  722.8 9.1 %psum.43 = bf16[128,128]{1,0:T(8,128)(2,1)S(1)} all-reduce(bf16[128,128]{1,0:T(8,128)(2,1)} %bitcast.439), channel_id=1, replica_groups=mesh['dp'=2,'col'=4,'row'=4] {'dp'}, use_global_device_ids=true, to_apply=%region_27.28 | all-reduce | flops 16384 | bytes 65536 | tf_op jit(solution)/shard_map/psum | solution.py:301
  732.6 5.5 fusion.151
  744.5 23.9 %reduce-scatter.5.cloned.1.call-done = bf16[1,128,384]{2,1,0:T(8,128)(2,1)} async-done(((bf16[16,128,384]{2,1,0:T(8,128)(2,1)}), bf16[1,128,384]{2,1,0:T(8,128)(2,1)}) %reduce-scatter.5.cloned.1.call-update) | async-done | bytes 98320 | tf_op jit(solution)/shard_map/reduce_scatter | solution.py:292
  773.2 4.8 reshape.543
  780.7 40.5 %all-reduce = (f32[8,512]{1,0:T(8,128)}, f32[2048]{0:T(1024)}) all-reduce(f32[8,512]{1,0:T(8,128)S(1)} %stack.51, f32[2048]{0:T(1024)S(1)} %copy-done.67), channel_id=1, replica_groups=mesh['dp'=2,'col'=4,'row'=4] {'dp','col','row'}, use_global_device_ids=true, to_apply=%region_40.41 | all-reduce | flops 6144 | bytes 49152 | tf_op jit(solution)/shard_map/psum | solution.py:317
  (506 shorter events, 321.0 us)
Async XLA Ops:
  7.2 46.1 %all-gather.8.cloned.1.call-start = ((), (), s32[]{:S(2)}) async-start(), calls=%async_computation.12 | async-start | bytes 1671168 | tf_op jit(solution)/shard_map/all_gather | solution.py:205
  8.9 46.9 %copy-start.61 = (f32[512]{0:T(512)S(1)}, f32[512]{0:T(512)}, u32[]{:S(2)}) copy-start(f32[512]{0:T(512)} %param.26) | copy-start | bytes 6148
  8.9 46.9 %copy-start.73 = (f32[512]{0:T(512)S(1)}, f32[512]{0:T(512)}, u32[]{:S(2)}) copy-start(f32[512]{0:T(512)} %param.27) | copy-start | bytes 6148
  13.0 46.7 %copy-start.53 = (f32[1024]{0:T(1024)}, f32[1024]{0:T(1024)S(1)}, u32[]{:S(2)}) copy-start(f32[1024]{0:T(1024)S(1)} %rsqrt.23) | copy-start | bytes 12292
  13.6 46.2 %copy-start.50 = (f32[1,4,2,128]{3,1,2,0:T(4,128)}, f32[1,4,2,128]{3,1,2,0:T(4,128)S(1)}, u32[]{:S(2)}) copy-start(f32[1,4,2,128]{3,1,2,0:T(4,128)S(1)} %copy.378) | copy-start | bytes 12292
  75.8 47.7 %all-to-all-start = ((bf16[2,512,3,512]{1,0,2,3:T(2,128)(2,1)}), bf16[2,512,3,512]{1,0,2,3:T(2,128)(2,1)S(1)}, u32[]{:S(2)}, u32[]{:S(2)}) async-start(bf16[2,512,3,512]{1,0,2,3:T(2,128)(2,1)} %copy.302), calls=%async_computation | async-start | bytes 6291456 | tf_op jit(solution)/shard_map/all_to_all | solution.py:215
  79.6 195.4 %all-gather.10.cloned.1.call-start = ((), (), s32[]{:S(2)}) async-start(), calls=%async_computation.13 | async-start | bytes 2228224 | tf_op jit(solution)/shard_map/all_gather | solution.py:225
  134.9 39.3 %copy-start.32 = (bf16[1,2048,1,128]{3,1,2,0:T(8,128)(2,1)S(1)}, bf16[1,2048,1,128]{3,1,2,0:T(8,128)(2,1)}, u32[]{:S(2)}) copy-start(bf16[1,2048,1,128]{3,1,2,0:T(8,128)(2,1)} %get-tuple-element.531) | copy-start | bytes 1572868
  135.0 39.5 %copy-start.31 = (bf16[1,2048,1,128]{3,1,2,0:T(8,128)(2,1)S(1)}, bf16[1,2048,1,128]{3,1,2,0:T(8,128)(2,1)}, u32[]{:S(2)}) copy-start(bf16[1,2048,1,128]{3,1,2,0:T(8,128)(2,1)} %get-tuple-element.527) | copy-start | bytes 1572868
  174.8 37.2 %copy-start.37 = (bf16[4,512,2,64]{1,3,2,0:T(8,128)(2,1)S(1)}, bf16[4,512,2,64]{1,3,2,0:T(8,128)(2,1)}, u32[]{:S(2)}) copy-start(bf16[4,512,2,64]{1,3,2,0:T(8,128)(2,1)} %copy-done.36) | copy-start | bytes 1572868
  213.6 9.2 %copy-start.48 = (f32[512,128]{1,0:T(8,128)S(1)}, f32[512,128]{1,0:T(8,128)}, u32[]{:S(2)}) copy-start(f32[512,128]{1,0:T(8,128)} %param.37) | copy-start | bytes 786436
  214.0 9.6 %copy-start.15 = (bf16[2,512,512]{2,1,0:T(8,128)(2,1)S(1)}, bf16[2,512,512]{2,1,0:T(8,128)(2,1)}, u32[]{:S(2)}) copy-start(bf16[2,512,512]{2,1,0:T(8,128)(2,1)} %param.24) | copy-start | bytes 3145732
  218.5 60.7 %all-to-all-start.1 = ((bf16[2,2048,128]{2,0,1:T(2,128)(2,1)}), bf16[2,2048,128]{2,0,1:T(2,128)(2,1)}, u32[]{:S(2)}, u32[]{:S(2)}) async-start(bf16[2,2048,128]{2,0,1:T(2,128)(2,1)} %copy.313), calls=%async_computation.1 | async-start | bytes 2097152 | tf_op jit(solution)/shard_map/all_to_all | solution.py:228
  222.8 82.4 %all-gather.12.cloned.1.call-start = ((), (), s32[]{:S(2)}) async-start(), calls=%async_computation.14 | async-start | bytes 2228224 | tf_op jit(solution)/shard_map/all_gather | solution.py:226
  223.5 499.3 %reduce-scatter.7.cloned.1.call-start = ((), (), s32[]{:S(2)}) async-start(), calls=%async_computation.9 | async-start | bytes 557056 | tf_op jit(solution)/shard_map/reduce_scatter | solution.py:295
  227.2 53.4 %copy-start.7 = (f32[1024,512]{0,1:T(8,128)}, f32[1024,512]{0,1:T(8,128)S(1)}, u32[]{:S(2)}) copy-start(f32[1024,512]{0,1:T(8,128)S(1)} %copy.359) | copy-start | bytes 6291460
  283.3 21.9 %copy-start.45 = (bf16[1024,512]{0,1:T(8,128)(2,1)}, bf16[1024,512]{0,1:T(8,128)(2,1)S(1)}, u32[]{:S(2)}) copy-start(bf16[1024,512]{0,1:T(8,128)(2,1)S(1)} %add_convert_fusion.2) | copy-start | bytes 3145732
  283.4 21.8 %copy-start.44 = (bf16[1024,4,128]{2,1,0:T(4,128)(2,1)S(1)}, bf16[1024,4,128]{2,1,0:T(4,128)(2,1)}, u32[]{:S(2)}) copy-start(bf16[1024,4,128]{2,1,0:T(4,128)(2,1)} %reshape_reshape.13) | copy-start | bytes 3145732
  305.2 10.0 %copy-start.33 = (bf16[2048,512]{1,0:T(8,128)(2,1)S(1)}, bf16[2048,512]{1,0:T(8,128)(2,1)}, u32[]{:S(2)}) copy-start(bf16[2048,512]{1,0:T(8,128)(2,1)} %all-gather.10.cloned.1.call-done) | copy-start | bytes 6291460
  328.1 10.1 %copy-start.46 = (bf16[1024,512]{0,1:T(8,128)(2,1)}, bf16[1024,512]{0,1:T(8,128)(2,1)S(1)}, u32[]{:S(2)}) copy-start(bf16[1024,512]{0,1:T(8,128)(2,1)S(1)} %get-tuple-element.514) | copy-start | bytes 3145732
  330.1 414.4 %reduce-scatter.9.cloned.1.call-start = ((), (), s32[]{:S(2)}) async-start(), calls=%async_computation.10 | async-start | bytes 2228224 | tf_op jit(solution)/shard_map/reduce_scatter | solution.py:256
  350.3 20.1 %all-to-all-start.2 = ((bf16[2,512,512]{1,0,2:T(2,128)(2,1)}), bf16[2,512,512]{1,0,2:T(2,128)(2,1)}, u32[]{:S(2)}, u32[]{:S(2)}) async-start(bf16[2,512,512]{1,0,2:T(2,128)(2,1)} %copy.327), calls=%async_computation.2 | async-start | bytes 2097152 | tf_op jit(solution)/shard_map/all_to_all | solution.py:270
  354.5 390.0 %reduce-scatter.11.cloned.1.call-start = ((), (), s32[]{:S(2)}) async-start(), calls=%async_computation.11 | async-start | bytes 2228224 | tf_op jit(solution)/shard_map/reduce_scatter | solution.py:259
  377.3 6.9 copy-start.5
  387.1 6.8 slice-start
  410.0 6.9 copy-start.5
  419.8 6.8 slice-start
  419.8 6.8 slice-start.1
  442.4 6.9 copy-start.5
  452.2 6.8 slice-start
  475.1 6.9 copy-start.5
  484.9 6.8 slice-start
  484.9 6.8 slice-start.1
  507.5 8.8 %copy-start.3 = (bf16[2048,2,64]{0,2,1:T(8,128)(2,1)S(1)}, bf16[2048,2,64]{0,2,1:T(8,128)(2,1)}, u32[]{:S(2)}) copy-start(bf16[2048,2,64]{0,2,1:T(8,128)(2,1)} %copy-done.2) | copy-start | bytes 1572868
  507.5 8.8 %copy-start.39 = (s32[1,2048]{1,0:T(1,128)S(1)}, s32[1,2048]{1,0:T(1,128)}, u32[]{:S(2)}) copy-start(s32[1,2048]{1,0:T(1,128)} %copy-done.38) | copy-start | bytes 24580
  518.0 8.9 %copy-start.18 = (bf16[2048,2,64]{0,2,1:T(8,128)(2,1)S(1)}, bf16[2048,2,64]{0,2,1:T(8,128)(2,1)}, u32[]{:S(2)}) copy-start(bf16[2048,2,64]{0,2,1:T(8,128)(2,1)} %get-tuple-element.998) | copy-start | bytes 1572868 | tf_op jit(solution)/shard_map/while
  549.6 8.9 %copy-start.18 = (bf16[2048,2,64]{0,2,1:T(8,128)(2,1)S(1)}, bf16[2048,2,64]{0,2,1:T(8,128)(2,1)}, u32[]{:S(2)}) copy-start(bf16[2048,2,64]{0,2,1:T(8,128)(2,1)} %get-tuple-element.998) | copy-start | bytes 1572868 | tf_op jit(solution)/shard_map/while
  581.2 8.9 %copy-start.18 = (bf16[2048,2,64]{0,2,1:T(8,128)(2,1)S(1)}, bf16[2048,2,64]{0,2,1:T(8,128)(2,1)}, u32[]{:S(2)}) copy-start(bf16[2048,2,64]{0,2,1:T(8,128)(2,1)} %get-tuple-element.998) | copy-start | bytes 1572868 | tf_op jit(solution)/shard_map/while
  612.9 8.9 %copy-start.18 = (bf16[2048,2,64]{0,2,1:T(8,128)(2,1)S(1)}, bf16[2048,2,64]{0,2,1:T(8,128)(2,1)}, u32[]{:S(2)}) copy-start(bf16[2048,2,64]{0,2,1:T(8,128)(2,1)} %get-tuple-element.998) | copy-start | bytes 1572868 | tf_op jit(solution)/shard_map/while
  654.1 41.8 %all-to-all-start.3 = ((bf16[2,2048,3,128]{3,0,2,1:T(2,128)(2,1)}), bf16[2,2048,3,128]{3,0,2,1:T(2,128)(2,1)}, u32[]{:S(2)}, u32[]{:S(2)}) async-start(bf16[2,2048,3,128]{3,0,2,1:T(2,128)(2,1)} %copy.332), calls=%async_computation.3 | async-start | bytes 6291456 | tf_op jit(solution)/shard_map/all_to_all | solution.py:280
  658.9 109.6 %reduce-scatter.5.cloned.1.call-start = ((), (), s32[]{:S(2)}) async-start(), calls=%async_computation.8 | async-start | bytes 1671168 | tf_op jit(solution)/shard_map/reduce_scatter | solution.py:292
  700.2 8.6 %copy-start.13 = (bf16[2,4,512,3,128]{4,1,3,2,0:T(4,128)(2,1)}, bf16[2,4,512,3,128]{4,1,3,2,0:T(4,128)(2,1)S(1)}, u32[]{:S(2)}) copy-start(bf16[2,4,512,3,128]{4,1,3,2,0:T(4,128)(2,1)S(1)} %copy.435) | copy-start | bytes 9437188
  711.6 109.6 %all-reduce.4.cloned.1.call-start = ((), (), s32[]{:S(2)}) async-start(), calls=%async_computation.15 | async-start | bytes 720896 | tf_op jit(solution)/shard_map/psum | solution.py:300
  741.4 27.1 %copy-start.56 = (f32[1024]{0:T(1024)S(1)}, f32[1024]{0:T(1024)}, u32[]{:S(2)}) copy-start(f32[1024]{0:T(1024)} %copy-done.55) | copy-start | bytes 12292
  773.2 7.4 copy-start.65
  773.2 7.4 copy-start.66
  773.2 7.4 copy-start.72
  773.2 7.5 copy-start.67
  (88 other events, 333.4 us)
Sparse Core Ops, SparseCore 0:
  10.9 42.3 all-gather.7
  83.2 46.6 all-gather.9
  226.4 42.9 all-gather.11
  330.2 55.5 reduce-scatter.6
  389.4 60.8 reduce-scatter.8
  453.9 60.7 reduce-scatter.10
  711.7 56.7 reduce-scatter.4
  770.9 24.1 all-reduce.3
where the time goes:
time: 840 us; the launch traced here: 833 us
  matrix products  296 us (35%)
  local copies, waits for them, and re-layouts  147 us (18%)
  waiting for transfers between devices  143 us (17%)
  other arithmetic  94.5 us (11%)
  blocking collectives  91.2 us (11%)
  loops' own time  29 us (3%)
  starting transfers between devices  17.5 us (2%)
  between operations  15.5 us (2%)
    dot_general x8, matrix products, back_block(): jnp.einsum('qhd,khd->hqk', grad_rows, values, preferred_element_type=jnp....  49.7 us
    dot_general x8, matrix products, back_block(): jnp.einsum('qhd,khd->hqk', query_rows, key_rows, preferred_element_type=j...  44.1 us
    all_to_all x1, waiting for transfers between devices, body(): lax.all_to_all(qkv_rows.reshape(seq_count, block_len, 3, model_width), 'c...  42.8 us
    all_gather x1, blocking collectives, body(): lax.all_gather(mix_shard, ('col', 'row'), axis=0, tiled=True)  41.7 us
    psum x1, blocking collectives, body(): lax.psum((vector_local, up_bias_grad), ('dp', 'col', 'row'))  40.5 us
    dot_general x8, matrix products, back_block(): jnp.einsum('hqk,qhd->khd', probs_low, grad_rows, preferred_element_type=j...  39.9 us
    all_gather x1, waiting for transfers between devices, body(): lax.all_gather(qkv_shard, ('col', 'row'), axis=0, tiled=True)  39.6 us
    all_to_all x1, waiting for transfers between devices, body(): lax.all_to_all(grad_heads, 'col', split_axis=1, concat_axis=3, tiled=True)  35.1 us
  transfers between devices with their start and end apart: 12, of which 5 were waited for; matrix products, arithmetic and copies ran while one was open for 58% of the time, Pallas kernels for 0%

commit v1 on v0

v1 whole, which is shorter than its diff:
```python
import functools

import jax
import jax.numpy as jnp
from jax import lax
from jax.experimental import pallas as pl
from jax.experimental.pallas import tpu as pltpu
from jax.sharding import PartitionSpec as P

HEAD_DIM = 64
EPS = 1e-05
NEG = -1e30
BF = jnp.bfloat16
F32 = jnp.float32
VM = pl.BlockSpec(memory_space=pltpu.VMEM)
SM = pl.BlockSpec(memory_space=pltpu.SMEM)
HBM = pl.BlockSpec(memory_space=pl.ANY)
TQ = 256
TK = 256
FC = 512
RT = 256
KEEP_LB = ((0, 1, 4), (1, 4, 5))
SEND_LB = ((2, 3, 5), (0, 2, 3))


def sds(shape, dtype):
    return jax.ShapeDtypeStruct(shape, dtype)


def call(kernel, name, ins, outs, scratch=(), flops=0, nbytes=0, trans=0, **kw):
    return pl.pallas_call(
        kernel,
        name=name,
        out_shape=tuple(o for o in outs),
        in_specs=[spec for _, spec in ins],
        out_specs=tuple(VM for _ in outs),
        scratch_shapes=list(scratch),
        compiler_params=pltpu.CompilerParams(vmem_limit_bytes=60 * 1024 * 1024, **kw),
        cost_estimate=pl.CostEstimate(flops=flops, bytes_accessed=nbytes, transcendentals=trans),
    )(*[a for a, _ in ins])


def nt(a, b):
    return lax.dot_general(a, b, (((1,), (1,)), ((), ())), preferred_element_type=F32)


def nn(a, b):
    return lax.dot_general(a, b, (((1,), (0,)), ((), ())), preferred_element_type=F32)


def tn(a, b):
    return lax.dot_general(a, b, (((0,), (0,)), ((), ())), preferred_element_type=F32)


def al(value, unit):
    return pl.multiple_of(value, unit)


def normed(v):
    mean = jnp.mean(v, axis=-1, keepdims=True)
    center = v - mean
    rstd = lax.rsqrt(jnp.mean(center * center, axis=-1, keepdims=True) + EPS)
    return center * rstd, rstd


class Geo:
    def __init__(self, dp, col, row, block_len, width, hidden):
        self.dp, self.C, self.R = dp, col, row
        self.G = col // 2
        self.BL = block_len
        self.L = block_len * col
        self.T = 2 * block_len
        self.D = width
        self.FF = hidden
        self.HL = width // self.G
        self.NH = self.HL // HEAD_DIM
        self.fast = (
            dp == 2 and col == 4 and row == 4 and width == 512 and hidden == 2048 and block_len % 256 == 0
        )

    def where(self, meta):
        col = meta[1]
        return col // self.G, col % self.G

    def block(self, s, g, e, d):
        half = s if e == 0 else 1 - s
        return half * self.G + lax.rem(g - d + self.G, self.G)


def norm_kernel(geo, meta, gain, shift, *refs):
    s, g = geo.where(meta)
    pieces, out = refs[:-1], refs[-1]
    for e in range(2):
        for d in range(geo.G):
            src = pieces[e * geo.G + d]
            base = geo.block(s, g, e, d) * geo.BL

            def step(i, carry):
                v = src[pl.ds(al(i * 128, 128), 128), :].astype(F32)
                xhat, _ = normed(v)
                out[pl.ds(al(base + i * 128, 128), 128), :] = (xhat * gain[...] + shift[...]).astype(BF)
                return carry

            lax.fori_loop(0, geo.BL // 128, step, 0, unroll=2)


def qkv_kernel(geo, meta, h1, bias, *refs):
    s, g = geo.where(meta)
    HL, D = geo.HL, geo.D
    if geo.fast:
        pieces, (q, k, v, wown, wscr, sem) = refs[:8], refs[8:]
        x, z = meta[0], meta[2]
        y, c = meta[1] // 2, meta[1] % 2
        copies = []
        for quad in range(4):
            yy = y if quad < 2 else 1 - y
            hh = x if quad % 2 == 0 else 1 - x
            for cc in range(2):
                cp = c if cc == 0 else 1 - c
                for d in range(4):
                    zz = lax.rem(z - d + 4, 4)
                    copies.append(
                        pltpu.make_async_copy(
                            pieces[quad * 2 + cc].at[d],
                            wscr.at[
                                pl.ds(al(zz * 128 + hh * 64, 64), 64),
                                pl.ds(al((2 * yy + cp) * 384, 128), 384),
                            ],
                            sem,
                        )
                    )
        for cpy in copies:
            cpy.start()
        for cpy in copies:
            cpy.wait()
    else:
        w, (q, k, v, wown) = refs[0], refs[1:]
        wscr = w
    for part in range(3):
        cols = pl.ds(al(part * D + g * HL, 128), HL)
        wown[:, part * HL : (part + 1) * HL] = wscr[:, cols]
    outs = (q, k, v)

    def step(i, carry):
        rows = pl.ds(al(i * 256, 256), 256)
        a = h1[rows, :]
        for part in range(3):
            cols = pl.ds(al(part * D + g * HL, 128), HL)
            res = nn(a, wown[:, part * HL : (part + 1) * HL]) + bias[:, cols]
            outs[part][rows, :] = res.astype(BF)
        return carry

    lax.fori_loop(0, geo.L // 256, step, 0)


def doc_ends(doc, s):
    ends, total = [], 0
    for i in range(8):
        total = total + doc[s, i]
        ends.append(total)
    return ends


def span_start(ends, t):
    best = 0
    for e in ends:
        best = jnp.where(e <= t, e, best)
    return best


def span_end(ends, t, full):
    best = full
    for e in reversed(ends):
        best = jnp.where(e > t, e, best)
    return best


def fill_segments(geo, ends, segk, segq):
    def step(i, carry):
        rows = lax.broadcasted_iota(jnp.int32, (TK, 128), 0) + i * TK
        cols = lax.broadcasted_iota(jnp.int32, (8, TQ), 1) + i * TQ
        a = jnp.zeros((TK, 128), jnp.int32)
        b = jnp.zeros((8, TQ), jnp.int32)
        for e in ends:
            a += (rows >= e).astype(jnp.int32)
            b += (cols >= e).astype(jnp.int32)
        segk[pl.ds(al(i * TK, TK), TK), :] = a
        segq[:, pl.ds(al(i * TQ, TQ), TQ)] = b
        return carry

    lax.fori_loop(0, geo.L // TK, step, 0)


def mask_bias(segk, segq, k0, q0):
    a = segk[pl.ds(k0, TK), :]
    b = segq[0:1, pl.ds(q0, TQ)]
    same = jnp.concatenate([a] * (TQ // 128), axis=1) == b
    return jnp.where(same, 0.0, NEG)


def head_mask(HL, h, rows):
    lane = lax.broadcasted_iota(jnp.int32, (rows, HL), 1)
    return (lane // HEAD_DIM) == h


def attn_kernel(geo, meta, doc, q, k, v, *refs):
    G, HL, NH, L, BL = geo.G, geo.HL, geo.NH, geo.L, geo.BL
    outs, lse = refs[:G], refs[G]
    vT, segk, segq, acc, stat = refs[G + 1 :]
    s, g = geo.where(meta)
    ends = doc_ends(doc, s)
    fill_segments(geo, ends, segk, segq)

    def flip(i, carry):
        rows = pl.ds(al(i * TK, TK), TK)
        vT[:, rows] = jnp.transpose(v[rows, :])
        return carry

    lax.fori_loop(0, L // TK, flip, 0)

    def q_step(i, carry):
        q0 = al(i * TQ, TQ)
        klo = span_start(ends, q0) // TK
        khi = (span_end(ends, q0 + TQ - 1, L) + TK - 1) // TK
        qt = q[pl.ds(q0, TQ), :] * jnp.asarray(HEAD_DIM ** (-0.5), BF)
        zero = jnp.zeros_like(qt)
        qm = [jnp.where(head_mask(HL, h, TQ), qt, zero) for h in range(NH)]
        acc[...] = jnp.zeros_like(acc)
        m0 = tuple(jnp.full((1, TQ), -3e38, F32) for _ in range(NH))
        l0 = tuple(jnp.zeros((1, TQ), F32) for _ in range(NH))

        def k_step(j, ml):
            ms, ls = ml
            k0 = al(j * TK, TK)
            kt = k[pl.ds(k0, TK), :]
            bias = mask_bias(segk, segq, k0, q0)
            new_m, new_l = [], []
            for h in range(NH):
                hs = slice(h * HEAD_DIM, (h + 1) * HEAD_DIM)
                st = nt(kt, qm[h]) + bias
                mn = jnp.maximum(ms[h], jnp.max(st, axis=0, keepdims=True))
                p = jnp.exp(st - mn)
                alpha = jnp.exp(ms[h] - mn)
                new_m.append(mn)
                new_l.append(alpha * ls[h] + jnp.sum(p, axis=0, keepdims=True))
                acc[hs, :] = acc[hs, :] * alpha + nn(vT[hs, pl.ds(k0, TK)], p.astype(BF))
            return tuple(new_m), tuple(new_l)

        ms, ls = lax.fori_loop(klo, khi, k_step, (m0, l0))
        for h in range(NH):
            hs = slice(h * HEAD_DIM, (h + 1) * HEAD_DIM)
            acc[hs, :] = acc[hs, :] * (1.0 / ls[h])
            lse[h : h + 1, pl.ds(q0, TQ)] = ms[h] + jnp.log(ls[h])
        res = jnp.transpose(acc[...]).astype(BF)
        b = q0 // BL
        half, gp = b // G, lax.rem(b, G)
        e = jnp.where(half == s, 0, 1)
        off = al(q0 - b * BL, TQ)
        for d in range(G):
            @pl.when(lax.rem(g - gp + G, G) == d)
            def _():
                outs[d][e, pl.ds(off, TQ), :] = res
        return carry

    lax.fori_loop(0, L // TQ, q_step, 0)


def attn_back_kernel(geo, meta, doc, q, k, v, lse, *refs):
    G, HL, NH, L, BL = geo.G, geo.HL, geo.NH, geo.L, geo.BL
    mixed, grads = refs[:G], refs[G : 2 * G]
    out = refs[2 * G]
    qm, gm, kT, dqT, delta, segk, segq, dk, dv = refs[2 * G + 1 :]
    s, g = geo.where(meta)
    ends = doc_ends(doc, s)
    fill_segments(geo, ends, segk, segq)
    scale = HEAD_DIM ** (-0.5)
    for e in range(2):
        for d in range(G):
            base = geo.block(s, g, e, d) * BL

            def load(i, carry):
                src = pl.ds(al(i * 256, 256), 256)
                dst = pl.ds(al(base + i * 256, 256), 256)
                gt = grads[d][e, src, :]
                zero = jnp.zeros_like(gt)
                prod = jnp.transpose(gt.astype(F32) * mixed[d][e, src, :].astype(F32))
                qt = q[dst, :] * jnp.asarray(scale, BF)
                for h in range(NH):
                    hs = slice(h * HEAD_DIM, (h + 1) * HEAD_DIM)
                    keep = head_mask(HL, h, 256)
                    gm[h, dst, :] = jnp.where(keep, gt, zero)
                    qm[h, dst, :] = jnp.where(keep, qt, zero)
                    delta[h : h + 1, dst] = jnp.sum(prod[hs, :], axis=0, keepdims=True)
                kT[:, dst] = jnp.transpose(k[dst, :])
                dqT[:, dst] = jnp.zeros((HL, 256), F32)
                return carry

            lax.fori_loop(0, BL // 256, load, 0)

    def k_step(j, carry):
        k0 = al(j * TK, TK)
        qlo = span_start(ends, k0) // TQ
        qhi = (span_end(ends, k0 + TK - 1, L) + TQ - 1) // TQ
        kt = k[pl.ds(k0, TK), :]
        vt = v[pl.ds(k0, TK), :]
        dk[...] = jnp.zeros_like(dk)
        dv[...] = jnp.zeros_like(dv)

        def q_step(i, c2):
            q0 = al(i * TQ, TQ)
            qs = pl.ds(q0, TQ)
            bias = mask_bias(segk, segq, k0, q0)
            for h in range(NH):
                hs = slice(h * HEAD_DIM, (h + 1) * HEAD_DIM)
                qh, gh = qm[h, qs, :], gm[h, qs, :]
                p = jnp.exp(nt(kt, qh) + (bias - lse[h : h + 1, qs]))
                ds = (p * (nt(vt, gh) - delta[h : h + 1, qs])).astype(BF)
                dv[...] += nn(p.astype(BF), gh)
                dk[...] += nn(ds, qh)
                dqT[hs, qs] += nn(kT[hs, pl.ds(k0, TK)], ds)
            return c2

        lax.fori_loop(qlo, qhi, q_step, 0)
        out[pl.ds(k0, TK), HL : 2 * HL] = dk[...].astype(BF)
        out[pl.ds(k0, TK), 2 * HL : 3 * HL] = dv[...].astype(BF)
        return carry

    lax.fori_loop(0, L // TK, k_step, 0)

    def last(i, carry):
        rows = pl.ds(al(i * TQ, TQ), TQ)
        out[rows, 0:HL] = (jnp.transpose(dqT[:, rows]) * scale).astype(BF)
        return carry

    lax.fori_loop(0, L // TQ, last, 0)


def gelu_parts(u):
    phi = 0.5 + 0.5 * lax.erf(u * (2.0 ** -0.5))
    pdf = jnp.exp(-0.5 * (u * u)) * 0.3989422804014327
    return phi, pdf


def ffn_kernel(geo, meta, *refs):
    G, HL, D, FF, BL, T = geo.G, geo.HL, geo.D, geo.FF, geo.BL, geo.T
    s, g = geo.where(meta)
    x0, x1, cot, cot1, mixb, gain, shift, upb, downb = refs[:9]
    refs = refs[9:]
    mixed, refs = refs[:G], refs[G:]
    nw = 8 if geo.fast else 3
    wts, refs = refs[:nw], refs[nw:]
    out_own, out_send, g_resid = refs[:3]
    refs = refs[3:]
    gmix, refs = refs[:G], refs[G:]
    ng = 2 if geo.fast else 3
    packs, refs = refs[:ng], refs[ng:]
    vec, refs = refs[0], refs[1:]
    resid, h2, ffn, gh2, act_s, gu_s, ga_s, mg = refs[:8]
    refs = refs[8:]
    if geo.fast:
        wo, wu, wd, wg, sems = refs
        x, z = meta[0], meta[2]
        y, c = meta[1] // 2, meta[1] % 2
        groups = [[], [], []]
        for quad in range(4):
            yy = y if quad < 2 else 1 - y
            hh = x if quad % 2 == 0 else 1 - x
            for cc in range(2):
                cl = 2 * yy + (c if cc == 0 else 1 - c)
                src = wts[quad * 2 + cc]
                for d in range(4):
                    zz = lax.rem(z - d + 4, 4)
                    groups[0].append(
                        pltpu.make_async_copy(
                            src.at[d, pl.ds(512, 64), :],
                            wo.at[pl.ds(al(zz * 128 + hh * 64, 64), 64), pl.ds(al(cl * 128, 128), 128)],
                            sems.at[0],
                        )
                    )
                    for b in range(4):
                        groups[1].append(
                            pltpu.make_async_copy(
                                src.at[d, pl.ds(b * 64, 64), :],
                                wu.at[
                                    pl.ds(al(zz * 128 + hh * 64, 64), 64),
                                    pl.ds(al(cl * 512 + b * 128, 128), 128),
                                ],
                                sems.at[1],
                            )
                        )
                    groups[2].append(
                        pltpu.make_async_copy(
                            src.at[d, pl.ds(256, 256), :],
                            wd.at[pl.ds(al(zz * 512 + hh * 256, 256), 256), pl.ds(al(cl * 128, 128), 128)],
                            sems.at[2],
                        )
                    )
        for group in groups:
            for cpy in group:
                cpy.start()
        for cpy in groups[0]:
            cpy.wait()
    else:
        wo, wu, wd = wts
        (wg,) = refs

    zrow = jnp.zeros((1, D), F32)
    vec[...] = jnp.zeros_like(vec)

    for e in range(2):
        xe = x0 if e == 0 else x1
        ce = cot if e == 0 else cot1

        def first(i, carry):
            rows = pl.ds(al(i * RT, RT), RT)
            to = pl.ds(al(e * BL + i * RT, RT), RT)
            r = xe[rows, :].astype(F32) + mixb[...]
            for d in range(G):
                gp = lax.rem(g - d + G, G)
                r = r + nn(mixed[d][e, rows, :], wo[pl.ds(al(gp * HL, 128), HL), :])
            resid[to, :] = r
            xhat, _ = normed(r)
            h2[to, :] = (xhat * gain[...] + shift[...]).astype(BF)
            ffn[to, :] = jnp.zeros((RT, D), F32)
            gh2[to, :] = jnp.zeros((RT, D), F32)
            return carry

        lax.fori_loop(0, BL // RT, first, 0)
    ga_s[0:BL, :] = cot[...]
    ga_s[BL:T, :] = cot1[...]
    if geo.fast:
        for group in groups[1:]:
            for cpy in group:
                cpy.wait()

    def chunk(f, carry):
        f0 = al(f * FC, FC)
        fs = pl.ds(f0, FC)

        def rows_step(i, hs):
            rows = pl.ds(al(i * RT, RT), RT)
            u = nn(h2[rows, :], wu[:, fs]) + upb[:, fs]
            phi, pdf = gelu_parts(u)
            act = (u * phi).astype(BF)
            gu = (nt(ga_s[rows, :], wd[fs, :]) * (phi + u * pdf)).astype(BF)
            act_s[rows, :] = act
            gu_s[rows, :] = gu
            ffn[rows, :] += nn(act, wd[fs, :])
            gh2[rows, :] += nt(gu, wu[:, fs])
            return hs + jnp.sum(gu.astype(F32), axis=0, keepdims=True)

        hsum = lax.fori_loop(0, T // RT, rows_step, jnp.zeros((1, FC), F32))
        per = D // FC
        vec[pl.ds(8 + f // per, 1), pl.ds(al(lax.rem(f, per) * FC, 128), FC)] = hsum
        dn = tn(act_s[...], ga_s[...])
        if geo.fast:
            wg[...] = dn.astype(BF)
            zr = lax.rem(f - z + 4, 4)
            for cr in range(2):
                for yr in range(2):
                    cl = 2 * (y if yr == 0 else 1 - y) + (c if cr == 0 else 1 - c)
                    for hr in range(2):
                        hh = x if hr == 0 else 1 - x
                        packs[cr][yr * 2 + hr, zr, 256:512, :] = wg[
                            pl.ds(al(hh * 256, 256), 256), pl.ds(al(cl * 128, 128), 128)
                        ]
        else:
            packs[1][fs, :] = dn.astype(BF)
        up = tn(h2[...], gu_s[...])
        if geo.fast:
            wg[...] = up.astype(BF)
            fy, fcr = f // 2, lax.rem(f, 2)
            yr = jnp.where(fy == y, 0, 1)
            for cr in range(2):
                @pl.when((fcr == c) if cr == 0 else (fcr != c))
                def _():
                    for hr in range(2):
                        hh = x if hr == 0 else 1 - x
                        for k in range(4):
                            zz = lax.rem(z + k, 4)
                            for b in range(4):
                                packs[cr][yr * 2 + hr, k, b * 64 : b * 64 + 64, :] = wg[
                                    pl.ds(al(zz * 128 + hh * 64, 64), 64), b * 128 : b * 128 + 128
                                ]
        else:
            packs[0][:, fs] = up.astype(BF)
        return carry

    lax.fori_loop(0, FF // FC, chunk, 0)

    sums = (zrow, zrow, zrow, zrow)
    for e in range(2):
        ce = cot if e == 0 else cot1
        oe = out_own if e == 0 else out_send

        def back(i, carry):
            mb, fg, fs_, db = carry
            rows = pl.ds(al(i * RT, RT), RT)
            to = pl.ds(al(e * BL + i * RT, RT), RT)
            r = resid[to, :]
            oe[rows, :] = (r + ffn[to, :] + downb[...]).astype(BF)
            xhat, rstd = normed(r)
            gh = gh2[to, :]
            ct = ce[rows, :].astype(F32)
            gx = gh * gain[...]
            gr = ct + rstd * (
                gx
                - jnp.mean(gx, axis=-1, keepdims=True)
                - xhat * jnp.mean(gx * xhat, axis=-1, keepdims=True)
            )
            g_resid[to, :] = gr
            ga = gr.astype(BF)
            gu_s[to, 0:D] = ga
            for d in range(G):
                gp = lax.rem(g + d, G)
                gmix[d][e, rows, :] = nt(ga, wo[pl.ds(al(gp * HL, 128), HL), :]).astype(BF)
            return (
                mb + jnp.sum(ga.astype(F32), axis=0, keepdims=True),
                fg + jnp.sum(gh * xhat, axis=0, keepdims=True),
                fs_ + jnp.sum(gh, axis=0, keepdims=True),
                db + jnp.sum(ct, axis=0, keepdims=True),
            )

        sums = lax.fori_loop(0, BL // RT, back, sums)
    for i in range(4):
        vec[4 + i : 5 + i, :] = sums[i]
    for d in range(G):
        gp = lax.rem(g - d + G, G)
        part = tn(mixed[d][0], gu_s[0:BL, 0:D]) + tn(mixed[d][1], gu_s[BL:T, 0:D])
        mg[pl.ds(al(gp * HL, 128), HL), :] = part.astype(BF)
    if geo.fast:
        for cr in range(2):
            for yr in range(2):
                cl = 2 * (y if yr == 0 else 1 - y) + (c if cr == 0 else 1 - c)
                for hr in range(2):
                    hh = x if hr == 0 else 1 - x
                    for k in range(4):
                        zz = lax.rem(z + k, 4)
                        packs[cr][yr * 2 + hr, k, 512:576, :] = mg[
                            pl.ds(al(zz * 128 + hh * 64, 64), 64), pl.ds(al(cl * 128, 128), 128)
                        ]
    else:
        packs[2][...] = mg[...]


def qkv_back_kernel(geo, meta, gq, h1, w, vec_in, gain, shift, *refs):
    G, HL, D, BL, L = geo.G, geo.HL, geo.D, geo.BL, geo.L
    s, g = geo.where(meta)
    pieces, refs = refs[: 2 * G], refs[2 * G :]
    ghs, refs = refs[:G], refs[G:]
    ng = 2 if geo.fast else 1
    packs, refs = refs[:ng], refs[ng:]
    vec, wg = refs
    vec[...] = vec_in[...]
    part = tn(h1[...], gq[...])
    wg[...] = part.astype(BF)
    if geo.fast:
        x, z, c = meta[0], meta[2], meta[1] % 2
        for cr, table in ((0, KEEP_LB), (1, SEND_LB)):
            for b in range(3):
                lb = jnp.where(c == 0, table[0][b], table[1][b])
                for hr in range(2):
                    hh = x if hr == 0 else 1 - x
                    for k in range(4):
                        zz = lax.rem(z + k, 4)
                        packs[cr][b, hr, k] = wg[
                            pl.ds(al(zz * 128 + hh * 64, 64), 64), pl.ds(al(lb * 128, 128), 128)
                        ]
    else:
        for p in range(3):
            packs[0][:, pl.ds(al(p * D + g * HL, 128), HL)] = wg[:, p * HL : (p + 1) * HL]
    zrow = jnp.zeros((1, D), F32)
    zh = jnp.zeros((1, HL), F32)
    sums = (zrow, zrow, zh, zh)
    for e in range(2):
        for d in range(G):
            base = geo.block(s, g, e, d) * BL
            src = pieces[e * G + d]

            def step(i, carry):
                ng_, ns, qb, vb = carry
                rows = pl.ds(al(i * RT, RT), RT)
                at = pl.ds(al(base + i * RT, RT), RT)
                xhat, _ = normed(src[rows, :].astype(F32))
                gt = gq[at, :]
                gh = nt(gt, w[...])
                ghs[d][e, rows, :] = gh.astype(ghs[d].dtype)
                return (
                    ng_ + jnp.sum(gh * xhat, axis=0, keepdims=True),
                    ns + jnp.sum(gh, axis=0, keepdims=True),
                    qb + jnp.sum(gt[:, 0:HL].astype(F32), axis=0, keepdims=True),
                    vb + jnp.sum(gt[:, 2 * HL : 3 * HL].astype(F32), axis=0, keepdims=True),
                )

            sums = lax.fori_loop(0, BL // RT, step, sums)
    vec[0:1, :] = sums[0]
    vec[1:2, :] = sums[1]
    cols = pl.ds(al(g * HL, 128), HL)
    vec[2:3, cols] = sums[2]
    vec[3:4, cols] = sums[3]


def last_kernel(geo, meta, gain, g_resid, gh, *refs):
    G, D, BL = geo.G, geo.D, geo.BL
    s, _ = geo.where(meta)
    recv, refs = refs[: G - 1], refs[G - 1 :]
    x0, x1, out, send = refs
    for e in range(2):
        xe = x0 if e == 0 else x1

        def step(i, carry):
            rows = pl.ds(al(i * RT, RT), RT)
            to = pl.ds(al(e * BL + i * RT, RT), RT)
            xhat, rstd = normed(xe[rows, :].astype(F32))
            total = gh[e, rows, :]
            for r in recv:
                total = total + r[e, rows, :].astype(F32)
            gx = total * gain[...]
            res = g_resid[to, :] + rstd * (
                gx
                - jnp.mean(gx, axis=-1, keepdims=True)
                - xhat * jnp.mean(gx * xhat, axis=-1, keepdims=True)
            )
            if e == 0:
                out[s, rows, :] = res.astype(BF)
            else:
                send[rows, :] = res.astype(BF)
            return carry

        lax.fori_loop(0, BL // RT, step, 0)


def core_sum_kernel(own, recv, *outs):
    for q in range(4):
        outs[q][...] = (own[q].astype(F32) + recv[q].astype(F32)).astype(BF)


def arrange_kernel(geo, meta, keep, recv, vec, vrecv, p0, p1, p2, p3, vout):
    y, c = meta[1] // 2, meta[1] % 2
    outs = (p0, p1, p2, p3)
    vout[...] = vec[...] + vrecv[...]
    for cs in range(2):
        mine = sorted((lb // 2) * 4 + 2 * cs + lb % 2 for lb in KEEP_LB[cs])
        theirs = sorted((lb // 2) * 4 + 2 * (1 - cs) + lb % 2 for lb in SEND_LB[1 - cs])
        for ys in range(2):
            @pl.when(jnp.logical_and(c == cs, y == ys))
            def _():
                for yr in range(2):
                    first = 3 * (2 * (ys ^ yr) + cs)
                    for o in range(3):
                        b = first + o
                        src, slot = (keep, mine.index(b)) if b in mine else (recv, theirs.index(b))
                        for hr in range(2):
                            outs[yr * 2 + hr][:, o * 64 : o * 64 + 64, :] = src[slot, hr]


def plane_sum_kernel(has_vec, a, b, c, d, *refs):
    if has_vec:
        va, vb, vc, vd = refs[:4]
        refs = refs[4:]
        refs[4][...] = (va[...] + vb[...]) + (vc[...] + vd[...])
    for k in range(4):
        refs[k][...] = (
            (a[k].astype(F32) + b[k].astype(F32)) + (c[k].astype(F32) + d[k].astype(F32))
        ).astype(BF)


def line_sum_kernel(has_vec, a, b, c, d, *refs):
    if has_vec:
        va, vb, vc, vd = refs[:4]
        refs = refs[4:]
        refs[1][...] = (va[...] + vc[...]) + (vb[...] + vd[...])
    refs[0][...] = (
        (a[...].astype(F32) + b[...].astype(F32)) + (c[...].astype(F32) + d[...].astype(F32))
    ).astype(BF)


def finish_kernel(meta, r, o, qr, qo, qkv, mix, up, down):
    x = meta[0]
    for src, qsrc, h in ((r, qr, x), (o, qo, 1 - x)):
        rows = pl.ds(al(h * 64, 64), 64)
        for b in range(4):
            up[rows, b * 128 : b * 128 + 128] = src[b * 64 : b * 64 + 64, :].astype(F32)
        down[pl.ds(al(h * 256, 256), 256), :] = src[256:512, :].astype(F32)
        mix[rows, :] = src[512:576, :].astype(F32)
        for b in range(3):
            qkv[rows, b * 128 : b * 128 + 128] = qsrc[b * 64 : b * 64 + 64, :].astype(F32)


def pack_kernel(meta, qkv, mix, up, down, first, rest):
    h = meta[0]
    rows = pl.ds(al(h * 64, 64), 64)
    first[...] = qkv[rows, :].astype(BF)
    for b in range(4):
        rest[b * 64 : b * 64 + 64, :] = up[rows, b * 128 : b * 128 + 128].astype(BF)
    rest[256:512, :] = down[pl.ds(al(h * 256, 256), 256), :].astype(BF)
    rest[512:576, :] = mix[rows, :].astype(BF)


def body(
    tokens,
    doc_lengths,
    norm_gain,
    norm_shift,
    qkv_weight,
    query_bias,
    value_bias,
    mix_weight,
    mix_bias,
    ffn_gain,
    ffn_shift,
    up_weight,
    up_bias,
    down_weight,
    down_bias,
    cotangent,
):
    DP, C, R = lax.axis_size("dp"), lax.axis_size("col"), lax.axis_size("row")
    _, BL, D = tokens.shape
    FF = up_bias.shape[0]
    geo = Geo(DP, C, R, BL, D, FF)
    G, HL, L, T = geo.G, geo.HL, geo.L, geo.T
    ix, ic, iz = lax.axis_index("dp"), lax.axis_index("col"), lax.axis_index("row")
    s = ic // G
    meta = jnp.stack([ix, ic, iz]).astype(jnp.int32)

    def swap_half(v):
        return lax.ppermute(v, "col", [(i, (i + G) % C) for i in range(C)])

    def turn(v, d):
        return lax.ppermute(v, "col", [(i, (i // G) * G + (i % G + d) % G) for i in range(C)])

    def plane(v, dx, dy):
        pairs = [
            (i * C + j, ((i + dx) % 2) * C + (j + dy * G) % C) for i in range(2) for j in range(C)
        ]
        return lax.ppermute(v, ("dp", "col"), pairs)

    def line(v, d):
        return lax.ppermute(v, "row", [(i, (i + d) % R) for i in range(R)])

    def row2(v):
        return v.reshape(1, v.shape[0])

    def pick(v, i):
        return lax.dynamic_index_in_dim(v, i, 0, keepdims=False)

    x0 = pick(tokens, s)
    x_send = pick(tokens, 1 - s)
    x1 = swap_half(x_send)
    if geo.fast:
        half_qkv, half_rest = call(
            pack_kernel,
            "pack",
            [(meta, SM), (qkv_weight, VM), (mix_weight, VM), (up_weight, VM), (down_weight, VM)],
            [sds((64, 384), BF), sds((576, 128), BF)],
            nbytes=2 << 20,
        )

        def spread(v):
            lines = jnp.stack([v] + [line(v, d) for d in range(1, 4)])
            quads = [lines, plane(lines, 1, 0), plane(lines, 0, 1), plane(lines, 1, 1)]
            return [p for q in quads for p in (q, turn(q, 1))]

        w_qkv = spread(half_qkv)
        w_rest = spread(half_rest)
    else:
        def whole(w):
            w = lax.all_gather(w.astype(BF), "row", axis=0, tiled=True)
            return lax.all_gather(w, "col", axis=1, tiled=True)

        w_qkv = [whole(qkv_weight)]
        w_rest = [whole(mix_weight), whole(up_weight), whole(down_weight)]
    pieces = [x0] + [turn(x0, d) for d in range(1, G)]
    pieces += [x1] + [turn(x1, d) for d in range(1, G)]
    gain1, shift1 = row2(norm_gain), row2(norm_shift)
    (h1,) = call(
        functools.partial(norm_kernel, geo),
        "norm_one",
        [(meta, SM), (gain1, VM), (shift1, VM)] + [(p, VM) for p in pieces],
        [sds((L, D), BF)],
        flops=L * D * 10,
        nbytes=L * D * 4,
    )
    bias = row2(jnp.concatenate([query_bias, jnp.zeros_like(query_bias), value_bias]))
    wspec = HBM if geo.fast else VM
    q, k, v, w_own = call(
        functools.partial(qkv_kernel, geo),
        "qkv",
        [(meta, SM), (h1, VM), (bias, VM)] + [(w, wspec) for w in w_qkv],
        [sds((L, HL), BF)] * 3 + [sds((D, 3 * HL), BF)],
        scratch=[pltpu.VMEM((D, 3 * D), BF), pltpu.SemaphoreType.DMA(())] if geo.fast else [],
        flops=2 * L * D * 3 * HL,
        nbytes=L * D * 2 + L * HL * 6 + D * D * 6,
    )
    attn = call(
        functools.partial(attn_kernel, geo),
        "attend",
        [(meta, SM), (doc_lengths, SM), (q, VM), (k, VM), (v, VM)],
        [sds((2, BL, HL), BF)] * G + [sds((8, L), F32)],
        scratch=[
            pltpu.VMEM((HL, L), BF),
            pltpu.VMEM((L, 128), jnp.int32),
            pltpu.VMEM((8, L), jnp.int32),
            pltpu.VMEM((HL, TQ), F32),
            pltpu.VMEM((8, TQ), F32),
        ],
        flops=2 * L * L * HL * 4,
        nbytes=L * HL * 8,
        trans=L * L * geo.NH // 2,
    )
    mixed_all, lse = attn[:G], attn[G]
    mixed = [mixed_all[0]] + [turn(mixed_all[G - d], d) for d in range(1, G)]
    cot0 = pick(cotangent, s)
    cot1 = swap_half(pick(cotangent, 1 - s))
    packs_out = [sds((4, 4, 576, 128), BF)] * 2 if geo.fast else [sds((D, FF), BF), sds((FF, D), BF), sds((D, D), BF)]
    weights_scr = (
        [
            pltpu.VMEM((D, D), BF),
            pltpu.VMEM((D, FF), BF),
            pltpu.VMEM((FF, D), BF),
            pltpu.VMEM((FC, FC), BF),
            pltpu.SemaphoreType.DMA((3,)),
        ]
        if geo.fast
        else [pltpu.VMEM((8, 128), BF)]
    )
    res = call(
        functools.partial(ffn_kernel, geo),
        "ffn",
        [(meta, SM), (x0, VM), (x1, VM), (cot0, VM), (cot1, VM)]
        + [(row2(a), VM) for a in (mix_bias, ffn_gain, ffn_shift, up_bias, down_bias)]
        + [(m, VM) for m in mixed]
        + [(w, wspec) for w in w_rest],
        [sds((BL, D), BF), sds((BL, D), BF), sds((T, D), F32)]
        + [sds((2, BL, HL), BF)] * G
        + packs_out
        + [sds((16, D), F32)],
        scratch=[
            pltpu.VMEM((T, D), F32),
            pltpu.VMEM((T, D), BF),
            pltpu.VMEM((T, D), F32),
            pltpu.VMEM((T, D), F32),
            pltpu.VMEM((T, FC), BF),
            pltpu.VMEM((T, FC), BF),
            pltpu.VMEM((T, D), BF),
            pltpu.VMEM((D, D), BF),
        ]
        + weights_scr,
        flops=6 * T * D * (2 * FF + D),
        nbytes=20 << 20,
        trans=2 * T * FF,
    )
    out_own, out_send, g_resid = res[:3]
    gmix = res[3 : 3 + G]
    packs = res[3 + G : -1]
    vec1 = res[-1]
    ghead = [gmix[0]] + [turn(gmix[d], d) for d in range(1, G)]
    (gq,) = call(
        functools.partial(attn_back_kernel, geo),
        "attend_back",
        [(meta, SM), (doc_lengths, SM), (q, VM), (k, VM), (v, VM), (lse, VM)]
        + [(m, VM) for m in mixed_all]
        + [(m, VM) for m in ghead],
        [sds((L, 3 * HL), BF)],
        scratch=[
            pltpu.VMEM((geo.NH, L, HL), BF),
            pltpu.VMEM((geo.NH, L, HL), BF),
            pltpu.VMEM((HL, L), BF),
            pltpu.VMEM((HL, L), F32),
            pltpu.VMEM((8, L), F32),
            pltpu.VMEM((L, 128), jnp.int32),
            pltpu.VMEM((8, L), jnp.int32),
            pltpu.VMEM((TK, HL), F32),
            pltpu.VMEM((TK, HL), F32),
        ],
        flops=2 * L * L * HL * 10,
        nbytes=L * HL * 20,
        trans=L * L * geo.NH // 2,
    )
    packs2_out = [sds((3, 2, 4, 64, 128), BF)] * 2 if geo.fast else [sds((D, 3 * D), BF)]
    res2 = call(
        functools.partial(qkv_back_kernel, geo),
        "qkv_back",
        [(meta, SM), (gq, VM), (h1, VM), (w_own, VM), (vec1, VM), (gain1, VM), (shift1, VM)]
        + [(p, VM) for p in pieces],
        [sds((2, BL, D), F32)] + [sds((2, BL, D), BF)] * (G - 1) + packs2_out + [sds((16, D), F32)],
        scratch=[pltpu.VMEM((D, 3 * HL), BF)],
        flops=4 * L * D * 3 * HL,
        nbytes=16 << 20,
    )
    ghs = res2[:G]
    packs2 = res2[G:-1]
    vec2 = res2[-1]
    gh_recv = [turn(ghs[G - d], d) for d in range(1, G)]
    tgrad, tgrad_send = call(
        functools.partial(last_kernel, geo),
        "norm_back",
        [(meta, SM), (gain1, VM), (g_resid, VM), (ghs[0], VM)]
        + [(r, VM) for r in gh_recv]
        + [(x0, VM), (x1, VM)],
        [sds((2, BL, D), BF), sds((BL, D), BF)],
        flops=T * D * 30,
        nbytes=8 << 20,
    )

    if geo.fast:
        def step_plane(parts, vec=None):
            a = [parts[0], plane(parts[1], 1, 0), plane(parts[2], 0, 1), plane(parts[3], 1, 1)]
            n = parts[0].shape[1]
            outs = [sds((n, 128), BF)] * 4
            if vec is not None:
                a += [vec, plane(vec, 1, 0), plane(vec, 0, 1), plane(vec, 1, 1)]
                outs += [sds(vec.shape, F32)]
            return call(
                functools.partial(plane_sum_kernel, vec is not None),
                "plane_sum",
                [(t, VM) for t in a],
                outs,
                nbytes=n * 128 * 40,
            )

        def step_line(parts, vec=None):
            a = [parts[0]] + [line(parts[d], d) for d in range(1, 4)]
            outs = [sds(parts[0].shape, BF)]
            if vec is not None:
                a += [vec] + [line(vec, d) for d in range(1, 4)]
                outs += [sds(vec.shape, F32)]
            return call(
                functools.partial(line_sum_kernel, vec is not None),
                "line_sum",
                [(t, VM) for t in a],
                outs,
                nbytes=parts[0].size * 10,
            )

        first = call(
            core_sum_kernel,
            "core_sum",
            [(packs[0], VM), (turn(packs[1], 1), VM)],
            [sds((4, 576, 128), BF)] * 4,
            nbytes=8 << 20,
        )
        first = step_plane(first)
        (first,) = step_line(first)
        first_other = plane(first, 1, 0)
        second = call(
            functools.partial(arrange_kernel, geo),
            "arrange",
            [(meta, SM), (packs2[0], VM), (turn(packs2[1], 1), VM), (vec2, VM), (turn(vec2, 1), VM)],
            [sds((4, 192, 128), BF)] * 4 + [sds(vec2.shape, F32)],
            nbytes=2 << 20,
        )
        second = step_plane(second[:4], second[4])
        second, vec = step_line(second[:4], second[4])
        second_other = plane(second, 1, 0)
        grads = call(
            finish_kernel,
            "finish",
            [(meta, SM), (first, VM), (first_other, VM), (second, VM), (second_other, VM)],
            [
                sds(qkv_weight.shape, F32),
                sds(mix_weight.shape, F32),
                sds(up_weight.shape, F32),
                sds(down_weight.shape, F32),
            ],
            nbytes=2 << 20,
        )
    else:
        def reduced(w):
            w = lax.psum_scatter(w, "col", scatter_dimension=1, tiled=True)
            w = lax.psum_scatter(w, "row", scatter_dimension=0, tiled=True)
            return lax.psum(w, "dp").astype(F32)

        grads = (reduced(packs2[0]), reduced(packs[2]), reduced(packs[0]), reduced(packs[1]))
        vec = lax.psum(vec2, ("dp", "col", "row"))

    def join(own, other):
        return lax.dynamic_update_slice(own, other[None], (1 - s, 0, 0))

    out_pair = jnp.where(s == 0, jnp.stack([out_own, swap_half(out_send)]), jnp.stack([swap_half(out_send), out_own]))
    tgrad = join(tgrad, swap_half(tgrad_send))
    return (
        out_pair,
        tgrad,
        *grads,
        vec[:8],
        vec[8 : 8 + FF // D].reshape(FF),
    )


def solution(mesh):
    return jax.shard_map(
        body,
        mesh=mesh,
        in_specs=(
            P(("dp", "row"), "col", None),
            P(("dp", "row"), None),
            P(),
            P(),
            P("row", "col"),
            P(),
            P(),
            P("row", "col"),
            P(),
            P(),
            P(),
            P("row", "col"),
            P(),
            P("row", "col"),
            P(),
            P(("dp", "row"), "col", None),
        ),
        out_specs=(
            P(("dp", "row"), "col", None),
            P(("dp", "row"), "col", None),
            P("row", "col"),
            P("row", "col"),
            P("row", "col"),
            P("row", "col"),
            P(),
            P(),
        ),
        check_vma=False,
    )
```

time: 840 us -> 308 us (0.37)
  matrix products: 296 us -> 0 us
  Pallas kernels: 0 us -> 171 us
  local copies, waits for them, and re-layouts: 147 us -> 12.9 us
  blocking collectives: 91.2 us -> 0 us
  other arithmetic: 94.5 us -> 3.54 us
  waiting for transfers between devices: 143 us -> 71.3 us
  starting transfers between devices: 17.5 us -> 46.9 us
  loops' own time: 29 us -> 0 us
  between operations: 15.5 us -> 1.04 us
    dot_general x68 -> x0, matrix products: 296 us -> none  [the longest x8 49.7 us: back_block(): jnp.einsum('qhd,khd->hqk', grad_rows, values, preferred_element_type=jnp....]
    pallas_call x0 -> x15, Pallas kernels: none -> 171 us  [call(): pl.pallas_call(kernel, name=name, out_shape=tuple((o for o in outs)), in_...]
    all_to_all x4 -> x0, waiting for transfers between devices: 79.2 us -> none  [the longest x1 42.8 us: body(): lax.all_to_all(qkv_rows.reshape(seq_count, block_len, 3, model_width), 'c...]
    ppermute x0 -> x52, waiting for transfers between devices: none -> 71.3 us  [the longest x15 32.4 us: line(): return lax.ppermute(v, 'row', [(i, (i + d) % R) for i in range(R)])]
    reshape x10 -> x1, local copies, waits for them, and re-layouts: 51.2 us -> 0.6 us  [row2(): return v.reshape(1, v.shape[0])]
    psum x2 -> x0, blocking collectives: 49.6 us -> none  [the longest x1 40.5 us: body(): lax.psum((vector_local, up_bias_grad), ('dp', 'col', 'row'))]
    ppermute x0 -> x52, starting transfers between devices: none -> 46.9 us  [the longest x15 21.3 us: line(): return lax.ppermute(v, 'row', [(i, (i + d) % R) for i in range(R)])]
    convert_element_type x20 -> x0, other arithmetic: 45.4 us -> none  [the longest x8 30.8 us: back_block(): grad_scores = (probs * (grad_probs - inner)).astype(jnp.bfloat16)]
  transfers between devices with their start and end apart: 12 -> 52, of which waited for: 5 -> 22; matrix products, arithmetic and copies ran while one was open for 58% -> 3% of each run, Pallas kernels for 0% -> 45%
where the time goes in v1:
time: 308 us; the launch traced here: 307 us
  Pallas kernels  171 us (56%)
  waiting for transfers between devices  71.3 us (23%)
  starting transfers between devices  46.9 us (15%)
  local copies, waits for them, and re-layouts  12.9 us (4%)
  other arithmetic  3.54 us (1%)
    pallas_call x15, Pallas kernels, call(): pl.pallas_call(kernel, name=name, out_shape=tuple((o for o in outs)), in_...  171 us
    ppermute x15, waiting for transfers between devices, line(): return lax.ppermute(v, 'row', [(i, (i + d) % R) for i in range(R)])  32.4 us
    ppermute x17, waiting for transfers between devices, plane(): return lax.ppermute(v, ('dp', 'col'), pairs)  32.3 us
    ppermute x15, starting transfers between devices, line(): return lax.ppermute(v, 'row', [(i, (i + d) % R) for i in range(R)])  21.3 us
    ppermute x17, starting transfers between devices, plane(): return lax.ppermute(v, ('dp', 'col'), pairs)  18.5 us
    unnamed x92, local copies, waits for them, and re-layouts  6.75 us
    ppermute x16, waiting for transfers between devices, turn(): lax.ppermute(v, 'col', [(i, i // G * G + (i % G + d) % G) for i in range(...  6.58 us
  transfers between devices with their start and end apart: 52, of which 22 were waited for; matrix products, arithmetic and copies ran while one was open for 3% of the time, Pallas kernels for 45%

profile of v1, /device:TPU:0, one launch (start us, length us, event | category | flops | bytes accessed | tf_op | source)
XLA Modules:
  0.0 306.9 jit_solution(17791199119026354771)
XLA Ops:
  2.0 3.1 collective-permute-start
  5.7 1.9 pack.1
  7.6 3.6 %collective-permute-start.6 = (bf16[64,384]{1,0:T(8,128)(2,1)}, bf16[64,384]{1,0:T(8,128)(2,1)S(1)}, u32[]{:S(2)}, u32[]{:S(2)}) collective-permute-start(bf16[64,384]{1,0:T(8,128)(2,1)} %get-tuple-element.56), channel_id=1, source_target_pairs={{0,3},{1,0},{2,1},{3,2},{4,7},{5,4},{6,5},{7,6},{8,11},{9,8},{10,9... | collective-permute-start | bytes 147464 | tf_op jit(solution)/shard_map/ppermute | solution.py:740
  12.2 2.8 collective-permute-start.17
  15.0 2.0 collective-permute-done.5
  18.6 1.5 collective-permute-start.12
  20.1 1.5 collective-permute-start.10
  21.6 3.6 %collective-permute-start.16 = (bf16[576,128]{1,0:T(8,128)(2,1)}, bf16[576,128]{1,0:T(8,128)(2,1)S(1)}, u32[]{:S(2)}, u32[]{:S(2)}) collective-permute-start(bf16[576,128]{1,0:T(8,128)(2,1)} %get-tuple-element.62), channel_id=1, source_target_pairs={{0,2},{1,3},{2,0},{3,1},{4,6},{5,7},{6,4},{7,5},{8,10},{9,11},{10,... | collective-permute-start | bytes 442376 | tf_op jit(solution)/shard_map/ppermute | solution.py:740
  25.2 5.0 %collective-permute-done.16 = bf16[576,128]{1,0:T(8,128)(2,1)S(1)} collective-permute-done((bf16[576,128]{1,0:T(8,128)(2,1)}, bf16[576,128]{1,0:T(8,128)(2,1)S(1)}, u32[]{:S(2)}, u32[]{:S(2)}) %collective-permute-start.16) | collective-permute-done | bytes 147488 | tf_op jit(solution)/shard_map/ppermute | solution.py:740
  30.8 1.6 collective-permute-done.15
  34.4 1.6 collective-permute-done.8.refs_2_
  36.5 1.5 collective-permute-start.21
  41.8 5.0 %norm_one.1.h1 = bf16[2048,512]{1,0:T(8,128)(2,1)} custom-call(s32[3]{0:T(128)} %pad_add_fusion.meta, f32[1,512]{1,0:T(1,128)} %bitcast.43, f32[1,512]{1,0:T(1,128)} %bitcast.47, bf16[512,512]{1,0:T(8,128)(2,1)} %copy-done, bf16[512,512]{1,0:T(8,128)(2,1)} %copy-done.10, bf16[512,512]{1,0:T(8,128)(2,1)} %copy-done.2, bf16[512,512]{1,0:T(8,128)(2,1)} %copy-done.11), custom_call_target="tpu_custom_call" | custom-call | flops 10485760 | bytes 4194304 | tf_op jit(solution)/shard_map/norm_one/pallas_call | solution.py:31
  47.4 5.8 %collective-permute-done.23.refs_17_ = bf16[4,576,128]{2,1,0:T(8,128)(2,1)} collective-permute-done((bf16[4,576,128]{2,1,0:T(8,128)(2,1)S(1)}, bf16[4,576,128]{2,1,0:T(8,128)(2,1)}, u32[]{:S(2)}, u32[]{:S(2)}) %collective-permute-start.23) | collective-permute-done | bytes 589856 | tf_op jit(solution)/shard_map/ppermute | solution.py:737
  53.2 10.4 %collective-permute-done.21.refs_15_ = bf16[4,576,128]{2,1,0:T(8,128)(2,1)} collective-permute-done((bf16[4,576,128]{2,1,0:T(8,128)(2,1)S(1)}, bf16[4,576,128]{2,1,0:T(8,128)(2,1)}, u32[]{:S(2)}, u32[]{:S(2)}) %collective-permute-start.21) | collective-permute-done | bytes 589856 | tf_op jit(solution)/shard_map/ppermute | solution.py:737
  64.2 7.6 %qkv.3 = (bf16[2048,256]{1,0:T(8,128)(2,1)}, bf16[2048,256]{1,0:T(8,128)(2,1)}, bf16[2048,256]{1,0:T(8,128)(2,1)}, bf16[512,768]{1,0:T(8,128)(2,1)}) custom-call(s32[3]{0:T(128)} %pad_add_fusion.meta, bf16[2048,512]{1,0:T(8,128)(2,1)} %norm_one.1.h1, f32[1,1536]{1,0:T(1,128)} %reshape.50.bias, bf16[4,64,384]{2,1,0:T(8,128)(2,1)} %copy-done.14, ...), custom_call_target="tpu_custom_call" | custom-call | flops 1610612736 | bytes 6815744 | tf_op jit(solution)/shard_map/qkv/pallas_call | solution.py:31
  71.8 44.0 %attend.1 = (bf16[2,512,256]{2,1,0:T(8,128)(2,1)}, bf16[2,512,256]{2,1,0:T(8,128)(2,1)}, f32[8,2048]{1,0:T(8,128)}) custom-call(s32[3]{0:T(128)} %pad_add_fusion.meta, s32[2,8]{1,0:T(2,128)} %doc.3, bf16[2048,256]{1,0:T(8,128)(2,1)} %get-tuple-element.57.q, bf16[2048,256]{1,0:T(8,128)(2,1)} %get-tuple-element.58.k, bf16[2048,256]{1,0:T(8,128)(2,1)} %get-tuple-element.59.v), custom_call_target="tpu_custom_call" | custom-call | flops 8589934592 | bytes 4194304 | tf_op jit(solution)/shard_map/attend/pallas_call | solution.py:31
  116.0 2.0 collective-permute-done.14.refs_10_
  118.8 30.6 %ffn.1 = (bf16[512,512]{1,0:T(8,128)(2,1)}, bf16[512,512]{1,0:T(8,128)(2,1)}, f32[1024,512]{1,0:T(8,128)}, bf16[2,512,256]{2,1,0:T(8,128)(2,1)}, bf16[2,512,256]...) custom-call(s32[3]{0:T(128)} %pad_add_fusion.meta, ...), custom_call_target="tpu_custom_call" | custom-call | flops 14495514624 | bytes 20971520 | tf_op jit(solution)/shard_map/ffn/pallas_call | solution.py:31
  150.0 1.6 collective-permute-done.26.refs_3_
  152.4 50.7 %attend_back.1.gq = bf16[2048,768]{1,0:T(8,128)(2,1)} custom-call(s32[3]{0:T(128)} %pad_add_fusion.meta, s32[2,8]{1,0:T(2,128)} %doc.3, bf16[2048,256]{1,0:T(8,128)(2,1)} %get-tuple-element.57.q, bf16[2048,256]{1,0:T(8,128)(2,1)} %get-tuple-element.58.k, bf16[2048,256]{1,0:T(8,128)(2,1)} %get-tuple-element.59.v, f32[8,2048]{1,0:T(8,128)} %get-tuple-element.66.lse, ...), custom_call_target="tpu_custom_call" | custom-call | flops 21474836480 | bytes 10485760 | tf_op jit(solution)/shard_map/attend_back/pallas_call | solution.py:31
  203.1 10.4 %qkv_back.1 = (f32[2,512,512]{2,1,0:T(8,128)}, bf16[2,512,512]{2,1,0:T(8,128)(2,1)}, bf16[3,2,4,64,128]{4,3,2,1,0:T(8,128)(2,1)}, bf16[3,2,4,64,128]{4,3,2,1,0:T(8,128)(2,1)}, f32[16,512]{1,0:T(8,128)}) custom-call(s32[3]{0:T(128)} %pad_add_fusion.meta, bf16[2048,768]{1,0:T(8,128)(2,1)} %attend_back.1.gq, bf16[2048,512]{1,0:T(8,128)(2,1)} %norm_one.1.h1, ...), custom_call_target="tpu_custom_call" | custom-call | flops 3221225472 | bytes 16777216 | tf_op jit(solution)/shard_map/qkv_back/pallas_call | solution.py:31
  214.2 2.9 collective-permute-done.38.vrecv
  217.7 2.1 arrange.1
  220.2 1.5 collective-permute-start.43
  221.7 3.0 collective-permute-done.44.refs_3_
  225.3 4.7 %collective-permute-done.43.refs_2_ = f32[16,512]{1,0:T(8,128)S(1)} collective-permute-done((f32[16,512]{1,0:T(8,128)}, f32[16,512]{1,0:T(8,128)S(1)}, u32[]{:S(2)}, u32[]{:S(2)}) %collective-permute-start.43) | collective-permute-done | bytes 32800 | tf_op jit(solution)/shard_map/ppermute | solution.py:737
  231.0 2.5 collective-permute-start.41
  233.5 3.9 %core_sum.1 = (bf16[4,576,128]{2,1,0:T(8,128)(2,1)}, bf16[4,576,128]{2,1,0:T(8,128)(2,1)}, bf16[4,576,128]{2,1,0:T(8,128)(2,1)}, bf16[4,576,128]{2,1,0:T(8,128)(2,1)}) custom-call(bf16[4,4,576,128]{3,2,1,0:T(8,128)(2,1)} %get-tuple-element.75.own, bf16[4,4,576,128]{3,2,1,0:T(8,128)(2,1)} %copy-done.1), custom_call_target="tpu_custom_call" | custom-call | bytes 8388608 | tf_op jit(solution)/shard_map/core_sum/pallas_call | solution.py:31
  238.5 1.9 collective-permute-done.40.c
  240.4 1.7 collective-permute-done.41.d
  242.0 3.2 %collective-permute-start.32 = (bf16[4,576,128]{2,1,0:T(8,128)(2,1)}, bf16[4,576,128]{2,1,0:T(8,128)(2,1)S(1)}, u32[]{:S(2)}, u32[]{:S(2)}) collective-permute-start(bf16[4,576,128]{2,1,0:T(8,128)(2,1)} %get-tuple-element.80), channel_id=1, source_target_pairs={{0,24},{4,28},{8,16},{12,20},{16,8},{20,12},{24,0},{28,4},{1,25},{... | collective-permute-start | bytes 1769480 | tf_op jit(solution)/shard_map/ppermute | solution.py:737
  245.2 2.0 plane_sum.3
  247.2 3.1 %collective-permute-start.50 = (f32[16,512]{1,0:T(8,128)}, f32[16,512]{1,0:T(8,128)S(1)}, u32[]{:S(2)}, u32[]{:S(2)}) collective-permute-start(f32[16,512]{1,0:T(8,128)} %get-tuple-element.97.refs_0_), channel_id=1, source_target_pairs={{0,3},{1,0},{2,1},{3,2},{4,7},{5,4},{6,5},{7,6},{8,11},{9,8},{10,9... | collective-permute-start | bytes 98312 | tf_op jit(solution)/shard_map/ppermute | solution.py:740
  250.2 2.9 collective-permute-start.49
  253.2 5.2 %norm_back.1 = (bf16[2,512,512]{2,1,0:T(8,128)(2,1)}, bf16[512,512]{1,0:T(8,128)(2,1)}) custom-call(s32[3]{0:T(128)} %pad_add_fusion.meta, f32[1,512]{1,0:T(1,128)} %bitcast.45, f32[1024,512]{1,0:T(8,128)} %get-tuple-element.65.g_resid, f32[2,512,512]{2,1,0:T(8,128)} %get-tuple-element.71.gh, bf16[2,512,512]{2,1,0:T(8,128)(2,1)} %copy-done.4, ...), custom_call_target="tpu_custom_call" | custom-call | flops 15728640 | bytes 8388608 | tf_op jit(solution)/shard_map/norm_back/pallas_call | solution.py:31
  258.9 5.3 %collective-permute-done.48.refs_1_ = f32[16,512]{1,0:T(8,128)S(1)} collective-permute-done((f32[16,512]{1,0:T(8,128)S(1)}, f32[16,512]{1,0:T(8,128)S(1)}, u32[]{:S(2)}, u32[]{:S(2)}) %collective-permute-start.48) | collective-permute-done | bytes 32800 | tf_op jit(solution)/shard_map/ppermute | solution.py:740
  264.2 6.4 %collective-permute-done.45.b = bf16[192,128]{1,0:T(8,128)(2,1)S(1)} collective-permute-done((bf16[192,128]{1,0:T(8,128)(2,1)}, bf16[192,128]{1,0:T(8,128)(2,1)S(1)}, u32[]{:S(2)}, u32[]{:S(2)}) %collective-permute-start.45) | collective-permute-done | bytes 49184 | tf_op jit(solution)/shard_map/ppermute | solution.py:740
  270.7 5.0 %collective-permute-done.46.c = bf16[192,128]{1,0:T(8,128)(2,1)S(1)} collective-permute-done((bf16[192,128]{1,0:T(8,128)(2,1)S(1)}, bf16[192,128]{1,0:T(8,128)(2,1)S(1)}, u32[]{:S(2)}, u32[]{:S(2)}) %collective-permute-start.46) | collective-permute-done | bytes 49184 | tf_op jit(solution)/shard_map/ppermute | solution.py:740
  276.8 2.9 collective-permute-done.47.d
  280.4 1.6 line_sum.3
  284.5 2.5 plane_sum.2
  287.0 2.4 collective-permute-start.34
  294.4 2.1 collective-permute-done.34.c
  297.1 1.9 line_sum.2.r
  299.8 1.9 bitcast_dynamic-update-slice_fusion
  301.7 2.6 collective-permute-done.36.o
  305.0 1.9 finish.1
  (174 shorter events, 31.1 us)
Async XLA Ops:
  2.0 31.0 %collective-permute-start = (bf16[512,512]{1,0:T(8,128)(2,1)S(1)}, bf16[512,512]{1,0:T(8,128)(2,1)S(1)}, u32[]{:S(2)}, u32[]{:S(2)}) collective-permute-start(bf16[512,512]{1,0:T(8,128)(2,1)S(1)} %get-tuple-element.106), channel_id=1, source_target_pairs={{0,8},{4,12},{8,0},{12,4},{1,9},{5,13},{9,1},{13,5},{2,10},{6,14},... | collective-permute-start | bytes 1572872 | tf_op jit(solution)/shard_map/ppermute | solution.py:728
  7.6 7.4 %collective-permute-start.6 = (bf16[64,384]{1,0:T(8,128)(2,1)}, bf16[64,384]{1,0:T(8,128)(2,1)S(1)}, u32[]{:S(2)}, u32[]{:S(2)}) collective-permute-start(bf16[64,384]{1,0:T(8,128)(2,1)} %get-tuple-element.56), channel_id=1, source_target_pairs={{0,3},{1,0},{2,1},{3,2},{4,7},{5,4},{6,5},{7,6},{8,11},{9,8},{10,9... | collective-permute-start | bytes 147464 | tf_op jit(solution)/shard_map/ppermute | solution.py:740
  11.2 5.9 %collective-permute-start.5 = (bf16[64,384]{1,0:T(8,128)(2,1)}, bf16[64,384]{1,0:T(8,128)(2,1)S(1)}, u32[]{:S(2)}, u32[]{:S(2)}) collective-permute-start(bf16[64,384]{1,0:T(8,128)(2,1)} %get-tuple-element.56), channel_id=1, source_target_pairs={{0,2},{1,3},{2,0},{3,1},{4,6},{5,7},{6,4},{7,5},{8,10},{9,11},{10,... | collective-permute-start | bytes 147464 | tf_op jit(solution)/shard_map/ppermute | solution.py:740
  11.2 6.6 %collective-permute-start.4 = (bf16[64,384]{1,0:T(8,128)(2,1)}, bf16[64,384]{1,0:T(8,128)(2,1)S(1)}, u32[]{:S(2)}, u32[]{:S(2)}) collective-permute-start(bf16[64,384]{1,0:T(8,128)(2,1)} %get-tuple-element.56), channel_id=1, source_target_pairs={{0,1},{1,2},{2,3},{3,0},{4,5},{5,6},{6,7},{7,4},{8,9},{9,10},{10,1... | collective-permute-start | bytes 147464 | tf_op jit(solution)/shard_map/ppermute | solution.py:740
  12.2 13.1 %collective-permute-start.17 = (bf16[576,128]{1,0:T(8,128)(2,1)}, bf16[576,128]{1,0:T(8,128)(2,1)S(1)}, u32[]{:S(2)}, u32[]{:S(2)}) collective-permute-start(bf16[576,128]{1,0:T(8,128)(2,1)} %get-tuple-element.62), channel_id=1, source_target_pairs={{0,3},{1,0},{2,1},{3,2},{4,7},{5,4},{6,5},{7,6},{8,11},{9,8},{10,9... | collective-permute-start | bytes 442376 | tf_op jit(solution)/shard_map/ppermute | solution.py:740
  18.6 13.8 %collective-permute-start.12 = (bf16[4,64,384]{2,1,0:T(8,128)(2,1)S(1)}, bf16[4,64,384]{2,1,0:T(8,128)(2,1)S(1)}, u32[]{:S(2)}, u32[]{:S(2)}) collective-permute-start(bf16[4,64,384]{2,1,0:T(8,128)(2,1)S(1)} %pad_maximum_fusion.1.refs_0_), channel_id=1, source_target_pairs={{0,24},{4,28},{8,16},{12,20},{16,8},{20,12},{24,0},{28,4},{1,25},{... | collective-permute-start | bytes 589832 | tf_op jit(solution)/shard_map/ppermute | solution.py:737
  20.1 12.8 %collective-permute-start.10 = (bf16[4,64,384]{2,1,0:T(8,128)(2,1)S(1)}, bf16[4,64,384]{2,1,0:T(8,128)(2,1)}, u32[]{:S(2)}, u32[]{:S(2)}) collective-permute-start(bf16[4,64,384]{2,1,0:T(8,128)(2,1)S(1)} %pad_maximum_fusion.1.refs_0_), channel_id=1, source_target_pairs={{0,8},{4,12},{8,0},{12,4},{16,24},{20,28},{24,16},{28,20},{1,9},{5... | collective-permute-start | bytes 589832 | tf_op jit(solution)/shard_map/ppermute | solution.py:737
  21.6 8.6 %collective-permute-start.16 = (bf16[576,128]{1,0:T(8,128)(2,1)}, bf16[576,128]{1,0:T(8,128)(2,1)S(1)}, u32[]{:S(2)}, u32[]{:S(2)}) collective-permute-start(bf16[576,128]{1,0:T(8,128)(2,1)} %get-tuple-element.62), channel_id=1, source_target_pairs={{0,2},{1,3},{2,0},{3,1},{4,6},{5,7},{6,4},{7,5},{8,10},{9,11},{10,... | collective-permute-start | bytes 442376 | tf_op jit(solution)/shard_map/ppermute | solution.py:740
  25.2 7.2 %collective-permute-start.15 = (bf16[576,128]{1,0:T(8,128)(2,1)}, bf16[576,128]{1,0:T(8,128)(2,1)S(1)}, u32[]{:S(2)}, u32[]{:S(2)}) collective-permute-start(bf16[576,128]{1,0:T(8,128)(2,1)} %get-tuple-element.62), channel_id=1, source_target_pairs={{0,1},{1,2},{2,3},{3,0},{4,5},{5,6},{6,7},{7,4},{8,9},{9,10},{10,1... | collective-permute-start | bytes 442376 | tf_op jit(solution)/shard_map/ppermute | solution.py:740
  30.3 5.8 %collective-permute-start.8 = (bf16[4,64,384]{2,1,0:T(8,128)(2,1)S(1)}, bf16[4,64,384]{2,1,0:T(8,128)(2,1)}, u32[]{:S(2)}, u32[]{:S(2)}) collective-permute-start(bf16[4,64,384]{2,1,0:T(8,128)(2,1)S(1)} %pad_maximum_fusion.1.refs_0_), channel_id=1, source_target_pairs={{0,16},{4,20},{8,24},{12,28},{16,0},{20,4},{24,8},{28,12},{1,17},{... | collective-permute-start | bytes 589832 | tf_op jit(solution)/shard_map/ppermute | solution.py:737
  32.4 4.1 %collective-permute-start.7 = (bf16[4,64,384]{2,1,0:T(8,128)(2,1)S(1)}, bf16[4,64,384]{2,1,0:T(8,128)(2,1)S(1)}, u32[]{:S(2)}, u32[]{:S(2)}) collective-permute-start(bf16[4,64,384]{2,1,0:T(8,128)(2,1)S(1)} %pad_maximum_fusion.1.refs_0_), channel_id=1, source_target_pairs={{0,4},{4,0},{8,12},{12,8},{1,5},{5,1},{9,13},{13,9},{2,6},{6,2},{1... | collective-permute-start | bytes 589832 | tf_op jit(solution)/shard_map/ppermute | solution.py:731
  32.4 5.6 %collective-permute-start.13 = (bf16[4,64,384]{2,1,0:T(8,128)(2,1)S(1)}, bf16[4,64,384]{2,1,0:T(8,128)(2,1)S(1)}, u32[]{:S(2)}, u32[]{:S(2)}) collective-permute-start(bf16[4,64,384]{2,1,0:T(8,128)(2,1)S(1)} %collective-permute-done.12.refs_6_), channel_id=1, source_target_pairs={{0,4},{4,0},{8,12},{12,8},{1,5},{5,1},{9,13},{13,9},{2,6},{6,2},{1... | collective-permute-start | bytes 589832 | tf_op jit(solution)/shard_map/ppermute | solution.py:731
  32.9 6.6 %collective-permute-start.2 = (bf16[512,512]{1,0:T(8,128)(2,1)S(1)}, bf16[512,512]{1,0:T(8,128)(2,1)S(1)}, u32[]{:S(2)}, u32[]{:S(2)}) collective-permute-start(bf16[512,512]{1,0:T(8,128)(2,1)S(1)} %get-tuple-element.107.refs_0_.refs_1_), channel_id=1, source_target_pairs={{0,4},{4,0},{8,12},{12,8},{1,5},{5,1},{9,13},{13,9},{2,6},{6,2},{1... | collective-permute-start | bytes 1572872 | tf_op jit(solution)/shard_map/ppermute | solution.py:731
  33.0 6.6 %collective-permute-start.3 = (bf16[512,512]{1,0:T(8,128)(2,1)S(1)}, bf16[512,512]{1,0:T(8,128)(2,1)S(1)}, u32[]{:S(2)}, u32[]{:S(2)}) collective-permute-start(bf16[512,512]{1,0:T(8,128)(2,1)S(1)} %collective-permute-done.refs_2_.refs_1_), channel_id=1, source_target_pairs={{0,4},{4,0},{8,12},{12,8},{1,5},{5,1},{9,13},{13,9},{2,6},{6,2},{1... | collective-permute-start | bytes 1572872 | tf_op jit(solution)/shard_map/ppermute | solution.py:731
  36.0 17.2 %collective-permute-start.23 = (bf16[4,576,128]{2,1,0:T(8,128)(2,1)S(1)}, bf16[4,576,128]{2,1,0:T(8,128)(2,1)}, u32[]{:S(2)}, u32[]{:S(2)}) collective-permute-start(bf16[4,576,128]{2,1,0:T(8,128)(2,1)S(1)} %pad_maximum_fusion.refs_11_), channel_id=1, source_target_pairs={{0,24},{4,28},{8,16},{12,20},{16,8},{20,12},{24,0},{28,4},{1,25},{... | collective-permute-start | bytes 1769480 | tf_op jit(solution)/shard_map/ppermute | solution.py:737
  36.5 27.2 %collective-permute-start.21 = (bf16[4,576,128]{2,1,0:T(8,128)(2,1)S(1)}, bf16[4,576,128]{2,1,0:T(8,128)(2,1)}, u32[]{:S(2)}, u32[]{:S(2)}) collective-permute-start(bf16[4,576,128]{2,1,0:T(8,128)(2,1)S(1)} %pad_maximum_fusion.refs_11_), channel_id=1, source_target_pairs={{0,8},{4,12},{8,0},{12,4},{16,24},{20,28},{24,16},{28,20},{1,9},{5... | collective-permute-start | bytes 1769480 | tf_op jit(solution)/shard_map/ppermute | solution.py:737
  38.0 25.6 %collective-permute-start.19 = (bf16[4,576,128]{2,1,0:T(8,128)(2,1)S(1)}, bf16[4,576,128]{2,1,0:T(8,128)(2,1)}, u32[]{:S(2)}, u32[]{:S(2)}) collective-permute-start(bf16[4,576,128]{2,1,0:T(8,128)(2,1)S(1)} %pad_maximum_fusion.refs_11_), channel_id=1, source_target_pairs={{0,16},{4,20},{8,24},{12,28},{16,0},{20,4},{24,8},{28,12},{1,17},{... | collective-permute-start | bytes 1769480 | tf_op jit(solution)/shard_map/ppermute | solution.py:737
  39.5 7.3 %collective-permute-start.11 = (bf16[4,64,384]{2,1,0:T(8,128)(2,1)}, bf16[4,64,384]{2,1,0:T(8,128)(2,1)}, u32[]{:S(2)}, u32[]{:S(2)}) collective-permute-start(bf16[4,64,384]{2,1,0:T(8,128)(2,1)} %collective-permute-done.10.refs_4_), channel_id=1, source_target_pairs={{0,4},{4,0},{8,12},{12,8},{1,5},{5,1},{9,13},{13,9},{2,6},{6,2},{1... | collective-permute-start | bytes 589832 | tf_op jit(solution)/shard_map/ppermute | solution.py:731
  39.6 7.8 %collective-permute-start.9 = (bf16[4,64,384]{2,1,0:T(8,128)(2,1)}, bf16[4,64,384]{2,1,0:T(8,128)(2,1)}, u32[]{:S(2)}, u32[]{:S(2)}) collective-permute-start(bf16[4,64,384]{2,1,0:T(8,128)(2,1)} %collective-permute-done.8.refs_2_), channel_id=1, source_target_pairs={{0,4},{4,0},{8,12},{12,8},{1,5},{5,1},{9,13},{13,9},{2,6},{6,2},{1... | collective-permute-start | bytes 589832 | tf_op jit(solution)/shard_map/ppermute | solution.py:731
  46.8 69.0 %collective-permute-start.1 = (bf16[512,512]{1,0:T(8,128)(2,1)S(1)}, bf16[512,512]{1,0:T(8,128)(2,1)S(1)}, u32[]{:S(2)}, u32[]{:S(2)}) collective-permute-start(bf16[512,512]{1,0:T(8,128)(2,1)S(1)} %copy-done.12), channel_id=1, source_target_pairs={{0,8},{4,12},{8,0},{12,4},{1,9},{5,13},{9,1},{13,5},{2,10},{6,14},... | collective-permute-start | bytes 1572872 | tf_op jit(solution)/shard_map/ppermute | solution.py:728
  47.4 68.5 %collective-permute-start.18 = (bf16[4,576,128]{2,1,0:T(8,128)(2,1)S(1)}, bf16[4,576,128]{2,1,0:T(8,128)(2,1)S(1)}, u32[]{:S(2)}, u32[]{:S(2)}) collective-permute-start(bf16[4,576,128]{2,1,0:T(8,128)(2,1)S(1)} %pad_maximum_fusion.refs_11_), channel_id=1, source_target_pairs={{0,4},{4,0},{8,12},{12,8},{1,5},{5,1},{9,13},{13,9},{2,6},{6,2},{1... | collective-permute-start | bytes 1769480 | tf_op jit(solution)/shard_map/ppermute | solution.py:731
  53.2 62.7 %collective-permute-start.24 = (bf16[4,576,128]{2,1,0:T(8,128)(2,1)}, bf16[4,576,128]{2,1,0:T(8,128)(2,1)S(1)}, u32[]{:S(2)}, u32[]{:S(2)}) collective-permute-start(bf16[4,576,128]{2,1,0:T(8,128)(2,1)} %collective-permute-done.23.refs_17_), channel_id=1, source_target_pairs={{0,4},{4,0},{8,12},{12,8},{1,5},{5,1},{9,13},{13,9},{2,6},{6,2},{1... | collective-permute-start | bytes 1769480 | tf_op jit(solution)/shard_map/ppermute | solution.py:731
  63.7 52.3 %collective-permute-start.22 = (bf16[4,576,128]{2,1,0:T(8,128)(2,1)}, bf16[4,576,128]{2,1,0:T(8,128)(2,1)S(1)}, u32[]{:S(2)}, u32[]{:S(2)}) collective-permute-start(bf16[4,576,128]{2,1,0:T(8,128)(2,1)} %collective-permute-done.21.refs_15_), channel_id=1, source_target_pairs={{0,4},{4,0},{8,12},{12,8},{1,5},{5,1},{9,13},{13,9},{2,6},{6,2},{1... | collective-permute-start | bytes 1769480 | tf_op jit(solution)/shard_map/ppermute | solution.py:731
  63.7 52.3 %collective-permute-start.20 = (bf16[4,576,128]{2,1,0:T(8,128)(2,1)}, bf16[4,576,128]{2,1,0:T(8,128)(2,1)}, u32[]{:S(2)}, u32[]{:S(2)}) collective-permute-start(bf16[4,576,128]{2,1,0:T(8,128)(2,1)} %collective-permute-done.19.refs_13_), channel_id=1, source_target_pairs={{0,4},{4,0},{8,12},{12,8},{1,5},{5,1},{9,13},{13,9},{2,6},{6,2},{1... | collective-permute-start | bytes 1769480 | tf_op jit(solution)/shard_map/ppermute | solution.py:731
  149.6 81.4 %collective-permute-start.29 = (bf16[4,4,576,128]{3,2,1,0:T(8,128)(2,1)}, bf16[4,4,576,128]{3,2,1,0:T(8,128)(2,1)S(1)}, u32[]{:S(2)}, u32[]{:S(2)}) collective-permute-start(bf16[4,4,576,128]{3,2,1,0:T(8,128)(2,1)} %get-tuple-element.76), channel_id=1, source_target_pairs={{0,4},{4,0},{8,12},{12,8},{1,5},{5,1},{9,13},{13,9},{2,6},{6,2},{1... | collective-permute-start | bytes 7077896 | tf_op jit(solution)/shard_map/ppermute | solution.py:731
  213.5 36.7 %collective-permute-start.27 = (bf16[2,512,512]{2,1,0:T(8,128)(2,1)}, bf16[2,512,512]{2,1,0:T(8,128)(2,1)S(1)}, u32[]{:S(2)}, u32[]{:S(2)}) collective-permute-start(bf16[2,512,512]{2,1,0:T(8,128)(2,1)} %get-tuple-element.72), channel_id=1, source_target_pairs={{0,4},{4,0},{8,12},{12,8},{1,5},{5,1},{9,13},{13,9},{2,6},{6,2},{1... | collective-permute-start | bytes 3145736 | tf_op jit(solution)/shard_map/ppermute | solution.py:731
  214.2 33.0 %collective-permute-start.25 = (bf16[512,512]{1,0:T(8,128)(2,1)}, bf16[512,512]{1,0:T(8,128)(2,1)S(1)}, u32[]{:S(2)}, u32[]{:S(2)}) collective-permute-start(bf16[512,512]{1,0:T(8,128)(2,1)} %get-tuple-element.64), channel_id=1, source_target_pairs={{0,8},{4,12},{8,0},{12,4},{1,9},{5,13},{9,1},{13,5},{2,10},{6,14},... | collective-permute-start | bytes 1572872 | tf_op jit(solution)/shard_map/ppermute | solution.py:728
  219.7 5.0 %collective-permute-start.44 = (f32[16,512]{1,0:T(8,128)}, f32[16,512]{1,0:T(8,128)S(1)}, u32[]{:S(2)}, u32[]{:S(2)}) collective-permute-start(f32[16,512]{1,0:T(8,128)} %get-tuple-element.92.refs_0_), channel_id=1, source_target_pairs={{0,24},{4,28},{8,16},{12,20},{16,8},{20,12},{24,0},{28,4},{1,25},{... | collective-permute-start | bytes 98312 | tf_op jit(solution)/shard_map/ppermute | solution.py:737
  220.2 9.7 %collective-permute-start.43 = (f32[16,512]{1,0:T(8,128)}, f32[16,512]{1,0:T(8,128)S(1)}, u32[]{:S(2)}, u32[]{:S(2)}) collective-permute-start(f32[16,512]{1,0:T(8,128)} %get-tuple-element.92.refs_0_), channel_id=1, source_target_pairs={{0,8},{4,12},{8,0},{12,4},{16,24},{20,28},{24,16},{28,20},{1,9},{5... | collective-permute-start | bytes 98312 | tf_op jit(solution)/shard_map/ppermute | solution.py:737
  224.8 5.7 %collective-permute-start.42 = (f32[16,512]{1,0:T(8,128)}, f32[16,512]{1,0:T(8,128)S(1)}, u32[]{:S(2)}, u32[]{:S(2)}) collective-permute-start(f32[16,512]{1,0:T(8,128)} %get-tuple-element.92.refs_0_), channel_id=1, source_target_pairs={{0,16},{4,20},{8,24},{12,28},{16,0},{20,4},{24,8},{28,12},{1,17},{... | collective-permute-start | bytes 98312 | tf_op jit(solution)/shard_map/ppermute | solution.py:737
  230.0 8.0 %collective-permute-start.39 = (bf16[4,192,128]{2,1,0:T(8,128)(2,1)}, bf16[4,192,128]{2,1,0:T(8,128)(2,1)S(1)}, u32[]{:S(2)}, u32[]{:S(2)}) collective-permute-start(bf16[4,192,128]{2,1,0:T(8,128)(2,1)} %get-tuple-element.89), channel_id=1, source_target_pairs={{0,16},{4,20},{8,24},{12,28},{16,0},{20,4},{24,8},{28,12},{1,17},{... | collective-permute-start | bytes 589832 | tf_op jit(solution)/shard_map/ppermute | solution.py:737
  230.5 9.9 %collective-permute-start.40 = (bf16[4,192,128]{2,1,0:T(8,128)(2,1)}, bf16[4,192,128]{2,1,0:T(8,128)(2,1)}, u32[]{:S(2)}, u32[]{:S(2)}) collective-permute-start(bf16[4,192,128]{2,1,0:T(8,128)(2,1)} %get-tuple-element.90), channel_id=1, source_target_pairs={{0,8},{4,12},{8,0},{12,4},{16,24},{20,28},{24,16},{28,20},{1,9},{5... | collective-permute-start | bytes 589832 | tf_op jit(solution)/shard_map/ppermute | solution.py:737
  231.0 11.0 %collective-permute-start.41 = (bf16[4,192,128]{2,1,0:T(8,128)(2,1)}, bf16[4,192,128]{2,1,0:T(8,128)(2,1)}, u32[]{:S(2)}, u32[]{:S(2)}) collective-permute-start(bf16[4,192,128]{2,1,0:T(8,128)(2,1)} %get-tuple-element.91), channel_id=1, source_target_pairs={{0,24},{4,28},{8,16},{12,20},{16,8},{20,12},{24,0},{28,4},{1,25},{... | collective-permute-start | bytes 589832 | tf_op jit(solution)/shard_map/ppermute | solution.py:737
  237.9 45.3 %collective-permute-start.30 = (bf16[4,576,128]{2,1,0:T(8,128)(2,1)}, bf16[4,576,128]{2,1,0:T(8,128)(2,1)S(1)}, u32[]{:S(2)}, u32[]{:S(2)}) collective-permute-start(bf16[4,576,128]{2,1,0:T(8,128)(2,1)} %get-tuple-element.78), channel_id=1, source_target_pairs={{0,16},{4,20},{8,24},{12,28},{16,0},{20,4},{24,8},{28,12},{1,17},{... | collective-permute-start | bytes 1769480 | tf_op jit(solution)/shard_map/ppermute | solution.py:737
  240.3 42.9 %collective-permute-start.31 = (bf16[4,576,128]{2,1,0:T(8,128)(2,1)}, bf16[4,576,128]{2,1,0:T(8,128)(2,1)S(1)}, u32[]{:S(2)}, u32[]{:S(2)}) collective-permute-start(bf16[4,576,128]{2,1,0:T(8,128)(2,1)} %get-tuple-element.79), channel_id=1, source_target_pairs={{0,8},{4,12},{8,0},{12,4},{16,24},{20,28},{24,16},{28,20},{1,9},{5... | collective-permute-start | bytes 1769480 | tf_op jit(solution)/shard_map/ppermute | solution.py:737
  242.0 41.2 %collective-permute-start.32 = (bf16[4,576,128]{2,1,0:T(8,128)(2,1)}, bf16[4,576,128]{2,1,0:T(8,128)(2,1)S(1)}, u32[]{:S(2)}, u32[]{:S(2)}) collective-permute-start(bf16[4,576,128]{2,1,0:T(8,128)(2,1)} %get-tuple-element.80), channel_id=1, source_target_pairs={{0,24},{4,28},{8,16},{12,20},{16,8},{20,12},{24,0},{28,4},{1,25},{... | collective-permute-start | bytes 1769480 | tf_op jit(solution)/shard_map/ppermute | solution.py:737
  247.2 11.2 %collective-permute-start.50 = (f32[16,512]{1,0:T(8,128)}, f32[16,512]{1,0:T(8,128)S(1)}, u32[]{:S(2)}, u32[]{:S(2)}) collective-permute-start(f32[16,512]{1,0:T(8,128)} %get-tuple-element.97.refs_0_), channel_id=1, source_target_pairs={{0,3},{1,0},{2,1},{3,2},{4,7},{5,4},{6,5},{7,6},{8,11},{9,8},{10,9... | collective-permute-start | bytes 98312 | tf_op jit(solution)/shard_map/ppermute | solution.py:740
  250.2 8.2 %collective-permute-start.49 = (f32[16,512]{1,0:T(8,128)}, f32[16,512]{1,0:T(8,128)S(1)}, u32[]{:S(2)}, u32[]{:S(2)}) collective-permute-start(f32[16,512]{1,0:T(8,128)} %get-tuple-element.97.refs_0_), channel_id=1, source_target_pairs={{0,2},{1,3},{2,0},{3,1},{4,6},{5,7},{6,4},{7,5},{8,10},{9,11},{10,... | collective-permute-start | bytes 98312 | tf_op jit(solution)/shard_map/ppermute | solution.py:740
  258.3 41.5 %collective-permute-start.28 = (bf16[512,512]{1,0:T(8,128)(2,1)}, bf16[512,512]{1,0:T(8,128)(2,1)}, u32[]{:S(2)}, u32[]{:S(2)}) collective-permute-start(bf16[512,512]{1,0:T(8,128)(2,1)} %get-tuple-element.74), channel_id=1, source_target_pairs={{0,8},{4,12},{8,0},{12,4},{1,9},{5,13},{9,1},{13,5},{2,10},{6,14},... | collective-permute-start | bytes 1572872 | tf_op jit(solution)/shard_map/ppermute | solution.py:728
  258.5 5.8 %collective-permute-start.48 = (f32[16,512]{1,0:T(8,128)S(1)}, f32[16,512]{1,0:T(8,128)S(1)}, u32[]{:S(2)}, u32[]{:S(2)}) collective-permute-start(f32[16,512]{1,0:T(8,128)S(1)} %copy-done.24), channel_id=1, source_target_pairs={{0,1},{1,2},{2,3},{3,0},{4,5},{5,6},{6,7},{7,4},{8,9},{9,10},{10,1... | collective-permute-start | bytes 98312 | tf_op jit(solution)/shard_map/ppermute | solution.py:740
  264.2 6.4 %collective-permute-start.45 = (bf16[192,128]{1,0:T(8,128)(2,1)}, bf16[192,128]{1,0:T(8,128)(2,1)S(1)}, u32[]{:S(2)}, u32[]{:S(2)}) collective-permute-start(bf16[192,128]{1,0:T(8,128)(2,1)} %get-tuple-element.94), channel_id=1, source_target_pairs={{0,1},{1,2},{2,3},{3,0},{4,5},{5,6},{6,7},{7,4},{8,9},{9,10},{10,1... | collective-permute-start | bytes 147464 | tf_op jit(solution)/shard_map/ppermute | solution.py:740
  270.7 5.0 %collective-permute-start.46 = (bf16[192,128]{1,0:T(8,128)(2,1)S(1)}, bf16[192,128]{1,0:T(8,128)(2,1)S(1)}, u32[]{:S(2)}, u32[]{:S(2)}) collective-permute-start(bf16[192,128]{1,0:T(8,128)(2,1)S(1)} %copy-done.44), channel_id=1, source_target_pairs={{0,2},{1,3},{2,0},{3,1},{4,6},{5,7},{6,4},{7,5},{8,10},{9,11},{10,... | collective-permute-start | bytes 147464 | tf_op jit(solution)/shard_map/ppermute | solution.py:740
  275.7 4.1 %collective-permute-start.47 = (bf16[192,128]{1,0:T(8,128)(2,1)S(1)}, bf16[192,128]{1,0:T(8,128)(2,1)S(1)}, u32[]{:S(2)}, u32[]{:S(2)}) collective-permute-start(bf16[192,128]{1,0:T(8,128)(2,1)S(1)} %copy-done.43), channel_id=1, source_target_pairs={{0,3},{1,0},{2,1},{3,2},{4,7},{5,4},{6,5},{7,6},{8,11},{9,8},{10,9... | collective-permute-start | bytes 147464 | tf_op jit(solution)/shard_map/ppermute | solution.py:740
  287.0 7.4 %collective-permute-start.33 = (bf16[576,128]{1,0:T(8,128)(2,1)}, bf16[576,128]{1,0:T(8,128)(2,1)S(1)}, u32[]{:S(2)}, u32[]{:S(2)}) collective-permute-start(bf16[576,128]{1,0:T(8,128)(2,1)} %get-tuple-element.82), channel_id=1, source_target_pairs={{0,1},{1,2},{2,3},{3,0},{4,5},{5,6},{6,7},{7,4},{8,9},{9,10},{10,1... | collective-permute-start | bytes 442376 | tf_op jit(solution)/shard_map/ppermute | solution.py:740
  287.0 9.4 %collective-permute-start.34 = (bf16[576,128]{1,0:T(8,128)(2,1)}, bf16[576,128]{1,0:T(8,128)(2,1)S(1)}, u32[]{:S(2)}, u32[]{:S(2)}) collective-permute-start(bf16[576,128]{1,0:T(8,128)(2,1)} %get-tuple-element.83), channel_id=1, source_target_pairs={{0,2},{1,3},{2,0},{3,1},{4,6},{5,7},{6,4},{7,5},{8,10},{9,11},{10,... | collective-permute-start | bytes 442376 | tf_op jit(solution)/shard_map/ppermute | solution.py:740
  289.4 7.1 %collective-permute-start.35 = (bf16[576,128]{1,0:T(8,128)(2,1)}, bf16[576,128]{1,0:T(8,128)(2,1)S(1)}, u32[]{:S(2)}, u32[]{:S(2)}) collective-permute-start(bf16[576,128]{1,0:T(8,128)(2,1)} %get-tuple-element.84), channel_id=1, source_target_pairs={{0,3},{1,0},{2,1},{3,2},{4,7},{5,4},{6,5},{7,6},{8,11},{9,8},{10,9... | collective-permute-start | bytes 442376 | tf_op jit(solution)/shard_map/ppermute | solution.py:740
  292.2 9.5 %collective-permute-start.51 = (bf16[192,128]{1,0:T(8,128)(2,1)S(1)}, bf16[192,128]{1,0:T(8,128)(2,1)S(1)}, u32[]{:S(2)}, u32[]{:S(2)}) collective-permute-start(bf16[192,128]{1,0:T(8,128)(2,1)S(1)} %copy-done.19), channel_id=1, source_target_pairs={{0,16},{4,20},{8,24},{12,28},{16,0},{20,4},{24,8},{28,12},{1,17},{... | collective-permute-start | bytes 147464 | tf_op jit(solution)/shard_map/ppermute | solution.py:737
  299.0 5.4 %collective-permute-start.36 = (bf16[576,128]{1,0:T(8,128)(2,1)}, bf16[576,128]{1,0:T(8,128)(2,1)S(1)}, u32[]{:S(2)}, u32[]{:S(2)}) collective-permute-start(bf16[576,128]{1,0:T(8,128)(2,1)} %line_sum.2.r), channel_id=1, source_target_pairs={{0,16},{4,20},{8,24},{12,28},{16,0},{20,4},{24,8},{28,12},{1,17},{... | collective-permute-start | bytes 442376 | tf_op jit(solution)/shard_map/ppermute | solution.py:737
  (49 other events, 427.0 us)

commit v2 on v1

--- a/solution.py
+++ b/solution.py
@@ -10,6 +10,9 @@
 HEAD_DIM = 64
 EPS = 1e-05
 NEG = -1e30
+LOG2E = 1.4426950408889634
+PW = 128
+
 BF = jnp.bfloat16
 F32 = jnp.float32
 VM = pl.BlockSpec(memory_space=pltpu.VMEM)
@@ -73,7 +76,8 @@
         self.D = width
         self.FF = hidden
         self.HL = width // self.G
-        self.NH = self.HL // HEAD_DIM
+        self.NP = self.HL // PW
+        self.TQ = min(512, block_len)
         self.fast = (
             dp == 2 and col == 4 and row == 4 and width == 512 and hidden == 2048 and block_len % 256 == 0
         )
@@ -87,9 +91,10 @@
         return half * self.G + lax.rem(g - d + self.G, self.G)
 
 
-def norm_kernel(geo, meta, gain, shift, *refs):
+def norm_kernel(geo, meta, doc, gain, shift, *refs):
     s, g = geo.where(meta)
-    pieces, out = refs[:-1], refs[-1]
+    pieces, (out, segk, segq) = refs[:-3], refs[-3:]
+    fill_segments(geo, doc_ends(doc, s), segk, segq)
     for e in range(2):
         for d in range(geo.G):
             src = pieces[e * geo.G + d]
@@ -106,9 +111,10 @@
 
 def qkv_kernel(geo, meta, h1, bias, *refs):
     s, g = geo.where(meta)
-    HL, D = geo.HL, geo.D
+    HL, D, NP = geo.HL, geo.D, geo.NP
+    outs = refs[-(4 * NP) - 2 : -2] if geo.fast else refs[-(4 * NP) :]
     if geo.fast:
-        pieces, (q, k, v, wown, wscr, sem) = refs[:8], refs[8:]
+        pieces, (wscr, sem) = refs[:8], refs[-2:]
         x, z = meta[0], meta[2]
         y, c = meta[1] // 2, meta[1] % 2
         copies = []
@@ -134,20 +140,24 @@
         for cpy in copies:
             cpy.wait()
     else:
-        w, (q, k, v, wown) = refs[0], refs[1:]
-        wscr = w
-    for part in range(3):
-        cols = pl.ds(al(part * D + g * HL, 128), HL)
-        wown[:, part * HL : (part + 1) * HL] = wscr[:, cols]
-    outs = (q, k, v)
+        wscr = refs[0]
+
+    def cols(part, p):
+        return pl.ds(al(part * D + g * HL + p * PW, 128), PW)
+
+    for p in range(NP):
+        for part in range(3):
+            outs[3 * NP + p][:, part * PW : (part + 1) * PW] = wscr[:, cols(part, p)]
 
     def step(i, carry):
         rows = pl.ds(al(i * 256, 256), 256)
         a = h1[rows, :]
-        for part in range(3):
-            cols = pl.ds(al(part * D + g * HL, 128), HL)
-            res = nn(a, wown[:, part * HL : (part + 1) * HL]) + bias[:, cols]
-            outs[part][rows, :] = res.astype(BF)
+        for p in range(NP):
+            res = nn(a, outs[3 * NP + p][...])
+            for part in range(3):
+                outs[part * NP + p][rows, :] = (
+                    res[:, part * PW : (part + 1) * PW] + bias[:, cols(part, p)]
+                ).astype(BF)
         return carry
 
     lax.fori_loop(0, geo.L // 256, step, 0)
@@ -191,88 +201,114 @@
     lax.fori_loop(0, geo.L // TK, step, 0)
 
 
-def mask_bias(segk, segq, k0, q0):
+def mask_bias(segk, segq, k0, q0, tq):
     a = segk[pl.ds(k0, TK), :]
-    b = segq[0:1, pl.ds(q0, TQ)]
-    same = jnp.concatenate([a] * (TQ // 128), axis=1) == b
+    b = segq[0:1, pl.ds(q0, tq)]
+    same = jnp.concatenate([a] * (tq // 128), axis=1) == b
     return jnp.where(same, 0.0, NEG)
 
 
-def head_mask(HL, h, rows):
-    lane = lax.broadcasted_iota(jnp.int32, (rows, HL), 1)
+def head_mask(h, rows):
+    lane = lax.broadcasted_iota(jnp.int32, (rows, PW), 1)
     return (lane // HEAD_DIM) == h
 
 
-def attn_kernel(geo, meta, doc, q, k, v, *refs):
-    G, HL, NH, L, BL = geo.G, geo.HL, geo.NH, geo.L, geo.BL
-    outs, lse = refs[:G], refs[G]
-    vT, segk, segq, acc, stat = refs[G + 1 :]
+def ranges(first, last, one, lo, hi, tile):
+    a = jnp.where(one, jnp.minimum((first + tile - 1) // tile, hi), hi)
+    b = jnp.where(one, jnp.minimum(jnp.maximum(last // tile, a), hi), hi)
+    return ((lo, a, True), (a, b, False), (b, hi, True))
+
+
+HR = HEAD_DIM + 16
+
+
+def attn_kernel(geo, dlist, meta, doc, segk, segq, *refs):
+    G, NP, L, BL, TQF = geo.G, geo.NP, geo.L, geo.BL, geo.TQ
+    q, k, v, refs = refs[:NP], refs[NP : 2 * NP], refs[2 * NP : 3 * NP], refs[3 * NP :]
+    nd = len(dlist)
+    outs, lses = refs[: nd * NP], refs[nd * NP : nd * NP + nd]
+    vT, acc, sc = refs[nd * NP + nd :]
     s, g = geo.where(meta)
     ends = doc_ends(doc, s)
-    fill_segments(geo, ends, segk, segq)
+    heads = [(p, h) for p in range(NP) for h in range(2)]
 
     def flip(i, carry):
         rows = pl.ds(al(i * TK, TK), TK)
-        vT[:, rows] = jnp.transpose(v[rows, :])
+        for p in range(NP):
+            t = jnp.transpose(v[p][rows, :])
+            for h in range(2):
+                b = (2 * p + h) * HR
+                vT[b : b + HEAD_DIM, rows] = t[h * HEAD_DIM : (h + 1) * HEAD_DIM, :]
+                vT[b + HEAD_DIM : b + HR, rows] = jnp.ones((16, TK), BF)
         return carry
 
     lax.fori_loop(0, L // TK, flip, 0)
 
-    def q_step(i, carry):
-        q0 = al(i * TQ, TQ)
-        klo = span_start(ends, q0) // TK
-        khi = (span_end(ends, q0 + TQ - 1, L) + TK - 1) // TK
-        qt = q[pl.ds(q0, TQ), :] * jnp.asarray(HEAD_DIM ** (-0.5), BF)
-        zero = jnp.zeros_like(qt)
-        qm = [jnp.where(head_mask(HL, h, TQ), qt, zero) for h in range(NH)]
-        acc[...] = jnp.zeros_like(acc)
-        m0 = tuple(jnp.full((1, TQ), -3e38, F32) for _ in range(NH))
-        l0 = tuple(jnp.zeros((1, TQ), F32) for _ in range(NH))
-
-        def k_step(j, ml):
-            ms, ls = ml
-            k0 = al(j * TK, TK)
-            kt = k[pl.ds(k0, TK), :]
-            bias = mask_bias(segk, segq, k0, q0)
-            new_m, new_l = [], []
-            for h in range(NH):
-                hs = slice(h * HEAD_DIM, (h + 1) * HEAD_DIM)
-                st = nt(kt, qm[h]) + bias
-                mn = jnp.maximum(ms[h], jnp.max(st, axis=0, keepdims=True))
-                p = jnp.exp(st - mn)
-                alpha = jnp.exp(ms[h] - mn)
-                new_m.append(mn)
-                new_l.append(alpha * ls[h] + jnp.sum(p, axis=0, keepdims=True))
-                acc[hs, :] = acc[hs, :] * alpha + nn(vT[hs, pl.ds(k0, TK)], p.astype(BF))
-            return tuple(new_m), tuple(new_l)
-
-        ms, ls = lax.fori_loop(klo, khi, k_step, (m0, l0))
-        for h in range(NH):
-            hs = slice(h * HEAD_DIM, (h + 1) * HEAD_DIM)
-            acc[hs, :] = acc[hs, :] * (1.0 / ls[h])
-            lse[h : h + 1, pl.ds(q0, TQ)] = ms[h] + jnp.log(ls[h])
-        res = jnp.transpose(acc[...]).astype(BF)
-        b = q0 // BL
-        half, gp = b // G, lax.rem(b, G)
-        e = jnp.where(half == s, 0, 1)
-        off = al(q0 - b * BL, TQ)
-        for d in range(G):
-            @pl.when(lax.rem(g - gp + G, G) == d)
-            def _():
-                outs[d][e, pl.ds(off, TQ), :] = res
-        return carry
-
-    lax.fori_loop(0, L // TQ, q_step, 0)
-
-
-def attn_back_kernel(geo, meta, doc, q, k, v, lse, *refs):
-    G, HL, NH, L, BL = geo.G, geo.HL, geo.NH, geo.L, geo.BL
-    mixed, grads = refs[:G], refs[G : 2 * G]
-    out = refs[2 * G]
-    qm, gm, kT, dqT, delta, segk, segq, dk, dv = refs[2 * G + 1 :]
+    for di, d in enumerate(dlist):
+
+        def q_step(i, carry):
+            e = i // (BL // TQF)
+            off = al(lax.rem(i, BL // TQF) * TQF, TQF)
+            half = jnp.where(e == 0, s, 1 - s)
+            q0 = al((half * G + lax.rem(g - d + G, G)) * BL + off, TQF)
+            first, last = span_start(ends, q0), span_end(ends, q0 + TQF - 1, L)
+            one = first == span_start(ends, q0 + TQF - 1)
+            klo = first // TK
+            khi = (last + TK - 1) // TK
+            qm = []
+            for p, h in heads:
+                qt = q[p][pl.ds(q0, TQF), :] * jnp.asarray(HEAD_DIM ** (-0.5), BF)
+                qm.append(jnp.where(head_mask(h, TQF), qt, jnp.zeros_like(qt)))
+            acc[...] = jnp.zeros_like(acc)
+
+            def scores(masked, j, ms):
+                k0 = al(j * TK, TK)
+                if masked:
+                    bias = mask_bias(segk, segq, k0, q0, TQF)
+                out = []
+                for n, (p, h) in enumerate(heads):
+                    st = nt(k[p][pl.ds(k0, TK), :], qm[n])
+                    if masked:
+                        st = st + bias
+                    sc[n, pl.ds(k0, TK), :] = st
+                    out.append(jnp.maximum(ms[n], jnp.max(st.reshape(TK // 8, 8, TQF), axis=0)))
+                return tuple(out)
+
+            ms = tuple(jnp.full((8, TQF), -3e38, F32) for _ in heads)
+            for lo, hi, masked in ranges(first, last, one, klo, khi, TK):
+                ms = lax.fori_loop(lo, hi, functools.partial(scores, masked), ms)
+            ms = [jnp.max(m, axis=0, keepdims=True) for m in ms]
+            ml = [m * LOG2E for m in ms]
+
+            def values(j, c2):
+                k0 = al(j * TK, TK)
+                for n in range(len(heads)):
+                    pr = jnp.exp2(sc[n, pl.ds(k0, TK), :] * LOG2E - ml[n])
+                    hs = slice(n * HR, (n + 1) * HR)
+                    acc[hs, :] += nn(vT[hs, pl.ds(k0, TK)], pr.astype(BF))
+                return c2
+
+            lax.fori_loop(klo, khi, values, 0)
+            for p in range(NP):
+                parts = []
+                for n in (2 * p, 2 * p + 1):
+                    ls = acc[n * HR + HEAD_DIM : n * HR + HEAD_DIM + 1, :]
+                    parts.append(acc[n * HR : n * HR + HEAD_DIM, :] * (1.0 / ls))
+                    lses[di][e, n : n + 1, pl.ds(off, TQF)] = ms[n] + jnp.log(ls)
+                res = jnp.transpose(jnp.concatenate(parts, axis=0)).astype(BF)
+                outs[di * NP + p][e, pl.ds(off, TQF), :] = res
+            return carry
+
+        lax.fori_loop(0, 2 * BL // TQF, q_step, 0)
+
+
+def attn_back_kernel(geo, p, meta, doc, segk, segq, q, k, v, *refs):
+    G, L, BL = geo.G, geo.L, geo.BL
+    lses, mixed, grads = refs[:G], refs[G : 2 * G], refs[2 * G : 3 * G]
+    out = refs[3 * G]
+    qm, gm, kT, dqT, delta, lse, dk, dv = refs[3 * G + 1 :]
     s, g = geo.where(meta)
     ends = doc_ends(doc, s)
-    fill_segments(geo, ends, segk, segq)
     scale = HEAD_DIM ** (-0.5)
     for e in range(2):
         for d in range(G):
@@ -285,54 +321,108 @@
                 zero = jnp.zeros_like(gt)
                 prod = jnp.transpose(gt.astype(F32) * mixed[d][e, src, :].astype(F32))
                 qt = q[dst, :] * jnp.asarray(scale, BF)
-                for h in range(NH):
+                for h in range(2):
                     hs = slice(h * HEAD_DIM, (h + 1) * HEAD_DIM)
-                    keep = head_mask(HL, h, 256)
+                    keep = head_mask(h, 256)
                     gm[h, dst, :] = jnp.where(keep, gt, zero)
                     qm[h, dst, :] = jnp.where(keep, qt, zero)
                     delta[h : h + 1, dst] = jnp.sum(prod[hs, :], axis=0, keepdims=True)
+                lse[:, dst] = lses[d][e, :, src]
                 kT[:, dst] = jnp.transpose(k[dst, :])
-                dqT[:, dst] = jnp.zeros((HL, 256), F32)
+                dqT[:, dst] = jnp.zeros((PW, 256), F32)
                 return carry
 
             lax.fori_loop(0, BL // 256, load, 0)
 
     def k_step(j, carry):
         k0 = al(j * TK, TK)
-        qlo = span_start(ends, k0) // TQ
-        qhi = (span_end(ends, k0 + TK - 1, L) + TQ - 1) // TQ
+        first, last = span_start(ends, k0), span_end(ends, k0 + TK - 1, L)
+        one = first == span_start(ends, k0 + TK - 1)
+        qlo = first // TQ
+        qhi = (last + TQ - 1) // TQ
         kt = k[pl.ds(k0, TK), :]
         vt = v[pl.ds(k0, TK), :]
         dk[...] = jnp.zeros_like(dk)
         dv[...] = jnp.zeros_like(dv)
 
-        def q_step(i, c2):
+        def q_step(masked, i, c2):
             q0 = al(i * TQ, TQ)
             qs = pl.ds(q0, TQ)
-            bias = mask_bias(segk, segq, k0, q0)
-            for h in range(NH):
+            if masked:
+                bias = mask_bias(segk, segq, k0, q0, TQ)
+            for h in range(2):
                 hs = slice(h * HEAD_DIM, (h + 1) * HEAD_DIM)
                 qh, gh = qm[h, qs, :], gm[h, qs, :]
-                p = jnp.exp(nt(kt, qh) + (bias - lse[h : h + 1, qs]))
-                ds = (p * (nt(vt, gh) - delta[h : h + 1, qs])).astype(BF)
-                dv[...] += nn(p.astype(BF), gh)
+                n = 2 * p + h
+                st = nt(kt, qh) - lse[n : n + 1, qs]
+                if masked:
+                    st = st + bias
+                pr = jnp.exp(st)
+                ds = (pr * (nt(vt, gh) - delta[h : h + 1, qs])).astype(BF)
+                dv[...] += nn(pr.astype(BF), gh)
                 dk[...] += nn(ds, qh)
                 dqT[hs, qs] += nn(kT[hs, pl.ds(k0, TK)], ds)
             return c2
 
-        lax.fori_loop(qlo, qhi, q_step, 0)
-        out[pl.ds(k0, TK), HL : 2 * HL] = dk[...].astype(BF)
-        out[pl.ds(k0, TK), 2 * HL : 3 * HL] = dv[...].astype(BF)
+        for lo, hi, masked in ranges(first, last, one, qlo, qhi, TQ):
+            lax.fori_loop(lo, hi, functools.partial(q_step, masked), 0)
+        out[pl.ds(k0, TK), PW : 2 * PW] = dk[...].astype(BF)
+        out[pl.ds(k0, TK), 2 * PW : 3 * PW] = dv[...].astype(BF)
         return carry
 
     lax.fori_loop(0, L // TK, k_step, 0)
 
-    def last(i, carry):
+    def last_step(i, carry):
         rows = pl.ds(al(i * TQ, TQ), TQ)
-        out[rows, 0:HL] = (jnp.transpose(dqT[:, rows]) * scale).astype(BF)
+        out[rows, 0:PW] = (jnp.transpose(dqT[:, rows]) * scale).astype(BF)
         return carry
 
-    lax.fori_loop(0, L // TQ, last, 0)
+    lax.fori_loop(0, L // TQ, last_step, 0)
+
+
+def attend_call(geo, dlist, meta, doc, segs, q, k, v):
+    NP, L, BL, nd = geo.NP, geo.L, geo.BL, len(dlist)
+    share = nd / geo.G
+    res = call(
+        functools.partial(attn_kernel, geo, dlist),
+        "attend",
+        [(meta, SM), (doc, SM), (segs[0], VM), (segs[1], VM)] + [(t, VM) for t in (*q, *k, *v)],
+        [sds((2, BL, PW), BF)] * (nd * NP) + [sds((2, 8, BL), F32)] * nd,
+        scratch=[
+            pltpu.VMEM((2 * NP * HR, L), BF),
+            pltpu.VMEM((2 * NP * HR, geo.TQ), F32),
+            pltpu.VMEM((2 * NP, L, geo.TQ), F32),
+        ],
+        flops=int(2 * L * L * geo.HL * 4 * share),
+        nbytes=L * geo.HL * 8,
+        trans=int(L * L * NP * share),
+    )
+    mixed = [res[i * NP : (i + 1) * NP] for i in range(nd)]
+    return mixed, res[nd * NP :]
+
+
+def attend_back_call(geo, p, meta, doc, segs, q, k, v, lses, mixed, grads):
+    L = geo.L
+    return call(
+        functools.partial(attn_back_kernel, geo, p),
+        "attend_back",
+        [(meta, SM), (doc, SM), (segs[0], VM), (segs[1], VM), (q, VM), (k, VM), (v, VM)]
+        + [(t, VM) for t in (*lses, *mixed, *grads)],
+        [sds((L, 3 * PW), BF)],
+        scratch=[
+            pltpu.VMEM((2, L, PW), BF),
+            pltpu.VMEM((2, L, PW), BF),
+            pltpu.VMEM((PW, L), BF),
+            pltpu.VMEM((PW, L), F32),
+            pltpu.VMEM((8, L), F32),
+            pltpu.VMEM((8, L), F32),
+            pltpu.VMEM((TK, PW), F32),
+            pltpu.VMEM((TK, PW), F32),
+        ],
+        flops=2 * L * L * PW * 10,
+        nbytes=L * PW * 20,
+        trans=L * L,
+    )[0]
 
 
 def gelu_parts(u):
@@ -342,16 +432,17 @@
 
 
 def ffn_kernel(geo, meta, *refs):
-    G, HL, D, FF, BL, T = geo.G, geo.HL, geo.D, geo.FF, geo.BL, geo.T
+    G, HL, D, FF, BL, T, NP = geo.G, geo.HL, geo.D, geo.FF, geo.BL, geo.T, geo.NP
     s, g = geo.where(meta)
+    pairs = [(d, p) for d in range(G) for p in range(NP)]
     x0, x1, cot, cot1, mixb, gain, shift, upb, downb = refs[:9]
     refs = refs[9:]
-    mixed, refs = refs[:G], refs[G:]
+    mixed, refs = refs[: G * NP], refs[G * NP :]
     nw = 8 if geo.fast else 3
     wts, refs = refs[:nw], refs[nw:]
     out_own, out_send, g_resid = refs[:3]
     refs = refs[3:]
-    gmix, refs = refs[:G], refs[G:]
+    gmix, refs = refs[: G * NP], refs[G * NP :]
     ng = 2 if geo.fast else 3
     packs, refs = refs[:ng], refs[ng:]
     vec, refs = refs[0], refs[1:]
@@ -415,9 +506,9 @@
             rows = pl.ds(al(i * RT, RT), RT)
             to = pl.ds(al(e * BL + i * RT, RT), RT)
             r = xe[rows, :].astype(F32) + mixb[...]
-            for d in range(G):
+            for n, (d, p) in enumerate(pairs):
                 gp = lax.rem(g - d + G, G)
-                r = r + nn(mixed[d][e, rows, :], wo[pl.ds(al(gp * HL, 128), HL), :])
+                r = r + nn(mixed[n][e, rows, :], wo[pl.ds(al(gp * HL + p * PW, 128), PW), :])
             resid[to, :] = r
             xhat, _ = normed(r)
             h2[to, :] = (xhat * gain[...] + shift[...]).astype(BF)
@@ -511,9 +602,9 @@
             g_resid[to, :] = gr
             ga = gr.astype(BF)
             gu_s[to, 0:D] = ga
-            for d in range(G):
+            for n, (d, p) in enumerate(pairs):
                 gp = lax.rem(g + d, G)
-                gmix[d][e, rows, :] = nt(ga, wo[pl.ds(al(gp * HL, 128), HL), :]).astype(BF)
+                gmix[n][e, rows, :] = nt(ga, wo[pl.ds(al(gp * HL + p * PW, 128), PW), :]).astype(BF)
             return (
                 mb + jnp.sum(ga.astype(F32), axis=0, keepdims=True),
                 fg + jnp.sum(gh * xhat, axis=0, keepdims=True),
@@ -524,10 +615,10 @@
         sums = lax.fori_loop(0, BL // RT, back, sums)
     for i in range(4):
         vec[4 + i : 5 + i, :] = sums[i]
-    for d in range(G):
+    for n, (d, p) in enumerate(pairs):
         gp = lax.rem(g - d + G, G)
-        part = tn(mixed[d][0], gu_s[0:BL, 0:D]) + tn(mixed[d][1], gu_s[BL:T, 0:D])
-        mg[pl.ds(al(gp * HL, 128), HL), :] = part.astype(BF)
+        part = tn(mixed[n][0], gu_s[0:BL, 0:D]) + tn(mixed[n][1], gu_s[BL:T, 0:D])
+        mg[pl.ds(al(gp * HL + p * PW, 128), PW), :] = part.astype(BF)
     if geo.fast:
         for cr in range(2):
             for yr in range(2):
@@ -543,66 +634,83 @@
         packs[2][...] = mg[...]
 
 
-def qkv_back_kernel(geo, meta, gq, h1, w, vec_in, gain, shift, *refs):
-    G, HL, D, BL, L = geo.G, geo.HL, geo.D, geo.BL, geo.L
+def wgrad_kernel(geo, meta, h1, *refs):
+    G, HL, D, NP = geo.G, geo.HL, geo.D, geo.NP
     s, g = geo.where(meta)
-    pieces, refs = refs[: 2 * G], refs[2 * G :]
-    ghs, refs = refs[:G], refs[G:]
-    ng = 2 if geo.fast else 1
-    packs, refs = refs[:ng], refs[ng:]
-    vec, wg = refs
-    vec[...] = vec_in[...]
-    part = tn(h1[...], gq[...])
-    wg[...] = part.astype(BF)
+    gq, refs = refs[:NP], refs[NP:]
+    packs, wg = refs[:-1], refs[-1]
+    for p in range(NP):
+        wg[:, p * 3 * PW : (p + 1) * 3 * PW] = tn(h1[...], gq[p][...]).astype(BF)
     if geo.fast:
         x, z, c = meta[0], meta[2], meta[1] % 2
         for cr, table in ((0, KEEP_LB), (1, SEND_LB)):
             for b in range(3):
-                lb = jnp.where(c == 0, table[0][b], table[1][b])
+                lb = [(t[b] % 2) * 3 + t[b] // 2 for t in table]
+                at = jnp.where(c == 0, lb[0], lb[1])
                 for hr in range(2):
                     hh = x if hr == 0 else 1 - x
                     for k in range(4):
                         zz = lax.rem(z + k, 4)
                         packs[cr][b, hr, k] = wg[
-                            pl.ds(al(zz * 128 + hh * 64, 64), 64), pl.ds(al(lb * 128, 128), 128)
+                            pl.ds(al(zz * 128 + hh * 64, 64), 64), pl.ds(al(at * 128, 128), 128)
                         ]
     else:
-        for p in range(3):
-            packs[0][:, pl.ds(al(p * D + g * HL, 128), HL)] = wg[:, p * HL : (p + 1) * HL]
+        packs[0][...] = jnp.zeros_like(packs[0])
+        for p in range(NP):
+            for part in range(3):
+                packs[0][:, pl.ds(al(part * D + g * HL + p * PW, 128), PW)] = wg[
+                    :, (3 * p + part) * PW : (3 * p + part + 1) * PW
+                ]
+
+
+def qkv_back_kernel(geo, meta, vec_in, *refs):
+    G, HL, D, BL, NP = geo.G, geo.HL, geo.D, geo.BL, geo.NP
+    s, g = geo.where(meta)
+    gq, w, refs = refs[:NP], refs[NP : 2 * NP], refs[2 * NP :]
+    pieces, refs = refs[: 2 * G], refs[2 * G :]
+    ghs, vec = refs[:G], refs[G]
+    vec[...] = vec_in[...]
     zrow = jnp.zeros((1, D), F32)
-    zh = jnp.zeros((1, HL), F32)
-    sums = (zrow, zrow, zh, zh)
+    zh = jnp.zeros((1, PW), F32)
+    sums = (zrow, zrow) + (zh,) * (2 * NP)
     for e in range(2):
         for d in range(G):
             base = geo.block(s, g, e, d) * BL
             src = pieces[e * G + d]
 
             def step(i, carry):
-                ng_, ns, qb, vb = carry
                 rows = pl.ds(al(i * RT, RT), RT)
                 at = pl.ds(al(base + i * RT, RT), RT)
                 xhat, _ = normed(src[rows, :].astype(F32))
-                gt = gq[at, :]
-                gh = nt(gt, w[...])
+                gts = [t[at, :] for t in gq]
+                gh = nt(gts[0], w[0][...])
+                for p in range(1, NP):
+                    gh = gh + nt(gts[p], w[p][...])
                 ghs[d][e, rows, :] = gh.astype(ghs[d].dtype)
-                return (
-                    ng_ + jnp.sum(gh * xhat, axis=0, keepdims=True),
-                    ns + jnp.sum(gh, axis=0, keepdims=True),
-                    qb + jnp.sum(gt[:, 0:HL].astype(F32), axis=0, keepdims=True),
-                    vb + jnp.sum(gt[:, 2 * HL : 3 * HL].astype(F32), axis=0, keepdims=True),
-                )
+                new = [
+                    carry[0] + jnp.sum(gh * xhat, axis=0, keepdims=True),
+                    carry[1] + jnp.sum(gh, axis=0, keepdims=True),
+                ]
+                for p in range(NP):
+                    for n, part in enumerate((0, 2)):
+                        cut = gts[p][:, part * PW : (part + 1) * PW].astype(F32)
+                        new.append(carry[2 + 2 * p + n] + jnp.sum(cut, axis=0, keepdims=True))
+                return tuple(new)
 
             sums = lax.fori_loop(0, BL // RT, step, sums)
     vec[0:1, :] = sums[0]
     vec[1:2, :] = sums[1]
-    cols = pl.ds(al(g * HL, 128), HL)
-    vec[2:3, cols] = sums[2]
-    vec[3:4, cols] = sums[3]
-
-
-def last_kernel(geo, meta, gain, g_resid, gh, *refs):
+    for p in range(NP):
+        cols = pl.ds(al(g * HL + p * PW, 128), PW)
+        vec[2:3, cols] = sums[2 + 2 * p]
+        vec[3:4, cols] = sums[3 + 2 * p]
+
+
+def last_kernel(geo, meta, gain, vec, vrecv, g_resid, gh, *refs):
     G, D, BL = geo.G, geo.D, geo.BL
     s, _ = geo.where(meta)
+    refs, vout = refs[:-1], refs[-1]
+    vout[...] = vec[...] + vrecv[...]
     recv, refs = refs[: G - 1], refs[G - 1 :]
     x0, x1, out, send = refs
     for e in range(2):
@@ -635,10 +743,8 @@
         outs[q][...] = (own[q].astype(F32) + recv[q].astype(F32)).astype(BF)
 
 
-def arrange_kernel(geo, meta, keep, recv, vec, vrecv, p0, p1, p2, p3, vout):
+def arrange_kernel(geo, meta, keep, recv, *outs):
     y, c = meta[1] // 2, meta[1] % 2
-    outs = (p0, p1, p2, p3)
-    vout[...] = vec[...] + vrecv[...]
     for cs in range(2):
         mine = sorted((lb // 2) * 4 + 2 * cs + lb % 2 for lb in KEEP_LB[cs])
         theirs = sorted((lb // 2) * 4 + 2 * (1 - cs) + lb % 2 for lb in SEND_LB[1 - cs])
@@ -675,16 +781,21 @@
     ).astype(BF)
 
 
-def finish_kernel(meta, r, o, qr, qo, qkv, mix, up, down):
+def finish_kernel(meta, r, o, mix, up, down):
     x = meta[0]
-    for src, qsrc, h in ((r, qr, x), (o, qo, 1 - x)):
+    for src, h in ((r, x), (o, 1 - x)):
         rows = pl.ds(al(h * 64, 64), 64)
         for b in range(4):
             up[rows, b * 128 : b * 128 + 128] = src[b * 64 : b * 64 + 64, :].astype(F32)
         down[pl.ds(al(h * 256, 256), 256), :] = src[256:512, :].astype(F32)
         mix[rows, :] = src[512:576, :].astype(F32)
+
+
+def finish_qkv_kernel(meta, r, o, qkv):
+    x = meta[0]
+    for src, h in ((r, x), (o, 1 - x)):
         for b in range(3):
-            qkv[rows, b * 128 : b * 128 + 128] = qsrc[b * 64 : b * 64 + 64, :].astype(F32)
+            qkv[pl.ds(al(h * 64, 64), 64), b * 128 : b * 128 + 128] = src[b * 64 : b * 64 + 64, :].astype(F32)
 
 
 def pack_kernel(meta, qkv, mix, up, down, first, rest):
@@ -745,9 +856,10 @@
     def pick(v, i):
         return lax.dynamic_index_in_dim(v, i, 0, keepdims=False)
 
-    x0 = pick(tokens, s)
-    x_send = pick(tokens, 1 - s)
-    x1 = swap_half(x_send)
+    def after(v, dep):
+        return lax.optimization_barrier((v, dep))[0]
+
+    NP = geo.NP
     if geo.fast:
         half_qkv, half_rest = call(
             pack_kernel,
@@ -757,14 +869,23 @@
             nbytes=2 << 20,
         )
 
-        def spread(v):
-            lines = jnp.stack([v] + [line(v, d) for d in range(1, 4)])
-            quads = [lines, plane(lines, 1, 0), plane(lines, 0, 1), plane(lines, 1, 1)]
-            return [p for q in quads for p in (q, turn(q, 1))]
-
-        w_qkv = spread(half_qkv)
-        w_rest = spread(half_rest)
+        def lines(v):
+            return [v] + [line(v, d) for d in range(1, 4)]
+
+        def quads(v):
+            return [v, plane(v, 1, 0), plane(v, 0, 1), plane(v, 1, 1)]
+
+        lines_qkv = lines(half_qkv)
+        x0 = pick(tokens, s)
+        x1 = swap_half(pick(after(tokens, half_qkv), 1 - s))
+        lines_rest = lines(half_rest)
+        quads_qkv = quads(jnp.stack(lines_qkv))
+        w_qkv = [t for q in quads_qkv for t in (q, turn(q, 1))]
+        quads_rest = quads(jnp.stack(after(tuple(lines_rest), w_qkv[1])))
     else:
+        x0 = pick(tokens, s)
+        x1 = swap_half(pick(tokens, 1 - s))
+
         def whole(w):
             w = lax.all_gather(w.astype(BF), "row", axis=0, tiled=True)
             return lax.all_gather(w, "col", axis=1, tiled=True)
@@ -774,46 +895,45 @@
     pieces = [x0] + [turn(x0, d) for d in range(1, G)]
     pieces += [x1] + [turn(x1, d) for d in range(1, G)]
     gain1, shift1 = row2(norm_gain), row2(norm_shift)
-    (h1,) = call(
+    h1, segk, segq = call(
         functools.partial(norm_kernel, geo),
         "norm_one",
-        [(meta, SM), (gain1, VM), (shift1, VM)] + [(p, VM) for p in pieces],
-        [sds((L, D), BF)],
+        [(meta, SM), (doc_lengths, SM), (gain1, VM), (shift1, VM)] + [(p, VM) for p in pieces],
+        [sds((L, D), BF), sds((L, 128), jnp.int32), sds((8, L), jnp.int32)],
         flops=L * D * 10,
         nbytes=L * D * 4,
     )
+    segs = (segk, segq)
     bias = row2(jnp.concatenate([query_bias, jnp.zeros_like(query_bias), value_bias]))
     wspec = HBM if geo.fast else VM
-    q, k, v, w_own = call(
+    res = call(
         functools.partial(qkv_kernel, geo),
         "qkv",
         [(meta, SM), (h1, VM), (bias, VM)] + [(w, wspec) for w in w_qkv],
-        [sds((L, HL), BF)] * 3 + [sds((D, 3 * HL), BF)],
+        [sds((L, PW), BF)] * (3 * NP) + [sds((D, 3 * PW), BF)] * NP,
         scratch=[pltpu.VMEM((D, 3 * D), BF), pltpu.SemaphoreType.DMA(())] if geo.fast else [],
         flops=2 * L * D * 3 * HL,
         nbytes=L * D * 2 + L * HL * 6 + D * D * 6,
     )
-    attn = call(
-        functools.partial(attn_kernel, geo),
-        "attend",
-        [(meta, SM), (doc_lengths, SM), (q, VM), (k, VM), (v, VM)],
-        [sds((2, BL, HL), BF)] * G + [sds((8, L), F32)],
-        scratch=[
-            pltpu.VMEM((HL, L), BF),
-            pltpu.VMEM((L, 128), jnp.int32),
-            pltpu.VMEM((8, L), jnp.int32),
-            pltpu.VMEM((HL, TQ), F32),
-            pltpu.VMEM((8, TQ), F32),
-        ],
-        flops=2 * L * L * HL * 4,
-        nbytes=L * HL * 8,
-        trans=L * L * geo.NH // 2,
-    )
-    mixed_all, lse = attn[:G], attn[G]
-    mixed = [mixed_all[0]] + [turn(mixed_all[G - d], d) for d in range(1, G)]
+    q, k, v, w_own = (res[n * NP : (n + 1) * NP] for n in range(4))
     cot0 = pick(cotangent, s)
     cot1 = swap_half(pick(cotangent, 1 - s))
-    packs_out = [sds((4, 4, 576, 128), BF)] * 2 if geo.fast else [sds((D, FF), BF), sds((FF, D), BF), sds((D, D), BF)]
+    far, lse_far = attend_call(geo, tuple(range(1, G)), meta, doc_lengths, segs, q, k, v)
+    q_own = list(after(tuple(q), far[0][0]))
+    if geo.fast:
+        quads_rest = after(tuple(quads_rest), far[0][0])
+        w_rest = [t for u in quads_rest for t in (u, turn(u, 1))]
+    own, lse_own = attend_call(geo, (0,), meta, doc_lengths, segs, q_own, k, v)
+    made = [own[0]] + list(far)
+    lses = list(lse_own) + list(lse_far)
+    mixed = [t for t in made[0]]
+    for d in range(1, G):
+        mixed += [turn(t, d) for t in made[G - d]]
+    packs_out = (
+        [sds((4, 4, 576, 128), BF)] * 2
+        if geo.fast
+        else [sds((D, FF), BF), sds((FF, D), BF), sds((D, D), BF)]
+    )
     weights_scr = (
         [
             pltpu.VMEM((D, D), BF),
@@ -833,7 +953,7 @@
         + [(m, VM) for m in mixed]
         + [(w, wspec) for w in w_rest],
         [sds((BL, D), BF), sds((BL, D), BF), sds((T, D), F32)]
-        + [sds((2, BL, HL), BF)] * G
+        + [sds((2, BL, PW), BF)] * (G * NP)
         + packs_out
         + [sds((16, D), F32)],
         scratch=[
@@ -852,120 +972,130 @@
         trans=2 * T * FF,
     )
     out_own, out_send, g_resid = res[:3]
-    gmix = res[3 : 3 + G]
-    packs = res[3 + G : -1]
+    gmix = [res[3 + d * NP : 3 + (d + 1) * NP] for d in range(G)]
+    packs = res[3 + G * NP : -1]
     vec1 = res[-1]
-    ghead = [gmix[0]] + [turn(gmix[d], d) for d in range(1, G)]
-    (gq,) = call(
-        functools.partial(attn_back_kernel, geo),
-        "attend_back",
-        [(meta, SM), (doc_lengths, SM), (q, VM), (k, VM), (v, VM), (lse, VM)]
-        + [(m, VM) for m in mixed_all]
-        + [(m, VM) for m in ghead],
-        [sds((L, 3 * HL), BF)],
-        scratch=[
-            pltpu.VMEM((geo.NH, L, HL), BF),
-            pltpu.VMEM((geo.NH, L, HL), BF),
-            pltpu.VMEM((HL, L), BF),
-            pltpu.VMEM((HL, L), F32),
-            pltpu.VMEM((8, L), F32),
-            pltpu.VMEM((L, 128), jnp.int32),
-            pltpu.VMEM((8, L), jnp.int32),
-            pltpu.VMEM((TK, HL), F32),
-            pltpu.VMEM((TK, HL), F32),
-        ],
-        flops=2 * L * L * HL * 10,
-        nbytes=L * HL * 20,
-        trans=L * L * geo.NH // 2,
+
+    def back(p, q_p):
+        return attend_back_call(
+            geo, p, meta, doc_lengths, segs, q_p, k[p], v[p], lses, [m[p] for m in made], ghead[p]
+        )
+
+    ghead = [[gmix[0][p]] + [turn(gmix[d][p], d) for d in range(1, G)] for p in range(NP)]
+
+    def step_plane(parts, vec=None):
+        a = [parts[0], plane(parts[1], 1, 0), plane(parts[2], 0, 1), plane(parts[3], 1, 1)]
+        n = parts[0].shape[1]
+        outs = [sds((n, 128), BF)] * 4
+        if vec is not None:
+            a += [vec, plane(vec, 1, 0), plane(vec, 0, 1), plane(vec, 1, 1)]
+            outs += [sds(vec.shape, F32)]
+        return a, outs
+
+    def plane_sum(a, outs):
+        return call(
+            functools.partial(plane_sum_kernel, len(outs) > 4),
+            "plane_sum",
+            [(t, VM) for t in a],
+            outs,
+            nbytes=8 << 20,
+        )
+
+    def step_line(parts, vec=None):
+        a = [parts[0]] + [line(parts[d], d) for d in range(1, 4)]
+        outs = [sds(parts[0].shape, BF)]
+        if vec is not None:
+            a += [vec] + [line(vec, d) for d in range(1, 4)]
+            outs += [sds(vec.shape, F32)]
+        return a, outs
+
+    def line_sum(a, outs):
+        return call(
+            functools.partial(line_sum_kernel, len(outs) > 1),
+            "line_sum",
+            [(t, VM) for t in a],
+            outs,
+            nbytes=2 << 20,
+        )
+
+    gq = [back(0, q[0])]
+    if geo.fast:
+        sums = call(
+            core_sum_kernel,
+            "core_sum",
+            [(after(packs[0], gq[0]), VM), (turn(after(packs[1], ghead[0][1]), 1), VM)],
+            [sds((4, 576, 128), BF)] * 4,
+            nbytes=8 << 20,
+        )
+        a1, o1 = step_plane(sums)
+        gq += [back(p, after(q[p], sums[0])) for p in range(1, NP)]
+    else:
+        gq += [back(p, q[p]) for p in range(1, NP)]
+    packs2_out = [sds((3, 2, 4, 64, 128), BF)] * 2 if geo.fast else [sds((D, 3 * D), BF)]
+    packs2 = call(
+        functools.partial(wgrad_kernel, geo),
+        "wgrad",
+        [(meta, SM), (h1, VM)] + [(t, VM) for t in gq],
+        packs2_out,
+        scratch=[pltpu.VMEM((D, 3 * HL), BF)],
+        flops=2 * L * D * 3 * HL,
+        nbytes=8 << 20,
     )
-    packs2_out = [sds((3, 2, 4, 64, 128), BF)] * 2 if geo.fast else [sds((D, 3 * D), BF)]
+    if geo.fast:
+        q1 = plane_sum(list(after(tuple(a1), packs2[0])), o1)
+        b1, p1 = step_line(q1)
+        parts2 = call(
+            functools.partial(arrange_kernel, geo),
+            "arrange",
+            [(meta, SM), (after(packs2[0], q1[0]), VM), (turn(packs2[1], 1), VM)],
+            [sds((4, 192, 128), BF)] * 4,
+            nbytes=2 << 20,
+        )
+        a2, o2 = step_plane(parts2)
+        gq = list(after(tuple(gq), parts2[0]))
     res2 = call(
         functools.partial(qkv_back_kernel, geo),
         "qkv_back",
-        [(meta, SM), (gq, VM), (h1, VM), (w_own, VM), (vec1, VM), (gain1, VM), (shift1, VM)]
-        + [(p, VM) for p in pieces],
-        [sds((2, BL, D), F32)] + [sds((2, BL, D), BF)] * (G - 1) + packs2_out + [sds((16, D), F32)],
-        scratch=[pltpu.VMEM((D, 3 * HL), BF)],
-        flops=4 * L * D * 3 * HL,
-        nbytes=16 << 20,
+        [(meta, SM), (vec1, VM)] + [(t, VM) for t in (*gq, *w_own)] + [(t, VM) for t in pieces],
+        [sds((2, BL, D), F32)] + [sds((2, BL, D), BF)] * (G - 1) + [sds((16, D), F32)],
+        flops=2 * L * D * 3 * HL,
+        nbytes=12 << 20,
     )
-    ghs = res2[:G]
-    packs2 = res2[G:-1]
-    vec2 = res2[-1]
+    ghs, vec2 = res2[:G], res2[G]
     gh_recv = [turn(ghs[G - d], d) for d in range(1, G)]
-    tgrad, tgrad_send = call(
+    tgrad, tgrad_send, vec3 = call(
         functools.partial(last_kernel, geo),
         "norm_back",
-        [(meta, SM), (gain1, VM), (g_resid, VM), (ghs[0], VM)]
+        [(meta, SM), (gain1, VM), (vec2, VM)]
+        + [(turn(vec2, 1) if geo.fast else jnp.zeros_like(vec2), VM), (g_resid, VM), (ghs[0], VM)]
         + [(r, VM) for r in gh_recv]
         + [(x0, VM), (x1, VM)],
-        [sds((2, BL, D), BF), sds((BL, D), BF)],
+        [sds((2, BL, D), BF), sds((BL, D), BF), sds((16, D), F32)],
         flops=T * D * 30,
         nbytes=8 << 20,
     )
-
     if geo.fast:
-        def step_plane(parts, vec=None):
-            a = [parts[0], plane(parts[1], 1, 0), plane(parts[2], 0, 1), plane(parts[3], 1, 1)]
-            n = parts[0].shape[1]
-            outs = [sds((n, 128), BF)] * 4
-            if vec is not None:
-                a += [vec, plane(vec, 1, 0), plane(vec, 0, 1), plane(vec, 1, 1)]
-                outs += [sds(vec.shape, F32)]
-            return call(
-                functools.partial(plane_sum_kernel, vec is not None),
-                "plane_sum",
-                [(t, VM) for t in a],
-                outs,
-                nbytes=n * 128 * 40,
-            )
-
-        def step_line(parts, vec=None):
-            a = [parts[0]] + [line(parts[d], d) for d in range(1, 4)]
-            outs = [sds(parts[0].shape, BF)]
-            if vec is not None:
-                a += [vec] + [line(vec, d) for d in range(1, 4)]
-                outs += [sds(vec.shape, F32)]
-            return call(
-                functools.partial(line_sum_kernel, vec is not None),
-                "line_sum",
-                [(t, VM) for t in a],
-                outs,
-                nbytes=parts[0].size * 10,
-            )
-
-        first = call(
-            core_sum_kernel,
-            "core_sum",
-            [(packs[0], VM), (turn(packs[1], 1), VM)],
-            [sds((4, 576, 128), BF)] * 4,
-            nbytes=8 << 20,
-        )
-        first = step_plane(first)
-        (first,) = step_line(first)
-        first_other = plane(first, 1, 0)
-        second = call(
-            functools.partial(arrange_kernel, geo),
-            "arrange",
-            [(meta, SM), (packs2[0], VM), (turn(packs2[1], 1), VM), (vec2, VM), (turn(vec2, 1), VM)],
-            [sds((4, 192, 128), BF)] * 4 + [sds(vec2.shape, F32)],
+        (r1,) = line_sum(list(after(tuple(b1), tgrad_send)), p1)
+        other1 = plane(r1, 1, 0)
+        va = [vec3, plane(vec3, 1, 0), plane(vec3, 0, 1), plane(vec3, 1, 1)]
+        *q2, vec4 = plane_sum(a2 + va, o2 + [sds(vec3.shape, F32)])
+        b2, p2 = step_line(q2, vec4)
+        mix_g, up_g, down_g = call(
+            finish_kernel,
+            "finish",
+            [(meta, SM), (after(r1, q2[0]), VM), (other1, VM)],
+            [sds(w.shape, F32) for w in (mix_weight, up_weight, down_weight)],
             nbytes=2 << 20,
         )
-        second = step_plane(second[:4], second[4])
-        second, vec = step_line(second[:4], second[4])
-        second_other = plane(second, 1, 0)
-        grads = call(
-            finish_kernel,
-            "finish",
-            [(meta, SM), (first, VM), (first_other, VM), (second, VM), (second_other, VM)],
-            [
-                sds(qkv_weight.shape, F32),
-                sds(mix_weight.shape, F32),
-                sds(up_weight.shape, F32),
-                sds(down_weight.shape, F32),
-            ],
-            nbytes=2 << 20,
+        r2, vec = line_sum(b2, p2)
+        (qkv_g,) = call(
+            finish_qkv_kernel,
+            "finish_qkv",
+            [(meta, SM), (r2, VM), (plane(r2, 1, 0), VM)],
+            [sds(qkv_weight.shape, F32)],
+            nbytes=1 << 20,
         )
+        grads = (qkv_g, mix_g, up_g, down_g)
     else:
         def reduced(w):
             w = lax.psum_scatter(w, "col", scatter_dimension=1, tiled=True)
@@ -973,7 +1103,7 @@
             return lax.psum(w, "dp").astype(F32)
 
         grads = (reduced(packs2[0]), reduced(packs[2]), reduced(packs[0]), reduced(packs[1]))
-        vec = lax.psum(vec2, ("dp", "col", "row"))
+        vec = lax.psum(vec3, ("dp", "col", "row"))
 
     def join(own, other):
         return lax.dynamic_update_slice(own, other[None], (1 - s, 0, 0))

time: 308 us -> 280 us (0.909)
  waiting for transfers between devices: 71.3 us -> 30.3 us
  starting transfers between devices: 46.9 us -> 75.5 us
  Pallas kernels: 171 us -> 154 us
    ppermute x15, waiting for transfers between devices: 32.4 us -> 9.23 us  [line(): return lax.ppermute(v, 'row', [(i, (i + d) % R) for i in range(R)])]
    ppermute x17, starting transfers between devices: 18.5 us -> 37.3 us  [plane(): return lax.ppermute(v, ('dp', 'col'), pairs)]
    pallas_call x15 -> x19, Pallas kernels: 171 us -> 154 us  [call(): pl.pallas_call(kernel, name=name, out_shape=tuple((o for o in outs)), in_...]
    ppermute x17, waiting for transfers between devices: 32.3 us -> 18.9 us  [plane(): return lax.ppermute(v, ('dp', 'col'), pairs)]
    ppermute x15, starting transfers between devices: 21.3 us -> 29 us  [line(): return lax.ppermute(v, 'row', [(i, (i + d) % R) for i in range(R)])]
    ppermute x16 -> x18, waiting for transfers between devices: 6.58 us -> 1.78 us  [turn(): lax.ppermute(v, 'col', [(i, i // G * G + (i % G + d) % G) for i in range(...]
    unnamed x92 -> x94, local copies, waits for them, and re-layouts: 6.75 us -> 9.77 us
  transfers between devices with their start and end apart: 52 -> 54, of which waited for: 22 -> 9; matrix products, arithmetic and copies ran while one was open for 3% -> 3% of each run, Pallas kernels for 45% -> 40%
where the time goes in v2:
time: 280 us; the launch traced here: 278 us
  Pallas kernels  154 us (55%)
  starting transfers between devices  75.5 us (27%)
  waiting for transfers between devices  30.3 us (11%)
  local copies, waits for them, and re-layouts  13.7 us (5%)
  other arithmetic  3.61 us (1%)
    pallas_call x19, Pallas kernels, call(): pl.pallas_call(kernel, name=name, out_shape=tuple((o for o in outs)), in_...  154 us
    ppermute x17, starting transfers between devices, plane(): return lax.ppermute(v, ('dp', 'col'), pairs)  37.3 us
    ppermute x15, starting transfers between devices, line(): return lax.ppermute(v, 'row', [(i, (i + d) % R) for i in range(R)])  29 us
    ppermute x17, waiting for transfers between devices, plane(): return lax.ppermute(v, ('dp', 'col'), pairs)  18.9 us
    unnamed x94, local copies, waits for them, and re-layouts  9.77 us
    ppermute x15, waiting for transfers between devices, line(): return lax.ppermute(v, 'row', [(i, (i + d) % R) for i in range(R)])  9.23 us
    ppermute x4, starting transfers between devices, swap_half(): return lax.ppermute(v, 'col', [(i, (i + G) % C) for i in range(C)])  6.14 us
  transfers between devices with their start and end apart: 54, of which 9 were waited for; matrix products, arithmetic and copies ran while one was open for 3% of the time, Pallas kernels for 40%

profile of v2, /device:TPU:0, one launch (start us, length us, event | category | flops | bytes accessed | tf_op | source)
XLA Modules:
  0.0 278.2 jit_solution(16906904200464613537)
XLA Ops:
  1.3 1.9 pack.1
  3.3 3.1 %collective-permute-start = (bf16[512,512]{1,0:T(8,128)(2,1)S(1)}, bf16[512,512]{1,0:T(8,128)(2,1)S(1)}, u32[]{:S(2)}, u32[]{:S(2)}) collective-permute-start(bf16[512,512]{1,0:T(8,128)(2,1)S(1)} %dynamic-slice_bitcast_fusion.2), channel_id=1, source_target_pairs={{0,8},{4,12},{8,0},{12,4},{1,9},{5,13},{9,1},{13,5},{2,10},{6,14},... | collective-permute-start | bytes 1572872 | tf_op jit(solution)/shard_map/ppermute | solution.py:839
  6.3 3.6 %collective-permute-start.6 = (bf16[64,384]{1,0:T(8,128)(2,1)}, bf16[64,384]{1,0:T(8,128)(2,1)S(1)}, u32[]{:S(2)}, u32[]{:S(2)}) collective-permute-start(bf16[64,384]{1,0:T(8,128)(2,1)} %get-tuple-element.93), channel_id=1, source_target_pairs={{0,3},{1,0},{2,1},{3,2},{4,7},{5,4},{6,5},{7,6},{8,11},{9,8},{10,9... | collective-permute-start | bytes 147464 | tf_op jit(solution)/shard_map/ppermute | solution.py:851
  10.9 2.8 %collective-permute-start.18 = (bf16[576,128]{1,0:T(8,128)(2,1)}, bf16[576,128]{1,0:T(8,128)(2,1)S(1)}, u32[]{:S(2)}, u32[]{:S(2)}) collective-permute-start(bf16[576,128]{1,0:T(8,128)(2,1)} %get-tuple-element.111), channel_id=1, source_target_pairs={{0,3},{1,0},{2,1},{3,2},{4,7},{5,4},{6,5},{7,6},{8,11},{9,8},{10,9... | collective-permute-start | bytes 442376 | tf_op jit(solution)/shard_map/ppermute | solution.py:851
  17.6 1.5 collective-permute-start.12
  19.8 8.3 %collective-permute-done.17 = bf16[576,128]{1,0:T(8,128)(2,1)S(1)} collective-permute-done((bf16[576,128]{1,0:T(8,128)(2,1)}, bf16[576,128]{1,0:T(8,128)(2,1)S(1)}, u32[]{:S(2)}, u32[]{:S(2)}) %collective-permute-start.17) | collective-permute-done | bytes 147488 | tf_op jit(solution)/shard_map/ppermute | solution.py:851
  28.6 1.5 collective-permute-start.8
  31.1 2.8 %collective-permute-done.10.refs_4_ = bf16[4,64,384]{2,1,0:T(8,128)(2,1)} collective-permute-done((bf16[4,64,384]{2,1,0:T(8,128)(2,1)S(1)}, bf16[4,64,384]{2,1,0:T(8,128)(2,1)}, u32[]{:S(2)}, u32[]{:S(2)}) %collective-permute-start.10) | collective-permute-done | bytes 196640 | tf_op jit(solution)/shard_map/ppermute | solution.py:848
  36.5 1.6 collective-permute-start.1
  38.1 1.4 collective-permute-start.21
  39.6 6.1 %norm_one.1 = (bf16[2048,512]{1,0:T(8,128)(2,1)}, s32[2048,128]{1,0:T(8,128)}, s32[8,2048]{1,0:T(8,128)}) custom-call(s32[3]{0:T(128)} %pad_add_fusion.meta, s32[2,8]{1,0:T(2,128)} %doc.9, f32[1,512]{1,0:T(1,128)} %bitcast.44, f32[1,512]{1,0:T(1,128)} %bitcast.46, bf16[512,512]{1,0:T(8,128)(2,1)} %copy-done.1, bf16[512,512]{1,0:T(8,128)(2,1)} %copy-done.4, ...), custom_call_target="tpu_custom_call" | custom-call | flops 10485760 | bytes 4194304 | tf_op jit(solution)/shard_map/norm_one/pallas_call | solution.py:34
  45.7 1.6 collective-permute-start.20
  47.8 8.3 %qkv.3 = (bf16[2048,128]{1,0:T(8,128)(2,1)}, bf16[2048,128]{1,0:T(8,128)(2,1)}, bf16[2048,128]{1,0:T(8,128)(2,1)}, bf16[2048,128]{1,0:T(8,128)(2,1)}, bf16[2048,...) custom-call(s32[3]{0:T(128)} %pad_add_fusion.meta, ...), custom_call_target="tpu_custom_call" | custom-call | flops 1610612736 | bytes 6815744 | tf_op jit(solution)/shard_map/qkv/pallas_call | solution.py:34
  56.1 10.9 %attend.2 = (bf16[2,512,128]{2,1,0:T(8,128)(2,1)}, bf16[2,512,128]{2,1,0:T(8,128)(2,1)}, f32[2,8,512]{2,1,0:T(8,128)}) custom-call(s32[3]{0:T(128)} %pad_add_fusion.meta, s32[2,8]{1,0:T(2,128)} %doc.9, s32[2048,128]{1,0:T(8,128)} %get-tuple-element.95.segk, s32[8,2048]{1,0:T(8,128)} %get-tuple-element.96.segq, ...), custom_call_target="tpu_custom_call" | custom-call | flops 4294967296 | bytes 4194304 | tf_op jit(solution)/shard_map/attend/pallas_call | solution.py:34
  67.0 9.1 %collective-permute-done.20.refs_17_ = bf16[4,576,128]{2,1,0:T(8,128)(2,1)S(1)} collective-permute-done((bf16[4,576,128]{2,1,0:T(8,128)(2,1)S(1)}, bf16[4,576,128]{2,1,0:T(8,128)(2,1)S(1)}, u32[]{:S(2)}, u32[]{:S(2)}) %collective-permute-start.20) | collective-permute-done | bytes 589856 | tf_op jit(solution)/shard_map/ppermute | solution.py:848
  77.2 11.8 %attend.3 = (bf16[2,512,128]{2,1,0:T(8,128)(2,1)}, bf16[2,512,128]{2,1,0:T(8,128)(2,1)}, f32[2,8,512]{2,1,0:T(8,128)}) custom-call(s32[3]{0:T(128)} %pad_add_fusion.meta, s32[2,8]{1,0:T(2,128)} %doc.9, s32[2048,128]{1,0:T(8,128)} %get-tuple-element.95.segk, s32[8,2048]{1,0:T(8,128)} %get-tuple-element.96.segq, ...), custom_call_target="tpu_custom_call" | custom-call | flops 4294967296 | bytes 4194304 | tf_op jit(solution)/shard_map/attend/pallas_call | solution.py:34
  89.7 31.6 %ffn.1 = (bf16[512,512]{1,0:T(8,128)(2,1)}, bf16[512,512]{1,0:T(8,128)(2,1)}, f32[1024,512]{1,0:T(8,128)}, bf16[2,512,128]{2,1,0:T(8,128)(2,1)}, bf16[2,512,128]...) custom-call(s32[3]{0:T(128)} %pad_add_fusion.meta, ...), custom_call_target="tpu_custom_call" | custom-call | flops 14495514624 | bytes 20971520 | tf_op jit(solution)/shard_map/ffn/pallas_call | solution.py:34
  121.4 1.7 collective-permute-done.27.refs_5_
  123.8 23.7 %attend_back.2.refs_0_ = bf16[2048,384]{1,0:T(8,128)(2,1)} custom-call(s32[3]{0:T(128)} %pad_add_fusion.meta, s32[2,8]{1,0:T(2,128)} %doc.9, s32[2048,128]{1,0:T(8,128)} %get-tuple-element.95.segk, s32[8,2048]{1,0:T(8,128)} %get-tuple-element.96.segq, bf16[2048,128]{1,0:T(8,128)(2,1)} %get-tuple-element.105.refs_0_.q, ...), custom_call_target="tpu_custom_call" | custom-call | flops 10737418240 | bytes 5242880 | tf_op jit(solution)/shard_map/attend_back/pallas_call | solution.py:34
  147.6 1.4 copy-done.3
  149.0 3.9 %core_sum.1 = (bf16[4,576,128]{2,1,0:T(8,128)(2,1)}, bf16[4,576,128]{2,1,0:T(8,128)(2,1)}, bf16[4,576,128]{2,1,0:T(8,128)(2,1)}, bf16[4,576,128]{2,1,0:T(8,128)(2,1)}) custom-call(bf16[4,4,576,128]{3,2,1,0:T(8,128)(2,1)} %get-tuple-element.127.own, bf16[4,4,576,128]{3,2,1,0:T(8,128)(2,1)} %copy-done.3), custom_call_target="tpu_custom_call" | custom-call | bytes 8388608 | tf_op jit(solution)/shard_map/core_sum/pallas_call | solution.py:34
  152.9 10.6 %collective-permute-start.31 = (bf16[4,576,128]{2,1,0:T(8,128)(2,1)}, bf16[4,576,128]{2,1,0:T(8,128)(2,1)S(1)}, u32[]{:S(2)}, u32[]{:S(2)}) collective-permute-start(bf16[4,576,128]{2,1,0:T(8,128)(2,1)} %get-tuple-element.136), channel_id=1, source_target_pairs={{0,8},{4,12},{8,0},{12,4},{16,24},{20,28},{24,16},{28,20},{1,9},{5... | collective-permute-start | bytes 1769480 | tf_op jit(solution)/shard_map/ppermute | solution.py:848
  164.2 23.6 %attend_back.3.refs_1_ = bf16[2048,384]{1,0:T(8,128)(2,1)} custom-call(s32[3]{0:T(128)} %pad_add_fusion.meta, s32[2,8]{1,0:T(2,128)} %doc.9, s32[2048,128]{1,0:T(8,128)} %get-tuple-element.95.segk, s32[8,2048]{1,0:T(8,128)} %get-tuple-element.96.segq, bf16[2048,128]{1,0:T(8,128)(2,1)} %get-tuple-element.131.refs_1_.q, ...), custom_call_target="tpu_custom_call" | custom-call | flops 10737418240 | bytes 5242880 | tf_op jit(solution)/shard_map/attend_back/pallas_call | solution.py:34
  187.8 5.8 %wgrad.1 = (bf16[3,2,4,64,128]{4,3,2,1,0:T(8,128)(2,1)}, bf16[3,2,4,64,128]{4,3,2,1,0:T(8,128)(2,1)}) custom-call(s32[3]{0:T(128)} %pad_add_fusion.meta, bf16[2048,512]{1,0:T(8,128)(2,1)} %get-tuple-element.97.h1, bf16[2048,384]{1,0:T(8,128)(2,1)} %attend_back.2.refs_0_, bf16[2048,384]{1,0:T(8,128)(2,1)} %attend_back.3.refs_1_), custom_call_target="tpu_custom_call" | custom-call | flops 1610612736 | bytes 8388608 | tf_op jit(solution)/shard_map/wgrad/pallas_call | solution.py:34
  194.8 2.5 plane_sum.2
  198.1 2.1 arrange.1
  200.2 8.0 %qkv_back.1 = (f32[2,512,512]{2,1,0:T(8,128)}, bf16[2,512,512]{2,1,0:T(8,128)(2,1)}, f32[16,512]{1,0:T(8,128)}) custom-call(s32[3]{0:T(128)} %pad_add_fusion.meta, f32[16,512]{1,0:T(8,128)} %get-tuple-element.121.vec_in, bf16[2048,384]{1,0:T(8,128)(2,1)} %attend_back.2.refs_0_, bf16[2048,384]{1,0:T(8,128)(2,1)} %attend_back.3.refs_1_, ...), custom_call_target="tpu_custom_call" | custom-call | flops 1610612736 | bytes 12582912 | tf_op jit(solution)/shard_map/qkv_back/pallas_call | solution.py:34
  208.9 7.1 %collective-permute-start.37 = (bf16[4,192,128]{2,1,0:T(8,128)(2,1)}, bf16[4,192,128]{2,1,0:T(8,128)(2,1)S(1)}, u32[]{:S(2)}, u32[]{:S(2)}) collective-permute-start(bf16[4,192,128]{2,1,0:T(8,128)(2,1)} %get-tuple-element.156), channel_id=1, source_target_pairs={{0,16},{4,20},{8,24},{12,28},{16,0},{20,4},{24,8},{28,12},{1,17},{... | collective-permute-start | bytes 589832 | tf_op jit(solution)/shard_map/ppermute | solution.py:848
  216.1 1.9 collective-permute-start.39
  219.0 5.2 %norm_back.1 = (bf16[2,512,512]{2,1,0:T(8,128)(2,1)}, bf16[512,512]{1,0:T(8,128)(2,1)}, f32[16,512]{1,0:T(8,128)}) custom-call(s32[3]{0:T(128)} %pad_add_fusion.meta, f32[1,512]{1,0:T(1,128)} %bitcast.45, f32[16,512]{1,0:T(8,128)} %get-tuple-element.150.vec, f32[16,512]{1,0:T(8,128)} %copy-done.28, f32[1024,512]{1,0:T(8,128)} %get-tuple-element.151.g_resid, ...), custom_call_target="tpu_custom_call" | custom-call | flops 15728640 | bytes 8388608 | tf_op jit(solution)/shard_map/norm_back/pallas_call | solution.py:34
  225.3 2.0 collective-permute-start.41
  227.2 5.0 %collective-permute-done.38.c = bf16[4,192,128]{2,1,0:T(8,128)(2,1)S(1)} collective-permute-done((bf16[4,192,128]{2,1,0:T(8,128)(2,1)}, bf16[4,192,128]{2,1,0:T(8,128)(2,1)S(1)}, u32[]{:S(2)}, u32[]{:S(2)}) %collective-permute-start.38) | collective-permute-done | bytes 196640 | tf_op jit(solution)/shard_map/ppermute | solution.py:848
  232.2 5.6 %collective-permute-start.40 = (f32[16,512]{1,0:T(8,128)}, f32[16,512]{1,0:T(8,128)S(1)}, u32[]{:S(2)}, u32[]{:S(2)}) collective-permute-start(f32[16,512]{1,0:T(8,128)} %get-tuple-element.159.refs_0_), channel_id=1, source_target_pairs={{0,16},{4,20},{8,24},{12,28},{16,0},{20,4},{24,8},{28,12},{1,17},{... | collective-permute-start | bytes 98312 | tf_op jit(solution)/shard_map/ppermute | solution.py:848
  237.8 2.4 collective-permute-start.50
  240.2 1.3 collective-permute-start.36
  242.0 2.0 collective-permute-start.52
  244.0 2.0 plane_sum.3
  246.0 2.0 collective-permute-start.48
  248.0 5.3 %collective-permute-start.47 = (f32[16,512]{1,0:T(8,128)}, f32[16,512]{1,0:T(8,128)S(1)}, u32[]{:S(2)}, u32[]{:S(2)}) collective-permute-start(f32[16,512]{1,0:T(8,128)} %get-tuple-element.164.refs_0_), channel_id=1, source_target_pairs={{0,2},{1,3},{2,0},{3,1},{4,6},{5,7},{6,4},{7,5},{8,10},{9,11},{10,... | collective-permute-start | bytes 98312 | tf_op jit(solution)/shard_map/ppermute | solution.py:851
  255.6 2.2 collective-permute-start.44
  257.8 2.8 %collective-permute-start.45 = (bf16[192,128]{1,0:T(8,128)(2,1)}, bf16[192,128]{1,0:T(8,128)(2,1)S(1)}, u32[]{:S(2)}, u32[]{:S(2)}) collective-permute-start(bf16[192,128]{1,0:T(8,128)(2,1)} %get-tuple-element.163), channel_id=1, source_target_pairs={{0,3},{1,0},{2,1},{3,2},{4,7},{5,4},{6,5},{7,6},{8,11},{9,8},{10,9... | collective-permute-start | bytes 147464 | tf_op jit(solution)/shard_map/ppermute | solution.py:851
  261.8 1.9 line_sum.3.r
  263.7 1.9 collective-permute-start.53
  266.9 1.6 line_sum.2
  269.2 1.3 slice.6
  271.2 1.6 collective-permute-done.49.o
  273.3 1.5 finish_qkv.1
  275.5 1.8 finish.1
  (185 shorter events, 27.7 us)
Async XLA Ops:
  3.3 16.4 %collective-permute-start = (bf16[512,512]{1,0:T(8,128)(2,1)S(1)}, bf16[512,512]{1,0:T(8,128)(2,1)S(1)}, u32[]{:S(2)}, u32[]{:S(2)}) collective-permute-start(bf16[512,512]{1,0:T(8,128)(2,1)S(1)} %dynamic-slice_bitcast_fusion.2), channel_id=1, source_target_pairs={{0,8},{4,12},{8,0},{12,4},{1,9},{5,13},{9,1},{13,5},{2,10},{6,14},... | collective-permute-start | bytes 1572872 | tf_op jit(solution)/shard_map/ppermute | solution.py:839
  6.3 7.4 %collective-permute-start.6 = (bf16[64,384]{1,0:T(8,128)(2,1)}, bf16[64,384]{1,0:T(8,128)(2,1)S(1)}, u32[]{:S(2)}, u32[]{:S(2)}) collective-permute-start(bf16[64,384]{1,0:T(8,128)(2,1)} %get-tuple-element.93), channel_id=1, source_target_pairs={{0,3},{1,0},{2,1},{3,2},{4,7},{5,4},{6,5},{7,6},{8,11},{9,8},{10,9... | collective-permute-start | bytes 147464 | tf_op jit(solution)/shard_map/ppermute | solution.py:851
  9.9 6.8 %collective-permute-start.4 = (bf16[64,384]{1,0:T(8,128)(2,1)}, bf16[64,384]{1,0:T(8,128)(2,1)S(1)}, u32[]{:S(2)}, u32[]{:S(2)}) collective-permute-start(bf16[64,384]{1,0:T(8,128)(2,1)} %get-tuple-element.93), channel_id=1, source_target_pairs={{0,1},{1,2},{2,3},{3,0},{4,5},{5,6},{6,7},{7,4},{8,9},{9,10},{10,1... | collective-permute-start | bytes 147464 | tf_op jit(solution)/shard_map/ppermute | solution.py:851
  10.9 8.2 %collective-permute-start.18 = (bf16[576,128]{1,0:T(8,128)(2,1)}, bf16[576,128]{1,0:T(8,128)(2,1)S(1)}, u32[]{:S(2)}, u32[]{:S(2)}) collective-permute-start(bf16[576,128]{1,0:T(8,128)(2,1)} %get-tuple-element.111), channel_id=1, source_target_pairs={{0,3},{1,0},{2,1},{3,2},{4,7},{5,4},{6,5},{7,6},{8,11},{9,8},{10,9... | collective-permute-start | bytes 442376 | tf_op jit(solution)/shard_map/ppermute | solution.py:851
  13.8 14.3 %collective-permute-start.17 = (bf16[576,128]{1,0:T(8,128)(2,1)}, bf16[576,128]{1,0:T(8,128)(2,1)S(1)}, u32[]{:S(2)}, u32[]{:S(2)}) collective-permute-start(bf16[576,128]{1,0:T(8,128)(2,1)} %get-tuple-element.111), channel_id=1, source_target_pairs={{0,2},{1,3},{2,0},{3,1},{4,6},{5,7},{6,4},{7,5},{8,10},{9,11},{10,... | collective-permute-start | bytes 442376 | tf_op jit(solution)/shard_map/ppermute | solution.py:851
  15.8 12.8 %collective-permute-start.16 = (bf16[576,128]{1,0:T(8,128)(2,1)}, bf16[576,128]{1,0:T(8,128)(2,1)S(1)}, u32[]{:S(2)}, u32[]{:S(2)}) collective-permute-start(bf16[576,128]{1,0:T(8,128)(2,1)} %get-tuple-element.111), channel_id=1, source_target_pairs={{0,1},{1,2},{2,3},{3,0},{4,5},{5,6},{6,7},{7,4},{8,9},{9,10},{10,1... | collective-permute-start | bytes 442376 | tf_op jit(solution)/shard_map/ppermute | solution.py:851
  17.6 12.5 %collective-permute-start.12 = (bf16[4,64,384]{2,1,0:T(8,128)(2,1)S(1)}, bf16[4,64,384]{2,1,0:T(8,128)(2,1)}, u32[]{:S(2)}, u32[]{:S(2)}) collective-permute-start(bf16[4,64,384]{2,1,0:T(8,128)(2,1)S(1)} %pad_maximum_fusion.1.refs_0_), channel_id=1, source_target_pairs={{0,24},{4,28},{8,16},{12,20},{16,8},{20,12},{24,0},{28,4},{1,25},{... | collective-permute-start | bytes 589832 | tf_op jit(solution)/shard_map/ppermute | solution.py:848
  19.2 17.3 %collective-permute-start.2 = (bf16[512,512]{1,0:T(8,128)(2,1)S(1)}, bf16[512,512]{1,0:T(8,128)(2,1)S(1)}, u32[]{:S(2)}, u32[]{:S(2)}) collective-permute-start(bf16[512,512]{1,0:T(8,128)(2,1)S(1)} %dynamic-slice_bitcast_fusion.3.refs_0_.refs_4_.refs_1_), channel_id=1, source_target_pairs={{0,4},{4,0},{8,12},{12,8},{1,5},{5,1},{9,13},{13,9},{2,6},{6,2},{1... | collective-permute-start | bytes 1572872 | tf_op jit(solution)/shard_map/ppermute | solution.py:842
  19.6 18.5 %collective-permute-start.3 = (bf16[512,512]{1,0:T(8,128)(2,1)S(1)}, bf16[512,512]{1,0:T(8,128)(2,1)S(1)}, u32[]{:S(2)}, u32[]{:S(2)}) collective-permute-start(bf16[512,512]{1,0:T(8,128)(2,1)S(1)} %collective-permute-done.refs_2_.refs_1_.refs_6_), channel_id=1, source_target_pairs={{0,4},{4,0},{8,12},{12,8},{1,5},{5,1},{9,13},{13,9},{2,6},{6,2},{1... | collective-permute-start | bytes 1572872 | tf_op jit(solution)/shard_map/ppermute | solution.py:842
  28.1 5.9 %collective-permute-start.10 = (bf16[4,64,384]{2,1,0:T(8,128)(2,1)S(1)}, bf16[4,64,384]{2,1,0:T(8,128)(2,1)}, u32[]{:S(2)}, u32[]{:S(2)}) collective-permute-start(bf16[4,64,384]{2,1,0:T(8,128)(2,1)S(1)} %pad_maximum_fusion.1.refs_0_), channel_id=1, source_target_pairs={{0,8},{4,12},{8,0},{12,4},{16,24},{20,28},{24,16},{28,20},{1,9},{5... | collective-permute-start | bytes 589832 | tf_op jit(solution)/shard_map/ppermute | solution.py:848
  34.0 11.7 %collective-permute-start.13 = (bf16[4,64,384]{2,1,0:T(8,128)(2,1)}, bf16[4,64,384]{2,1,0:T(8,128)(2,1)}, u32[]{:S(2)}, u32[]{:S(2)}) collective-permute-start(bf16[4,64,384]{2,1,0:T(8,128)(2,1)} %collective-permute-done.12.refs_6_), channel_id=1, source_target_pairs={{0,4},{4,0},{8,12},{12,8},{1,5},{5,1},{9,13},{13,9},{2,6},{6,2},{1... | collective-permute-start | bytes 589832 | tf_op jit(solution)/shard_map/ppermute | solution.py:842
  34.4 12.9 %collective-permute-start.11 = (bf16[4,64,384]{2,1,0:T(8,128)(2,1)}, bf16[4,64,384]{2,1,0:T(8,128)(2,1)}, u32[]{:S(2)}, u32[]{:S(2)}) collective-permute-start(bf16[4,64,384]{2,1,0:T(8,128)(2,1)} %collective-permute-done.10.refs_4_), channel_id=1, source_target_pairs={{0,4},{4,0},{8,12},{12,8},{1,5},{5,1},{9,13},{13,9},{2,6},{6,2},{1... | collective-permute-start | bytes 589832 | tf_op jit(solution)/shard_map/ppermute | solution.py:842
  34.5 13.3 %collective-permute-start.9 = (bf16[4,64,384]{2,1,0:T(8,128)(2,1)}, bf16[4,64,384]{2,1,0:T(8,128)(2,1)}, u32[]{:S(2)}, u32[]{:S(2)}) collective-permute-start(bf16[4,64,384]{2,1,0:T(8,128)(2,1)} %collective-permute-done.8.refs_2_), channel_id=1, source_target_pairs={{0,4},{4,0},{8,12},{12,8},{1,5},{5,1},{9,13},{13,9},{2,6},{6,2},{1... | collective-permute-start | bytes 589832 | tf_op jit(solution)/shard_map/ppermute | solution.py:842
  36.5 40.2 %collective-permute-start.1 = (bf16[512,512]{1,0:T(8,128)(2,1)}, bf16[512,512]{1,0:T(8,128)(2,1)}, u32[]{:S(2)}, u32[]{:S(2)}) collective-permute-start(bf16[512,512]{1,0:T(8,128)(2,1)} %get-tuple-element.178), channel_id=1, source_target_pairs={{0,8},{4,12},{8,0},{12,4},{1,9},{5,13},{9,1},{13,5},{2,10},{6,14},... | collective-permute-start | bytes 1572872 | tf_op jit(solution)/shard_map/ppermute | solution.py:839
  38.1 28.9 %collective-permute-start.21 = (bf16[4,576,128]{2,1,0:T(8,128)(2,1)S(1)}, bf16[4,576,128]{2,1,0:T(8,128)(2,1)}, u32[]{:S(2)}, u32[]{:S(2)}) collective-permute-start(bf16[4,576,128]{2,1,0:T(8,128)(2,1)S(1)} %pad_maximum_fusion.refs_13_), channel_id=1, source_target_pairs={{0,24},{4,28},{8,16},{12,20},{16,8},{20,12},{24,0},{28,4},{1,25},{... | collective-permute-start | bytes 1769480 | tf_op jit(solution)/shard_map/ppermute | solution.py:848
  45.7 30.4 %collective-permute-start.20 = (bf16[4,576,128]{2,1,0:T(8,128)(2,1)S(1)}, bf16[4,576,128]{2,1,0:T(8,128)(2,1)S(1)}, u32[]{:S(2)}, u32[]{:S(2)}) collective-permute-start(bf16[4,576,128]{2,1,0:T(8,128)(2,1)S(1)} %pad_maximum_fusion.refs_13_), channel_id=1, source_target_pairs={{0,8},{4,12},{8,0},{12,4},{16,24},{20,28},{24,16},{28,20},{1,9},{5... | collective-permute-start | bytes 1769480 | tf_op jit(solution)/shard_map/ppermute | solution.py:848
  47.2 28.8 %collective-permute-start.19 = (bf16[4,576,128]{2,1,0:T(8,128)(2,1)S(1)}, bf16[4,576,128]{2,1,0:T(8,128)(2,1)S(1)}, u32[]{:S(2)}, u32[]{:S(2)}) collective-permute-start(bf16[4,576,128]{2,1,0:T(8,128)(2,1)S(1)} %pad_maximum_fusion.refs_13_), channel_id=1, source_target_pairs={{0,16},{4,20},{8,24},{12,28},{16,0},{20,4},{24,8},{28,12},{1,17},{... | collective-permute-start | bytes 1769480 | tf_op jit(solution)/shard_map/ppermute | solution.py:848
  67.0 10.2 %collective-permute-start.15 = (bf16[2,512,128]{2,1,0:T(8,128)(2,1)}, bf16[2,512,128]{2,1,0:T(8,128)(2,1)S(1)}, u32[]{:S(2)}, u32[]{:S(2)}) collective-permute-start(bf16[2,512,128]{2,1,0:T(8,128)(2,1)} %get-tuple-element.109.refs_3_), channel_id=1, source_target_pairs={{0,4},{4,0},{8,12},{12,8},{1,5},{5,1},{9,13},{13,9},{2,6},{6,2},{1... | collective-permute-start | bytes 786440 | tf_op jit(solution)/shard_map/ppermute | solution.py:842
  76.1 13.0 %collective-permute-start.22 = (bf16[4,576,128]{2,1,0:T(8,128)(2,1)S(1)}, bf16[4,576,128]{2,1,0:T(8,128)(2,1)}, u32[]{:S(2)}, u32[]{:S(2)}) collective-permute-start(bf16[4,576,128]{2,1,0:T(8,128)(2,1)S(1)} %pad_maximum_fusion.refs_13_), channel_id=1, source_target_pairs={{0,4},{4,0},{8,12},{12,8},{1,5},{5,1},{9,13},{13,9},{2,6},{6,2},{1... | collective-permute-start | bytes 1769480 | tf_op jit(solution)/shard_map/ppermute | solution.py:842
  76.1 12.9 %collective-permute-start.23 = (bf16[4,576,128]{2,1,0:T(8,128)(2,1)S(1)}, bf16[4,576,128]{2,1,0:T(8,128)(2,1)}, u32[]{:S(2)}, u32[]{:S(2)}) collective-permute-start(bf16[4,576,128]{2,1,0:T(8,128)(2,1)S(1)} %collective-permute-done.19.refs_15_), channel_id=1, source_target_pairs={{0,4},{4,0},{8,12},{12,8},{1,5},{5,1},{9,13},{13,9},{2,6},{6,2},{1... | collective-permute-start | bytes 1769480 | tf_op jit(solution)/shard_map/ppermute | solution.py:842
  76.6 12.4 %collective-permute-start.24 = (bf16[4,576,128]{2,1,0:T(8,128)(2,1)S(1)}, bf16[4,576,128]{2,1,0:T(8,128)(2,1)}, u32[]{:S(2)}, u32[]{:S(2)}) collective-permute-start(bf16[4,576,128]{2,1,0:T(8,128)(2,1)S(1)} %collective-permute-done.20.refs_17_), channel_id=1, source_target_pairs={{0,4},{4,0},{8,12},{12,8},{1,5},{5,1},{9,13},{13,9},{2,6},{6,2},{1... | collective-permute-start | bytes 1769480 | tf_op jit(solution)/shard_map/ppermute | solution.py:842
  76.7 12.4 %collective-permute-start.25 = (bf16[4,576,128]{2,1,0:T(8,128)(2,1)}, bf16[4,576,128]{2,1,0:T(8,128)(2,1)}, u32[]{:S(2)}, u32[]{:S(2)}) collective-permute-start(bf16[4,576,128]{2,1,0:T(8,128)(2,1)} %collective-permute-done.21.refs_19_), channel_id=1, source_target_pairs={{0,4},{4,0},{8,12},{12,8},{1,5},{5,1},{9,13},{13,9},{2,6},{6,2},{1... | collective-permute-start | bytes 1769480 | tf_op jit(solution)/shard_map/ppermute | solution.py:842
  77.2 11.9 %collective-permute-start.14 = (bf16[2,512,128]{2,1,0:T(8,128)(2,1)}, bf16[2,512,128]{2,1,0:T(8,128)(2,1)S(1)}, u32[]{:S(2)}, u32[]{:S(2)}) collective-permute-start(bf16[2,512,128]{2,1,0:T(8,128)(2,1)} %get-tuple-element.104.refs_3_), channel_id=1, source_target_pairs={{0,4},{4,0},{8,12},{12,8},{1,5},{5,1},{9,13},{13,9},{2,6},{6,2},{1... | collective-permute-start | bytes 786440 | tf_op jit(solution)/shard_map/ppermute | solution.py:842
  123.1 24.4 %collective-permute-start.28 = (bf16[4,4,576,128]{3,2,1,0:T(8,128)(2,1)}, bf16[4,4,576,128]{3,2,1,0:T(8,128)(2,1)S(1)}, u32[]{:S(2)}, u32[]{:S(2)}) collective-permute-start(bf16[4,4,576,128]{3,2,1,0:T(8,128)(2,1)} %get-tuple-element.129), channel_id=1, source_target_pairs={{0,4},{4,0},{8,12},{12,8},{1,5},{5,1},{9,13},{13,9},{2,6},{6,2},{1... | collective-permute-start | bytes 7077896 | tf_op jit(solution)/shard_map/ppermute | solution.py:842
  123.3 40.2 %collective-permute-start.29 = (bf16[2,512,128]{2,1,0:T(8,128)(2,1)}, bf16[2,512,128]{2,1,0:T(8,128)(2,1)S(1)}, u32[]{:S(2)}, u32[]{:S(2)}) collective-permute-start(bf16[2,512,128]{2,1,0:T(8,128)(2,1)} %get-tuple-element.133), channel_id=1, source_target_pairs={{0,4},{4,0},{8,12},{12,8},{1,5},{5,1},{9,13},{13,9},{2,6},{6,2},{1... | collective-permute-start | bytes 786440 | tf_op jit(solution)/shard_map/ppermute | solution.py:842
  152.9 40.7 %collective-permute-start.30 = (bf16[4,576,128]{2,1,0:T(8,128)(2,1)}, bf16[4,576,128]{2,1,0:T(8,128)(2,1)S(1)}, u32[]{:S(2)}, u32[]{:S(2)}) collective-permute-start(bf16[4,576,128]{2,1,0:T(8,128)(2,1)} %get-tuple-element.135), channel_id=1, source_target_pairs={{0,16},{4,20},{8,24},{12,28},{16,0},{20,4},{24,8},{28,12},{1,17},{... | collective-permute-start | bytes 1769480 | tf_op jit(solution)/shard_map/ppermute | solution.py:848
  152.9 40.7 %collective-permute-start.31 = (bf16[4,576,128]{2,1,0:T(8,128)(2,1)}, bf16[4,576,128]{2,1,0:T(8,128)(2,1)S(1)}, u32[]{:S(2)}, u32[]{:S(2)}) collective-permute-start(bf16[4,576,128]{2,1,0:T(8,128)(2,1)} %get-tuple-element.136), channel_id=1, source_target_pairs={{0,8},{4,12},{8,0},{12,4},{16,24},{20,28},{24,16},{28,20},{1,9},{5... | collective-permute-start | bytes 1769480 | tf_op jit(solution)/shard_map/ppermute | solution.py:848
  163.5 30.1 %collective-permute-start.32 = (bf16[4,576,128]{2,1,0:T(8,128)(2,1)}, bf16[4,576,128]{2,1,0:T(8,128)(2,1)S(1)}, u32[]{:S(2)}, u32[]{:S(2)}) collective-permute-start(bf16[4,576,128]{2,1,0:T(8,128)(2,1)} %get-tuple-element.137), channel_id=1, source_target_pairs={{0,24},{4,28},{8,16},{12,20},{16,8},{20,12},{24,0},{28,4},{1,25},{... | collective-permute-start | bytes 1769480 | tf_op jit(solution)/shard_map/ppermute | solution.py:848
  208.2 9.8 %collective-permute-start.35 = (bf16[2,512,512]{2,1,0:T(8,128)(2,1)}, bf16[2,512,512]{2,1,0:T(8,128)(2,1)S(1)}, u32[]{:S(2)}, u32[]{:S(2)}) collective-permute-start(bf16[2,512,512]{2,1,0:T(8,128)(2,1)} %get-tuple-element.153), channel_id=1, source_target_pairs={{0,4},{4,0},{8,12},{12,8},{1,5},{5,1},{9,13},{13,9},{2,6},{6,2},{1... | collective-permute-start | bytes 3145736 | tf_op jit(solution)/shard_map/ppermute | solution.py:842
  208.7 37.3 %collective-permute-start.26 = (bf16[512,512]{1,0:T(8,128)(2,1)}, bf16[512,512]{1,0:T(8,128)(2,1)S(1)}, u32[]{:S(2)}, u32[]{:S(2)}) collective-permute-start(bf16[512,512]{1,0:T(8,128)(2,1)} %get-tuple-element.120), channel_id=1, source_target_pairs={{0,8},{4,12},{8,0},{12,4},{1,9},{5,13},{9,1},{13,5},{2,10},{6,14},... | collective-permute-start | bytes 1572872 | tf_op jit(solution)/shard_map/ppermute | solution.py:839
  208.9 7.2 %collective-permute-start.34 = (f32[16,512]{1,0:T(8,128)}, f32[16,512]{1,0:T(8,128)S(1)}, u32[]{:S(2)}, u32[]{:S(2)}) collective-permute-start(f32[16,512]{1,0:T(8,128)} %get-tuple-element.150.vec), channel_id=1, source_target_pairs={{0,4},{4,0},{8,12},{12,8},{1,5},{5,1},{9,13},{13,9},{2,6},{6,2},{1... | collective-permute-start | bytes 98312 | tf_op jit(solution)/shard_map/ppermute | solution.py:842
  208.9 16.3 %collective-permute-start.37 = (bf16[4,192,128]{2,1,0:T(8,128)(2,1)}, bf16[4,192,128]{2,1,0:T(8,128)(2,1)S(1)}, u32[]{:S(2)}, u32[]{:S(2)}) collective-permute-start(bf16[4,192,128]{2,1,0:T(8,128)(2,1)} %get-tuple-element.156), channel_id=1, source_target_pairs={{0,16},{4,20},{8,24},{12,28},{16,0},{20,4},{24,8},{28,12},{1,17},{... | collective-permute-start | bytes 589832 | tf_op jit(solution)/shard_map/ppermute | solution.py:848
  216.0 16.2 %collective-permute-start.38 = (bf16[4,192,128]{2,1,0:T(8,128)(2,1)}, bf16[4,192,128]{2,1,0:T(8,128)(2,1)S(1)}, u32[]{:S(2)}, u32[]{:S(2)}) collective-permute-start(bf16[4,192,128]{2,1,0:T(8,128)(2,1)} %get-tuple-element.157), channel_id=1, source_target_pairs={{0,8},{4,12},{8,0},{12,4},{16,24},{20,28},{24,16},{28,20},{1,9},{5... | collective-permute-start | bytes 589832 | tf_op jit(solution)/shard_map/ppermute | solution.py:848
  216.1 21.7 %collective-permute-start.39 = (bf16[4,192,128]{2,1,0:T(8,128)(2,1)S(1)}, bf16[4,192,128]{2,1,0:T(8,128)(2,1)S(1)}, u32[]{:S(2)}, u32[]{:S(2)}) collective-permute-start(bf16[4,192,128]{2,1,0:T(8,128)(2,1)S(1)} %copy-done.44), channel_id=1, source_target_pairs={{0,24},{4,28},{8,16},{12,20},{16,8},{20,12},{24,0},{28,4},{1,25},{... | collective-permute-start | bytes 589832 | tf_op jit(solution)/shard_map/ppermute | solution.py:848
  224.2 16.0 %collective-permute-start.42 = (f32[16,512]{1,0:T(8,128)}, f32[16,512]{1,0:T(8,128)S(1)}, u32[]{:S(2)}, u32[]{:S(2)}) collective-permute-start(f32[16,512]{1,0:T(8,128)} %get-tuple-element.159.refs_0_), channel_id=1, source_target_pairs={{0,24},{4,28},{8,16},{12,20},{16,8},{20,12},{24,0},{28,4},{1,25},{... | collective-permute-start | bytes 98312 | tf_op jit(solution)/shard_map/ppermute | solution.py:848
  225.3 16.3 %collective-permute-start.41 = (f32[16,512]{1,0:T(8,128)}, f32[16,512]{1,0:T(8,128)S(1)}, u32[]{:S(2)}, u32[]{:S(2)}) collective-permute-start(f32[16,512]{1,0:T(8,128)} %get-tuple-element.159.refs_0_), channel_id=1, source_target_pairs={{0,8},{4,12},{8,0},{12,4},{16,24},{20,28},{24,16},{28,20},{1,9},{5... | collective-permute-start | bytes 98312 | tf_op jit(solution)/shard_map/ppermute | solution.py:848
  232.2 9.7 %collective-permute-start.40 = (f32[16,512]{1,0:T(8,128)}, f32[16,512]{1,0:T(8,128)S(1)}, u32[]{:S(2)}, u32[]{:S(2)}) collective-permute-start(f32[16,512]{1,0:T(8,128)} %get-tuple-element.159.refs_0_), channel_id=1, source_target_pairs={{0,16},{4,20},{8,24},{12,28},{16,0},{20,4},{24,8},{28,12},{1,17},{... | collective-permute-start | bytes 98312 | tf_op jit(solution)/shard_map/ppermute | solution.py:848
  237.8 10.2 %collective-permute-start.50 = (bf16[576,128]{1,0:T(8,128)(2,1)S(1)}, bf16[576,128]{1,0:T(8,128)(2,1)S(1)}, u32[]{:S(2)}, u32[]{:S(2)}) collective-permute-start(bf16[576,128]{1,0:T(8,128)(2,1)S(1)} %copy-done.45), channel_id=1, source_target_pairs={{0,1},{1,2},{2,3},{3,0},{4,5},{5,6},{6,7},{7,4},{8,9},{9,10},{10,1... | collective-permute-start | bytes 442376 | tf_op jit(solution)/shard_map/ppermute | solution.py:851
  240.2 37.2 %collective-permute-start.36 = (bf16[512,512]{1,0:T(8,128)(2,1)}, bf16[512,512]{1,0:T(8,128)(2,1)S(1)}, u32[]{:S(2)}, u32[]{:S(2)}) collective-permute-start(bf16[512,512]{1,0:T(8,128)(2,1)} %get-tuple-element.155), channel_id=1, source_target_pairs={{0,8},{4,12},{8,0},{12,4},{1,9},{5,13},{9,1},{13,5},{2,10},{6,14},... | collective-permute-start | bytes 1572872 | tf_op jit(solution)/shard_map/ppermute | solution.py:839
  241.5 11.8 %collective-permute-start.51 = (bf16[576,128]{1,0:T(8,128)(2,1)}, bf16[576,128]{1,0:T(8,128)(2,1)S(1)}, u32[]{:S(2)}, u32[]{:S(2)}) collective-permute-start(bf16[576,128]{1,0:T(8,128)(2,1)} %get-tuple-element.167), channel_id=1, source_target_pairs={{0,2},{1,3},{2,0},{3,1},{4,6},{5,7},{6,4},{7,5},{8,10},{9,11},{10,... | collective-permute-start | bytes 442376 | tf_op jit(solution)/shard_map/ppermute | solution.py:851
  242.0 12.5 %collective-permute-start.52 = (bf16[576,128]{1,0:T(8,128)(2,1)}, bf16[576,128]{1,0:T(8,128)(2,1)S(1)}, u32[]{:S(2)}, u32[]{:S(2)}) collective-permute-start(bf16[576,128]{1,0:T(8,128)(2,1)} %get-tuple-element.168), channel_id=1, source_target_pairs={{0,3},{1,0},{2,1},{3,2},{4,7},{5,4},{6,5},{7,6},{8,11},{9,8},{10,9... | collective-permute-start | bytes 442376 | tf_op jit(solution)/shard_map/ppermute | solution.py:851
  246.0 9.7 %collective-permute-start.48 = (f32[16,512]{1,0:T(8,128)}, f32[16,512]{1,0:T(8,128)S(1)}, u32[]{:S(2)}, u32[]{:S(2)}) collective-permute-start(f32[16,512]{1,0:T(8,128)} %get-tuple-element.164.refs_0_), channel_id=1, source_target_pairs={{0,3},{1,0},{2,1},{3,2},{4,7},{5,4},{6,5},{7,6},{8,11},{9,8},{10,9... | collective-permute-start | bytes 98312 | tf_op jit(solution)/shard_map/ppermute | solution.py:851
  248.0 9.9 %collective-permute-start.47 = (f32[16,512]{1,0:T(8,128)}, f32[16,512]{1,0:T(8,128)S(1)}, u32[]{:S(2)}, u32[]{:S(2)}) collective-permute-start(f32[16,512]{1,0:T(8,128)} %get-tuple-element.164.refs_0_), channel_id=1, source_target_pairs={{0,2},{1,3},{2,0},{3,1},{4,6},{5,7},{6,4},{7,5},{8,10},{9,11},{10,... | collective-permute-start | bytes 98312 | tf_op jit(solution)/shard_map/ppermute | solution.py:851
  253.3 10.4 %collective-permute-start.46 = (f32[16,512]{1,0:T(8,128)}, f32[16,512]{1,0:T(8,128)S(1)}, u32[]{:S(2)}, u32[]{:S(2)}) collective-permute-start(f32[16,512]{1,0:T(8,128)} %get-tuple-element.164.refs_0_), channel_id=1, source_target_pairs={{0,1},{1,2},{2,3},{3,0},{4,5},{5,6},{6,7},{7,4},{8,9},{9,10},{10,1... | collective-permute-start | bytes 98312 | tf_op jit(solution)/shard_map/ppermute | solution.py:851
  254.5 11.1 %collective-permute-start.43 = (bf16[192,128]{1,0:T(8,128)(2,1)}, bf16[192,128]{1,0:T(8,128)(2,1)S(1)}, u32[]{:S(2)}, u32[]{:S(2)}) collective-permute-start(bf16[192,128]{1,0:T(8,128)(2,1)} %get-tuple-element.161), channel_id=1, source_target_pairs={{0,1},{1,2},{2,3},{3,0},{4,5},{5,6},{6,7},{7,4},{8,9},{9,10},{10,1... | collective-permute-start | bytes 147464 | tf_op jit(solution)/shard_map/ppermute | solution.py:851
  255.6 10.0 %collective-permute-start.44 = (bf16[192,128]{1,0:T(8,128)(2,1)}, bf16[192,128]{1,0:T(8,128)(2,1)S(1)}, u32[]{:S(2)}, u32[]{:S(2)}) collective-permute-start(bf16[192,128]{1,0:T(8,128)(2,1)} %get-tuple-element.162), channel_id=1, source_target_pairs={{0,2},{1,3},{2,0},{3,1},{4,6},{5,7},{6,4},{7,5},{8,10},{9,11},{10,... | collective-permute-start | bytes 147464 | tf_op jit(solution)/shard_map/ppermute | solution.py:851
  257.8 7.8 %collective-permute-start.45 = (bf16[192,128]{1,0:T(8,128)(2,1)}, bf16[192,128]{1,0:T(8,128)(2,1)S(1)}, u32[]{:S(2)}, u32[]{:S(2)}) collective-permute-start(bf16[192,128]{1,0:T(8,128)(2,1)} %get-tuple-element.163), channel_id=1, source_target_pairs={{0,3},{1,0},{2,1},{3,2},{4,7},{5,4},{6,5},{7,6},{8,11},{9,8},{10,9... | collective-permute-start | bytes 147464 | tf_op jit(solution)/shard_map/ppermute | solution.py:851
  263.7 11.2 %collective-permute-start.53 = (bf16[576,128]{1,0:T(8,128)(2,1)}, bf16[576,128]{1,0:T(8,128)(2,1)S(1)}, u32[]{:S(2)}, u32[]{:S(2)}) collective-permute-start(bf16[576,128]{1,0:T(8,128)(2,1)} %line_sum.3.r), channel_id=1, source_target_pairs={{0,16},{4,20},{8,24},{12,28},{16,0},{20,4},{24,8},{28,12},{1,17},{... | collective-permute-start | bytes 442376 | tf_op jit(solution)/shard_map/ppermute | solution.py:848
  (52 other events, 483.1 us)

commit v3 on v2

--- a/solution.py
+++ b/solution.py
@@ -30,6 +30,13 @@
     return jax.ShapeDtypeStruct(shape, dtype)
 
 
+NEAR = ('core_sum', 'plane_sum', 'arrange', 'plane_sum_qkv', 'line_sum_qkv', 'finish', 'finish_qkv', 'norm_back')
+
+
+def near(a):
+    return pltpu.with_memory_space_constraint(a, pltpu.VMEM)
+
+
 def call(kernel, name, ins, outs, scratch=(), flops=0, nbytes=0, trans=0, **kw):
     return pl.pallas_call(
         kernel,
@@ -38,9 +45,9 @@
         in_specs=[spec for _, spec in ins],
         out_specs=tuple(VM for _ in outs),
         scratch_shapes=list(scratch),
-        compiler_params=pltpu.CompilerParams(vmem_limit_bytes=60 * 1024 * 1024, **kw),
+        compiler_params=pltpu.CompilerParams(vmem_limit_bytes=(60 if name == "ffn" else 36) * 1024 * 1024, **kw),
         cost_estimate=pl.CostEstimate(flops=flops, bytes_accessed=nbytes, transcendentals=trans),
-    )(*[a for a, _ in ins])
+    )(*[near(a) if spec is VM and name in NEAR and a.ndim > 1 else a for a, spec in ins])
 
 
 def nt(a, b):
@@ -114,27 +121,22 @@
     HL, D, NP = geo.HL, geo.D, geo.NP
     outs = refs[-(4 * NP) - 2 : -2] if geo.fast else refs[-(4 * NP) :]
     if geo.fast:
-        pieces, (wscr, sem) = refs[:8], refs[-2:]
-        x, z = meta[0], meta[2]
+        pieces, (wscr, sem) = refs[:4], refs[-2:]
+        z = meta[2]
         y, c = meta[1] // 2, meta[1] % 2
         copies = []
-        for quad in range(4):
-            yy = y if quad < 2 else 1 - y
-            hh = x if quad % 2 == 0 else 1 - x
-            for cc in range(2):
-                cp = c if cc == 0 else 1 - c
-                for d in range(4):
-                    zz = lax.rem(z - d + 4, 4)
-                    copies.append(
-                        pltpu.make_async_copy(
-                            pieces[quad * 2 + cc].at[d],
-                            wscr.at[
-                                pl.ds(al(zz * 128 + hh * 64, 64), 64),
-                                pl.ds(al((2 * yy + cp) * 384, 128), 384),
-                            ],
-                            sem,
-                        )
+        for n in range(4):
+            yy = y if n < 2 else 1 - y
+            cp = c if n % 2 == 0 else 1 - c
+            for d in range(4):
+                zz = lax.rem(z - d + 4, 4)
+                copies.append(
+                    pltpu.make_async_copy(
+                        pieces[n].at[d],
+                        wscr.at[pl.ds(al(zz * 128, 128), 128), pl.ds(al((2 * yy + cp) * 384, 128), 384)],
+                        sem,
                     )
+                )
         for cpy in copies:
             cpy.start()
         for cpy in copies:
@@ -226,8 +228,8 @@
     G, NP, L, BL, TQF = geo.G, geo.NP, geo.L, geo.BL, geo.TQ
     q, k, v, refs = refs[:NP], refs[NP : 2 * NP], refs[2 * NP : 3 * NP], refs[3 * NP :]
     nd = len(dlist)
-    outs, lses = refs[: nd * NP], refs[nd * NP : nd * NP + nd]
-    vT, acc, sc = refs[nd * NP + nd :]
+    outs, lses = refs[:nd], refs[nd : 2 * nd]
+    vT, acc, sc = refs[2 * nd :]
     s, g = geo.where(meta)
     ends = doc_ends(doc, s)
     heads = [(p, h) for p in range(NP) for h in range(2)]
@@ -296,7 +298,7 @@
                     parts.append(acc[n * HR : n * HR + HEAD_DIM, :] * (1.0 / ls))
                     lses[di][e, n : n + 1, pl.ds(off, TQF)] = ms[n] + jnp.log(ls)
                 res = jnp.transpose(jnp.concatenate(parts, axis=0)).astype(BF)
-                outs[di * NP + p][e, pl.ds(off, TQF), :] = res
+                outs[di][p, e, pl.ds(off, TQF), :] = res
             return carry
 
         lax.fori_loop(0, 2 * BL // TQF, q_step, 0)
@@ -319,7 +321,7 @@
                 dst = pl.ds(al(base + i * 256, 256), 256)
                 gt = grads[d][e, src, :]
                 zero = jnp.zeros_like(gt)
-                prod = jnp.transpose(gt.astype(F32) * mixed[d][e, src, :].astype(F32))
+                prod = jnp.transpose(gt.astype(F32) * mixed[d][p, e, src, :].astype(F32))
                 qt = q[dst, :] * jnp.asarray(scale, BF)
                 for h in range(2):
                     hs = slice(h * HEAD_DIM, (h + 1) * HEAD_DIM)
@@ -387,7 +389,7 @@
         functools.partial(attn_kernel, geo, dlist),
         "attend",
         [(meta, SM), (doc, SM), (segs[0], VM), (segs[1], VM)] + [(t, VM) for t in (*q, *k, *v)],
-        [sds((2, BL, PW), BF)] * (nd * NP) + [sds((2, 8, BL), F32)] * nd,
+        [sds((NP, 2, BL, PW), BF)] * nd + [sds((2, 8, BL), F32)] * nd,
         scratch=[
             pltpu.VMEM((2 * NP * HR, L), BF),
             pltpu.VMEM((2 * NP * HR, geo.TQ), F32),
@@ -397,8 +399,7 @@
         nbytes=L * geo.HL * 8,
         trans=int(L * L * NP * share),
     )
-    mixed = [res[i * NP : (i + 1) * NP] for i in range(nd)]
-    return mixed, res[nd * NP :]
+    return res[:nd], res[nd:]
 
 
 def attend_back_call(geo, p, meta, doc, segs, q, k, v, lses, mixed, grads):
@@ -437,7 +438,7 @@
     pairs = [(d, p) for d in range(G) for p in range(NP)]
     x0, x1, cot, cot1, mixb, gain, shift, upb, downb = refs[:9]
     refs = refs[9:]
-    mixed, refs = refs[: G * NP], refs[G * NP :]
+    mixed, refs = refs[:G], refs[G:]
     nw = 8 if geo.fast else 3
     wts, refs = refs[:nw], refs[nw:]
     out_own, out_send, g_resid = refs[:3]
@@ -506,9 +507,9 @@
             rows = pl.ds(al(i * RT, RT), RT)
             to = pl.ds(al(e * BL + i * RT, RT), RT)
             r = xe[rows, :].astype(F32) + mixb[...]
-            for n, (d, p) in enumerate(pairs):
+            for d, p in pairs:
                 gp = lax.rem(g - d + G, G)
-                r = r + nn(mixed[n][e, rows, :], wo[pl.ds(al(gp * HL + p * PW, 128), PW), :])
+                r = r + nn(mixed[d][p, e, rows, :], wo[pl.ds(al(gp * HL + p * PW, 128), PW), :])
             resid[to, :] = r
             xhat, _ = normed(r)
             h2[to, :] = (xhat * gain[...] + shift[...]).astype(BF)
@@ -615,9 +616,9 @@
         sums = lax.fori_loop(0, BL // RT, back, sums)
     for i in range(4):
         vec[4 + i : 5 + i, :] = sums[i]
-    for n, (d, p) in enumerate(pairs):
+    for d, p in pairs:
         gp = lax.rem(g - d + G, G)
-        part = tn(mixed[n][0], gu_s[0:BL, 0:D]) + tn(mixed[n][1], gu_s[BL:T, 0:D])
+        part = tn(mixed[d][p, 0], gu_s[0:BL, 0:D]) + tn(mixed[d][p, 1], gu_s[BL:T, 0:D])
         mg[pl.ds(al(gp * HL + p * PW, 128), PW), :] = part.astype(BF)
     if geo.fast:
         for cr in range(2):
@@ -634,13 +635,54 @@
         packs[2][...] = mg[...]
 
 
-def wgrad_kernel(geo, meta, h1, *refs):
+def put_vec(ref, base, v):
+    hi = v.astype(BF)
+    lo = (v - hi.astype(F32)).astype(BF)
+    for n, t in enumerate((hi, lo)):
+        for b in range(4):
+            at = base + (n * 4 + b) * 16
+            ref[at : at + 16, :] = t[:, b * 128 : b * 128 + 128]
+
+
+def get_vec(ref, base):
+    def term(n):
+        at = base + n * 64
+        return jnp.concatenate([ref[at + b * 16 : at + b * 16 + 16, :] for b in range(4)], axis=1).astype(F32)
+
+    return term(0) + term(1)
+
+
+def wgrad_kernel(geo, meta, vec_in, gain, shift, h1, *refs):
     G, HL, D, NP = geo.G, geo.HL, geo.D, geo.NP
     s, g = geo.where(meta)
-    gq, refs = refs[:NP], refs[NP:]
-    packs, wg = refs[:-1], refs[-1]
+    gq, w, refs = refs[:NP], refs[NP : 2 * NP], refs[2 * NP :]
+    if geo.fast:
+        a, b, c, d, *refs = refs
+        refs[2][...] = add4(a[...], b[...], c[...], d[...]).astype(BF)
+        refs = refs[:2] + refs[3:]
+    packs, (wg, vec, acc) = refs[:-3], refs[-3:]
+    vec[...] = vec_in[...]
+    ones = jnp.ones((16, geo.L), BF)
+    back = jnp.zeros((16, D), F32)
     for p in range(NP):
-        wg[:, p * 3 * PW : (p + 1) * 3 * PW] = tn(h1[...], gq[p][...]).astype(BF)
+        part = tn(h1[...], gq[p][...])
+        wg[:, p * 3 * PW : (p + 1) * 3 * PW] = part.astype(BF)
+        prod = part * w[p][...].astype(F32)
+        prod = prod[:, 0:PW] + prod[:, PW : 2 * PW] + prod[:, 2 * PW : 3 * PW]
+        if p == 0:
+            acc[...] = prod
+        else:
+            acc[...] += prod
+        total = nn(ones, gq[p][...])
+        hi = total.astype(BF)
+        lo = (total - hi.astype(F32)).astype(BF)
+        back = back + nt(hi, w[p][...]) + nt(lo, w[p][...])
+        cols = pl.ds(al(g * HL + p * PW, 128), PW)
+        vec[2:3, cols] = total[0:1, 0:PW]
+        vec[3:4, cols] = total[0:1, 2 * PW : 3 * PW]
+    first = jnp.sum(jnp.transpose(acc[...]), axis=0, keepdims=True)
+    vec[0:1, :] = (first - shift[...] * back[0:1, :]) / gain[...]
+    vec[1:2, :] = back[0:1, :]
     if geo.fast:
         x, z, c = meta[0], meta[2], meta[1] % 2
         for cr, table in ((0, KEEP_LB), (1, SEND_LB)):
@@ -651,10 +693,13 @@
                     hh = x if hr == 0 else 1 - x
                     for k in range(4):
                         zz = lax.rem(z + k, 4)
-                        packs[cr][b, hr, k] = wg[
+                        to = ((b * 2 + hr) * 4 + k) * 64
+                        packs[cr][to : to + 64, :] = wg[
                             pl.ds(al(zz * 128 + hh * 64, 64), 64), pl.ds(al(at * 128, 128), 128)
                         ]
+            put_vec(packs[cr], 1536, vec[...])
     else:
+        packs[1][...] = vec[...]
         packs[0][...] = jnp.zeros_like(packs[0])
         for p in range(NP):
             for part in range(3):
@@ -663,56 +708,30 @@
                 ]
 
 
-def qkv_back_kernel(geo, meta, vec_in, *refs):
-    G, HL, D, BL, NP = geo.G, geo.HL, geo.D, geo.BL, geo.NP
+def qkv_back_kernel(geo, meta, *refs):
+    G, BL, NP = geo.G, geo.BL, geo.NP
     s, g = geo.where(meta)
-    gq, w, refs = refs[:NP], refs[NP : 2 * NP], refs[2 * NP :]
-    pieces, refs = refs[: 2 * G], refs[2 * G :]
-    ghs, vec = refs[:G], refs[G]
-    vec[...] = vec_in[...]
-    zrow = jnp.zeros((1, D), F32)
-    zh = jnp.zeros((1, PW), F32)
-    sums = (zrow, zrow) + (zh,) * (2 * NP)
+    gq, w, ghs = refs[:NP], refs[NP : 2 * NP], refs[2 * NP :]
     for e in range(2):
         for d in range(G):
             base = geo.block(s, g, e, d) * BL
-            src = pieces[e * G + d]
 
             def step(i, carry):
                 rows = pl.ds(al(i * RT, RT), RT)
                 at = pl.ds(al(base + i * RT, RT), RT)
-                xhat, _ = normed(src[rows, :].astype(F32))
-                gts = [t[at, :] for t in gq]
-                gh = nt(gts[0], w[0][...])
+                gh = nt(gq[0][at, :], w[0][...])
                 for p in range(1, NP):
-                    gh = gh + nt(gts[p], w[p][...])
+                    gh = gh + nt(gq[p][at, :], w[p][...])
                 ghs[d][e, rows, :] = gh.astype(ghs[d].dtype)
-                new = [
-                    carry[0] + jnp.sum(gh * xhat, axis=0, keepdims=True),
-                    carry[1] + jnp.sum(gh, axis=0, keepdims=True),
-                ]
-                for p in range(NP):
-                    for n, part in enumerate((0, 2)):
-                        cut = gts[p][:, part * PW : (part + 1) * PW].astype(F32)
-                        new.append(carry[2 + 2 * p + n] + jnp.sum(cut, axis=0, keepdims=True))
-                return tuple(new)
-
-            sums = lax.fori_loop(0, BL // RT, step, sums)
-    vec[0:1, :] = sums[0]
-    vec[1:2, :] = sums[1]
-    for p in range(NP):
-        cols = pl.ds(al(g * HL + p * PW, 128), PW)
-        vec[2:3, cols] = sums[2 + 2 * p]
-        vec[3:4, cols] = sums[3 + 2 * p]
-
-
-def last_kernel(geo, meta, gain, vec, vrecv, g_resid, gh, *refs):
+                return carry
+
+            lax.fori_loop(0, BL // RT, step, 0)
+
+
+def last_kernel(geo, meta, gain, g_resid, gh, *refs):
     G, D, BL = geo.G, geo.D, geo.BL
     s, _ = geo.where(meta)
-    refs, vout = refs[:-1], refs[-1]
-    vout[...] = vec[...] + vrecv[...]
-    recv, refs = refs[: G - 1], refs[G - 1 :]
-    x0, x1, out, send = refs
+    recv, (x0, x1, out, send) = refs[: G - 1], refs[G - 1 :]
     for e in range(2):
         xe = x0 if e == 0 else x1
 
@@ -745,6 +764,9 @@
 
 def arrange_kernel(geo, meta, keep, recv, *outs):
     y, c = meta[1] // 2, meta[1] % 2
+    total = get_vec(keep, 1536) + get_vec(recv, 1536)
+    for out in outs:
+        put_vec(out, 768, total)
     for cs in range(2):
         mine = sorted((lb // 2) * 4 + 2 * cs + lb % 2 for lb in KEEP_LB[cs])
         theirs = sorted((lb // 2) * 4 + 2 * (1 - cs) + lb % 2 for lb in SEND_LB[1 - cs])
@@ -757,28 +779,34 @@
                         b = first + o
                         src, slot = (keep, mine.index(b)) if b in mine else (recv, theirs.index(b))
                         for hr in range(2):
-                            outs[yr * 2 + hr][:, o * 64 : o * 64 + 64, :] = src[slot, hr]
-
-
-def plane_sum_kernel(has_vec, a, b, c, d, *refs):
-    if has_vec:
-        va, vb, vc, vd = refs[:4]
-        refs = refs[4:]
-        refs[4][...] = (va[...] + vb[...]) + (vc[...] + vd[...])
+                            for k in range(4):
+                                at = ((slot * 2 + hr) * 4 + k) * 64
+                                to = k * 192 + o * 64
+                                outs[yr * 2 + hr][to : to + 64, :] = src[at : at + 64, :]
+
+
+def add4(a, b, c, d):
+    return (a.astype(F32) + b.astype(F32)) + (c.astype(F32) + d.astype(F32))
+
+
+def plane_sum_kernel(a, b, c, d, *outs):
     for k in range(4):
-        refs[k][...] = (
-            (a[k].astype(F32) + b[k].astype(F32)) + (c[k].astype(F32) + d[k].astype(F32))
-        ).astype(BF)
-
-
-def line_sum_kernel(has_vec, a, b, c, d, *refs):
-    if has_vec:
-        va, vb, vc, vd = refs[:4]
-        refs = refs[4:]
-        refs[1][...] = (va[...] + vc[...]) + (vb[...] + vd[...])
-    refs[0][...] = (
-        (a[...].astype(F32) + b[...].astype(F32)) + (c[...].astype(F32) + d[...].astype(F32))
-    ).astype(BF)
+        outs[k][...] = add4(a[k], b[k], c[k], d[k]).astype(BF)
+
+
+def plane_sum_qkv_kernel(a, b, c, d, *outs):
+    va, vb, vc, vd = (get_vec(t, 768) for t in (a, b, c, d))
+    total = (va + vb) + (vc + vd)
+    for k in range(4):
+        at = slice(k * 192, k * 192 + 192)
+        outs[k][0:192, :] = add4(a[at, :], b[at, :], c[at, :], d[at, :]).astype(BF)
+        put_vec(outs[k], 192, total)
+
+
+def line_sum_qkv_kernel(a, b, c, d, out, vec):
+    va, vb, vc, vd = (get_vec(t, 192) for t in (a, b, c, d))
+    vec[...] = (va + vc) + (vb + vd)
+    out[...] = add4(a[0:192, :], b[0:192, :], c[0:192, :], d[0:192, :]).astype(BF)
 
 
 def finish_kernel(meta, r, o, mix, up, down):
@@ -798,10 +826,9 @@
             qkv[pl.ds(al(h * 64, 64), 64), b * 128 : b * 128 + 128] = src[b * 64 : b * 64 + 64, :].astype(F32)
 
 
-def pack_kernel(meta, qkv, mix, up, down, first, rest):
+def pack_kernel(meta, mix, up, down, rest):
     h = meta[0]
     rows = pl.ds(al(h * 64, 64), 64)
-    first[...] = qkv[rows, :].astype(BF)
     for b in range(4):
         rest[b * 64 : b * 64 + 64, :] = up[rows, b * 128 : b * 128 + 128].astype(BF)
     rest[256:512, :] = down[pl.ds(al(h * 256, 256), 256), :].astype(BF)
@@ -861,27 +888,24 @@
 
     NP = geo.NP
     if geo.fast:
-        half_qkv, half_rest = call(
+        def lines(v):
+            return [v] + [line(v, d) for d in range(1, 4)]
+
+        wq = qkv_weight.astype(BF)
+        lines_qkv = lines(wq)
+        x0 = pick(after(tokens, wq), s)
+        x1 = swap_half(pick(after(tokens, wq), 1 - s))
+        (half_rest,) = call(
             pack_kernel,
             "pack",
-            [(meta, SM), (qkv_weight, VM), (mix_weight, VM), (up_weight, VM), (down_weight, VM)],
-            [sds((64, 384), BF), sds((576, 128), BF)],
+            [(after(meta, wq), SM), (mix_weight, VM), (up_weight, VM), (down_weight, VM)],
+            [sds((576, 128), BF)],
             nbytes=2 << 20,
         )
-
-        def lines(v):
-            return [v] + [line(v, d) for d in range(1, 4)]
-
-        def quads(v):
-            return [v, plane(v, 1, 0), plane(v, 0, 1), plane(v, 1, 1)]
-
-        lines_qkv = lines(half_qkv)
-        x0 = pick(tokens, s)
-        x1 = swap_half(pick(after(tokens, half_qkv), 1 - s))
-        lines_rest = lines(half_rest)
-        quads_qkv = quads(jnp.stack(lines_qkv))
-        w_qkv = [t for q in quads_qkv for t in (q, turn(q, 1))]
-        quads_rest = quads(jnp.stack(after(tuple(lines_rest), w_qkv[1])))
+        turn0 = turn(x0, 1)
+        own_qkv = jnp.stack(after(tuple(lines_qkv), half_rest))
+        across = swap_half(after(own_qkv, turn0))
+        lines_rest = lines(after(half_rest, own_qkv))
     else:
         x0 = pick(tokens, s)
         x1 = swap_half(pick(tokens, 1 - s))
@@ -892,7 +916,7 @@
 
         w_qkv = [whole(qkv_weight)]
         w_rest = [whole(mix_weight), whole(up_weight), whole(down_weight)]
-    pieces = [x0] + [turn(x0, d) for d in range(1, G)]
+    pieces = [x0] + ([turn0] if geo.fast else [turn(x0, d) for d in range(1, G)])
     pieces += [x1] + [turn(x1, d) for d in range(1, G)]
     gain1, shift1 = row2(norm_gain), row2(norm_shift)
     h1, segk, segq = call(
@@ -904,6 +928,8 @@
         nbytes=L * D * 4,
     )
     segs = (segk, segq)
+    if geo.fast:
+        w_qkv = [own_qkv, turn(own_qkv, 1), across, turn(after(across, h1), 1)]
     bias = row2(jnp.concatenate([query_bias, jnp.zeros_like(query_bias), value_bias]))
     wspec = HBM if geo.fast else VM
     res = call(
@@ -917,18 +943,24 @@
     )
     q, k, v, w_own = (res[n * NP : (n + 1) * NP] for n in range(4))
     cot0 = pick(cotangent, s)
-    cot1 = swap_half(pick(cotangent, 1 - s))
+    cot1 = swap_half(pick(after(cotangent, x1) if geo.fast else cotangent, 1 - s))
+    if geo.fast:
+        rest = jnp.stack(after(tuple(lines_rest), (q[0], cot1)))
+        quads_rest = [plane(rest, 1, 0), plane(rest, 0, 1), plane(rest, 1, 1)]
     far, lse_far = attend_call(geo, tuple(range(1, G)), meta, doc_lengths, segs, q, k, v)
-    q_own = list(after(tuple(q), far[0][0]))
-    if geo.fast:
-        quads_rest = after(tuple(quads_rest), far[0][0])
-        w_rest = [t for u in quads_rest for t in (u, turn(u, 1))]
+    if geo.fast:
+        w_rest = [rest, turn(rest, 1)]
+        w_rest += [t for u in after(tuple(quads_rest[:2]), (far[0], w_rest[1])) for t in (u, turn(u, 1))]
+        q_own = list(after(tuple(q), (far[0], w_rest[2], w_rest[4])))
+    else:
+        q_own = list(after(tuple(q), far[0]))
     own, lse_own = attend_call(geo, (0,), meta, doc_lengths, segs, q_own, k, v)
+    if geo.fast:
+        diag = after(quads_rest[2], own[0])
+        w_rest += [diag, turn(diag, 1)]
     made = [own[0]] + list(far)
     lses = list(lse_own) + list(lse_far)
-    mixed = [t for t in made[0]]
-    for d in range(1, G):
-        mixed += [turn(t, d) for t in made[G - d]]
+    mixed = [made[0]] + [turn(made[G - d], d) for d in range(1, G)]
     packs_out = (
         [sds((4, 4, 576, 128), BF)] * 2
         if geo.fast
@@ -978,108 +1010,86 @@
 
     def back(p, q_p):
         return attend_back_call(
-            geo, p, meta, doc_lengths, segs, q_p, k[p], v[p], lses, [m[p] for m in made], ghead[p]
+            geo, p, meta, doc_lengths, segs, q_p, k[p], v[p], lses, made, ghead[p]
         )
 
-    ghead = [[gmix[0][p]] + [turn(gmix[d][p], d) for d in range(1, G)] for p in range(NP)]
-
-    def step_plane(parts, vec=None):
-        a = [parts[0], plane(parts[1], 1, 0), plane(parts[2], 0, 1), plane(parts[3], 1, 1)]
-        n = parts[0].shape[1]
-        outs = [sds((n, 128), BF)] * 4
-        if vec is not None:
-            a += [vec, plane(vec, 1, 0), plane(vec, 0, 1), plane(vec, 1, 1)]
-            outs += [sds(vec.shape, F32)]
-        return a, outs
-
-    def plane_sum(a, outs):
-        return call(
-            functools.partial(plane_sum_kernel, len(outs) > 4),
-            "plane_sum",
-            [(t, VM) for t in a],
-            outs,
-            nbytes=8 << 20,
-        )
-
-    def step_line(parts, vec=None):
-        a = [parts[0]] + [line(parts[d], d) for d in range(1, 4)]
-        outs = [sds(parts[0].shape, BF)]
-        if vec is not None:
-            a += [vec] + [line(vec, d) for d in range(1, 4)]
-            outs += [sds(vec.shape, F32)]
-        return a, outs
-
-    def line_sum(a, outs):
-        return call(
-            functools.partial(line_sum_kernel, len(outs) > 1),
-            "line_sum",
-            [(t, VM) for t in a],
-            outs,
-            nbytes=2 << 20,
-        )
-
-    gq = [back(0, q[0])]
-    if geo.fast:
-        sums = call(
-            core_sum_kernel,
-            "core_sum",
-            [(after(packs[0], gq[0]), VM), (turn(after(packs[1], ghead[0][1]), 1), VM)],
-            [sds((4, 576, 128), BF)] * 4,
-            nbytes=8 << 20,
-        )
-        a1, o1 = step_plane(sums)
-        gq += [back(p, after(q[p], sums[0])) for p in range(1, NP)]
+    def turned(p, dep):
+        return [gmix[0][p]] + [turn(after(gmix[d][p], dep), d) for d in range(1, G)]
+
+    def step_plane(parts):
+        return (parts[0], plane(parts[1], 1, 0), plane(parts[2], 0, 1), plane(parts[3], 1, 1))
+
+    def step_line(parts):
+        return (parts[0],) + tuple(line(parts[d], d) for d in range(1, 4))
+
+    def add(kernel, name, arrays, outs):
+        return call(kernel, name, [(t, VM) for t in arrays], outs, nbytes=4 << 20)
+
+    if geo.fast:
+        sums = add(core_sum_kernel, "core_sum", (packs[0], turn(packs[1], 1)), [sds((4, 576, 128), BF)] * 4)
+        a1 = step_plane(sums)
+        ghead = [turned(0, sums[0])]
+        gq = [back(0, after(q[0], sums[0]))]
+        q1 = add(plane_sum_kernel, "plane_sum", after(a1, gq[0]), [sds((576, 128), BF)] * 4)
+        b1 = step_line(q1)
+        out_recv = swap_half(after(out_send, q1[0]))
+        ghead.append(turned(1, q1[0]))
+        gq += [back(1, after(q[1], q1[0]))]
+        packs2_out = [sds((1664, 128), BF)] * 2 + [sds((576, 128), BF)]
     else:
-        gq += [back(p, q[p]) for p in range(1, NP)]
-    packs2_out = [sds((3, 2, 4, 64, 128), BF)] * 2 if geo.fast else [sds((D, 3 * D), BF)]
+        b1 = ()
+        ghead = [turned(p, q[p]) for p in range(NP)]
+        gq = [back(p, q[p]) for p in range(NP)]
+        out_recv = swap_half(out_send)
+        packs2_out = [sds((D, 3 * D), BF), sds((16, D), F32)]
     packs2 = call(
         functools.partial(wgrad_kernel, geo),
         "wgrad",
-        [(meta, SM), (h1, VM)] + [(t, VM) for t in gq],
+        [(meta, SM), (vec1, VM), (gain1, VM), (shift1, VM), (after(h1, out_recv), VM)]
+        + [(t, VM) for t in (*gq, *w_own, *b1)],
         packs2_out,
-        scratch=[pltpu.VMEM((D, 3 * HL), BF)],
+        scratch=[pltpu.VMEM((D, 3 * HL), BF), pltpu.VMEM((16, D), F32), pltpu.VMEM((D, PW), F32)],
         flops=2 * L * D * 3 * HL,
         nbytes=8 << 20,
     )
     if geo.fast:
-        q1 = plane_sum(list(after(tuple(a1), packs2[0])), o1)
-        b1, p1 = step_line(q1)
+        recv2, r1 = turn(packs2[1], 1), packs2[2]
+        gq = list(after(tuple(gq), r1))
+    ghs = call(
+        functools.partial(qkv_back_kernel, geo),
+        "qkv_back",
+        [(meta, SM)] + [(t, VM) for t in (*gq, *w_own)],
+        [sds((2, BL, D), F32)] + [sds((2, BL, D), BF)] * (G - 1),
+        flops=2 * L * D * 3 * HL,
+        nbytes=12 << 20,
+    )
+    gh_recv = [turn(ghs[G - d], d) for d in range(1, G)]
+    if geo.fast:
+        own2, recv2 = after((packs2[0], recv2), ghs[0])
         parts2 = call(
             functools.partial(arrange_kernel, geo),
             "arrange",
-            [(meta, SM), (after(packs2[0], q1[0]), VM), (turn(packs2[1], 1), VM)],
-            [sds((4, 192, 128), BF)] * 4,
+            [(meta, SM), (own2, VM), (recv2, VM)],
+            [sds((896, 128), BF)] * 4,
             nbytes=2 << 20,
         )
-        a2, o2 = step_plane(parts2)
-        gq = list(after(tuple(gq), parts2[0]))
-    res2 = call(
-        functools.partial(qkv_back_kernel, geo),
-        "qkv_back",
-        [(meta, SM), (vec1, VM)] + [(t, VM) for t in (*gq, *w_own)] + [(t, VM) for t in pieces],
-        [sds((2, BL, D), F32)] + [sds((2, BL, D), BF)] * (G - 1) + [sds((16, D), F32)],
-        flops=2 * L * D * 3 * HL,
-        nbytes=12 << 20,
-    )
-    ghs, vec2 = res2[:G], res2[G]
-    gh_recv = [turn(ghs[G - d], d) for d in range(1, G)]
-    tgrad, tgrad_send, vec3 = call(
+        a2 = step_plane(parts2)
+        other1 = plane(after(r1, parts2[0]), 1, 0)
+
+    tgrad, tgrad_send = call(
         functools.partial(last_kernel, geo),
         "norm_back",
-        [(meta, SM), (gain1, VM), (vec2, VM)]
-        + [(turn(vec2, 1) if geo.fast else jnp.zeros_like(vec2), VM), (g_resid, VM), (ghs[0], VM)]
+        [(meta, SM), (gain1, VM), (g_resid, VM), (after(ghs[0], parts2[0]) if geo.fast else ghs[0], VM)]
         + [(r, VM) for r in gh_recv]
         + [(x0, VM), (x1, VM)],
-        [sds((2, BL, D), BF), sds((BL, D), BF), sds((16, D), F32)],
+        [sds((2, BL, D), BF), sds((BL, D), BF)],
         flops=T * D * 30,
         nbytes=8 << 20,
     )
-    if geo.fast:
-        (r1,) = line_sum(list(after(tuple(b1), tgrad_send)), p1)
-        other1 = plane(r1, 1, 0)
-        va = [vec3, plane(vec3, 1, 0), plane(vec3, 0, 1), plane(vec3, 1, 1)]
-        *q2, vec4 = plane_sum(a2 + va, o2 + [sds(vec3.shape, F32)])
-        b2, p2 = step_line(q2, vec4)
+    tgrad_recv = swap_half(tgrad_send)
+    if geo.fast:
+        q2 = add(plane_sum_qkv_kernel, "plane_sum_qkv", after(a2, tgrad_send), [sds((320, 128), BF)] * 4)
+        b2 = step_line(q2)
         mix_g, up_g, down_g = call(
             finish_kernel,
             "finish",
@@ -1087,7 +1097,9 @@
             [sds(w.shape, F32) for w in (mix_weight, up_weight, down_weight)],
             nbytes=2 << 20,
         )
-        r2, vec = line_sum(b2, p2)
+        r2, vec = add(
+            line_sum_qkv_kernel, "line_sum_qkv", after(b2, mix_g), [sds((192, 128), BF), sds((16, D), F32)]
+        )
         (qkv_g,) = call(
             finish_qkv_kernel,
             "finish_qkv",
@@ -1103,13 +1115,13 @@
             return lax.psum(w, "dp").astype(F32)
 
         grads = (reduced(packs2[0]), reduced(packs[2]), reduced(packs[0]), reduced(packs[1]))
-        vec = lax.psum(vec3, ("dp", "col", "row"))
+        vec = lax.psum(packs2[1], ("dp", "col", "row"))
 
     def join(own, other):
         return lax.dynamic_update_slice(own, other[None], (1 - s, 0, 0))
 
-    out_pair = jnp.where(s == 0, jnp.stack([out_own, swap_half(out_send)]), jnp.stack([swap_half(out_send), out_own]))
-    tgrad = join(tgrad, swap_half(tgrad_send))
+    out_pair = jnp.where(s == 0, jnp.stack([out_own, out_recv]), jnp.stack([out_recv, out_own]))
+    tgrad = join(tgrad, tgrad_recv)
     return (
         out_pair,
         tgrad,

time: 280 us -> 233 us (0.83)
  starting transfers between devices: 75.5 us -> 42 us
  Pallas kernels: 154 us -> 129 us
  waiting for transfers between devices: 30.3 us -> 44 us
  local copies, waits for them, and re-layouts: 13.7 us -> 9.83 us
    ppermute x17 -> x11, starting transfers between devices: 37.3 us -> 12.6 us  [plane(): return lax.ppermute(v, ('dp', 'col'), pairs)]
    pallas_call x19 -> x18, Pallas kernels: 154 us -> 129 us  [call(): pl.pallas_call(kernel, name=name, out_shape=tuple((o for o in outs)), in_...]
    ppermute x4 -> x5, waiting for transfers between devices: 0.39 us -> 13.4 us  [swap_half(): return lax.ppermute(v, 'col', [(i, (i + G) % C) for i in range(C)])]
    ppermute x15 -> x12, starting transfers between devices: 29 us -> 19.2 us  [line(): return lax.ppermute(v, 'row', [(i, (i + d) % R) for i in range(R)])]
    ppermute x18 -> x14, waiting for transfers between devices: 1.78 us -> 9.99 us  [turn(): lax.ppermute(v, 'col', [(i, i // G * G + (i % G + d) % G) for i in range(...]
    ppermute x17 -> x11, waiting for transfers between devices: 18.9 us -> 12.6 us  [plane(): return lax.ppermute(v, ('dp', 'col'), pairs)]
    unnamed x94 -> x114, local copies, waits for them, and re-layouts: 9.77 us -> 5.2 us
    ppermute x4 -> x5, starting transfers between devices: 6.14 us -> 7.84 us  [swap_half(): return lax.ppermute(v, 'col', [(i, (i + G) % C) for i in range(C)])]
  transfers between devices with their start and end apart: 54 -> 42, of which waited for: 9 -> 12; matrix products, arithmetic and copies ran while one was open for 3% -> 3% of each run, Pallas kernels for 40% -> 38%
where the time goes in v3:
time: 233 us; the launch traced here: 232 us
  Pallas kernels  129 us (55%)
  waiting for transfers between devices  44 us (19%)
  starting transfers between devices  42 us (18%)
  local copies, waits for them, and re-layouts  9.83 us (4%)
  other arithmetic  4.85 us (2%)
    pallas_call x18, Pallas kernels, call(): pl.pallas_call(kernel, name=name, out_shape=tuple((o for o in outs)), in_...  129 us
    ppermute x12, starting transfers between devices, line(): return lax.ppermute(v, 'row', [(i, (i + d) % R) for i in range(R)])  19.2 us
    ppermute x5, waiting for transfers between devices, swap_half(): return lax.ppermute(v, 'col', [(i, (i + G) % C) for i in range(C)])  13.4 us
    ppermute x11, starting transfers between devices, plane(): return lax.ppermute(v, ('dp', 'col'), pairs)  12.6 us
    ppermute x11, waiting for transfers between devices, plane(): return lax.ppermute(v, ('dp', 'col'), pairs)  12.6 us
    ppermute x14, waiting for transfers between devices, turn(): lax.ppermute(v, 'col', [(i, i // G * G + (i % G + d) % G) for i in range(...  9.99 us
    ppermute x12, waiting for transfers between devices, line(): return lax.ppermute(v, 'row', [(i, (i + d) % R) for i in range(R)])  7.99 us
    ppermute x5, starting transfers between devices, swap_half(): return lax.ppermute(v, 'col', [(i, (i + G) % C) for i in range(C)])  7.84 us
  transfers between devices with their start and end apart: 42, of which 12 were waited for; matrix products, arithmetic and copies ran while one was open for 3% of the time, Pallas kernels for 38%

profile of v3, /device:TPU:0, one launch (start us, length us, event | category | flops | bytes accessed | tf_op | source)
XLA Modules:
  0.0 231.8 jit_solution(2824504468221360548)
XLA Ops:
  0.7 1.0 convert_element_type.3
  1.8 2.1 dynamic-slice_bitcast_fusion.2
  3.9 3.0 %collective-permute-start = (bf16[512,512]{1,0:T(8,128)(2,1)}, bf16[512,512]{1,0:T(8,128)(2,1)S(1)}, u32[]{:S(2)}, u32[]{:S(2)}) collective-permute-start(bf16[512,512]{1,0:T(8,128)(2,1)} %get-tuple-element.202), channel_id=1, source_target_pairs={{0,8},{4,12},{8,0},{12,4},{1,9},{5,13},{9,1},{13,5},{2,10},{6,14},... | collective-permute-start | bytes 1572872 | tf_op jit(solution)/shard_map/ppermute | solution.py:866
  6.9 3.6 %collective-permute-start.6 = (bf16[128,384]{1,0:T(8,128)(2,1)S(1)}, bf16[128,384]{1,0:T(8,128)(2,1)S(1)}, u32[]{:S(2)}, u32[]{:S(2)}) collective-permute-start(bf16[128,384]{1,0:T(8,128)(2,1)S(1)} %convert_element_type.3), channel_id=1, source_target_pairs={{0,3},{1,0},{2,1},{3,2},{4,7},{5,4},{6,5},{7,6},{8,11},{9,8},{10,9... | collective-permute-start | bytes 294920 | tf_op jit(solution)/shard_map/ppermute | solution.py:878
  10.5 1.0 collective-permute-start.4
  11.5 7.5 %collective-permute-done.refs_2_.refs_1_ = bf16[512,512]{1,0:T(8,128)(2,1)S(1)} collective-permute-done((bf16[512,512]{1,0:T(8,128)(2,1)}, bf16[512,512]{1,0:T(8,128)(2,1)S(1)}, u32[]{:S(2)}, u32[]{:S(2)}) %collective-permute-start) | collective-permute-done | bytes 524320 | tf_op jit(solution)/shard_map/ppermute | solution.py:866
  20.2 1.0 pad_maximum_fusion.1.refs_0_
  21.2 1.3 collective-permute-start.8
  22.7 3.6 %norm_one.1 = (bf16[2048,512]{1,0:T(8,128)(2,1)S(1)}, s32[2048,128]{1,0:T(8,128)S(1)}, s32[8,2048]{1,0:T(8,128)S(1)}) custom-call(s32[3]{0:T(128)S(1)} %pad_add_fusion.meta, s32[2,8]{1,0:T(2,128)S(1)} %copy-done.17, f32[1,512]{1,0:T(1,128)S(1)} %bitcast.34, f32[1,512]{1,0:T(1,128)S(1)} %bitcast.37, bf16[512,512]{1,0:T(8,128)(2,1)S(1)} %get-tuple-element.203.refs_0_.refs_1_, ...), custom_call_target="tpu_custom_call" | custom-call | flops 10485760 | bytes 4194304 | tf_op jit(solution)/shard_map/norm_one/pallas_call | solution.py:41
  26.4 5.9 %collective-permute-done.8.refs_2_ = bf16[4,128,384]{2,1,0:T(8,128)(2,1)S(1)} collective-permute-done((bf16[4,128,384]{2,1,0:T(8,128)(2,1)S(1)}, bf16[4,128,384]{2,1,0:T(8,128)(2,1)S(1)}, u32[]{:S(2)}, u32[]{:S(2)}) %collective-permute-start.8) | collective-permute-done | bytes 393248 | tf_op jit(solution)/shard_map/ppermute | solution.py:866
  32.4 1.8 collective-permute-start.1
  34.2 3.7 %collective-permute-start.12 = (bf16[576,128]{1,0:T(8,128)(2,1)S(1)}, bf16[576,128]{1,0:T(8,128)(2,1)S(1)}, u32[]{:S(2)}, u32[]{:S(2)}) collective-permute-start(bf16[576,128]{1,0:T(8,128)(2,1)S(1)} %pack.1), channel_id=1, source_target_pairs={{0,3},{1,0},{2,1},{3,2},{4,7},{5,4},{6,5},{7,6},{8,11},{9,8},{10,9... | collective-permute-start | bytes 442376 | tf_op jit(solution)/shard_map/ppermute | solution.py:878
  37.9 1.0 collective-permute-start.10
  38.9 4.4 %qkv.1 = (bf16[2048,128]{1,0:T(8,128)(2,1)S(1)}, bf16[2048,128]{1,0:T(8,128)(2,1)S(1)}, bf16[2048,128]{1,0:T(8,128)(2,1)S(1)}, bf16[2048,128]{1,0:T(8,128)(2,1)S...) custom-call(s32[3]{0:T(128)S(1)} %pad_add_fusion.meta, ...), custom_call_target="tpu_custom_call" | custom-call | flops 1610612736 | bytes 6815744 | tf_op jit(solution)/shard_map/qkv/pallas_call | solution.py:41
  43.3 7.4 %collective-permute-done.11 = bf16[576,128]{1,0:T(8,128)(2,1)S(1)} collective-permute-done((bf16[576,128]{1,0:T(8,128)(2,1)S(1)}, bf16[576,128]{1,0:T(8,128)(2,1)S(1)}, u32[]{:S(2)}, u32[]{:S(2)}) %collective-permute-start.11) | collective-permute-done | bytes 147488 | tf_op jit(solution)/shard_map/ppermute | solution.py:878
  51.5 1.5 collective-permute-start.13
  53.0 1.5 collective-permute-start.19
  54.5 13.2 %attend.2 = (bf16[2,2,512,128]{3,2,1,0:T(8,128)(2,1)S(1)}, f32[2,8,512]{2,1,0:T(8,128)S(1)}) custom-call(s32[3]{0:T(128)S(1)} %pad_add_fusion.meta, s32[2,8]{1,0:T(2,128)S(1)} %copy-done.17, s32[2048,128]{1,0:T(8,128)S(1)} %get-tuple-element.107.segk, s32[8,2048]{1,0:T(8,128)S(1)} %get-tuple-element.108.segq, ...), custom_call_target="tpu_custom_call" | custom-call | flops 4294967296 | bytes 4194304 | tf_op jit(solution)/shard_map/attend/pallas_call | solution.py:41
  67.9 9.4 %attend.3 = (bf16[2,2,512,128]{3,2,1,0:T(8,128)(2,1)S(1)}, f32[2,8,512]{2,1,0:T(8,128)S(1)}) custom-call(s32[3]{0:T(128)S(1)} %pad_add_fusion.meta, s32[2,8]{1,0:T(2,128)S(1)} %copy-done.17, s32[2048,128]{1,0:T(8,128)S(1)} %get-tuple-element.107.segk, s32[8,2048]{1,0:T(8,128)S(1)} %get-tuple-element.108.segq, ...), custom_call_target="tpu_custom_call" | custom-call | flops 4294967296 | bytes 4194304 | tf_op jit(solution)/shard_map/attend/pallas_call | solution.py:41
  77.3 3.2 %collective-permute-done.19.refs_17_ = bf16[4,576,128]{2,1,0:T(8,128)(2,1)S(1)} collective-permute-done((bf16[4,576,128]{2,1,0:T(8,128)(2,1)S(1)}, bf16[4,576,128]{2,1,0:T(8,128)(2,1)S(1)}, u32[]{:S(2)}, u32[]{:S(2)}) %collective-permute-start.19) | collective-permute-done | bytes 589856 | tf_op jit(solution)/shard_map/ppermute | solution.py:875
  82.4 2.6 %collective-permute-done.16.refs_10_ = bf16[2,2,512,128]{3,2,1,0:T(8,128)(2,1)S(1)} collective-permute-done((bf16[2,2,512,128]{3,2,1,0:T(8,128)(2,1)S(1)}, bf16[2,2,512,128]{3,2,1,0:T(8,128)(2,1)S(1)}, u32[]{:S(2)}, u32[]{:S(2)}) %collective-permute-start.16) | collective-permute-done | bytes 524320 | tf_op jit(solution)/shard_map/ppermute | solution.py:869
  86.4 32.1 %ffn.1 = (bf16[512,512]{1,0:T(8,128)(2,1)}, bf16[512,512]{1,0:T(8,128)(2,1)}, f32[1024,512]{1,0:T(8,128)}, bf16[2,512,128]{2,1,0:T(8,128)(2,1)}, bf16[2,512,128]...) custom-call(s32[3]{0:T(128)} %copy-done.13, ...), custom_call_target="tpu_custom_call" | custom-call | flops 14495514624 | bytes 20971520 | tf_op jit(solution)/shard_map/ffn/pallas_call | solution.py:41
  118.7 4.6 %collective-permute-done.21.recv = bf16[4,4,576,128]{3,2,1,0:T(8,128)(2,1)S(1)} collective-permute-done((bf16[4,4,576,128]{3,2,1,0:T(8,128)(2,1)}, bf16[4,4,576,128]{3,2,1,0:T(8,128)(2,1)S(1)}, u32[]{:S(2)}, u32[]{:S(2)}) %collective-permute-start.21) | collective-permute-done | bytes 2359328 | tf_op jit(solution)/shard_map/ppermute | solution.py:869
  123.4 1.7 copy-done.3
  126.1 1.5 collective-permute-start.22
  128.1 1.5 collective-permute-start.24
  129.7 24.9 %attend_back.2.refs_0_ = bf16[2048,384]{1,0:T(8,128)(2,1)S(1)} custom-call(s32[3]{0:T(128)S(1)} %copy-done.14, s32[2,8]{1,0:T(2,128)S(1)} %copy-done.17, s32[2048,128]{1,0:T(8,128)S(1)} %copy-done.19, s32[8,2048]{1,0:T(8,128)S(1)} %get-tuple-element.108.segq, bf16[2048,128]{1,0:T(8,128)(2,1)S(1)} %copy-done.29, bf16[2048,128]{1,0:T(8,128)(2,1)S(1)} %copy-done.31, ...), custom_call_target="tpu_custom_call" | custom-call | flops 10737418240 | bytes 5242880 | tf_op jit(solution)/shard_map/attend_back/pallas_call | solution.py:41
  155.9 1.5 collective-permute-start.28
  157.4 1.8 collective-permute-start.29
  159.2 2.8 %collective-permute-start.30 = (bf16[576,128]{1,0:T(8,128)(2,1)S(1)}, bf16[576,128]{1,0:T(8,128)(2,1)S(1)}, u32[]{:S(2)}, u32[]{:S(2)}) collective-permute-start(bf16[576,128]{1,0:T(8,128)(2,1)S(1)} %get-tuple-element.166), channel_id=1, source_target_pairs={{0,3},{1,0},{2,1},{3,2},{4,7},{5,4},{6,5},{7,6},{8,11},{9,8},{10,9... | collective-permute-start | bytes 442376 | tf_op jit(solution)/shard_map/ppermute | solution.py:878
  162.0 1.7 collective-permute-start.26
  163.8 24.9 %attend_back.3.refs_1_ = bf16[2048,384]{1,0:T(8,128)(2,1)S(1)} custom-call(s32[3]{0:T(128)S(1)} %copy-done.14, s32[2,8]{1,0:T(2,128)S(1)} %copy-done.17, s32[2048,128]{1,0:T(8,128)S(1)} %copy-done.19, s32[8,2048]{1,0:T(8,128)S(1)} %get-tuple-element.108.segq, bf16[2048,128]{1,0:T(8,128)(2,1)S(1)} %copy-done.23, bf16[2048,128]{1,0:T(8,128)(2,1)S(1)} %copy-done.25, ...), custom_call_target="tpu_custom_call" | custom-call | flops 10737418240 | bytes 5242880 | tf_op jit(solution)/shard_map/attend_back/pallas_call | solution.py:41
  188.8 4.6 %wgrad.1 = (bf16[1664,128]{1,0:T(8,128)(2,1)S(1)}, bf16[1664,128]{1,0:T(8,128)(2,1)S(1)}, bf16[576,128]{1,0:T(8,128)(2,1)S(1)}) custom-call(s32[3]{0:T(128)S(1)} %copy-done.14, f32[16,512]{1,0:T(8,128)S(1)} %copy-done.12, f32[1,512]{1,0:T(1,128)S(1)} %bitcast.35, f32[1,512]{1,0:T(1,128)S(1)} %bitcast.38, bf16[2048,512]{1,0:T(8,128)(2,1)S(1)} %copy-done.5, ...), custom_call_target="tpu_custom_call" | custom-call | flops 1610612736 | bytes 8388608 | tf_op jit(solution)/shard_map/wgrad/pallas_call | solution.py:41
  193.4 4.3 %qkv_back.1 = (f32[2,512,512]{2,1,0:T(8,128)S(1)}, bf16[2,512,512]{2,1,0:T(8,128)(2,1)S(1)}) custom-call(s32[3]{0:T(128)S(1)} %copy-done.14, bf16[2048,384]{1,0:T(8,128)(2,1)S(1)} %attend_back.2.refs_0_, bf16[2048,384]{1,0:T(8,128)(2,1)S(1)} %attend_back.3.refs_1_, bf16[512,384]{1,0:T(8,128)(2,1)S(1)} %get-tuple-element.162.refs_2_, ...), custom_call_target="tpu_custom_call" | custom-call | flops 1610612736 | bytes 12582912 | tf_op jit(solution)/shard_map/qkv_back/pallas_call | solution.py:41
  198.3 2.8 %collective-permute-done.31.recv = bf16[1664,128]{1,0:T(8,128)(2,1)S(1)} collective-permute-done((bf16[1664,128]{1,0:T(8,128)(2,1)S(1)}, bf16[1664,128]{1,0:T(8,128)(2,1)S(1)}, u32[]{:S(2)}, u32[]{:S(2)}) %collective-permute-start.31) | collective-permute-done | bytes 426016 | tf_op jit(solution)/shard_map/ppermute | solution.py:869
  201.1 1.3 arrange.1
  202.9 2.9 %collective-permute-start.36 = (bf16[896,128]{1,0:T(8,128)(2,1)S(1)}, bf16[896,128]{1,0:T(8,128)(2,1)S(1)}, u32[]{:S(2)}, u32[]{:S(2)}) collective-permute-start(bf16[896,128]{1,0:T(8,128)(2,1)S(1)} %get-tuple-element.182), channel_id=1, source_target_pairs={{0,24},{4,28},{8,16},{12,20},{16,8},{20,12},{24,0},{28,4},{1,25},{... | collective-permute-start | bytes 688136 | tf_op jit(solution)/shard_map/ppermute | solution.py:875
  205.9 2.7 %norm_back.1 = (bf16[2,512,512]{2,1,0:T(8,128)(2,1)}, bf16[512,512]{1,0:T(8,128)(2,1)S(1)}) custom-call(s32[3]{0:T(128)S(1)} %copy-done.14, f32[1,512]{1,0:T(1,128)S(1)} %bitcast.36, f32[1024,512]{1,0:T(8,128)S(1)} %copy-done.6, f32[2,512,512]{2,1,0:T(8,128)S(1)} %get-tuple-element.176.gh, bf16[2,512,512]{2,1,0:T(8,128)(2,1)S(1)} %collective-permute-done.32.refs_0_, ...), custom_call_target="tpu_custom_call" | custom-call | flops 15728640 | bytes 8388608 | tf_op jit(solution)/shard_map/norm_back/pallas_call | solution.py:41
  209.1 1.9 collective-permute-done.34.b
  211.0 5.2 %collective-permute-done.35.c = bf16[896,128]{1,0:T(8,128)(2,1)S(1)} collective-permute-done((bf16[896,128]{1,0:T(8,128)(2,1)S(1)}, bf16[896,128]{1,0:T(8,128)(2,1)S(1)}, u32[]{:S(2)}, u32[]{:S(2)}) %collective-permute-start.35) | collective-permute-done | bytes 229408 | tf_op jit(solution)/shard_map/ppermute | solution.py:875
  217.0 3.2 %collective-permute-start.39 = (bf16[320,128]{1,0:T(8,128)(2,1)S(1)}, bf16[320,128]{1,0:T(8,128)(2,1)S(1)}, u32[]{:S(2)}, u32[]{:S(2)}) collective-permute-start(bf16[320,128]{1,0:T(8,128)(2,1)S(1)} %get-tuple-element.190), channel_id=1, source_target_pairs={{0,3},{1,0},{2,1},{3,2},{4,7},{5,4},{6,5},{7,6},{8,11},{9,8},{10,9... | collective-permute-start | bytes 245768 | tf_op jit(solution)/shard_map/ppermute | solution.py:878
  220.2 2.7 %maximum_select_fusion = bf16[2,512,512]{2,1,0:T(8,128)(2,1)} fusion(bf16[1,512,512]{2,1,0:T(8,128)(2,1)} %bitcast.40, bf16[1,512,512]{2,1,0:T(8,128)(2,1)} %bitcast.39, pred[]{:T(512)S(6)} %eq.3), kind=kLoop, calls=%fused_computation | loop fusion | flops 1572864 | bytes 2097153 | tf_op jit(solution)/shard_map/jit(_where)/select_n | solution.py:1123
  222.9 1.4 finish.1
  224.4 1.5 collective-permute-start.41
  227.1 1.4 collective-permute-done.41.o
  228.5 1.2 finish_qkv.1
  229.8 1.1 bitcast_dynamic-update-slice_fusion
  230.8 1.0 copy-done.43
  (181 shorter events, 12.5 us)
Async XLA Ops:
  0.6 31.7 %copy-start = (bf16[2,512,512]{2,1,0:T(8,128)(2,1)S(1)}, bf16[2,512,512]{2,1,0:T(8,128)(2,1)}, u32[]{:S(2)}) copy-start(bf16[2,512,512]{2,1,0:T(8,128)(2,1)} %param.31) | copy-start | bytes 3145732
  3.9 28.5 %copy-start.1 = (bf16[512,512]{1,0:T(8,128)(2,1)}, bf16[512,512]{1,0:T(8,128)(2,1)S(1)}, u32[]{:S(2)}) copy-start(bf16[512,512]{1,0:T(8,128)(2,1)S(1)} %get-tuple-element.203.refs_0_.refs_1_) | copy-start | bytes 1572868
  3.9 15.1 %collective-permute-start = (bf16[512,512]{1,0:T(8,128)(2,1)}, bf16[512,512]{1,0:T(8,128)(2,1)S(1)}, u32[]{:S(2)}, u32[]{:S(2)}) collective-permute-start(bf16[512,512]{1,0:T(8,128)(2,1)} %get-tuple-element.202), channel_id=1, source_target_pairs={{0,8},{4,12},{8,0},{12,4},{1,9},{5,13},{9,1},{13,5},{2,10},{6,14},... | collective-permute-start | bytes 1572872 | tf_op jit(solution)/shard_map/ppermute | solution.py:866
  6.9 14.3 %collective-permute-start.2 = (bf16[512,512]{1,0:T(8,128)(2,1)S(1)}, bf16[512,512]{1,0:T(8,128)(2,1)S(1)}, u32[]{:S(2)}, u32[]{:S(2)}) collective-permute-start(bf16[512,512]{1,0:T(8,128)(2,1)S(1)} %get-tuple-element.203.refs_0_.refs_1_), channel_id=1, source_target_pairs={{0,4},{4,0},{8,12},{12,8},{1,5},{5,1},{9,13},{13,9},{2,6},{6,2},{1... | collective-permute-start | bytes 1572872 | tf_op jit(solution)/shard_map/ppermute | solution.py:869
  6.9 12.8 %collective-permute-start.6 = (bf16[128,384]{1,0:T(8,128)(2,1)S(1)}, bf16[128,384]{1,0:T(8,128)(2,1)S(1)}, u32[]{:S(2)}, u32[]{:S(2)}) collective-permute-start(bf16[128,384]{1,0:T(8,128)(2,1)S(1)} %convert_element_type.3), channel_id=1, source_target_pairs={{0,3},{1,0},{2,1},{3,2},{4,7},{5,4},{6,5},{7,6},{8,11},{9,8},{10,9... | collective-permute-start | bytes 294920 | tf_op jit(solution)/shard_map/ppermute | solution.py:878
  10.5 9.8 %collective-permute-start.5 = (bf16[128,384]{1,0:T(8,128)(2,1)S(1)}, bf16[128,384]{1,0:T(8,128)(2,1)S(1)}, u32[]{:S(2)}, u32[]{:S(2)}) collective-permute-start(bf16[128,384]{1,0:T(8,128)(2,1)S(1)} %convert_element_type.3), channel_id=1, source_target_pairs={{0,2},{1,3},{2,0},{3,1},{4,6},{5,7},{6,4},{7,5},{8,10},{9,11},{10,... | collective-permute-start | bytes 294920 | tf_op jit(solution)/shard_map/ppermute | solution.py:878
  10.5 9.8 %collective-permute-start.4 = (bf16[128,384]{1,0:T(8,128)(2,1)S(1)}, bf16[128,384]{1,0:T(8,128)(2,1)}, u32[]{:S(2)}, u32[]{:S(2)}) collective-permute-start(bf16[128,384]{1,0:T(8,128)(2,1)S(1)} %convert_element_type.3), channel_id=1, source_target_pairs={{0,1},{1,2},{2,3},{3,0},{4,5},{5,6},{6,7},{7,4},{8,9},{9,10},{10,1... | collective-permute-start | bytes 294920 | tf_op jit(solution)/shard_map/ppermute | solution.py:878
  19.0 3.7 %collective-permute-start.3 = (bf16[512,512]{1,0:T(8,128)(2,1)S(1)}, bf16[512,512]{1,0:T(8,128)(2,1)S(1)}, u32[]{:S(2)}, u32[]{:S(2)}) collective-permute-start(bf16[512,512]{1,0:T(8,128)(2,1)S(1)} %collective-permute-done.refs_2_.refs_1_), channel_id=1, source_target_pairs={{0,4},{4,0},{8,12},{12,8},{1,5},{5,1},{9,13},{13,9},{2,6},{6,2},{1... | collective-permute-start | bytes 1572872 | tf_op jit(solution)/shard_map/ppermute | solution.py:869
  19.1 48.7 %copy-start.13 = (s32[3]{0:T(128)}, s32[3]{0:T(128)S(1)}, u32[]{:S(2)}) copy-start(s32[3]{0:T(128)S(1)} %pad_add_fusion.meta) | copy-start | bytes 40
  21.2 11.1 %collective-permute-start.8 = (bf16[4,128,384]{2,1,0:T(8,128)(2,1)S(1)}, bf16[4,128,384]{2,1,0:T(8,128)(2,1)S(1)}, u32[]{:S(2)}, u32[]{:S(2)}) collective-permute-start(bf16[4,128,384]{2,1,0:T(8,128)(2,1)S(1)} %pad_maximum_fusion.1.refs_0_), channel_id=1, source_target_pairs={{0,8},{4,12},{8,0},{12,4},{1,9},{5,13},{9,1},{13,5},{2,10},{6,14},... | collective-permute-start | bytes 1179656 | tf_op jit(solution)/shard_map/ppermute | solution.py:866
  22.5 15.3 %collective-permute-start.7 = (bf16[4,128,384]{2,1,0:T(8,128)(2,1)S(1)}, bf16[4,128,384]{2,1,0:T(8,128)(2,1)S(1)}, u32[]{:S(2)}, u32[]{:S(2)}) collective-permute-start(bf16[4,128,384]{2,1,0:T(8,128)(2,1)S(1)} %pad_maximum_fusion.1.refs_0_), channel_id=1, source_target_pairs={{0,4},{4,0},{8,12},{12,8},{1,5},{5,1},{9,13},{13,9},{2,6},{6,2},{1... | collective-permute-start | bytes 1179656 | tf_op jit(solution)/shard_map/ppermute | solution.py:869
  26.4 41.4 %copy-start.18 = (s32[2048,128]{1,0:T(8,128)}, s32[2048,128]{1,0:T(8,128)S(1)}, u32[]{:S(2)}) copy-start(s32[2048,128]{1,0:T(8,128)S(1)} %get-tuple-element.107.segk) | copy-start | bytes 3145732
  32.3 6.6 %collective-permute-start.9 = (bf16[4,128,384]{2,1,0:T(8,128)(2,1)S(1)}, bf16[4,128,384]{2,1,0:T(8,128)(2,1)S(1)}, u32[]{:S(2)}, u32[]{:S(2)}) collective-permute-start(bf16[4,128,384]{2,1,0:T(8,128)(2,1)S(1)} %collective-permute-done.8.refs_2_), channel_id=1, source_target_pairs={{0,4},{4,0},{8,12},{12,8},{1,5},{5,1},{9,13},{13,9},{2,6},{6,2},{1... | collective-permute-start | bytes 1179656 | tf_op jit(solution)/shard_map/ppermute | solution.py:869
  32.4 18.4 %collective-permute-start.1 = (bf16[512,512]{1,0:T(8,128)(2,1)S(1)}, bf16[512,512]{1,0:T(8,128)(2,1)S(1)}, u32[]{:S(2)}, u32[]{:S(2)}) collective-permute-start(bf16[512,512]{1,0:T(8,128)(2,1)S(1)} %dynamic-slice_bitcast_fusion), channel_id=1, source_target_pairs={{0,8},{4,12},{8,0},{12,4},{1,9},{5,13},{9,1},{13,5},{2,10},{6,14},... | collective-permute-start | bytes 1572872 | tf_op jit(solution)/shard_map/ppermute | solution.py:866
  34.2 9.1 %collective-permute-start.12 = (bf16[576,128]{1,0:T(8,128)(2,1)S(1)}, bf16[576,128]{1,0:T(8,128)(2,1)S(1)}, u32[]{:S(2)}, u32[]{:S(2)}) collective-permute-start(bf16[576,128]{1,0:T(8,128)(2,1)S(1)} %pack.1), channel_id=1, source_target_pairs={{0,3},{1,0},{2,1},{3,2},{4,7},{5,4},{6,5},{7,6},{8,11},{9,8},{10,9... | collective-permute-start | bytes 442376 | tf_op jit(solution)/shard_map/ppermute | solution.py:878
  37.8 12.9 %collective-permute-start.11 = (bf16[576,128]{1,0:T(8,128)(2,1)S(1)}, bf16[576,128]{1,0:T(8,128)(2,1)S(1)}, u32[]{:S(2)}, u32[]{:S(2)}) collective-permute-start(bf16[576,128]{1,0:T(8,128)(2,1)S(1)} %pack.1), channel_id=1, source_target_pairs={{0,2},{1,3},{2,0},{3,1},{4,6},{5,7},{6,4},{7,5},{8,10},{9,11},{10,... | collective-permute-start | bytes 442376 | tf_op jit(solution)/shard_map/ppermute | solution.py:878
  37.9 12.9 %collective-permute-start.10 = (bf16[576,128]{1,0:T(8,128)(2,1)S(1)}, bf16[576,128]{1,0:T(8,128)(2,1)S(1)}, u32[]{:S(2)}, u32[]{:S(2)}) collective-permute-start(bf16[576,128]{1,0:T(8,128)(2,1)S(1)} %pack.1), channel_id=1, source_target_pairs={{0,1},{1,2},{2,3},{3,0},{4,5},{5,6},{6,7},{7,4},{8,9},{9,10},{10,1... | collective-permute-start | bytes 442376 | tf_op jit(solution)/shard_map/ppermute | solution.py:878
  50.9 16.8 %collective-permute-start.15 = (bf16[4,576,128]{2,1,0:T(8,128)(2,1)S(1)}, bf16[4,576,128]{2,1,0:T(8,128)(2,1)S(1)}, u32[]{:S(2)}, u32[]{:S(2)}) collective-permute-start(bf16[4,576,128]{2,1,0:T(8,128)(2,1)S(1)} %pad_maximum_fusion.refs_11_), channel_id=1, source_target_pairs={{0,4},{4,0},{8,12},{12,8},{1,5},{5,1},{9,13},{13,9},{2,6},{6,2},{1... | collective-permute-start | bytes 1769480 | tf_op jit(solution)/shard_map/ppermute | solution.py:869
  51.0 16.8 %collective-permute-start.14 = (bf16[4,576,128]{2,1,0:T(8,128)(2,1)S(1)}, bf16[4,576,128]{2,1,0:T(8,128)(2,1)S(1)}, u32[]{:S(2)}, u32[]{:S(2)}) collective-permute-start(bf16[4,576,128]{2,1,0:T(8,128)(2,1)S(1)} %pad_maximum_fusion.refs_11_), channel_id=1, source_target_pairs={{0,8},{4,12},{8,0},{12,4},{16,24},{20,28},{24,16},{28,20},{1,9},{5... | collective-permute-start | bytes 1769480 | tf_op jit(solution)/shard_map/ppermute | solution.py:875
  51.5 16.2 %collective-permute-start.13 = (bf16[4,576,128]{2,1,0:T(8,128)(2,1)S(1)}, bf16[4,576,128]{2,1,0:T(8,128)(2,1)S(1)}, u32[]{:S(2)}, u32[]{:S(2)}) collective-permute-start(bf16[4,576,128]{2,1,0:T(8,128)(2,1)S(1)} %pad_maximum_fusion.refs_11_), channel_id=1, source_target_pairs={{0,16},{4,20},{8,24},{12,28},{16,0},{20,4},{24,8},{28,12},{1,17},{... | collective-permute-start | bytes 1769480 | tf_op jit(solution)/shard_map/ppermute | solution.py:875
  53.0 27.5 %collective-permute-start.19 = (bf16[4,576,128]{2,1,0:T(8,128)(2,1)S(1)}, bf16[4,576,128]{2,1,0:T(8,128)(2,1)S(1)}, u32[]{:S(2)}, u32[]{:S(2)}) collective-permute-start(bf16[4,576,128]{2,1,0:T(8,128)(2,1)S(1)} %pad_maximum_fusion.refs_11_), channel_id=1, source_target_pairs={{0,24},{4,28},{8,16},{12,20},{16,8},{20,12},{24,0},{28,4},{1,25},{... | collective-permute-start | bytes 1769480 | tf_op jit(solution)/shard_map/ppermute | solution.py:875
  80.5 4.4 %collective-permute-start.20 = (bf16[4,576,128]{2,1,0:T(8,128)(2,1)S(1)}, bf16[4,576,128]{2,1,0:T(8,128)(2,1)S(1)}, u32[]{:S(2)}, u32[]{:S(2)}) collective-permute-start(bf16[4,576,128]{2,1,0:T(8,128)(2,1)S(1)} %collective-permute-done.19.refs_17_), channel_id=1, source_target_pairs={{0,4},{4,0},{8,12},{12,8},{1,5},{5,1},{9,13},{13,9},{2,6},{6,2},{1... | collective-permute-start | bytes 1769480 | tf_op jit(solution)/shard_map/ppermute | solution.py:869
  80.5 4.5 %collective-permute-start.17 = (bf16[4,576,128]{2,1,0:T(8,128)(2,1)S(1)}, bf16[4,576,128]{2,1,0:T(8,128)(2,1)S(1)}, u32[]{:S(2)}, u32[]{:S(2)}) collective-permute-start(bf16[4,576,128]{2,1,0:T(8,128)(2,1)S(1)} %collective-permute-done.13.refs_13_), channel_id=1, source_target_pairs={{0,4},{4,0},{8,12},{12,8},{1,5},{5,1},{9,13},{13,9},{2,6},{6,2},{1... | collective-permute-start | bytes 1769480 | tf_op jit(solution)/shard_map/ppermute | solution.py:869
  81.0 4.0 %collective-permute-start.18 = (bf16[4,576,128]{2,1,0:T(8,128)(2,1)S(1)}, bf16[4,576,128]{2,1,0:T(8,128)(2,1)S(1)}, u32[]{:S(2)}, u32[]{:S(2)}) collective-permute-start(bf16[4,576,128]{2,1,0:T(8,128)(2,1)S(1)} %collective-permute-done.14.refs_15_), channel_id=1, source_target_pairs={{0,4},{4,0},{8,12},{12,8},{1,5},{5,1},{9,13},{13,9},{2,6},{6,2},{1... | collective-permute-start | bytes 1769480 | tf_op jit(solution)/shard_map/ppermute | solution.py:869
  81.1 3.9 %collective-permute-start.16 = (bf16[2,2,512,128]{3,2,1,0:T(8,128)(2,1)S(1)}, bf16[2,2,512,128]{3,2,1,0:T(8,128)(2,1)S(1)}, u32[]{:S(2)}, u32[]{:S(2)}) collective-permute-start(bf16[2,2,512,128]{3,2,1,0:T(8,128)(2,1)S(1)} %get-tuple-element.123.refs_3_), channel_id=1, source_target_pairs={{0,4},{4,0},{8,12},{12,8},{1,5},{5,1},{9,13},{13,9},{2,6},{6,2},{1... | collective-permute-start | bytes 1572872 | tf_op jit(solution)/shard_map/ppermute | solution.py:869
  118.5 4.8 %collective-permute-start.21 = (bf16[4,4,576,128]{3,2,1,0:T(8,128)(2,1)}, bf16[4,4,576,128]{3,2,1,0:T(8,128)(2,1)S(1)}, u32[]{:S(2)}, u32[]{:S(2)}) collective-permute-start(bf16[4,4,576,128]{3,2,1,0:T(8,128)(2,1)} %get-tuple-element.138), channel_id=1, source_target_pairs={{0,4},{4,0},{8,12},{12,8},{1,5},{5,1},{9,13},{13,9},{2,6},{6,2},{1... | collective-permute-start | bytes 7077896 | tf_op jit(solution)/shard_map/ppermute | solution.py:869
  126.0 3.6 %collective-permute-start.25 = (bf16[2,512,128]{2,1,0:T(8,128)(2,1)S(1)}, bf16[2,512,128]{2,1,0:T(8,128)(2,1)S(1)}, u32[]{:S(2)}, u32[]{:S(2)}) collective-permute-start(bf16[2,512,128]{2,1,0:T(8,128)(2,1)S(1)} %copy-done.55), channel_id=1, source_target_pairs={{0,4},{4,0},{8,12},{12,8},{1,5},{5,1},{9,13},{13,9},{2,6},{6,2},{1... | collective-permute-start | bytes 786440 | tf_op jit(solution)/shard_map/ppermute | solution.py:869
  126.1 28.5 %collective-permute-start.22 = (bf16[4,576,128]{2,1,0:T(8,128)(2,1)S(1)}, bf16[4,576,128]{2,1,0:T(8,128)(2,1)S(1)}, u32[]{:S(2)}, u32[]{:S(2)}) collective-permute-start(bf16[4,576,128]{2,1,0:T(8,128)(2,1)S(1)} %get-tuple-element.140), channel_id=1, source_target_pairs={{0,16},{4,20},{8,24},{12,28},{16,0},{20,4},{24,8},{28,12},{1,17},{... | collective-permute-start | bytes 1769480 | tf_op jit(solution)/shard_map/ppermute | solution.py:875
  127.6 28.0 %collective-permute-start.23 = (bf16[4,576,128]{2,1,0:T(8,128)(2,1)S(1)}, bf16[4,576,128]{2,1,0:T(8,128)(2,1)S(1)}, u32[]{:S(2)}, u32[]{:S(2)}) collective-permute-start(bf16[4,576,128]{2,1,0:T(8,128)(2,1)S(1)} %get-tuple-element.141), channel_id=1, source_target_pairs={{0,8},{4,12},{8,0},{12,4},{16,24},{20,28},{24,16},{28,20},{1,9},{5... | collective-permute-start | bytes 1769480 | tf_op jit(solution)/shard_map/ppermute | solution.py:875
  128.1 27.5 %collective-permute-start.24 = (bf16[4,576,128]{2,1,0:T(8,128)(2,1)S(1)}, bf16[4,576,128]{2,1,0:T(8,128)(2,1)S(1)}, u32[]{:S(2)}, u32[]{:S(2)}) collective-permute-start(bf16[4,576,128]{2,1,0:T(8,128)(2,1)S(1)} %get-tuple-element.142), channel_id=1, source_target_pairs={{0,24},{4,28},{8,16},{12,20},{16,8},{20,12},{24,0},{28,4},{1,25},{... | collective-permute-start | bytes 1769480 | tf_op jit(solution)/shard_map/ppermute | solution.py:875
  129.7 26.2 %copy-start.54 = (bf16[2,512,128]{2,1,0:T(8,128)(2,1)S(1)}, bf16[2,512,128]{2,1,0:T(8,128)(2,1)}, u32[]{:S(2)}) copy-start(bf16[2,512,128]{2,1,0:T(8,128)(2,1)} %get-tuple-element.159) | copy-start | bytes 786436
  155.9 7.9 %collective-permute-start.27 = (bf16[2,512,128]{2,1,0:T(8,128)(2,1)S(1)}, bf16[2,512,128]{2,1,0:T(8,128)(2,1)S(1)}, u32[]{:S(2)}, u32[]{:S(2)}) collective-permute-start(bf16[2,512,128]{2,1,0:T(8,128)(2,1)S(1)} %copy-done.54), channel_id=1, source_target_pairs={{0,4},{4,0},{8,12},{12,8},{1,5},{5,1},{9,13},{13,9},{2,6},{6,2},{1... | collective-permute-start | bytes 786440 | tf_op jit(solution)/shard_map/ppermute | solution.py:869
  155.9 32.8 %collective-permute-start.28 = (bf16[576,128]{1,0:T(8,128)(2,1)S(1)}, bf16[576,128]{1,0:T(8,128)(2,1)S(1)}, u32[]{:S(2)}, u32[]{:S(2)}) collective-permute-start(bf16[576,128]{1,0:T(8,128)(2,1)S(1)} %get-tuple-element.164), channel_id=1, source_target_pairs={{0,1},{1,2},{2,3},{3,0},{4,5},{5,6},{6,7},{7,4},{8,9},{9,10},{10,1... | collective-permute-start | bytes 442376 | tf_op jit(solution)/shard_map/ppermute | solution.py:878
  157.4 31.4 %collective-permute-start.29 = (bf16[576,128]{1,0:T(8,128)(2,1)S(1)}, bf16[576,128]{1,0:T(8,128)(2,1)S(1)}, u32[]{:S(2)}, u32[]{:S(2)}) collective-permute-start(bf16[576,128]{1,0:T(8,128)(2,1)S(1)} %get-tuple-element.165), channel_id=1, source_target_pairs={{0,2},{1,3},{2,0},{3,1},{4,6},{5,7},{6,4},{7,5},{8,10},{9,11},{10,... | collective-permute-start | bytes 442376 | tf_op jit(solution)/shard_map/ppermute | solution.py:878
  159.2 29.6 %collective-permute-start.30 = (bf16[576,128]{1,0:T(8,128)(2,1)S(1)}, bf16[576,128]{1,0:T(8,128)(2,1)S(1)}, u32[]{:S(2)}, u32[]{:S(2)}) collective-permute-start(bf16[576,128]{1,0:T(8,128)(2,1)S(1)} %get-tuple-element.166), channel_id=1, source_target_pairs={{0,3},{1,0},{2,1},{3,2},{4,7},{5,4},{6,5},{7,6},{8,11},{9,8},{10,9... | collective-permute-start | bytes 442376 | tf_op jit(solution)/shard_map/ppermute | solution.py:878
  162.0 26.7 %collective-permute-start.26 = (bf16[512,512]{1,0:T(8,128)(2,1)S(1)}, bf16[512,512]{1,0:T(8,128)(2,1)S(1)}, u32[]{:S(2)}, u32[]{:S(2)}) collective-permute-start(bf16[512,512]{1,0:T(8,128)(2,1)S(1)} %copy-done.52), channel_id=1, source_target_pairs={{0,8},{4,12},{8,0},{12,4},{1,9},{5,13},{9,1},{13,5},{2,10},{6,14},... | collective-permute-start | bytes 1572872 | tf_op jit(solution)/shard_map/ppermute | solution.py:866
  163.8 25.0 %copy-start.5 = (bf16[2048,512]{1,0:T(8,128)(2,1)S(1)}, bf16[2048,512]{1,0:T(8,128)(2,1)}, u32[]{:S(2)}) copy-start(bf16[2048,512]{1,0:T(8,128)(2,1)} %copy-done.4) | copy-start | bytes 6291460
  197.7 8.1 %collective-permute-start.32 = (bf16[2,512,512]{2,1,0:T(8,128)(2,1)S(1)}, bf16[2,512,512]{2,1,0:T(8,128)(2,1)S(1)}, u32[]{:S(2)}, u32[]{:S(2)}) collective-permute-start(bf16[2,512,512]{2,1,0:T(8,128)(2,1)S(1)} %get-tuple-element.177), channel_id=1, source_target_pairs={{0,4},{4,0},{8,12},{12,8},{1,5},{5,1},{9,13},{13,9},{2,6},{6,2},{1... | collective-permute-start | bytes 3145736 | tf_op jit(solution)/shard_map/ppermute | solution.py:869
  197.8 3.3 %collective-permute-start.31 = (bf16[1664,128]{1,0:T(8,128)(2,1)S(1)}, bf16[1664,128]{1,0:T(8,128)(2,1)S(1)}, u32[]{:S(2)}, u32[]{:S(2)}) collective-permute-start(bf16[1664,128]{1,0:T(8,128)(2,1)S(1)} %get-tuple-element.172), channel_id=1, source_target_pairs={{0,4},{4,0},{8,12},{12,8},{1,5},{5,1},{9,13},{13,9},{2,6},{6,2},{1... | collective-permute-start | bytes 1277960 | tf_op jit(solution)/shard_map/ppermute | solution.py:869
  202.4 8.7 %collective-permute-start.34 = (bf16[896,128]{1,0:T(8,128)(2,1)}, bf16[896,128]{1,0:T(8,128)(2,1)S(1)}, u32[]{:S(2)}, u32[]{:S(2)}) collective-permute-start(bf16[896,128]{1,0:T(8,128)(2,1)} %get-tuple-element.180), channel_id=1, source_target_pairs={{0,16},{4,20},{8,24},{12,28},{16,0},{20,4},{24,8},{28,12},{1,17},{... | collective-permute-start | bytes 688136 | tf_op jit(solution)/shard_map/ppermute | solution.py:875
  202.9 13.3 %collective-permute-start.35 = (bf16[896,128]{1,0:T(8,128)(2,1)S(1)}, bf16[896,128]{1,0:T(8,128)(2,1)S(1)}, u32[]{:S(2)}, u32[]{:S(2)}) collective-permute-start(bf16[896,128]{1,0:T(8,128)(2,1)S(1)} %get-tuple-element.181), channel_id=1, source_target_pairs={{0,8},{4,12},{8,0},{12,4},{16,24},{20,28},{24,16},{28,20},{1,9},{5... | collective-permute-start | bytes 688136 | tf_op jit(solution)/shard_map/ppermute | solution.py:875
  202.9 13.3 %collective-permute-start.36 = (bf16[896,128]{1,0:T(8,128)(2,1)S(1)}, bf16[896,128]{1,0:T(8,128)(2,1)S(1)}, u32[]{:S(2)}, u32[]{:S(2)}) collective-permute-start(bf16[896,128]{1,0:T(8,128)(2,1)S(1)} %get-tuple-element.182), channel_id=1, source_target_pairs={{0,24},{4,28},{8,16},{12,20},{16,8},{20,12},{24,0},{28,4},{1,25},{... | collective-permute-start | bytes 688136 | tf_op jit(solution)/shard_map/ppermute | solution.py:875
  208.6 21.2 %collective-permute-start.33 = (bf16[512,512]{1,0:T(8,128)(2,1)S(1)}, bf16[512,512]{1,0:T(8,128)(2,1)}, u32[]{:S(2)}, u32[]{:S(2)}) collective-permute-start(bf16[512,512]{1,0:T(8,128)(2,1)S(1)} %get-tuple-element.179), channel_id=1, source_target_pairs={{0,8},{4,12},{8,0},{12,4},{1,9},{5,13},{9,1},{13,5},{2,10},{6,14},... | collective-permute-start | bytes 1572872 | tf_op jit(solution)/shard_map/ppermute | solution.py:866
  208.6 14.3 %collective-permute-start.40 = (bf16[576,128]{1,0:T(8,128)(2,1)S(1)}, bf16[576,128]{1,0:T(8,128)(2,1)S(1)}, u32[]{:S(2)}, u32[]{:S(2)}) collective-permute-start(bf16[576,128]{1,0:T(8,128)(2,1)S(1)} %get-tuple-element.192.r), channel_id=1, source_target_pairs={{0,16},{4,20},{8,24},{12,28},{16,0},{20,4},{24,8},{28,12},{1,17},{... | collective-permute-start | bytes 442376 | tf_op jit(solution)/shard_map/ppermute | solution.py:875
  216.3 8.0 %collective-permute-start.37 = (bf16[320,128]{1,0:T(8,128)(2,1)S(1)}, bf16[320,128]{1,0:T(8,128)(2,1)S(1)}, u32[]{:S(2)}, u32[]{:S(2)}) collective-permute-start(bf16[320,128]{1,0:T(8,128)(2,1)S(1)} %get-tuple-element.188), channel_id=1, source_target_pairs={{0,1},{1,2},{2,3},{3,0},{4,5},{5,6},{6,7},{7,4},{8,9},{9,10},{10,1... | collective-permute-start | bytes 245768 | tf_op jit(solution)/shard_map/ppermute | solution.py:878
  216.4 7.9 %collective-permute-start.38 = (bf16[320,128]{1,0:T(8,128)(2,1)S(1)}, bf16[320,128]{1,0:T(8,128)(2,1)S(1)}, u32[]{:S(2)}, u32[]{:S(2)}) collective-permute-start(bf16[320,128]{1,0:T(8,128)(2,1)S(1)} %get-tuple-element.189), channel_id=1, source_target_pairs={{0,2},{1,3},{2,0},{3,1},{4,6},{5,7},{6,4},{7,5},{8,10},{9,11},{10,... | collective-permute-start | bytes 245768 | tf_op jit(solution)/shard_map/ppermute | solution.py:878
  217.0 7.3 %collective-permute-start.39 = (bf16[320,128]{1,0:T(8,128)(2,1)S(1)}, bf16[320,128]{1,0:T(8,128)(2,1)S(1)}, u32[]{:S(2)}, u32[]{:S(2)}) collective-permute-start(bf16[320,128]{1,0:T(8,128)(2,1)S(1)} %get-tuple-element.190), channel_id=1, source_target_pairs={{0,3},{1,0},{2,1},{3,2},{4,7},{5,4},{6,5},{7,6},{8,11},{9,8},{10,9... | collective-permute-start | bytes 245768 | tf_op jit(solution)/shard_map/ppermute | solution.py:878
  224.4 4.2 %collective-permute-start.41 = (bf16[192,128]{1,0:T(8,128)(2,1)S(1)}, bf16[192,128]{1,0:T(8,128)(2,1)S(1)}, u32[]{:S(2)}, u32[]{:S(2)}) collective-permute-start(bf16[192,128]{1,0:T(8,128)(2,1)S(1)} %get-tuple-element.198.r), channel_id=1, source_target_pairs={{0,16},{4,20},{8,24},{12,28},{16,0},{20,4},{24,8},{28,12},{1,17},{... | collective-permute-start | bytes 147464 | tf_op jit(solution)/shard_map/ppermute | solution.py:875
  (50 other events, 599.6 us)

commit v4 on v3

--- a/solution.py
+++ b/solution.py
@@ -45,7 +45,7 @@
         in_specs=[spec for _, spec in ins],
         out_specs=tuple(VM for _ in outs),
         scratch_shapes=list(scratch),
-        compiler_params=pltpu.CompilerParams(vmem_limit_bytes=(60 if name == "ffn" else 36) * 1024 * 1024, **kw),
+        compiler_params=pltpu.CompilerParams(vmem_limit_bytes=36 * 1024 * 1024, **kw),
         cost_estimate=pl.CostEstimate(flops=flops, bytes_accessed=nbytes, transcendentals=trans),
     )(*[near(a) if spec is VM and name in NEAR and a.ndim > 1 else a for a, spec in ins])
 
@@ -902,10 +902,11 @@
             [sds((576, 128), BF)],
             nbytes=2 << 20,
         )
-        turn0 = turn(x0, 1)
+        cot1 = swap_half(pick(after(cotangent, wq), 1 - s))
         own_qkv = jnp.stack(after(tuple(lines_qkv), half_rest))
-        across = swap_half(after(own_qkv, turn0))
-        lines_rest = lines(after(half_rest, own_qkv))
+        turns = [turn(after(t, own_qkv), 1) for t in (x0, x1)]
+        across = swap_half(own_qkv)
+        lines_rest = lines(after(half_rest, (own_qkv, *turns)))
     else:
         x0 = pick(tokens, s)
         x1 = swap_half(pick(tokens, 1 - s))
@@ -916,8 +917,10 @@
 
         w_qkv = [whole(qkv_weight)]
         w_rest = [whole(mix_weight), whole(up_weight), whole(down_weight)]
-    pieces = [x0] + ([turn0] if geo.fast else [turn(x0, d) for d in range(1, G)])
-    pieces += [x1] + [turn(x1, d) for d in range(1, G)]
+    if geo.fast:
+        pieces = [x0, turns[0], x1, turns[1]]
+    else:
+        pieces = [x0] + [turn(x0, d) for d in range(1, G)] + [x1] + [turn(x1, d) for d in range(1, G)]
     gain1, shift1 = row2(norm_gain), row2(norm_shift)
     h1, segk, segq = call(
         functools.partial(norm_kernel, geo),
@@ -929,7 +932,8 @@
     )
     segs = (segk, segq)
     if geo.fast:
-        w_qkv = [own_qkv, turn(own_qkv, 1), across, turn(after(across, h1), 1)]
+        own_turned = turn(after(own_qkv, h1), 1)
+        w_qkv = [own_qkv, own_turned, across, turn(after(across, (h1, *lines_rest)), 1)]
     bias = row2(jnp.concatenate([query_bias, jnp.zeros_like(query_bias), value_bias]))
     wspec = HBM if geo.fast else VM
     res = call(
@@ -938,12 +942,13 @@
         [(meta, SM), (h1, VM), (bias, VM)] + [(w, wspec) for w in w_qkv],
         [sds((L, PW), BF)] * (3 * NP) + [sds((D, 3 * PW), BF)] * NP,
         scratch=[pltpu.VMEM((D, 3 * D), BF), pltpu.SemaphoreType.DMA(())] if geo.fast else [],
-        flops=2 * L * D * 3 * HL,
-        nbytes=L * D * 2 + L * HL * 6 + D * D * 6,
+        flops=0,
+        nbytes=0,
     )
     q, k, v, w_own = (res[n * NP : (n + 1) * NP] for n in range(4))
     cot0 = pick(cotangent, s)
-    cot1 = swap_half(pick(after(cotangent, x1) if geo.fast else cotangent, 1 - s))
+    if not geo.fast:
+        cot1 = swap_half(pick(cotangent, 1 - s))
     if geo.fast:
         rest = jnp.stack(after(tuple(lines_rest), (q[0], cot1)))
         quads_rest = [plane(rest, 1, 0), plane(rest, 0, 1), plane(rest, 1, 1)]

time: 233 us -> 219 us (0.940)
  local copies, waits for them, and re-layouts: 9.83 us -> 4.69 us
  Pallas kernels: 129 us -> 126 us
    ppermute x5, waiting for transfers between devices: 13.4 us -> 1.1 us  [swap_half(): return lax.ppermute(v, 'col', [(i, (i + G) % C) for i in range(C)])]
    ppermute x12, waiting for transfers between devices: 7.99 us -> 13.2 us  [line(): return lax.ppermute(v, 'row', [(i, (i + d) % R) for i in range(R)])]
    ppermute x14, waiting for transfers between devices: 9.99 us -> 13.9 us  [turn(): lax.ppermute(v, 'col', [(i, i // G * G + (i % G + d) % G) for i in range(...]
    unnamed x114 -> x36, local copies, waits for them, and re-layouts: 5.2 us -> 1.65 us
    pallas_call x18, Pallas kernels: 129 us -> 126 us  [call(): pl.pallas_call(kernel, name=name, out_shape=tuple((o for o in outs)), in_...]
  transfers between devices with their start and end apart: 42 -> 42, of which waited for: 12 -> 17; matrix products, arithmetic and copies ran while one was open for 3% -> 2% of each run, Pallas kernels for 38% -> 40%
where the time goes in v4:
time: 219 us; the launch traced here: 218 us
  Pallas kernels  126 us (58%)
  waiting for transfers between devices  41.9 us (19%)
  starting transfers between devices  39.8 us (18%)
  local copies, waits for them, and re-layouts  4.69 us (2%)
  other arithmetic  4.5 us (2%)
    pallas_call x18, Pallas kernels, call(): pl.pallas_call(kernel, name=name, out_shape=tuple((o for o in outs)), in_...  126 us
    ppermute x12, starting transfers between devices, line(): return lax.ppermute(v, 'row', [(i, (i + d) % R) for i in range(R)])  18.2 us
    ppermute x14, waiting for transfers between devices, turn(): lax.ppermute(v, 'col', [(i, i // G * G + (i % G + d) % G) for i in range(...  13.9 us
    ppermute x11, waiting for transfers between devices, plane(): return lax.ppermute(v, ('dp', 'col'), pairs)  13.7 us
    ppermute x12, waiting for transfers between devices, line(): return lax.ppermute(v, 'row', [(i, (i + d) % R) for i in range(R)])  13.2 us
    ppermute x11, starting transfers between devices, plane(): return lax.ppermute(v, ('dp', 'col'), pairs)  11.4 us
    ppermute x5, starting transfers between devices, swap_half(): return lax.ppermute(v, 'col', [(i, (i + G) % C) for i in range(C)])  7.42 us
  transfers between devices with their start and end apart: 42, of which 17 were waited for; matrix products, arithmetic and copies ran while one was open for 2% of the time, Pallas kernels for 40%

profile of v4, /device:TPU:0, one launch (start us, length us, event | category | flops | bytes accessed | tf_op | source)
XLA Modules:
  0.0 218.2 jit_solution(13626608660061195061)
XLA Ops:
  0.7 1.1 convert_element_type.3
  1.8 1.3 dynamic-slice_bitcast_fusion.2
  3.1 3.1 %collective-permute-start = (bf16[512,512]{1,0:T(8,128)(2,1)S(1)}, bf16[512,512]{1,0:T(8,128)(2,1)S(1)}, u32[]{:S(2)}, u32[]{:S(2)}) collective-permute-start(bf16[512,512]{1,0:T(8,128)(2,1)S(1)} %get-tuple-element.206), channel_id=1, source_target_pairs={{0,8},{4,12},{8,0},{12,4},{1,9},{5,13},{9,1},{13,5},{2,10},{6,14},... | collective-permute-start | bytes 1572872 | tf_op jit(solution)/shard_map/ppermute | solution.py:866
  6.2 3.6 %collective-permute-start.4 = (bf16[128,384]{1,0:T(8,128)(2,1)S(1)}, bf16[128,384]{1,0:T(8,128)(2,1)S(1)}, u32[]{:S(2)}, u32[]{:S(2)}) collective-permute-start(bf16[128,384]{1,0:T(8,128)(2,1)S(1)} %convert_element_type.3), channel_id=1, source_target_pairs={{0,3},{1,0},{2,1},{3,2},{4,7},{5,4},{6,5},{7,6},{8,11},{9,8},{10,9... | collective-permute-start | bytes 294920 | tf_op jit(solution)/shard_map/ppermute | solution.py:878
  9.8 1.0 collective-permute-start.2
  11.4 1.5 collective-permute-done.4
  12.9 5.2 %collective-permute-done.3 = bf16[128,384]{1,0:T(8,128)(2,1)S(1)} collective-permute-done((bf16[128,384]{1,0:T(8,128)(2,1)S(1)}, bf16[128,384]{1,0:T(8,128)(2,1)S(1)}, u32[]{:S(2)}, u32[]{:S(2)}) %collective-permute-start.3) | collective-permute-done | bytes 98336 | tf_op jit(solution)/shard_map/ppermute | solution.py:878
  18.1 1.0 pad_maximum_fusion.1.refs_0_
  20.1 0.9 collective-permute-done.5.refs_1_
  21.8 2.0 collective-permute-start.11
  24.3 2.0 collective-permute-start.9
  26.9 3.6 %norm_one.1 = (bf16[2048,512]{1,0:T(8,128)(2,1)S(1)}, s32[2048,128]{1,0:T(8,128)S(1)}, s32[8,2048]{1,0:T(8,128)S(1)}) custom-call(s32[3]{0:T(128)S(1)} %pad_add_fusion.meta, s32[2,8]{1,0:T(2,128)S(1)} %copy-done.6, f32[1,512]{1,0:T(1,128)S(1)} %bitcast.35, f32[1,512]{1,0:T(1,128)S(1)} %bitcast.38, bf16[512,512]{1,0:T(8,128)(2,1)S(1)} %get-tuple-element.114.refs_0_.refs_1_, ...), custom_call_target="tpu_custom_call" | custom-call | flops 10485760 | bytes 4194304 | tf_op jit(solution)/shard_map/norm_one/pallas_call | solution.py:41
  30.5 1.1 collective-permute-done.8.refs_2_
  31.6 6.3 %collective-permute-done.10 = bf16[576,128]{1,0:T(8,128)(2,1)S(1)} collective-permute-done((bf16[576,128]{1,0:T(8,128)(2,1)S(1)}, bf16[576,128]{1,0:T(8,128)(2,1)S(1)}, u32[]{:S(2)}, u32[]{:S(2)}) %collective-permute-start.10) | collective-permute-done | bytes 147488 | tf_op jit(solution)/shard_map/ppermute | solution.py:878
  38.0 1.7 collective-permute-done.12.refs_3_
  39.6 4.4 %qkv.1 = (bf16[2048,128]{1,0:T(8,128)(2,1)S(1)}, bf16[2048,128]{1,0:T(8,128)(2,1)S(1)}, bf16[2048,128]{1,0:T(8,128)(2,1)S(1)}, bf16[2048,128]{1,0:T(8,128)(2,1)S...) custom-call(s32[3]{0:T(128)S(1)} %pad_add_fusion.meta, ...), custom_call_target="tpu_custom_call" | custom-call | tf_op jit(solution)/shard_map/qkv/pallas_call | solution.py:41
  44.8 1.5 collective-permute-start.13
  46.3 1.5 collective-permute-start.19
  47.8 13.1 %attend.2 = (bf16[2,2,512,128]{3,2,1,0:T(8,128)(2,1)S(1)}, f32[2,8,512]{2,1,0:T(8,128)S(1)}) custom-call(s32[3]{0:T(128)S(1)} %pad_add_fusion.meta, s32[2,8]{1,0:T(2,128)S(1)} %copy-done.6, s32[2048,128]{1,0:T(8,128)S(1)} %get-tuple-element.116.segk, s32[8,2048]{1,0:T(8,128)S(1)} %get-tuple-element.117.segq, ...), custom_call_target="tpu_custom_call" | custom-call | flops 4294967296 | bytes 4194304 | tf_op jit(solution)/shard_map/attend/pallas_call | solution.py:41
  61.0 9.4 %attend.3 = (bf16[2,2,512,128]{3,2,1,0:T(8,128)(2,1)S(1)}, f32[2,8,512]{2,1,0:T(8,128)S(1)}) custom-call(s32[3]{0:T(128)S(1)} %pad_add_fusion.meta, s32[2,8]{1,0:T(2,128)S(1)} %copy-done.6, s32[2048,128]{1,0:T(8,128)S(1)} %get-tuple-element.116.segk, s32[8,2048]{1,0:T(8,128)S(1)} %get-tuple-element.117.segq, ...), custom_call_target="tpu_custom_call" | custom-call | flops 4294967296 | bytes 4194304 | tf_op jit(solution)/shard_map/attend/pallas_call | solution.py:41
  70.4 3.3 %collective-permute-done.19.refs_17_ = bf16[4,576,128]{2,1,0:T(8,128)(2,1)S(1)} collective-permute-done((bf16[4,576,128]{2,1,0:T(8,128)(2,1)S(1)}, bf16[4,576,128]{2,1,0:T(8,128)(2,1)S(1)}, u32[]{:S(2)}, u32[]{:S(2)}) %collective-permute-start.19) | collective-permute-done | bytes 589856 | tf_op jit(solution)/shard_map/ppermute | solution.py:875
  74.8 3.4 %collective-permute-done.16.refs_10_ = bf16[2,2,512,128]{3,2,1,0:T(8,128)(2,1)S(1)} collective-permute-done((bf16[2,2,512,128]{3,2,1,0:T(8,128)(2,1)S(1)}, bf16[2,2,512,128]{3,2,1,0:T(8,128)(2,1)S(1)}, u32[]{:S(2)}, u32[]{:S(2)}) %collective-permute-start.16) | collective-permute-done | bytes 524320 | tf_op jit(solution)/shard_map/ppermute | solution.py:869
  78.2 28.1 %ffn.1 = (bf16[512,512]{1,0:T(8,128)(2,1)S(1)}, bf16[512,512]{1,0:T(8,128)(2,1)S(1)}, f32[1024,512]{1,0:T(8,128)S(1)}, bf16[2,512,128]{2,1,0:T(8,128)(2,1)S(1)},...) custom-call(s32[3]{0:T(128)S(1)} %pad_add_fusion.meta, ...), custom_call_target="tpu_custom_call" | custom-call | flops 14495514624 | bytes 20971520 | tf_op jit(solution)/shard_map/ffn/pallas_call | solution.py:41
  106.6 4.4 %collective-permute-done.21.recv = bf16[4,4,576,128]{3,2,1,0:T(8,128)(2,1)S(1)} collective-permute-done((bf16[4,4,576,128]{3,2,1,0:T(8,128)(2,1)S(1)}, bf16[4,4,576,128]{3,2,1,0:T(8,128)(2,1)S(1)}, u32[]{:S(2)}, u32[]{:S(2)}) %collective-permute-start.21) | collective-permute-done | bytes 2359328 | tf_op jit(solution)/shard_map/ppermute | solution.py:869
  111.7 1.5 collective-permute-start.22
  113.2 2.0 collective-permute-start.23
  115.2 24.7 %attend_back.2.refs_0_ = bf16[2048,384]{1,0:T(8,128)(2,1)S(1)} custom-call(s32[3]{0:T(128)S(1)} %pad_add_fusion.meta, s32[2,8]{1,0:T(2,128)S(1)} %copy-done.6, s32[2048,128]{1,0:T(8,128)S(1)} %get-tuple-element.116.segk, s32[8,2048]{1,0:T(8,128)S(1)} %get-tuple-element.117.segq, bf16[2048,128]{1,0:T(8,128)(2,1)S(1)} %get-tuple-element.147.refs_0_.q, ...), custom_call_target="tpu_custom_call" | custom-call | flops 10737418240 | bytes 5242880 | tf_op jit(solution)/shard_map/attend_back/pallas_call | solution.py:41
  140.0 1.5 collective-permute-done.23.c
  142.1 2.2 collective-permute-start.29
  144.3 2.7 %collective-permute-start.30 = (bf16[576,128]{1,0:T(8,128)(2,1)S(1)}, bf16[576,128]{1,0:T(8,128)(2,1)S(1)}, u32[]{:S(2)}, u32[]{:S(2)}) collective-permute-start(bf16[576,128]{1,0:T(8,128)(2,1)S(1)} %get-tuple-element.170), channel_id=1, source_target_pairs={{0,3},{1,0},{2,1},{3,2},{4,7},{5,4},{6,5},{7,6},{8,11},{9,8},{10,9... | collective-permute-start | bytes 442376 | tf_op jit(solution)/shard_map/ppermute | solution.py:878
  147.0 1.7 collective-permute-start.26
  148.8 24.7 %attend_back.3.refs_1_ = bf16[2048,384]{1,0:T(8,128)(2,1)S(1)} custom-call(s32[3]{0:T(128)S(1)} %pad_add_fusion.meta, s32[2,8]{1,0:T(2,128)S(1)} %copy-done.6, s32[2048,128]{1,0:T(8,128)S(1)} %get-tuple-element.116.segk, s32[8,2048]{1,0:T(8,128)S(1)} %get-tuple-element.117.segq, bf16[2048,128]{1,0:T(8,128)(2,1)S(1)} %get-tuple-element.160.refs_1_.q, ...), custom_call_target="tpu_custom_call" | custom-call | flops 10737418240 | bytes 5242880 | tf_op jit(solution)/shard_map/attend_back/pallas_call | solution.py:41
  173.5 5.1 %wgrad.1 = (bf16[1664,128]{1,0:T(8,128)(2,1)S(1)}, bf16[1664,128]{1,0:T(8,128)(2,1)S(1)}, bf16[576,128]{1,0:T(8,128)(2,1)}) custom-call(s32[3]{0:T(128)S(1)} %pad_add_fusion.meta, f32[16,512]{1,0:T(8,128)S(1)} %get-tuple-element.164.vec_in, f32[1,512]{1,0:T(1,128)S(1)} %bitcast.36, f32[1,512]{1,0:T(1,128)S(1)} %bitcast.39, ...), custom_call_target="tpu_custom_call" | custom-call | flops 1610612736 | bytes 8388608 | tf_op jit(solution)/shard_map/wgrad/pallas_call | solution.py:41
  178.7 4.3 %qkv_back.1 = (f32[2,512,512]{2,1,0:T(8,128)S(1)}, bf16[2,512,512]{2,1,0:T(8,128)(2,1)S(1)}) custom-call(s32[3]{0:T(128)S(1)} %pad_add_fusion.meta, bf16[2048,384]{1,0:T(8,128)(2,1)S(1)} %attend_back.2.refs_0_, bf16[2048,384]{1,0:T(8,128)(2,1)S(1)} %attend_back.3.refs_1_, bf16[512,384]{1,0:T(8,128)(2,1)S(1)} %get-tuple-element.166.refs_2_, ...), custom_call_target="tpu_custom_call" | custom-call | flops 1610612736 | bytes 12582912 | tf_op jit(solution)/shard_map/qkv_back/pallas_call | solution.py:41
  183.5 2.8 %collective-permute-done.31.recv = bf16[1664,128]{1,0:T(8,128)(2,1)S(1)} collective-permute-done((bf16[1664,128]{1,0:T(8,128)(2,1)S(1)}, bf16[1664,128]{1,0:T(8,128)(2,1)S(1)}, u32[]{:S(2)}, u32[]{:S(2)}) %collective-permute-start.31) | collective-permute-done | bytes 426016 | tf_op jit(solution)/shard_map/ppermute | solution.py:869
  186.3 1.5 arrange.1
  188.3 1.2 collective-permute-start.35
  189.5 1.8 collective-permute-start.36
  191.2 2.8 %norm_back.1 = (bf16[2,512,512]{2,1,0:T(8,128)(2,1)}, bf16[512,512]{1,0:T(8,128)(2,1)}) custom-call(s32[3]{0:T(128)S(1)} %pad_add_fusion.meta, f32[1,512]{1,0:T(1,128)S(1)} %bitcast.37, f32[1024,512]{1,0:T(8,128)S(1)} %get-tuple-element.159.g_resid, f32[2,512,512]{2,1,0:T(8,128)S(1)} %get-tuple-element.180.gh, ...), custom_call_target="tpu_custom_call" | custom-call | flops 15728640 | bytes 8388608 | tf_op jit(solution)/shard_map/norm_back/pallas_call | solution.py:41
  194.0 1.5 collective-permute-start.33
  196.4 5.9 %collective-permute-done.36.d = bf16[896,128]{1,0:T(8,128)(2,1)S(1)} collective-permute-done((bf16[896,128]{1,0:T(8,128)(2,1)}, bf16[896,128]{1,0:T(8,128)(2,1)S(1)}, u32[]{:S(2)}, u32[]{:S(2)}) %collective-permute-start.36) | collective-permute-done | bytes 229408 | tf_op jit(solution)/shard_map/ppermute | solution.py:875
  202.6 3.7 %collective-permute-start.39 = (bf16[320,128]{1,0:T(8,128)(2,1)S(1)}, bf16[320,128]{1,0:T(8,128)(2,1)S(1)}, u32[]{:S(2)}, u32[]{:S(2)}) collective-permute-start(bf16[320,128]{1,0:T(8,128)(2,1)S(1)} %get-tuple-element.194), channel_id=1, source_target_pairs={{0,3},{1,0},{2,1},{3,2},{4,7},{5,4},{6,5},{7,6},{8,11},{9,8},{10,9... | collective-permute-start | bytes 245768 | tf_op jit(solution)/shard_map/ppermute | solution.py:878
  206.4 2.3 %maximum_select_fusion = bf16[2,512,512]{2,1,0:T(8,128)(2,1)} fusion(bf16[1,512,512]{2,1,0:T(8,128)(2,1)} %bitcast.45, bf16[1,512,512]{2,1,0:T(8,128)(2,1)S(1)} %bitcast.34, pred[]{:T(512)S(6)} %eq.3), kind=kLoop, calls=%fused_computation | loop fusion | flops 1572864 | bytes 2097153 | tf_op jit(solution)/shard_map/jit(_where)/select_n | solution.py:1128
  208.7 1.8 finish.1
  212.7 2.3 %collective-permute-done.41.o = bf16[192,128]{1,0:T(8,128)(2,1)S(1)} collective-permute-done((bf16[192,128]{1,0:T(8,128)(2,1)S(1)}, bf16[192,128]{1,0:T(8,128)(2,1)S(1)}, u32[]{:S(2)}, u32[]{:S(2)}) %collective-permute-start.41) | collective-permute-done | bytes 49184 | tf_op jit(solution)/shard_map/ppermute | solution.py:875
  214.9 1.2 finish_qkv.1
  216.2 1.1 bitcast_dynamic-update-slice_fusion
  217.2 1.0 copy-done.16
  (103 shorter events, 11.6 us)
Async XLA Ops:
  0.6 25.7 %copy-start = (bf16[2,512,512]{2,1,0:T(8,128)(2,1)S(1)}, bf16[2,512,512]{2,1,0:T(8,128)(2,1)}, u32[]{:S(2)}) copy-start(bf16[2,512,512]{2,1,0:T(8,128)(2,1)} %param.31) | copy-start | bytes 3145732
  1.8 25.2 %copy-start.4 = (f32[512]{0:T(512)S(1)}, f32[512]{0:T(512)}, u32[]{:S(2)}) copy-start(f32[512]{0:T(512)} %param.18) | copy-start | bytes 6148
  1.8 25.1 %copy-start.5 = (f32[512]{0:T(512)S(1)}, f32[512]{0:T(512)}, u32[]{:S(2)}) copy-start(f32[512]{0:T(512)} %param.19) | copy-start | bytes 6148
  1.8 25.1 %copy-start.6 = (s32[2,8]{1,0:T(2,128)S(1)}, s32[2,8]{1,0:T(2,128)}, u32[]{:S(2)}) copy-start(s32[2,8]{1,0:T(2,128)} %doc.9) | copy-start | bytes 196
  3.1 16.1 %collective-permute-start = (bf16[512,512]{1,0:T(8,128)(2,1)S(1)}, bf16[512,512]{1,0:T(8,128)(2,1)S(1)}, u32[]{:S(2)}, u32[]{:S(2)}) collective-permute-start(bf16[512,512]{1,0:T(8,128)(2,1)S(1)} %get-tuple-element.206), channel_id=1, source_target_pairs={{0,8},{4,12},{8,0},{12,4},{1,9},{5,13},{9,1},{13,5},{2,10},{6,14},... | collective-permute-start | bytes 1572872 | tf_op jit(solution)/shard_map/ppermute | solution.py:866
  6.2 6.8 %collective-permute-start.4 = (bf16[128,384]{1,0:T(8,128)(2,1)S(1)}, bf16[128,384]{1,0:T(8,128)(2,1)S(1)}, u32[]{:S(2)}, u32[]{:S(2)}) collective-permute-start(bf16[128,384]{1,0:T(8,128)(2,1)S(1)} %convert_element_type.3), channel_id=1, source_target_pairs={{0,3},{1,0},{2,1},{3,2},{4,7},{5,4},{6,5},{7,6},{8,11},{9,8},{10,9... | collective-permute-start | bytes 294920 | tf_op jit(solution)/shard_map/ppermute | solution.py:878
  9.8 8.3 %collective-permute-start.3 = (bf16[128,384]{1,0:T(8,128)(2,1)S(1)}, bf16[128,384]{1,0:T(8,128)(2,1)S(1)}, u32[]{:S(2)}, u32[]{:S(2)}) collective-permute-start(bf16[128,384]{1,0:T(8,128)(2,1)S(1)} %convert_element_type.3), channel_id=1, source_target_pairs={{0,2},{1,3},{2,0},{3,1},{4,6},{5,7},{6,4},{7,5},{8,10},{9,11},{10,... | collective-permute-start | bytes 294920 | tf_op jit(solution)/shard_map/ppermute | solution.py:878
  9.8 8.3 %collective-permute-start.2 = (bf16[128,384]{1,0:T(8,128)(2,1)S(1)}, bf16[128,384]{1,0:T(8,128)(2,1)}, u32[]{:S(2)}, u32[]{:S(2)}) collective-permute-start(bf16[128,384]{1,0:T(8,128)(2,1)S(1)} %convert_element_type.3), channel_id=1, source_target_pairs={{0,1},{1,2},{2,3},{3,0},{4,5},{5,6},{6,7},{7,4},{8,9},{9,10},{10,1... | collective-permute-start | bytes 294920 | tf_op jit(solution)/shard_map/ppermute | solution.py:878
  11.4 26.5 %copy-start.13 = (f32[512]{0:T(512)S(1)}, f32[512]{0:T(512)}, u32[]{:S(2)}) copy-start(f32[512]{0:T(512)} %param.22) | copy-start | bytes 6148
  11.4 26.5 %copy-start.14 = (f32[512]{0:T(512)S(1)}, f32[512]{0:T(512)}, u32[]{:S(2)}) copy-start(f32[512]{0:T(512)} %param.21) | copy-start | bytes 6148
  19.1 2.0 collective-permute-start.5
  19.2 2.6 %collective-permute-start.6 = (bf16[512,512]{1,0:T(8,128)(2,1)S(1)}, bf16[512,512]{1,0:T(8,128)(2,1)S(1)}, u32[]{:S(2)}, u32[]{:S(2)}) collective-permute-start(bf16[512,512]{1,0:T(8,128)(2,1)S(1)} %collective-permute-done.refs_2_.refs_1_), channel_id=1, source_target_pairs={{0,4},{4,0},{8,12},{12,8},{1,5},{5,1},{9,13},{13,9},{2,6},{6,2},{1... | collective-permute-start | bytes 1572872 | tf_op jit(solution)/shard_map/ppermute | solution.py:869
  19.6 12.0 %collective-permute-start.8 = (bf16[4,128,384]{2,1,0:T(8,128)(2,1)S(1)}, bf16[4,128,384]{2,1,0:T(8,128)(2,1)S(1)}, u32[]{:S(2)}, u32[]{:S(2)}) collective-permute-start(bf16[4,128,384]{2,1,0:T(8,128)(2,1)S(1)} %pad_maximum_fusion.1.refs_0_), channel_id=1, source_target_pairs={{0,8},{4,12},{8,0},{12,4},{1,9},{5,13},{9,1},{13,5},{2,10},{6,14},... | collective-permute-start | bytes 1179656 | tf_op jit(solution)/shard_map/ppermute | solution.py:866
  21.8 9.8 %collective-permute-start.11 = (bf16[576,128]{1,0:T(8,128)(2,1)S(1)}, bf16[576,128]{1,0:T(8,128)(2,1)S(1)}, u32[]{:S(2)}, u32[]{:S(2)}) collective-permute-start(bf16[576,128]{1,0:T(8,128)(2,1)S(1)} %pack.1), channel_id=1, source_target_pairs={{0,3},{1,0},{2,1},{3,2},{4,7},{5,4},{6,5},{7,6},{8,11},{9,8},{10,9... | collective-permute-start | bytes 442376 | tf_op jit(solution)/shard_map/ppermute | solution.py:878
  23.8 14.1 %collective-permute-start.10 = (bf16[576,128]{1,0:T(8,128)(2,1)S(1)}, bf16[576,128]{1,0:T(8,128)(2,1)S(1)}, u32[]{:S(2)}, u32[]{:S(2)}) collective-permute-start(bf16[576,128]{1,0:T(8,128)(2,1)S(1)} %pack.1), channel_id=1, source_target_pairs={{0,2},{1,3},{2,0},{3,1},{4,6},{5,7},{6,4},{7,5},{8,10},{9,11},{10,... | collective-permute-start | bytes 442376 | tf_op jit(solution)/shard_map/ppermute | solution.py:878
  24.3 13.6 %collective-permute-start.9 = (bf16[576,128]{1,0:T(8,128)(2,1)S(1)}, bf16[576,128]{1,0:T(8,128)(2,1)S(1)}, u32[]{:S(2)}, u32[]{:S(2)}) collective-permute-start(bf16[576,128]{1,0:T(8,128)(2,1)S(1)} %pack.1), channel_id=1, source_target_pairs={{0,1},{1,2},{2,3},{3,0},{4,5},{5,6},{6,7},{7,4},{8,9},{9,10},{10,1... | collective-permute-start | bytes 442376 | tf_op jit(solution)/shard_map/ppermute | solution.py:878
  26.4 17.6 %collective-permute-start.1 = (bf16[512,512]{1,0:T(8,128)(2,1)S(1)}, bf16[512,512]{1,0:T(8,128)(2,1)S(1)}, u32[]{:S(2)}, u32[]{:S(2)}) collective-permute-start(bf16[512,512]{1,0:T(8,128)(2,1)S(1)} %dynamic-slice_bitcast_fusion), channel_id=1, source_target_pairs={{0,8},{4,12},{8,0},{12,4},{1,9},{5,13},{9,1},{13,5},{2,10},{6,14},... | collective-permute-start | bytes 1572872 | tf_op jit(solution)/shard_map/ppermute | solution.py:866
  31.6 6.3 %collective-permute-start.7 = (bf16[4,128,384]{2,1,0:T(8,128)(2,1)S(1)}, bf16[4,128,384]{2,1,0:T(8,128)(2,1)S(1)}, u32[]{:S(2)}, u32[]{:S(2)}) collective-permute-start(bf16[4,128,384]{2,1,0:T(8,128)(2,1)S(1)} %pad_maximum_fusion.1.refs_0_), channel_id=1, source_target_pairs={{0,4},{4,0},{8,12},{12,8},{1,5},{5,1},{9,13},{13,9},{2,6},{6,2},{1... | collective-permute-start | bytes 1179656 | tf_op jit(solution)/shard_map/ppermute | solution.py:869
  37.9 1.7 collective-permute-start.12
  44.1 16.8 %collective-permute-start.15 = (bf16[4,576,128]{2,1,0:T(8,128)(2,1)S(1)}, bf16[4,576,128]{2,1,0:T(8,128)(2,1)S(1)}, u32[]{:S(2)}, u32[]{:S(2)}) collective-permute-start(bf16[4,576,128]{2,1,0:T(8,128)(2,1)S(1)} %pad_maximum_fusion.refs_11_), channel_id=1, source_target_pairs={{0,4},{4,0},{8,12},{12,8},{1,5},{5,1},{9,13},{13,9},{2,6},{6,2},{1... | collective-permute-start | bytes 1769480 | tf_op jit(solution)/shard_map/ppermute | solution.py:869
  44.3 16.7 %collective-permute-start.14 = (bf16[4,576,128]{2,1,0:T(8,128)(2,1)S(1)}, bf16[4,576,128]{2,1,0:T(8,128)(2,1)S(1)}, u32[]{:S(2)}, u32[]{:S(2)}) collective-permute-start(bf16[4,576,128]{2,1,0:T(8,128)(2,1)S(1)} %pad_maximum_fusion.refs_11_), channel_id=1, source_target_pairs={{0,8},{4,12},{8,0},{12,4},{16,24},{20,28},{24,16},{28,20},{1,9},{5... | collective-permute-start | bytes 1769480 | tf_op jit(solution)/shard_map/ppermute | solution.py:875
  44.8 16.2 %collective-permute-start.13 = (bf16[4,576,128]{2,1,0:T(8,128)(2,1)S(1)}, bf16[4,576,128]{2,1,0:T(8,128)(2,1)S(1)}, u32[]{:S(2)}, u32[]{:S(2)}) collective-permute-start(bf16[4,576,128]{2,1,0:T(8,128)(2,1)S(1)} %pad_maximum_fusion.refs_11_), channel_id=1, source_target_pairs={{0,16},{4,20},{8,24},{12,28},{16,0},{20,4},{24,8},{28,12},{1,17},{... | collective-permute-start | bytes 1769480 | tf_op jit(solution)/shard_map/ppermute | solution.py:875
  46.3 27.4 %collective-permute-start.19 = (bf16[4,576,128]{2,1,0:T(8,128)(2,1)S(1)}, bf16[4,576,128]{2,1,0:T(8,128)(2,1)S(1)}, u32[]{:S(2)}, u32[]{:S(2)}) collective-permute-start(bf16[4,576,128]{2,1,0:T(8,128)(2,1)S(1)} %pad_maximum_fusion.refs_11_), channel_id=1, source_target_pairs={{0,24},{4,28},{8,16},{12,20},{16,8},{20,12},{24,0},{28,4},{1,25},{... | collective-permute-start | bytes 1769480 | tf_op jit(solution)/shard_map/ppermute | solution.py:875
  73.7 4.4 %collective-permute-start.20 = (bf16[4,576,128]{2,1,0:T(8,128)(2,1)S(1)}, bf16[4,576,128]{2,1,0:T(8,128)(2,1)S(1)}, u32[]{:S(2)}, u32[]{:S(2)}) collective-permute-start(bf16[4,576,128]{2,1,0:T(8,128)(2,1)S(1)} %collective-permute-done.19.refs_17_), channel_id=1, source_target_pairs={{0,4},{4,0},{8,12},{12,8},{1,5},{5,1},{9,13},{13,9},{2,6},{6,2},{1... | collective-permute-start | bytes 1769480 | tf_op jit(solution)/shard_map/ppermute | solution.py:869
  73.7 4.4 %collective-permute-start.17 = (bf16[4,576,128]{2,1,0:T(8,128)(2,1)S(1)}, bf16[4,576,128]{2,1,0:T(8,128)(2,1)S(1)}, u32[]{:S(2)}, u32[]{:S(2)}) collective-permute-start(bf16[4,576,128]{2,1,0:T(8,128)(2,1)S(1)} %collective-permute-done.13.refs_13_), channel_id=1, source_target_pairs={{0,4},{4,0},{8,12},{12,8},{1,5},{5,1},{9,13},{13,9},{2,6},{6,2},{1... | collective-permute-start | bytes 1769480 | tf_op jit(solution)/shard_map/ppermute | solution.py:869
  74.2 3.9 %collective-permute-start.18 = (bf16[4,576,128]{2,1,0:T(8,128)(2,1)S(1)}, bf16[4,576,128]{2,1,0:T(8,128)(2,1)S(1)}, u32[]{:S(2)}, u32[]{:S(2)}) collective-permute-start(bf16[4,576,128]{2,1,0:T(8,128)(2,1)S(1)} %collective-permute-done.14.refs_15_), channel_id=1, source_target_pairs={{0,4},{4,0},{8,12},{12,8},{1,5},{5,1},{9,13},{13,9},{2,6},{6,2},{1... | collective-permute-start | bytes 1769480 | tf_op jit(solution)/shard_map/ppermute | solution.py:869
  74.2 3.9 %collective-permute-start.16 = (bf16[2,2,512,128]{3,2,1,0:T(8,128)(2,1)S(1)}, bf16[2,2,512,128]{3,2,1,0:T(8,128)(2,1)S(1)}, u32[]{:S(2)}, u32[]{:S(2)}) collective-permute-start(bf16[2,2,512,128]{3,2,1,0:T(8,128)(2,1)S(1)} %get-tuple-element.128.refs_3_), channel_id=1, source_target_pairs={{0,4},{4,0},{8,12},{12,8},{1,5},{5,1},{9,13},{13,9},{2,6},{6,2},{1... | collective-permute-start | bytes 1572872 | tf_op jit(solution)/shard_map/ppermute | solution.py:869
  106.4 4.6 %collective-permute-start.21 = (bf16[4,4,576,128]{3,2,1,0:T(8,128)(2,1)S(1)}, bf16[4,4,576,128]{3,2,1,0:T(8,128)(2,1)S(1)}, u32[]{:S(2)}, u32[]{:S(2)}) collective-permute-start(bf16[4,4,576,128]{3,2,1,0:T(8,128)(2,1)S(1)} %get-tuple-element.142), channel_id=1, source_target_pairs={{0,4},{4,0},{8,12},{12,8},{1,5},{5,1},{9,13},{13,9},{2,6},{6,2},{1... | collective-permute-start | bytes 7077896 | tf_op jit(solution)/shard_map/ppermute | solution.py:869
  111.5 3.7 %collective-permute-start.25 = (bf16[2,512,128]{2,1,0:T(8,128)(2,1)S(1)}, bf16[2,512,128]{2,1,0:T(8,128)(2,1)S(1)}, u32[]{:S(2)}, u32[]{:S(2)}) collective-permute-start(bf16[2,512,128]{2,1,0:T(8,128)(2,1)S(1)} %get-tuple-element.152), channel_id=1, source_target_pairs={{0,4},{4,0},{8,12},{12,8},{1,5},{5,1},{9,13},{13,9},{2,6},{6,2},{1... | collective-permute-start | bytes 786440 | tf_op jit(solution)/shard_map/ppermute | solution.py:869
  111.7 28.3 %collective-permute-start.22 = (bf16[4,576,128]{2,1,0:T(8,128)(2,1)S(1)}, bf16[4,576,128]{2,1,0:T(8,128)(2,1)S(1)}, u32[]{:S(2)}, u32[]{:S(2)}) collective-permute-start(bf16[4,576,128]{2,1,0:T(8,128)(2,1)S(1)} %get-tuple-element.144), channel_id=1, source_target_pairs={{0,16},{4,20},{8,24},{12,28},{16,0},{20,4},{24,8},{28,12},{1,17},{... | collective-permute-start | bytes 1769480 | tf_op jit(solution)/shard_map/ppermute | solution.py:875
  113.2 28.3 %collective-permute-start.23 = (bf16[4,576,128]{2,1,0:T(8,128)(2,1)S(1)}, bf16[4,576,128]{2,1,0:T(8,128)(2,1)S(1)}, u32[]{:S(2)}, u32[]{:S(2)}) collective-permute-start(bf16[4,576,128]{2,1,0:T(8,128)(2,1)S(1)} %get-tuple-element.145), channel_id=1, source_target_pairs={{0,8},{4,12},{8,0},{12,4},{16,24},{20,28},{24,16},{28,20},{1,9},{5... | collective-permute-start | bytes 1769480 | tf_op jit(solution)/shard_map/ppermute | solution.py:875
  115.2 26.2 %collective-permute-start.24 = (bf16[4,576,128]{2,1,0:T(8,128)(2,1)S(1)}, bf16[4,576,128]{2,1,0:T(8,128)(2,1)S(1)}, u32[]{:S(2)}, u32[]{:S(2)}) collective-permute-start(bf16[4,576,128]{2,1,0:T(8,128)(2,1)S(1)} %get-tuple-element.146), channel_id=1, source_target_pairs={{0,24},{4,28},{8,16},{12,20},{16,8},{20,12},{24,0},{28,4},{1,25},{... | collective-permute-start | bytes 1769480 | tf_op jit(solution)/shard_map/ppermute | solution.py:875
  141.8 7.0 %collective-permute-start.27 = (bf16[2,512,128]{2,1,0:T(8,128)(2,1)S(1)}, bf16[2,512,128]{2,1,0:T(8,128)(2,1)S(1)}, u32[]{:S(2)}, u32[]{:S(2)}) collective-permute-start(bf16[2,512,128]{2,1,0:T(8,128)(2,1)S(1)} %get-tuple-element.163), channel_id=1, source_target_pairs={{0,4},{4,0},{8,12},{12,8},{1,5},{5,1},{9,13},{13,9},{2,6},{6,2},{1... | collective-permute-start | bytes 786440 | tf_op jit(solution)/shard_map/ppermute | solution.py:869
  141.8 31.7 %collective-permute-start.28 = (bf16[576,128]{1,0:T(8,128)(2,1)S(1)}, bf16[576,128]{1,0:T(8,128)(2,1)S(1)}, u32[]{:S(2)}, u32[]{:S(2)}) collective-permute-start(bf16[576,128]{1,0:T(8,128)(2,1)S(1)} %get-tuple-element.168), channel_id=1, source_target_pairs={{0,1},{1,2},{2,3},{3,0},{4,5},{5,6},{6,7},{7,4},{8,9},{9,10},{10,1... | collective-permute-start | bytes 442376 | tf_op jit(solution)/shard_map/ppermute | solution.py:878
  142.1 31.4 %collective-permute-start.29 = (bf16[576,128]{1,0:T(8,128)(2,1)S(1)}, bf16[576,128]{1,0:T(8,128)(2,1)S(1)}, u32[]{:S(2)}, u32[]{:S(2)}) collective-permute-start(bf16[576,128]{1,0:T(8,128)(2,1)S(1)} %get-tuple-element.169), channel_id=1, source_target_pairs={{0,2},{1,3},{2,0},{3,1},{4,6},{5,7},{6,4},{7,5},{8,10},{9,11},{10,... | collective-permute-start | bytes 442376 | tf_op jit(solution)/shard_map/ppermute | solution.py:878
  144.3 29.2 %collective-permute-start.30 = (bf16[576,128]{1,0:T(8,128)(2,1)S(1)}, bf16[576,128]{1,0:T(8,128)(2,1)S(1)}, u32[]{:S(2)}, u32[]{:S(2)}) collective-permute-start(bf16[576,128]{1,0:T(8,128)(2,1)S(1)} %get-tuple-element.170), channel_id=1, source_target_pairs={{0,3},{1,0},{2,1},{3,2},{4,7},{5,4},{6,5},{7,6},{8,11},{9,8},{10,9... | collective-permute-start | bytes 442376 | tf_op jit(solution)/shard_map/ppermute | solution.py:878
  147.0 26.5 %collective-permute-start.26 = (bf16[512,512]{1,0:T(8,128)(2,1)S(1)}, bf16[512,512]{1,0:T(8,128)(2,1)S(1)}, u32[]{:S(2)}, u32[]{:S(2)}) collective-permute-start(bf16[512,512]{1,0:T(8,128)(2,1)S(1)} %get-tuple-element.158), channel_id=1, source_target_pairs={{0,8},{4,12},{8,0},{12,4},{1,9},{5,13},{9,1},{13,5},{2,10},{6,14},... | collective-permute-start | bytes 1572872 | tf_op jit(solution)/shard_map/ppermute | solution.py:866
  183.0 8.3 %collective-permute-start.32 = (bf16[2,512,512]{2,1,0:T(8,128)(2,1)S(1)}, bf16[2,512,512]{2,1,0:T(8,128)(2,1)S(1)}, u32[]{:S(2)}, u32[]{:S(2)}) collective-permute-start(bf16[2,512,512]{2,1,0:T(8,128)(2,1)S(1)} %get-tuple-element.181), channel_id=1, source_target_pairs={{0,4},{4,0},{8,12},{12,8},{1,5},{5,1},{9,13},{13,9},{2,6},{6,2},{1... | collective-permute-start | bytes 3145736 | tf_op jit(solution)/shard_map/ppermute | solution.py:869
  183.0 3.3 %collective-permute-start.31 = (bf16[1664,128]{1,0:T(8,128)(2,1)S(1)}, bf16[1664,128]{1,0:T(8,128)(2,1)S(1)}, u32[]{:S(2)}, u32[]{:S(2)}) collective-permute-start(bf16[1664,128]{1,0:T(8,128)(2,1)S(1)} %get-tuple-element.176), channel_id=1, source_target_pairs={{0,4},{4,0},{8,12},{12,8},{1,5},{5,1},{9,13},{13,9},{2,6},{6,2},{1... | collective-permute-start | bytes 1277960 | tf_op jit(solution)/shard_map/ppermute | solution.py:869
  187.7 8.7 %collective-permute-start.34 = (bf16[896,128]{1,0:T(8,128)(2,1)}, bf16[896,128]{1,0:T(8,128)(2,1)S(1)}, u32[]{:S(2)}, u32[]{:S(2)}) collective-permute-start(bf16[896,128]{1,0:T(8,128)(2,1)} %get-tuple-element.184), channel_id=1, source_target_pairs={{0,16},{4,20},{8,24},{12,28},{16,0},{20,4},{24,8},{28,12},{1,17},{... | collective-permute-start | bytes 688136 | tf_op jit(solution)/shard_map/ppermute | solution.py:875
  188.3 8.1 %collective-permute-start.35 = (bf16[896,128]{1,0:T(8,128)(2,1)}, bf16[896,128]{1,0:T(8,128)(2,1)S(1)}, u32[]{:S(2)}, u32[]{:S(2)}) collective-permute-start(bf16[896,128]{1,0:T(8,128)(2,1)} %get-tuple-element.185), channel_id=1, source_target_pairs={{0,8},{4,12},{8,0},{12,4},{16,24},{20,28},{24,16},{28,20},{1,9},{5... | collective-permute-start | bytes 688136 | tf_op jit(solution)/shard_map/ppermute | solution.py:875
  189.5 12.9 %collective-permute-start.36 = (bf16[896,128]{1,0:T(8,128)(2,1)}, bf16[896,128]{1,0:T(8,128)(2,1)S(1)}, u32[]{:S(2)}, u32[]{:S(2)}) collective-permute-start(bf16[896,128]{1,0:T(8,128)(2,1)} %get-tuple-element.186), channel_id=1, source_target_pairs={{0,24},{4,28},{8,16},{12,20},{16,8},{20,12},{24,0},{28,4},{1,25},{... | collective-permute-start | bytes 688136 | tf_op jit(solution)/shard_map/ppermute | solution.py:875
  194.0 22.1 %collective-permute-start.33 = (bf16[512,512]{1,0:T(8,128)(2,1)}, bf16[512,512]{1,0:T(8,128)(2,1)}, u32[]{:S(2)}, u32[]{:S(2)}) collective-permute-start(bf16[512,512]{1,0:T(8,128)(2,1)} %get-tuple-element.183), channel_id=1, source_target_pairs={{0,8},{4,12},{8,0},{12,4},{1,9},{5,13},{9,1},{13,5},{2,10},{6,14},... | collective-permute-start | bytes 1572872 | tf_op jit(solution)/shard_map/ppermute | solution.py:866
  195.6 13.1 %collective-permute-start.40 = (bf16[576,128]{1,0:T(8,128)(2,1)}, bf16[576,128]{1,0:T(8,128)(2,1)S(1)}, u32[]{:S(2)}, u32[]{:S(2)}) collective-permute-start(bf16[576,128]{1,0:T(8,128)(2,1)} %get-tuple-element.196.r), channel_id=1, source_target_pairs={{0,16},{4,20},{8,24},{12,28},{16,0},{20,4},{24,8},{28,12},{1,17},{... | collective-permute-start | bytes 442376 | tf_op jit(solution)/shard_map/ppermute | solution.py:875
  202.5 8.0 %collective-permute-start.37 = (bf16[320,128]{1,0:T(8,128)(2,1)S(1)}, bf16[320,128]{1,0:T(8,128)(2,1)S(1)}, u32[]{:S(2)}, u32[]{:S(2)}) collective-permute-start(bf16[320,128]{1,0:T(8,128)(2,1)S(1)} %get-tuple-element.192), channel_id=1, source_target_pairs={{0,1},{1,2},{2,3},{3,0},{4,5},{5,6},{6,7},{7,4},{8,9},{9,10},{10,1... | collective-permute-start | bytes 245768 | tf_op jit(solution)/shard_map/ppermute | solution.py:878
  202.6 8.2 %collective-permute-start.38 = (bf16[320,128]{1,0:T(8,128)(2,1)S(1)}, bf16[320,128]{1,0:T(8,128)(2,1)S(1)}, u32[]{:S(2)}, u32[]{:S(2)}) collective-permute-start(bf16[320,128]{1,0:T(8,128)(2,1)S(1)} %get-tuple-element.193), channel_id=1, source_target_pairs={{0,2},{1,3},{2,0},{3,1},{4,6},{5,7},{6,4},{7,5},{8,10},{9,11},{10,... | collective-permute-start | bytes 245768 | tf_op jit(solution)/shard_map/ppermute | solution.py:878
  202.6 8.1 %collective-permute-start.39 = (bf16[320,128]{1,0:T(8,128)(2,1)S(1)}, bf16[320,128]{1,0:T(8,128)(2,1)S(1)}, u32[]{:S(2)}, u32[]{:S(2)}) collective-permute-start(bf16[320,128]{1,0:T(8,128)(2,1)S(1)} %get-tuple-element.194), channel_id=1, source_target_pairs={{0,3},{1,0},{2,1},{3,2},{4,7},{5,4},{6,5},{7,6},{8,11},{9,8},{10,9... | collective-permute-start | bytes 245768 | tf_op jit(solution)/shard_map/ppermute | solution.py:878
  210.8 4.2 %collective-permute-start.41 = (bf16[192,128]{1,0:T(8,128)(2,1)S(1)}, bf16[192,128]{1,0:T(8,128)(2,1)S(1)}, u32[]{:S(2)}, u32[]{:S(2)}) collective-permute-start(bf16[192,128]{1,0:T(8,128)(2,1)S(1)} %get-tuple-element.202.r), channel_id=1, source_target_pairs={{0,16},{4,20},{8,24},{12,28},{16,0},{20,4},{24,8},{28,12},{1,17},{... | collective-permute-start | bytes 147464 | tf_op jit(solution)/shard_map/ppermute | solution.py:875
  (11 other events, 143.1 us)

commit v5 on v4

--- a/solution.py
+++ b/solution.py
@@ -30,7 +30,7 @@
     return jax.ShapeDtypeStruct(shape, dtype)
 
 
-NEAR = ('core_sum', 'plane_sum', 'arrange', 'plane_sum_qkv', 'line_sum_qkv', 'finish', 'finish_qkv', 'norm_back')
+NEAR = ('core_sum', 'plane_sum', 'arrange', 'plane_sum_qkv', 'line_sum_qkv', 'finish', 'finish_qkv', 'token_back')
 
 
 def near(a):
@@ -119,7 +119,8 @@
 def qkv_kernel(geo, meta, h1, bias, *refs):
     s, g = geo.where(meta)
     HL, D, NP = geo.HL, geo.D, geo.NP
-    outs = refs[-(4 * NP) - 2 : -2] if geo.fast else refs[-(4 * NP) :]
+    no = (3 + geo.G) * NP
+    outs = refs[-no - 2 : -2] if geo.fast else refs[-no:]
     if geo.fast:
         pieces, (wscr, sem) = refs[:4], refs[-2:]
         z = meta[2]
@@ -147,9 +148,12 @@
     def cols(part, p):
         return pl.ds(al(part * D + g * HL + p * PW, 128), PW)
 
-    for p in range(NP):
-        for part in range(3):
-            outs[3 * NP + p][:, part * PW : (part + 1) * PW] = wscr[:, cols(part, p)]
+    for d in range(geo.G):
+        gd = lax.rem(g - d + geo.G, geo.G)
+        for p in range(NP):
+            for part in range(3):
+                at = pl.ds(al(part * D + gd * HL + p * PW, 128), PW)
+                outs[(3 + d) * NP + p][:, part * PW : (part + 1) * PW] = wscr[:, at]
 
     def step(i, carry):
         rows = pl.ds(al(i * 256, 256), 256)
@@ -307,8 +311,8 @@
 def attn_back_kernel(geo, p, meta, doc, segk, segq, q, k, v, *refs):
     G, L, BL = geo.G, geo.L, geo.BL
     lses, mixed, grads = refs[:G], refs[G : 2 * G], refs[2 * G : 3 * G]
-    out = refs[3 * G]
-    qm, gm, kT, dqT, delta, lse, dk, dv = refs[3 * G + 1 :]
+    out, sends = refs[3 * G], refs[3 * G + 1 : 4 * G]
+    qm, gm, kT, dqT, delta, lse, dk, dv = refs[4 * G :]
     s, g = geo.where(meta)
     ends = doc_ends(doc, s)
     scale = HEAD_DIM ** (-0.5)
@@ -380,6 +384,9 @@
         return carry
 
     lax.fori_loop(0, L // TQ, last_step, 0)
+    for d in range(1, G):
+        for e in range(2):
+            sends[d - 1][e] = out[pl.ds(al(geo.block(s, g, e, d) * BL, 256), BL), :]
 
 
 def attend_call(geo, dlist, meta, doc, segs, q, k, v):
@@ -409,7 +416,7 @@
         "attend_back",
         [(meta, SM), (doc, SM), (segs[0], VM), (segs[1], VM), (q, VM), (k, VM), (v, VM)]
         + [(t, VM) for t in (*lses, *mixed, *grads)],
-        [sds((L, 3 * PW), BF)],
+        [sds((L, 3 * PW), BF)] + [sds((2, geo.BL, 3 * PW), BF)] * (geo.G - 1),
         scratch=[
             pltpu.VMEM((2, L, PW), BF),
             pltpu.VMEM((2, L, PW), BF),
@@ -423,7 +430,7 @@
         flops=2 * L * L * PW * 10,
         nbytes=L * PW * 20,
         trans=L * L,
-    )[0]
+    )
 
 
 def gelu_parts(u):
@@ -708,40 +715,25 @@
                 ]
 
 
-def qkv_back_kernel(geo, meta, *refs):
+def token_back_kernel(geo, meta, gain, g_resid, x0, x1, *refs):
     G, BL, NP = geo.G, geo.BL, geo.NP
     s, g = geo.where(meta)
-    gq, w, ghs = refs[:NP], refs[NP : 2 * NP], refs[2 * NP :]
-    for e in range(2):
-        for d in range(G):
-            base = geo.block(s, g, e, d) * BL
-
-            def step(i, carry):
-                rows = pl.ds(al(i * RT, RT), RT)
-                at = pl.ds(al(base + i * RT, RT), RT)
-                gh = nt(gq[0][at, :], w[0][...])
-                for p in range(1, NP):
-                    gh = gh + nt(gq[p][at, :], w[p][...])
-                ghs[d][e, rows, :] = gh.astype(ghs[d].dtype)
-                return carry
-
-            lax.fori_loop(0, BL // RT, step, 0)
-
-
-def last_kernel(geo, meta, gain, g_resid, gh, *refs):
-    G, D, BL = geo.G, geo.D, geo.BL
-    s, _ = geo.where(meta)
-    recv, (x0, x1, out, send) = refs[: G - 1], refs[G - 1 :]
+    gq, recv, w = refs[:NP], refs[NP : G * NP], refs[G * NP : 2 * G * NP]
+    out, send = refs[2 * G * NP :]
     for e in range(2):
         xe = x0 if e == 0 else x1
+        base = geo.block(s, g, e, 0) * BL
 
         def step(i, carry):
             rows = pl.ds(al(i * RT, RT), RT)
             to = pl.ds(al(e * BL + i * RT, RT), RT)
+            at = pl.ds(al(base + i * RT, RT), RT)
+            total = nt(gq[0][at, :], w[0][...])
+            for p in range(1, NP):
+                total = total + nt(gq[p][at, :], w[p][...])
+            for n, r in enumerate(recv):
+                total = total + nt(r[e, rows, :], w[NP + n][...])
             xhat, rstd = normed(xe[rows, :].astype(F32))
-            total = gh[e, rows, :]
-            for r in recv:
-                total = total + r[e, rows, :].astype(F32)
             gx = total * gain[...]
             res = g_resid[to, :] + rstd * (
                 gx
@@ -940,12 +932,13 @@
         functools.partial(qkv_kernel, geo),
         "qkv",
         [(meta, SM), (h1, VM), (bias, VM)] + [(w, wspec) for w in w_qkv],
-        [sds((L, PW), BF)] * (3 * NP) + [sds((D, 3 * PW), BF)] * NP,
+        [sds((L, PW), BF)] * (3 * NP) + [sds((D, 3 * PW), BF)] * (G * NP),
         scratch=[pltpu.VMEM((D, 3 * D), BF), pltpu.SemaphoreType.DMA(())] if geo.fast else [],
         flops=0,
         nbytes=0,
     )
     q, k, v, w_own = (res[n * NP : (n + 1) * NP] for n in range(4))
+    w_all = res[3 * NP :]
     cot0 = pick(cotangent, s)
     if not geo.fast:
         cot1 = swap_half(pick(cotangent, 1 - s))
@@ -1021,6 +1014,9 @@
     def turned(p, dep):
         return [gmix[0][p]] + [turn(after(gmix[d][p], dep), d) for d in range(1, G)]
 
+    def exchanged(p, dep):
+        return [turn(after(made_back[p][G - d], dep), d) for d in range(1, G)]
+
     def step_plane(parts):
         return (parts[0], plane(parts[1], 1, 0), plane(parts[2], 0, 1), plane(parts[3], 1, 1))
 
@@ -1034,19 +1030,21 @@
         sums = add(core_sum_kernel, "core_sum", (packs[0], turn(packs[1], 1)), [sds((4, 576, 128), BF)] * 4)
         a1 = step_plane(sums)
         ghead = [turned(0, sums[0])]
-        gq = [back(0, after(q[0], sums[0]))]
-        q1 = add(plane_sum_kernel, "plane_sum", after(a1, gq[0]), [sds((576, 128), BF)] * 4)
+        made_back = [back(0, after(q[0], sums[0]))]
+        q1 = add(plane_sum_kernel, "plane_sum", after(a1, made_back[0][0]), [sds((576, 128), BF)] * 4)
         b1 = step_line(q1)
         out_recv = swap_half(after(out_send, q1[0]))
         ghead.append(turned(1, q1[0]))
-        gq += [back(1, after(q[1], q1[0]))]
+        made_back += [back(1, after(q[1], q1[0]))]
         packs2_out = [sds((1664, 128), BF)] * 2 + [sds((576, 128), BF)]
     else:
         b1 = ()
         ghead = [turned(p, q[p]) for p in range(NP)]
-        gq = [back(p, q[p]) for p in range(NP)]
+        made_back = [back(p, q[p]) for p in range(NP)]
+        gq_recv = [turn(made_back[p][G - d], d) for d in range(1, G) for p in range(NP)]
         out_recv = swap_half(out_send)
         packs2_out = [sds((D, 3 * D), BF), sds((16, D), F32)]
+    gq = [t[0] for t in made_back]
     packs2 = call(
         functools.partial(wgrad_kernel, geo),
         "wgrad",
@@ -1059,18 +1057,8 @@
     )
     if geo.fast:
         recv2, r1 = turn(packs2[1], 1), packs2[2]
-        gq = list(after(tuple(gq), r1))
-    ghs = call(
-        functools.partial(qkv_back_kernel, geo),
-        "qkv_back",
-        [(meta, SM)] + [(t, VM) for t in (*gq, *w_own)],
-        [sds((2, BL, D), F32)] + [sds((2, BL, D), BF)] * (G - 1),
-        flops=2 * L * D * 3 * HL,
-        nbytes=12 << 20,
-    )
-    gh_recv = [turn(ghs[G - d], d) for d in range(1, G)]
-    if geo.fast:
-        own2, recv2 = after((packs2[0], recv2), ghs[0])
+        gq_recv = exchanged(0, recv2) + exchanged(1, recv2)
+        own2 = packs2[0]
         parts2 = call(
             functools.partial(arrange_kernel, geo),
             "arrange",
@@ -1081,17 +1069,17 @@
         a2 = step_plane(parts2)
         other1 = plane(after(r1, parts2[0]), 1, 0)
 
+        gq = list(after(tuple(gq), parts2[0]))
     tgrad, tgrad_send = call(
-        functools.partial(last_kernel, geo),
-        "norm_back",
-        [(meta, SM), (gain1, VM), (g_resid, VM), (after(ghs[0], parts2[0]) if geo.fast else ghs[0], VM)]
-        + [(r, VM) for r in gh_recv]
-        + [(x0, VM), (x1, VM)],
+        functools.partial(token_back_kernel, geo),
+        "token_back",
+        [(meta, SM), (gain1, VM), (g_resid, VM), (x0, VM), (x1, VM)]
+        + [(t, VM) for t in (*gq, *gq_recv, *w_all)],
         [sds((2, BL, D), BF), sds((BL, D), BF)],
-        flops=T * D * 30,
+        flops=2 * T * D * 3 * D,
         nbytes=8 << 20,
     )
-    tgrad_recv = swap_half(tgrad_send)
+    tgrad = lax.dynamic_update_slice(tgrad, swap_half(tgrad_send)[None], (1 - s, 0, 0))
     if geo.fast:
         q2 = add(plane_sum_qkv_kernel, "plane_sum_qkv", after(a2, tgrad_send), [sds((320, 128), BF)] * 4)
         b2 = step_line(q2)
@@ -1108,7 +1096,7 @@
         (qkv_g,) = call(
             finish_qkv_kernel,
             "finish_qkv",
-            [(meta, SM), (r2, VM), (plane(r2, 1, 0), VM)],
+            [(meta, SM), (r2, VM), (after(plane(r2, 1, 0), tgrad), VM)],
             [sds(qkv_weight.shape, F32)],
             nbytes=1 << 20,
         )
@@ -1122,11 +1110,7 @@
         grads = (reduced(packs2[0]), reduced(packs[2]), reduced(packs[0]), reduced(packs[1]))
         vec = lax.psum(packs2[1], ("dp", "col", "row"))
 
-    def join(own, other):
-        return lax.dynamic_update_slice(own, other[None], (1 - s, 0, 0))
-
     out_pair = jnp.where(s == 0, jnp.stack([out_own, out_recv]), jnp.stack([out_recv, out_own]))
-    tgrad = join(tgrad, tgrad_recv)
     return (
         out_pair,
         tgrad,

time: 219 us -> 215 us (0.982)
  waiting for transfers between devices: 41.9 us -> 39.4 us
    ppermute x14 -> x15, waiting for transfers between devices: 13.9 us -> 12.9 us  [turn(): lax.ppermute(v, 'col', [(i, i // G * G + (i % G + d) % G) for i in range(...]
    pallas_call x18 -> x17, Pallas kernels: 126 us -> 125 us  [call(): pl.pallas_call(kernel, name=name, out_shape=tuple((o for o in outs)), in_...]
  transfers between devices with their start and end apart: 42 -> 43, of which waited for: 17 -> 17; matrix products, arithmetic and copies ran while one was open for 2% -> 3% of each run, Pallas kernels for 40% -> 42%
where the time goes in v5:
time: 215 us
  Pallas kernels  125 us (58%)
  starting transfers between devices  40.1 us (19%)
  waiting for transfers between devices  39.4 us (18%)
  local copies, waits for them, and re-layouts  4.6 us (2%)
  other arithmetic  4.5 us (2%)
    pallas_call x17, Pallas kernels, call(): pl.pallas_call(kernel, name=name, out_shape=tuple((o for o in outs)), in_...  125 us
    ppermute x12, starting transfers between devices, line(): return lax.ppermute(v, 'row', [(i, (i + d) % R) for i in range(R)])  18.9 us
    ppermute x12, waiting for transfers between devices, line(): return lax.ppermute(v, 'row', [(i, (i + d) % R) for i in range(R)])  13.2 us
    ppermute x15, waiting for transfers between devices, turn(): lax.ppermute(v, 'col', [(i, i // G * G + (i % G + d) % G) for i in range(...  12.9 us
    ppermute x11, waiting for transfers between devices, plane(): return lax.ppermute(v, ('dp', 'col'), pairs)  12.3 us
    ppermute x11, starting transfers between devices, plane(): return lax.ppermute(v, ('dp', 'col'), pairs)  12 us
    ppermute x5, starting transfers between devices, swap_half(): return lax.ppermute(v, 'col', [(i, (i + G) % C) for i in range(C)])  6.44 us
  transfers between devices with their start and end apart: 43, of which 17 were waited for; matrix products, arithmetic and copies ran while one was open for 3% of the time, Pallas kernels for 42%

profile of v5, /device:TPU:0, one launch (start us, length us, event | category | flops | bytes accessed | tf_op | source)
XLA Modules:
  0.0 215.2 jit_solution(4785836193950391461)
XLA Ops:
  0.7 1.1 convert_element_type.3
  1.8 1.3 dynamic-slice_bitcast_fusion.2
  3.1 3.1 %collective-permute-start = (bf16[512,512]{1,0:T(8,128)(2,1)S(1)}, bf16[512,512]{1,0:T(8,128)(2,1)S(1)}, u32[]{:S(2)}, u32[]{:S(2)}) collective-permute-start(bf16[512,512]{1,0:T(8,128)(2,1)S(1)} %get-tuple-element.214), channel_id=1, source_target_pairs={{0,8},{4,12},{8,0},{12,4},{1,9},{5,13},{9,1},{13,5},{2,10},{6,14},... | collective-permute-start | bytes 1572872 | tf_op jit(solution)/shard_map/ppermute | solution.py:858
  6.2 3.6 %collective-permute-start.4 = (bf16[128,384]{1,0:T(8,128)(2,1)S(1)}, bf16[128,384]{1,0:T(8,128)(2,1)S(1)}, u32[]{:S(2)}, u32[]{:S(2)}) collective-permute-start(bf16[128,384]{1,0:T(8,128)(2,1)S(1)} %convert_element_type.3), channel_id=1, source_target_pairs={{0,3},{1,0},{2,1},{3,2},{4,7},{5,4},{6,5},{7,6},{8,11},{9,8},{10,9... | collective-permute-start | bytes 294920 | tf_op jit(solution)/shard_map/ppermute | solution.py:870
  9.8 1.0 collective-permute-start.2
  11.4 1.5 collective-permute-done.4
  12.9 5.2 %collective-permute-done.3 = bf16[128,384]{1,0:T(8,128)(2,1)S(1)} collective-permute-done((bf16[128,384]{1,0:T(8,128)(2,1)S(1)}, bf16[128,384]{1,0:T(8,128)(2,1)S(1)}, u32[]{:S(2)}, u32[]{:S(2)}) %collective-permute-start.3) | collective-permute-done | bytes 98336 | tf_op jit(solution)/shard_map/ppermute | solution.py:870
  18.1 1.0 pad_maximum_fusion.1.refs_0_
  21.8 2.0 collective-permute-start.11
  24.3 2.0 collective-permute-start.9
  26.9 3.6 %norm_one.1 = (bf16[2048,512]{1,0:T(8,128)(2,1)S(1)}, s32[2048,128]{1,0:T(8,128)S(1)}, s32[8,2048]{1,0:T(8,128)S(1)}) custom-call(s32[3]{0:T(128)S(1)} %pad_add_fusion.meta, s32[2,8]{1,0:T(2,128)S(1)} %copy-done.6, f32[1,512]{1,0:T(1,128)S(1)} %bitcast.35, f32[1,512]{1,0:T(1,128)S(1)} %bitcast.38, bf16[512,512]{1,0:T(8,128)(2,1)S(1)} %get-tuple-element.118.refs_0_.x0, ...), custom_call_target="tpu_custom_call" | custom-call | flops 10485760 | bytes 4194304 | tf_op jit(solution)/shard_map/norm_one/pallas_call | solution.py:41
  30.6 1.1 collective-permute-done.8.refs_2_
  31.6 6.3 %collective-permute-done.10 = bf16[576,128]{1,0:T(8,128)(2,1)S(1)} collective-permute-done((bf16[576,128]{1,0:T(8,128)(2,1)S(1)}, bf16[576,128]{1,0:T(8,128)(2,1)S(1)}, u32[]{:S(2)}, u32[]{:S(2)}) %collective-permute-start.10) | collective-permute-done | bytes 147488 | tf_op jit(solution)/shard_map/ppermute | solution.py:870
  38.0 1.7 collective-permute-done.12.refs_3_
  39.6 4.5 %qkv.1 = (bf16[2048,128]{1,0:T(8,128)(2,1)S(1)}, bf16[2048,128]{1,0:T(8,128)(2,1)S(1)}, bf16[2048,128]{1,0:T(8,128)(2,1)S(1)}, bf16[2048,128]{1,0:T(8,128)(2,1)S...) custom-call(s32[3]{0:T(128)S(1)} %pad_add_fusion.meta, ...), custom_call_target="tpu_custom_call" | custom-call | tf_op jit(solution)/shard_map/qkv/pallas_call | solution.py:41
  45.0 1.5 collective-permute-start.13
  46.5 1.5 collective-permute-start.19
  48.0 9.4 %attend.2 = (bf16[2,2,512,128]{3,2,1,0:T(8,128)(2,1)S(1)}, f32[2,8,512]{2,1,0:T(8,128)S(1)}) custom-call(s32[3]{0:T(128)S(1)} %pad_add_fusion.meta, s32[2,8]{1,0:T(2,128)S(1)} %copy-done.6, s32[2048,128]{1,0:T(8,128)S(1)} %get-tuple-element.120.segk, s32[8,2048]{1,0:T(8,128)S(1)} %get-tuple-element.121.segq, ...), custom_call_target="tpu_custom_call" | custom-call | flops 4294967296 | bytes 4194304 | tf_op jit(solution)/shard_map/attend/pallas_call | solution.py:41
  57.4 2.7 %collective-permute-done.14.refs_15_ = bf16[4,576,128]{2,1,0:T(8,128)(2,1)S(1)} collective-permute-done((bf16[4,576,128]{2,1,0:T(8,128)(2,1)S(1)}, bf16[4,576,128]{2,1,0:T(8,128)(2,1)S(1)}, u32[]{:S(2)}, u32[]{:S(2)}) %collective-permute-start.14) | collective-permute-done | bytes 589856 | tf_op jit(solution)/shard_map/ppermute | solution.py:867
  60.1 1.1 collective-permute-done.13.refs_13_
  61.3 13.1 %attend.3 = (bf16[2,2,512,128]{3,2,1,0:T(8,128)(2,1)S(1)}, f32[2,8,512]{2,1,0:T(8,128)S(1)}) custom-call(s32[3]{0:T(128)S(1)} %pad_add_fusion.meta, s32[2,8]{1,0:T(2,128)S(1)} %copy-done.6, s32[2048,128]{1,0:T(8,128)S(1)} %get-tuple-element.120.segk, s32[8,2048]{1,0:T(8,128)S(1)} %get-tuple-element.121.segq, ...), custom_call_target="tpu_custom_call" | custom-call | flops 4294967296 | bytes 4194304 | tf_op jit(solution)/shard_map/attend/pallas_call | solution.py:41
  75.6 3.4 %collective-permute-done.16.refs_10_ = bf16[2,2,512,128]{3,2,1,0:T(8,128)(2,1)S(1)} collective-permute-done((bf16[2,2,512,128]{3,2,1,0:T(8,128)(2,1)S(1)}, bf16[2,2,512,128]{3,2,1,0:T(8,128)(2,1)S(1)}, u32[]{:S(2)}, u32[]{:S(2)}) %collective-permute-start.16) | collective-permute-done | bytes 524320 | tf_op jit(solution)/shard_map/ppermute | solution.py:861
  79.0 28.1 %ffn.1 = (bf16[512,512]{1,0:T(8,128)(2,1)S(1)}, bf16[512,512]{1,0:T(8,128)(2,1)S(1)}, f32[1024,512]{1,0:T(8,128)S(1)}, bf16[2,512,128]{2,1,0:T(8,128)(2,1)S(1)},...) custom-call(s32[3]{0:T(128)S(1)} %pad_add_fusion.meta, ...), custom_call_target="tpu_custom_call" | custom-call | flops 14495514624 | bytes 20971520 | tf_op jit(solution)/shard_map/ffn/pallas_call | solution.py:41
  108.1 4.4 %collective-permute-done.21.recv = bf16[4,4,576,128]{3,2,1,0:T(8,128)(2,1)S(1)} collective-permute-done((bf16[4,4,576,128]{3,2,1,0:T(8,128)(2,1)S(1)}, bf16[4,4,576,128]{3,2,1,0:T(8,128)(2,1)S(1)}, u32[]{:S(2)}, u32[]{:S(2)}) %collective-permute-start.21) | collective-permute-done | bytes 2359328 | tf_op jit(solution)/shard_map/ppermute | solution.py:861
  113.2 1.5 collective-permute-start.22
  114.7 1.5 collective-permute-start.23
  116.8 24.8 %attend_back.2 = (bf16[2048,384]{1,0:T(8,128)(2,1)S(1)}, bf16[2,512,384]{2,1,0:T(8,128)(2,1)S(1)}) custom-call(s32[3]{0:T(128)S(1)} %pad_add_fusion.meta, s32[2,8]{1,0:T(2,128)S(1)} %copy-done.6, s32[2048,128]{1,0:T(8,128)S(1)} %get-tuple-element.120.segk, s32[8,2048]{1,0:T(8,128)S(1)} %get-tuple-element.121.segq, ...), custom_call_target="tpu_custom_call" | custom-call | flops 10737418240 | bytes 5242880 | tf_op jit(solution)/shard_map/attend_back/pallas_call | solution.py:41
  141.6 1.1 collective-permute-done.23.c
  143.2 3.0 %collective-permute-start.29 = (bf16[576,128]{1,0:T(8,128)(2,1)S(1)}, bf16[576,128]{1,0:T(8,128)(2,1)S(1)}, u32[]{:S(2)}, u32[]{:S(2)}) collective-permute-start(bf16[576,128]{1,0:T(8,128)(2,1)S(1)} %get-tuple-element.175), channel_id=1, source_target_pairs={{0,2},{1,3},{2,0},{3,1},{4,6},{5,7},{6,4},{7,5},{8,10},{9,11},{10,... | collective-permute-start | bytes 442376 | tf_op jit(solution)/shard_map/ppermute | solution.py:870
  146.2 2.8 %collective-permute-start.30 = (bf16[576,128]{1,0:T(8,128)(2,1)S(1)}, bf16[576,128]{1,0:T(8,128)(2,1)S(1)}, u32[]{:S(2)}, u32[]{:S(2)}) collective-permute-start(bf16[576,128]{1,0:T(8,128)(2,1)S(1)} %get-tuple-element.176), channel_id=1, source_target_pairs={{0,3},{1,0},{2,1},{3,2},{4,7},{5,4},{6,5},{7,6},{8,11},{9,8},{10,9... | collective-permute-start | bytes 442376 | tf_op jit(solution)/shard_map/ppermute | solution.py:870
  149.3 24.8 %attend_back.3 = (bf16[2048,384]{1,0:T(8,128)(2,1)S(1)}, bf16[2,512,384]{2,1,0:T(8,128)(2,1)S(1)}) custom-call(s32[3]{0:T(128)S(1)} %pad_add_fusion.meta, s32[2,8]{1,0:T(2,128)S(1)} %copy-done.6, s32[2048,128]{1,0:T(8,128)S(1)} %copy-done.8, s32[8,2048]{1,0:T(8,128)S(1)} %get-tuple-element.121.segq, bf16[2048,128]{1,0:T(8,128)(2,1)S(1)} %copy-done.10, ...), custom_call_target="tpu_custom_call" | custom-call | flops 10737418240 | bytes 5242880 | tf_op jit(solution)/shard_map/attend_back/pallas_call | solution.py:41
  174.2 5.1 %wgrad.1 = (bf16[1664,128]{1,0:T(8,128)(2,1)S(1)}, bf16[1664,128]{1,0:T(8,128)(2,1)S(1)}, bf16[576,128]{1,0:T(8,128)(2,1)}) custom-call(s32[3]{0:T(128)S(1)} %pad_add_fusion.meta, f32[16,512]{1,0:T(8,128)S(1)} %get-tuple-element.170.vec_in, f32[1,512]{1,0:T(1,128)S(1)} %bitcast.36, f32[1,512]{1,0:T(1,128)S(1)} %bitcast.39, ...), custom_call_target="tpu_custom_call" | custom-call | flops 1610612736 | bytes 8388608 | tf_op jit(solution)/shard_map/wgrad/pallas_call | solution.py:41
  179.3 1.8 collective-permute-done.31.recv
  181.6 1.5 arrange.1
  183.0 1.5 collective-permute-start.35
  184.5 1.5 collective-permute-start.36
  186.0 1.5 collective-permute-start.37
  187.5 4.8 %token_back.1 = (bf16[2,512,512]{2,1,0:T(8,128)(2,1)}, bf16[512,512]{1,0:T(8,128)(2,1)}) custom-call(s32[3]{0:T(128)S(1)} %pad_add_fusion.meta, f32[1,512]{1,0:T(1,128)S(1)} %bitcast.37, f32[1024,512]{1,0:T(8,128)S(1)} %get-tuple-element.164.g_resid, bf16[512,512]{1,0:T(8,128)(2,1)S(1)} %get-tuple-element.118.refs_0_.x0, ...), custom_call_target="tpu_custom_call" | custom-call | flops 1610612736 | bytes 8388608 | tf_op jit(solution)/shard_map/token_back/pallas_call | solution.py:41
  192.3 2.0 collective-permute-start.34
  194.3 2.9 %collective-permute-done.36.c = bf16[896,128]{1,0:T(8,128)(2,1)} collective-permute-done((bf16[896,128]{1,0:T(8,128)(2,1)}, bf16[896,128]{1,0:T(8,128)(2,1)}, u32[]{:S(2)}, u32[]{:S(2)}) %collective-permute-start.36) | collective-permute-done | bytes 229408 | tf_op jit(solution)/shard_map/ppermute | solution.py:867
  197.3 2.0 collective-permute-done.37.d
  199.2 1.2 plane_sum_qkv.1
  200.5 3.7 %collective-permute-start.40 = (bf16[320,128]{1,0:T(8,128)(2,1)S(1)}, bf16[320,128]{1,0:T(8,128)(2,1)S(1)}, u32[]{:S(2)}, u32[]{:S(2)}) collective-permute-start(bf16[320,128]{1,0:T(8,128)(2,1)S(1)} %get-tuple-element.200), channel_id=1, source_target_pairs={{0,3},{1,0},{2,1},{3,2},{4,7},{5,4},{6,5},{7,6},{8,11},{9,8},{10,9... | collective-permute-start | bytes 245768 | tf_op jit(solution)/shard_map/ppermute | solution.py:870
  204.3 2.3 %maximum_select_fusion = bf16[2,512,512]{2,1,0:T(8,128)(2,1)} fusion(bf16[1,512,512]{2,1,0:T(8,128)(2,1)} %bitcast.45, bf16[1,512,512]{2,1,0:T(8,128)(2,1)S(1)} %bitcast.34, pred[]{:T(512)S(6)} %eq.3), kind=kLoop, calls=%fused_computation | loop fusion | flops 1572864 | bytes 2097153 | tf_op jit(solution)/shard_map/jit(_where)/select_n | solution.py:1113
  206.6 1.8 finish.1
  210.4 1.1 bitcast_dynamic-update-slice_fusion
  211.5 2.4 %collective-permute-done.42.o = bf16[192,128]{1,0:T(8,128)(2,1)S(1)} collective-permute-done((bf16[192,128]{1,0:T(8,128)(2,1)S(1)}, bf16[192,128]{1,0:T(8,128)(2,1)S(1)}, u32[]{:S(2)}, u32[]{:S(2)}) %collective-permute-start.42) | collective-permute-done | bytes 49184 | tf_op jit(solution)/shard_map/ppermute | solution.py:867
  214.0 1.2 finish_qkv.1
  (136 shorter events, 12.2 us)
Async XLA Ops:
  3.1 16.1 %collective-permute-start = (bf16[512,512]{1,0:T(8,128)(2,1)S(1)}, bf16[512,512]{1,0:T(8,128)(2,1)S(1)}, u32[]{:S(2)}, u32[]{:S(2)}) collective-permute-start(bf16[512,512]{1,0:T(8,128)(2,1)S(1)} %get-tuple-element.214), channel_id=1, source_target_pairs={{0,8},{4,12},{8,0},{12,4},{1,9},{5,13},{9,1},{13,5},{2,10},{6,14},... | collective-permute-start | bytes 1572872 | tf_op jit(solution)/shard_map/ppermute | solution.py:858
  6.2 6.8 %collective-permute-start.4 = (bf16[128,384]{1,0:T(8,128)(2,1)S(1)}, bf16[128,384]{1,0:T(8,128)(2,1)S(1)}, u32[]{:S(2)}, u32[]{:S(2)}) collective-permute-start(bf16[128,384]{1,0:T(8,128)(2,1)S(1)} %convert_element_type.3), channel_id=1, source_target_pairs={{0,3},{1,0},{2,1},{3,2},{4,7},{5,4},{6,5},{7,6},{8,11},{9,8},{10,9... | collective-permute-start | bytes 294920 | tf_op jit(solution)/shard_map/ppermute | solution.py:870
  9.8 8.3 %collective-permute-start.3 = (bf16[128,384]{1,0:T(8,128)(2,1)S(1)}, bf16[128,384]{1,0:T(8,128)(2,1)S(1)}, u32[]{:S(2)}, u32[]{:S(2)}) collective-permute-start(bf16[128,384]{1,0:T(8,128)(2,1)S(1)} %convert_element_type.3), channel_id=1, source_target_pairs={{0,2},{1,3},{2,0},{3,1},{4,6},{5,7},{6,4},{7,5},{8,10},{9,11},{10,... | collective-permute-start | bytes 294920 | tf_op jit(solution)/shard_map/ppermute | solution.py:870
  9.8 8.3 %collective-permute-start.2 = (bf16[128,384]{1,0:T(8,128)(2,1)S(1)}, bf16[128,384]{1,0:T(8,128)(2,1)}, u32[]{:S(2)}, u32[]{:S(2)}) collective-permute-start(bf16[128,384]{1,0:T(8,128)(2,1)S(1)} %convert_element_type.3), channel_id=1, source_target_pairs={{0,1},{1,2},{2,3},{3,0},{4,5},{5,6},{6,7},{7,4},{8,9},{9,10},{10,1... | collective-permute-start | bytes 294920 | tf_op jit(solution)/shard_map/ppermute | solution.py:870
  11.4 26.5 %copy-start.29 = (f32[512]{0:T(512)S(1)}, f32[512]{0:T(512)}, u32[]{:S(2)}) copy-start(f32[512]{0:T(512)} %param.22) | copy-start | bytes 6148
  19.1 2.0 collective-permute-start.5
  19.2 2.6 %collective-permute-start.6 = (bf16[512,512]{1,0:T(8,128)(2,1)S(1)}, bf16[512,512]{1,0:T(8,128)(2,1)S(1)}, u32[]{:S(2)}, u32[]{:S(2)}) collective-permute-start(bf16[512,512]{1,0:T(8,128)(2,1)S(1)} %collective-permute-done.refs_2_.refs_1_.x1), channel_id=1, source_target_pairs={{0,4},{4,0},{8,12},{12,8},{1,5},{5,1},{9,13},{13,9},{2,6},{6,2},{1... | collective-permute-start | bytes 1572872 | tf_op jit(solution)/shard_map/ppermute | solution.py:861
  19.6 12.0 %collective-permute-start.8 = (bf16[4,128,384]{2,1,0:T(8,128)(2,1)S(1)}, bf16[4,128,384]{2,1,0:T(8,128)(2,1)S(1)}, u32[]{:S(2)}, u32[]{:S(2)}) collective-permute-start(bf16[4,128,384]{2,1,0:T(8,128)(2,1)S(1)} %pad_maximum_fusion.1.refs_0_), channel_id=1, source_target_pairs={{0,8},{4,12},{8,0},{12,4},{1,9},{5,13},{9,1},{13,5},{2,10},{6,14},... | collective-permute-start | bytes 1179656 | tf_op jit(solution)/shard_map/ppermute | solution.py:858
  21.8 9.8 %collective-permute-start.11 = (bf16[576,128]{1,0:T(8,128)(2,1)S(1)}, bf16[576,128]{1,0:T(8,128)(2,1)S(1)}, u32[]{:S(2)}, u32[]{:S(2)}) collective-permute-start(bf16[576,128]{1,0:T(8,128)(2,1)S(1)} %pack.1), channel_id=1, source_target_pairs={{0,3},{1,0},{2,1},{3,2},{4,7},{5,4},{6,5},{7,6},{8,11},{9,8},{10,9... | collective-permute-start | bytes 442376 | tf_op jit(solution)/shard_map/ppermute | solution.py:870
  23.8 14.1 %collective-permute-start.10 = (bf16[576,128]{1,0:T(8,128)(2,1)S(1)}, bf16[576,128]{1,0:T(8,128)(2,1)S(1)}, u32[]{:S(2)}, u32[]{:S(2)}) collective-permute-start(bf16[576,128]{1,0:T(8,128)(2,1)S(1)} %pack.1), channel_id=1, source_target_pairs={{0,2},{1,3},{2,0},{3,1},{4,6},{5,7},{6,4},{7,5},{8,10},{9,11},{10,... | collective-permute-start | bytes 442376 | tf_op jit(solution)/shard_map/ppermute | solution.py:870
  24.3 13.6 %collective-permute-start.9 = (bf16[576,128]{1,0:T(8,128)(2,1)S(1)}, bf16[576,128]{1,0:T(8,128)(2,1)S(1)}, u32[]{:S(2)}, u32[]{:S(2)}) collective-permute-start(bf16[576,128]{1,0:T(8,128)(2,1)S(1)} %pack.1), channel_id=1, source_target_pairs={{0,1},{1,2},{2,3},{3,0},{4,5},{5,6},{6,7},{7,4},{8,9},{9,10},{10,1... | collective-permute-start | bytes 442376 | tf_op jit(solution)/shard_map/ppermute | solution.py:870
  26.4 17.8 %collective-permute-start.1 = (bf16[512,512]{1,0:T(8,128)(2,1)S(1)}, bf16[512,512]{1,0:T(8,128)(2,1)S(1)}, u32[]{:S(2)}, u32[]{:S(2)}) collective-permute-start(bf16[512,512]{1,0:T(8,128)(2,1)S(1)} %dynamic-slice_bitcast_fusion), channel_id=1, source_target_pairs={{0,8},{4,12},{8,0},{12,4},{1,9},{5,13},{9,1},{13,5},{2,10},{6,14},... | collective-permute-start | bytes 1572872 | tf_op jit(solution)/shard_map/ppermute | solution.py:858
  30.5 86.2 %copy-start.7 = (s32[2048,128]{1,0:T(8,128)}, s32[2048,128]{1,0:T(8,128)S(1)}, u32[]{:S(2)}) copy-start(s32[2048,128]{1,0:T(8,128)S(1)} %get-tuple-element.120.segk) | copy-start | bytes 3145732
  31.6 6.3 %collective-permute-start.7 = (bf16[4,128,384]{2,1,0:T(8,128)(2,1)S(1)}, bf16[4,128,384]{2,1,0:T(8,128)(2,1)S(1)}, u32[]{:S(2)}, u32[]{:S(2)}) collective-permute-start(bf16[4,128,384]{2,1,0:T(8,128)(2,1)S(1)} %pad_maximum_fusion.1.refs_0_), channel_id=1, source_target_pairs={{0,4},{4,0},{8,12},{12,8},{1,5},{5,1},{9,13},{13,9},{2,6},{6,2},{1... | collective-permute-start | bytes 1179656 | tf_op jit(solution)/shard_map/ppermute | solution.py:861
  37.9 1.7 collective-permute-start.12
  44.3 13.1 %collective-permute-start.15 = (bf16[4,576,128]{2,1,0:T(8,128)(2,1)S(1)}, bf16[4,576,128]{2,1,0:T(8,128)(2,1)S(1)}, u32[]{:S(2)}, u32[]{:S(2)}) collective-permute-start(bf16[4,576,128]{2,1,0:T(8,128)(2,1)S(1)} %pad_maximum_fusion.refs_11_), channel_id=1, source_target_pairs={{0,4},{4,0},{8,12},{12,8},{1,5},{5,1},{9,13},{13,9},{2,6},{6,2},{1... | collective-permute-start | bytes 1769480 | tf_op jit(solution)/shard_map/ppermute | solution.py:861
  44.5 15.6 %collective-permute-start.14 = (bf16[4,576,128]{2,1,0:T(8,128)(2,1)S(1)}, bf16[4,576,128]{2,1,0:T(8,128)(2,1)S(1)}, u32[]{:S(2)}, u32[]{:S(2)}) collective-permute-start(bf16[4,576,128]{2,1,0:T(8,128)(2,1)S(1)} %pad_maximum_fusion.refs_11_), channel_id=1, source_target_pairs={{0,8},{4,12},{8,0},{12,4},{16,24},{20,28},{24,16},{28,20},{1,9},{5... | collective-permute-start | bytes 1769480 | tf_op jit(solution)/shard_map/ppermute | solution.py:867
  45.0 16.2 %collective-permute-start.13 = (bf16[4,576,128]{2,1,0:T(8,128)(2,1)S(1)}, bf16[4,576,128]{2,1,0:T(8,128)(2,1)S(1)}, u32[]{:S(2)}, u32[]{:S(2)}) collective-permute-start(bf16[4,576,128]{2,1,0:T(8,128)(2,1)S(1)} %pad_maximum_fusion.refs_11_), channel_id=1, source_target_pairs={{0,16},{4,20},{8,24},{12,28},{16,0},{20,4},{24,8},{28,12},{1,17},{... | collective-permute-start | bytes 1769480 | tf_op jit(solution)/shard_map/ppermute | solution.py:867
  46.5 28.0 %collective-permute-start.19 = (bf16[4,576,128]{2,1,0:T(8,128)(2,1)S(1)}, bf16[4,576,128]{2,1,0:T(8,128)(2,1)S(1)}, u32[]{:S(2)}, u32[]{:S(2)}) collective-permute-start(bf16[4,576,128]{2,1,0:T(8,128)(2,1)S(1)} %pad_maximum_fusion.refs_11_), channel_id=1, source_target_pairs={{0,24},{4,28},{8,16},{12,20},{16,8},{20,12},{24,0},{28,4},{1,25},{... | collective-permute-start | bytes 1769480 | tf_op jit(solution)/shard_map/ppermute | solution.py:867
  74.4 32.7 %copy-start.26 = (bf16[2,2,512,128]{3,2,1,0:T(8,128)(2,1)}, bf16[2,2,512,128]{3,2,1,0:T(8,128)(2,1)S(1)}, u32[]{:S(2)}) copy-start(bf16[2,2,512,128]{3,2,1,0:T(8,128)(2,1)S(1)} %get-tuple-element.141.refs_9_.refs_2_) | copy-start | bytes 1572868
  74.5 4.5 %collective-permute-start.20 = (bf16[4,576,128]{2,1,0:T(8,128)(2,1)S(1)}, bf16[4,576,128]{2,1,0:T(8,128)(2,1)S(1)}, u32[]{:S(2)}, u32[]{:S(2)}) collective-permute-start(bf16[4,576,128]{2,1,0:T(8,128)(2,1)S(1)} %collective-permute-done.19.refs_17_), channel_id=1, source_target_pairs={{0,4},{4,0},{8,12},{12,8},{1,5},{5,1},{9,13},{13,9},{2,6},{6,2},{1... | collective-permute-start | bytes 1769480 | tf_op jit(solution)/shard_map/ppermute | solution.py:861
  74.5 4.4 %collective-permute-start.17 = (bf16[4,576,128]{2,1,0:T(8,128)(2,1)S(1)}, bf16[4,576,128]{2,1,0:T(8,128)(2,1)S(1)}, u32[]{:S(2)}, u32[]{:S(2)}) collective-permute-start(bf16[4,576,128]{2,1,0:T(8,128)(2,1)S(1)} %collective-permute-done.13.refs_13_), channel_id=1, source_target_pairs={{0,4},{4,0},{8,12},{12,8},{1,5},{5,1},{9,13},{13,9},{2,6},{6,2},{1... | collective-permute-start | bytes 1769480 | tf_op jit(solution)/shard_map/ppermute | solution.py:861
  75.0 3.9 %collective-permute-start.18 = (bf16[4,576,128]{2,1,0:T(8,128)(2,1)S(1)}, bf16[4,576,128]{2,1,0:T(8,128)(2,1)S(1)}, u32[]{:S(2)}, u32[]{:S(2)}) collective-permute-start(bf16[4,576,128]{2,1,0:T(8,128)(2,1)S(1)} %collective-permute-done.14.refs_15_), channel_id=1, source_target_pairs={{0,4},{4,0},{8,12},{12,8},{1,5},{5,1},{9,13},{13,9},{2,6},{6,2},{1... | collective-permute-start | bytes 1769480 | tf_op jit(solution)/shard_map/ppermute | solution.py:861
  75.1 3.9 %collective-permute-start.16 = (bf16[2,2,512,128]{3,2,1,0:T(8,128)(2,1)S(1)}, bf16[2,2,512,128]{3,2,1,0:T(8,128)(2,1)S(1)}, u32[]{:S(2)}, u32[]{:S(2)}) collective-permute-start(bf16[2,2,512,128]{3,2,1,0:T(8,128)(2,1)S(1)} %get-tuple-element.132.refs_3_), channel_id=1, source_target_pairs={{0,4},{4,0},{8,12},{12,8},{1,5},{5,1},{9,13},{13,9},{2,6},{6,2},{1... | collective-permute-start | bytes 1572872 | tf_op jit(solution)/shard_map/ppermute | solution.py:861
  108.0 4.5 %collective-permute-start.21 = (bf16[4,4,576,128]{3,2,1,0:T(8,128)(2,1)S(1)}, bf16[4,4,576,128]{3,2,1,0:T(8,128)(2,1)S(1)}, u32[]{:S(2)}, u32[]{:S(2)}) collective-permute-start(bf16[4,4,576,128]{3,2,1,0:T(8,128)(2,1)S(1)} %get-tuple-element.146), channel_id=1, source_target_pairs={{0,4},{4,0},{8,12},{12,8},{1,5},{5,1},{9,13},{13,9},{2,6},{6,2},{1... | collective-permute-start | bytes 7077896 | tf_op jit(solution)/shard_map/ppermute | solution.py:861
  113.0 3.7 %collective-permute-start.25 = (bf16[2,512,128]{2,1,0:T(8,128)(2,1)S(1)}, bf16[2,512,128]{2,1,0:T(8,128)(2,1)S(1)}, u32[]{:S(2)}, u32[]{:S(2)}) collective-permute-start(bf16[2,512,128]{2,1,0:T(8,128)(2,1)S(1)} %get-tuple-element.156), channel_id=1, source_target_pairs={{0,4},{4,0},{8,12},{12,8},{1,5},{5,1},{9,13},{13,9},{2,6},{6,2},{1... | collective-permute-start | bytes 786440 | tf_op jit(solution)/shard_map/ppermute | solution.py:861
  113.2 28.4 %collective-permute-start.22 = (bf16[4,576,128]{2,1,0:T(8,128)(2,1)S(1)}, bf16[4,576,128]{2,1,0:T(8,128)(2,1)S(1)}, u32[]{:S(2)}, u32[]{:S(2)}) collective-permute-start(bf16[4,576,128]{2,1,0:T(8,128)(2,1)S(1)} %get-tuple-element.148), channel_id=1, source_target_pairs={{0,16},{4,20},{8,24},{12,28},{16,0},{20,4},{24,8},{28,12},{1,17},{... | collective-permute-start | bytes 1769480 | tf_op jit(solution)/shard_map/ppermute | solution.py:867
  114.7 28.0 %collective-permute-start.23 = (bf16[4,576,128]{2,1,0:T(8,128)(2,1)S(1)}, bf16[4,576,128]{2,1,0:T(8,128)(2,1)S(1)}, u32[]{:S(2)}, u32[]{:S(2)}) collective-permute-start(bf16[4,576,128]{2,1,0:T(8,128)(2,1)S(1)} %get-tuple-element.149), channel_id=1, source_target_pairs={{0,8},{4,12},{8,0},{12,4},{16,24},{20,28},{24,16},{28,20},{1,9},{5... | collective-permute-start | bytes 1769480 | tf_op jit(solution)/shard_map/ppermute | solution.py:867
  116.3 26.5 %collective-permute-start.24 = (bf16[4,576,128]{2,1,0:T(8,128)(2,1)S(1)}, bf16[4,576,128]{2,1,0:T(8,128)(2,1)S(1)}, u32[]{:S(2)}, u32[]{:S(2)}) collective-permute-start(bf16[4,576,128]{2,1,0:T(8,128)(2,1)S(1)} %get-tuple-element.150), channel_id=1, source_target_pairs={{0,24},{4,28},{8,16},{12,20},{16,8},{20,12},{24,0},{28,4},{1,25},{... | collective-permute-start | bytes 1769480 | tf_op jit(solution)/shard_map/ppermute | solution.py:867
  116.8 32.2 %copy-start.20 = (bf16[512,512]{1,0:T(8,128)(2,1)S(1)}, bf16[512,512]{1,0:T(8,128)(2,1)}, u32[]{:S(2)}) copy-start(bf16[512,512]{1,0:T(8,128)(2,1)} %copy-done.19) | copy-start | bytes 1572868
  116.8 32.5 %copy-start.14 = (bf16[2048,128]{1,0:T(8,128)(2,1)S(1)}, bf16[2048,128]{1,0:T(8,128)(2,1)}, u32[]{:S(2)}) copy-start(bf16[2048,128]{1,0:T(8,128)(2,1)} %copy-done.13) | copy-start | bytes 1572868
  143.0 6.3 %collective-permute-start.27 = (bf16[2,512,128]{2,1,0:T(8,128)(2,1)S(1)}, bf16[2,512,128]{2,1,0:T(8,128)(2,1)S(1)}, u32[]{:S(2)}, u32[]{:S(2)}) collective-permute-start(bf16[2,512,128]{2,1,0:T(8,128)(2,1)S(1)} %get-tuple-element.168), channel_id=1, source_target_pairs={{0,4},{4,0},{8,12},{12,8},{1,5},{5,1},{9,13},{13,9},{2,6},{6,2},{1... | collective-permute-start | bytes 786440 | tf_op jit(solution)/shard_map/ppermute | solution.py:861
  143.1 31.0 %collective-permute-start.28 = (bf16[576,128]{1,0:T(8,128)(2,1)S(1)}, bf16[576,128]{1,0:T(8,128)(2,1)S(1)}, u32[]{:S(2)}, u32[]{:S(2)}) collective-permute-start(bf16[576,128]{1,0:T(8,128)(2,1)S(1)} %get-tuple-element.174), channel_id=1, source_target_pairs={{0,1},{1,2},{2,3},{3,0},{4,5},{5,6},{6,7},{7,4},{8,9},{9,10},{10,1... | collective-permute-start | bytes 442376 | tf_op jit(solution)/shard_map/ppermute | solution.py:870
  143.2 31.0 %collective-permute-start.29 = (bf16[576,128]{1,0:T(8,128)(2,1)S(1)}, bf16[576,128]{1,0:T(8,128)(2,1)S(1)}, u32[]{:S(2)}, u32[]{:S(2)}) collective-permute-start(bf16[576,128]{1,0:T(8,128)(2,1)S(1)} %get-tuple-element.175), channel_id=1, source_target_pairs={{0,2},{1,3},{2,0},{3,1},{4,6},{5,7},{6,4},{7,5},{8,10},{9,11},{10,... | collective-permute-start | bytes 442376 | tf_op jit(solution)/shard_map/ppermute | solution.py:870
  146.2 28.0 %collective-permute-start.30 = (bf16[576,128]{1,0:T(8,128)(2,1)S(1)}, bf16[576,128]{1,0:T(8,128)(2,1)S(1)}, u32[]{:S(2)}, u32[]{:S(2)}) collective-permute-start(bf16[576,128]{1,0:T(8,128)(2,1)S(1)} %get-tuple-element.176), channel_id=1, source_target_pairs={{0,3},{1,0},{2,1},{3,2},{4,7},{5,4},{6,5},{7,6},{8,11},{9,8},{10,9... | collective-permute-start | bytes 442376 | tf_op jit(solution)/shard_map/ppermute | solution.py:870
  149.0 25.1 %collective-permute-start.26 = (bf16[512,512]{1,0:T(8,128)(2,1)S(1)}, bf16[512,512]{1,0:T(8,128)(2,1)S(1)}, u32[]{:S(2)}, u32[]{:S(2)}) collective-permute-start(bf16[512,512]{1,0:T(8,128)(2,1)S(1)} %copy-done.20), channel_id=1, source_target_pairs={{0,8},{4,12},{8,0},{12,4},{1,9},{5,13},{9,1},{13,5},{2,10},{6,14},... | collective-permute-start | bytes 1572872 | tf_op jit(solution)/shard_map/ppermute | solution.py:858
  179.3 1.8 collective-permute-start.31
  181.1 6.4 %collective-permute-start.32 = (bf16[2,512,384]{2,1,0:T(8,128)(2,1)S(1)}, bf16[2,512,384]{2,1,0:T(8,128)(2,1)S(1)}, u32[]{:S(2)}, u32[]{:S(2)}) collective-permute-start(bf16[2,512,384]{2,1,0:T(8,128)(2,1)S(1)} %get-tuple-element.183), channel_id=1, source_target_pairs={{0,4},{4,0},{8,12},{12,8},{1,5},{5,1},{9,13},{13,9},{2,6},{6,2},{1... | collective-permute-start | bytes 2359304 | tf_op jit(solution)/shard_map/ppermute | solution.py:861
  181.2 6.3 %collective-permute-start.33 = (bf16[2,512,384]{2,1,0:T(8,128)(2,1)S(1)}, bf16[2,512,384]{2,1,0:T(8,128)(2,1)S(1)}, u32[]{:S(2)}, u32[]{:S(2)}) collective-permute-start(bf16[2,512,384]{2,1,0:T(8,128)(2,1)S(1)} %get-tuple-element.185), channel_id=1, source_target_pairs={{0,4},{4,0},{8,12},{12,8},{1,5},{5,1},{9,13},{13,9},{2,6},{6,2},{1... | collective-permute-start | bytes 2359304 | tf_op jit(solution)/shard_map/ppermute | solution.py:861
  183.0 11.3 %collective-permute-start.35 = (bf16[896,128]{1,0:T(8,128)(2,1)}, bf16[896,128]{1,0:T(8,128)(2,1)S(1)}, u32[]{:S(2)}, u32[]{:S(2)}) collective-permute-start(bf16[896,128]{1,0:T(8,128)(2,1)} %get-tuple-element.190), channel_id=1, source_target_pairs={{0,16},{4,20},{8,24},{12,28},{16,0},{20,4},{24,8},{28,12},{1,17},{... | collective-permute-start | bytes 688136 | tf_op jit(solution)/shard_map/ppermute | solution.py:867
  184.5 12.8 %collective-permute-start.36 = (bf16[896,128]{1,0:T(8,128)(2,1)}, bf16[896,128]{1,0:T(8,128)(2,1)}, u32[]{:S(2)}, u32[]{:S(2)}) collective-permute-start(bf16[896,128]{1,0:T(8,128)(2,1)} %get-tuple-element.191), channel_id=1, source_target_pairs={{0,8},{4,12},{8,0},{12,4},{16,24},{20,28},{24,16},{28,20},{1,9},{5... | collective-permute-start | bytes 688136 | tf_op jit(solution)/shard_map/ppermute | solution.py:867
  186.0 13.2 %collective-permute-start.37 = (bf16[896,128]{1,0:T(8,128)(2,1)}, bf16[896,128]{1,0:T(8,128)(2,1)}, u32[]{:S(2)}, u32[]{:S(2)}) collective-permute-start(bf16[896,128]{1,0:T(8,128)(2,1)} %get-tuple-element.192), channel_id=1, source_target_pairs={{0,24},{4,28},{8,16},{12,20},{16,8},{20,12},{24,0},{28,4},{1,25},{... | collective-permute-start | bytes 688136 | tf_op jit(solution)/shard_map/ppermute | solution.py:867
  192.3 18.1 %collective-permute-start.34 = (bf16[512,512]{1,0:T(8,128)(2,1)}, bf16[512,512]{1,0:T(8,128)(2,1)}, u32[]{:S(2)}, u32[]{:S(2)}) collective-permute-start(bf16[512,512]{1,0:T(8,128)(2,1)} %get-tuple-element.189), channel_id=1, source_target_pairs={{0,8},{4,12},{8,0},{12,4},{1,9},{5,13},{9,1},{13,5},{2,10},{6,14},... | collective-permute-start | bytes 1572872 | tf_op jit(solution)/shard_map/ppermute | solution.py:858
  194.3 12.3 %collective-permute-start.41 = (bf16[576,128]{1,0:T(8,128)(2,1)}, bf16[576,128]{1,0:T(8,128)(2,1)S(1)}, u32[]{:S(2)}, u32[]{:S(2)}) collective-permute-start(bf16[576,128]{1,0:T(8,128)(2,1)} %get-tuple-element.203.r), channel_id=1, source_target_pairs={{0,16},{4,20},{8,24},{12,28},{16,0},{20,4},{24,8},{28,12},{1,17},{... | collective-permute-start | bytes 442376 | tf_op jit(solution)/shard_map/ppermute | solution.py:867
  200.4 8.0 %collective-permute-start.38 = (bf16[320,128]{1,0:T(8,128)(2,1)S(1)}, bf16[320,128]{1,0:T(8,128)(2,1)S(1)}, u32[]{:S(2)}, u32[]{:S(2)}) collective-permute-start(bf16[320,128]{1,0:T(8,128)(2,1)S(1)} %get-tuple-element.198), channel_id=1, source_target_pairs={{0,1},{1,2},{2,3},{3,0},{4,5},{5,6},{6,7},{7,4},{8,9},{9,10},{10,1... | collective-permute-start | bytes 245768 | tf_op jit(solution)/shard_map/ppermute | solution.py:870
  200.4 8.2 %collective-permute-start.39 = (bf16[320,128]{1,0:T(8,128)(2,1)S(1)}, bf16[320,128]{1,0:T(8,128)(2,1)S(1)}, u32[]{:S(2)}, u32[]{:S(2)}) collective-permute-start(bf16[320,128]{1,0:T(8,128)(2,1)S(1)} %get-tuple-element.199), channel_id=1, source_target_pairs={{0,2},{1,3},{2,0},{3,1},{4,6},{5,7},{6,4},{7,5},{8,10},{9,11},{10,... | collective-permute-start | bytes 245768 | tf_op jit(solution)/shard_map/ppermute | solution.py:870
  200.5 8.1 %collective-permute-start.40 = (bf16[320,128]{1,0:T(8,128)(2,1)S(1)}, bf16[320,128]{1,0:T(8,128)(2,1)S(1)}, u32[]{:S(2)}, u32[]{:S(2)}) collective-permute-start(bf16[320,128]{1,0:T(8,128)(2,1)S(1)} %get-tuple-element.200), channel_id=1, source_target_pairs={{0,3},{1,0},{2,1},{3,2},{4,7},{5,4},{6,5},{7,6},{8,11},{9,8},{10,9... | collective-permute-start | bytes 245768 | tf_op jit(solution)/shard_map/ppermute | solution.py:870
  209.9 4.1 %collective-permute-start.42 = (bf16[192,128]{1,0:T(8,128)(2,1)S(1)}, bf16[192,128]{1,0:T(8,128)(2,1)S(1)}, u32[]{:S(2)}, u32[]{:S(2)}) collective-permute-start(bf16[192,128]{1,0:T(8,128)(2,1)S(1)} %get-tuple-element.209.r), channel_id=1, source_target_pairs={{0,16},{4,20},{8,24},{12,28},{16,0},{20,4},{24,8},{28,12},{1,17},{... | collective-permute-start | bytes 147464 | tf_op jit(solution)/shard_map/ppermute | solution.py:867
  (28 other events, 393.9 us)

commit v6 on v5

--- a/solution.py
+++ b/solution.py
@@ -21,6 +21,7 @@
 TQ = 256
 TK = 256
 FC = 512
+FT = 1024
 RT = 256
 KEEP_LB = ((0, 1, 4), (1, 4, 5))
 SEND_LB = ((2, 3, 5), (0, 2, 3))
@@ -532,12 +533,14 @@
             for cpy in group:
                 cpy.wait()
 
+    ft = FT if T % FT == 0 else RT
+
     def chunk(f, carry):
         f0 = al(f * FC, FC)
         fs = pl.ds(f0, FC)
 
         def rows_step(i, hs):
-            rows = pl.ds(al(i * RT, RT), RT)
+            rows = pl.ds(al(i * ft, ft), ft)
             u = nn(h2[rows, :], wu[:, fs]) + upb[:, fs]
             phi, pdf = gelu_parts(u)
             act = (u * phi).astype(BF)
@@ -548,7 +551,7 @@
             gh2[rows, :] += nt(gu, wu[:, fs])
             return hs + jnp.sum(gu.astype(F32), axis=0, keepdims=True)
 
-        hsum = lax.fori_loop(0, T // RT, rows_step, jnp.zeros((1, FC), F32))
+        hsum = lax.fori_loop(0, T // ft, rows_step, jnp.zeros((1, FC), F32))
         per = D // FC
         vec[pl.ds(8 + f // per, 1), pl.ds(al(lax.rem(f, per) * FC, 128), FC)] = hsum
         dn = tn(act_s[...], ga_s[...])

time: 215 us -> 211 us (0.981)
  Pallas kernels: 125 us -> 122 us
    pallas_call x17, Pallas kernels: 125 us -> 122 us  [call(): pl.pallas_call(kernel, name=name, out_shape=tuple((o for o in outs)), in_...]
    ppermute x11, waiting for transfers between devices: 12.3 us -> 9.97 us  [plane(): return lax.ppermute(v, ('dp', 'col'), pairs)]
  transfers between devices with their start and end apart: 43 -> 43, of which waited for: 17 -> 16; matrix products, arithmetic and copies ran while one was open for 3% -> 3% of each run, Pallas kernels for 42% -> 43%
where the time goes in v6:
time: 211 us; the launch traced here: 210 us
  Pallas kernels  122 us (58%)
  starting transfers between devices  40.7 us (19%)
  waiting for transfers between devices  37.3 us (18%)
  local copies, waits for them, and re-layouts  4.6 us (2%)
  other arithmetic  4.5 us (2%)
    pallas_call x17, Pallas kernels, call(): pl.pallas_call(kernel, name=name, out_shape=tuple((o for o in outs)), in_...  122 us
    ppermute x12, starting transfers between devices, line(): return lax.ppermute(v, 'row', [(i, (i + d) % R) for i in range(R)])  20 us
    ppermute x12, waiting for transfers between devices, line(): return lax.ppermute(v, 'row', [(i, (i + d) % R) for i in range(R)])  13.3 us
    ppermute x11, starting transfers between devices, plane(): return lax.ppermute(v, ('dp', 'col'), pairs)  13 us
    ppermute x15, waiting for transfers between devices, turn(): lax.ppermute(v, 'col', [(i, i // G * G + (i % G + d) % G) for i in range(...  12.9 us
    ppermute x11, waiting for transfers between devices, plane(): return lax.ppermute(v, ('dp', 'col'), pairs)  9.97 us
    ppermute x5, starting transfers between devices, swap_half(): return lax.ppermute(v, 'col', [(i, (i + G) % C) for i in range(C)])  5.02 us
  transfers between devices with their start and end apart: 43, of which 16 were waited for; matrix products, arithmetic and copies ran while one was open for 3% of the time, Pallas kernels for 43%

profile of v6, /device:TPU:0, one launch (start us, length us, event | category | flops | bytes accessed | tf_op | source)
XLA Modules:
  0.0 210.4 jit_solution(15237426182558580628)
XLA Ops:
  0.7 1.1 convert_element_type.3
  1.8 1.3 dynamic-slice_bitcast_fusion.2
  3.1 3.1 %collective-permute-start = (bf16[512,512]{1,0:T(8,128)(2,1)S(1)}, bf16[512,512]{1,0:T(8,128)(2,1)S(1)}, u32[]{:S(2)}, u32[]{:S(2)}) collective-permute-start(bf16[512,512]{1,0:T(8,128)(2,1)S(1)} %get-tuple-element.214), channel_id=1, source_target_pairs={{0,8},{4,12},{8,0},{12,4},{1,9},{5,13},{9,1},{13,5},{2,10},{6,14},... | collective-permute-start | bytes 1572872 | tf_op jit(solution)/shard_map/ppermute | solution.py:861
  6.2 3.6 %collective-permute-start.4 = (bf16[128,384]{1,0:T(8,128)(2,1)S(1)}, bf16[128,384]{1,0:T(8,128)(2,1)S(1)}, u32[]{:S(2)}, u32[]{:S(2)}) collective-permute-start(bf16[128,384]{1,0:T(8,128)(2,1)S(1)} %convert_element_type.3), channel_id=1, source_target_pairs={{0,3},{1,0},{2,1},{3,2},{4,7},{5,4},{6,5},{7,6},{8,11},{9,8},{10,9... | collective-permute-start | bytes 294920 | tf_op jit(solution)/shard_map/ppermute | solution.py:873
  9.8 1.0 collective-permute-start.2
  11.4 1.5 collective-permute-done.4
  12.9 5.2 %collective-permute-done.3 = bf16[128,384]{1,0:T(8,128)(2,1)S(1)} collective-permute-done((bf16[128,384]{1,0:T(8,128)(2,1)S(1)}, bf16[128,384]{1,0:T(8,128)(2,1)S(1)}, u32[]{:S(2)}, u32[]{:S(2)}) %collective-permute-start.3) | collective-permute-done | bytes 98336 | tf_op jit(solution)/shard_map/ppermute | solution.py:873
  18.1 1.0 pad_maximum_fusion.1.refs_0_
  20.1 0.9 collective-permute-done.5.refs_1_
  21.8 2.0 collective-permute-start.11
  24.3 2.0 collective-permute-start.9
  26.9 3.6 %norm_one.1 = (bf16[2048,512]{1,0:T(8,128)(2,1)S(1)}, s32[2048,128]{1,0:T(8,128)S(1)}, s32[8,2048]{1,0:T(8,128)S(1)}) custom-call(s32[3]{0:T(128)S(1)} %pad_add_fusion.meta, s32[2,8]{1,0:T(2,128)S(1)} %copy-done.6, f32[1,512]{1,0:T(1,128)S(1)} %bitcast.35, f32[1,512]{1,0:T(1,128)S(1)} %bitcast.38, bf16[512,512]{1,0:T(8,128)(2,1)S(1)} %get-tuple-element.118.refs_0_.x0, ...), custom_call_target="tpu_custom_call" | custom-call | flops 10485760 | bytes 4194304 | tf_op jit(solution)/shard_map/norm_one/pallas_call | solution.py:42
  30.6 1.1 collective-permute-done.8.refs_2_
  31.6 6.3 %collective-permute-done.10 = bf16[576,128]{1,0:T(8,128)(2,1)S(1)} collective-permute-done((bf16[576,128]{1,0:T(8,128)(2,1)S(1)}, bf16[576,128]{1,0:T(8,128)(2,1)S(1)}, u32[]{:S(2)}, u32[]{:S(2)}) %collective-permute-start.10) | collective-permute-done | bytes 147488 | tf_op jit(solution)/shard_map/ppermute | solution.py:873
  38.0 1.7 collective-permute-done.12.refs_3_
  39.6 4.5 %qkv.1 = (bf16[2048,128]{1,0:T(8,128)(2,1)S(1)}, bf16[2048,128]{1,0:T(8,128)(2,1)S(1)}, bf16[2048,128]{1,0:T(8,128)(2,1)S(1)}, bf16[2048,128]{1,0:T(8,128)(2,1)S...) custom-call(s32[3]{0:T(128)S(1)} %pad_add_fusion.meta, ...), custom_call_target="tpu_custom_call" | custom-call | tf_op jit(solution)/shard_map/qkv/pallas_call | solution.py:42
  45.0 1.5 collective-permute-start.13
  46.5 1.5 collective-permute-start.19
  48.0 9.4 %attend.2 = (bf16[2,2,512,128]{3,2,1,0:T(8,128)(2,1)S(1)}, f32[2,8,512]{2,1,0:T(8,128)S(1)}) custom-call(s32[3]{0:T(128)S(1)} %pad_add_fusion.meta, s32[2,8]{1,0:T(2,128)S(1)} %copy-done.6, s32[2048,128]{1,0:T(8,128)S(1)} %get-tuple-element.120.segk, s32[8,2048]{1,0:T(8,128)S(1)} %get-tuple-element.121.segq, ...), custom_call_target="tpu_custom_call" | custom-call | flops 4294967296 | bytes 4194304 | tf_op jit(solution)/shard_map/attend/pallas_call | solution.py:42
  57.4 2.7 %collective-permute-done.14.refs_15_ = bf16[4,576,128]{2,1,0:T(8,128)(2,1)S(1)} collective-permute-done((bf16[4,576,128]{2,1,0:T(8,128)(2,1)S(1)}, bf16[4,576,128]{2,1,0:T(8,128)(2,1)S(1)}, u32[]{:S(2)}, u32[]{:S(2)}) %collective-permute-start.14) | collective-permute-done | bytes 589856 | tf_op jit(solution)/shard_map/ppermute | solution.py:870
  60.1 1.1 collective-permute-done.13.refs_13_
  61.3 13.2 %attend.3 = (bf16[2,2,512,128]{3,2,1,0:T(8,128)(2,1)S(1)}, f32[2,8,512]{2,1,0:T(8,128)S(1)}) custom-call(s32[3]{0:T(128)S(1)} %pad_add_fusion.meta, s32[2,8]{1,0:T(2,128)S(1)} %copy-done.6, s32[2048,128]{1,0:T(8,128)S(1)} %get-tuple-element.120.segk, s32[8,2048]{1,0:T(8,128)S(1)} %get-tuple-element.121.segq, ...), custom_call_target="tpu_custom_call" | custom-call | flops 4294967296 | bytes 4194304 | tf_op jit(solution)/shard_map/attend/pallas_call | solution.py:42
  75.6 3.4 %collective-permute-done.16.refs_10_ = bf16[2,2,512,128]{3,2,1,0:T(8,128)(2,1)S(1)} collective-permute-done((bf16[2,2,512,128]{3,2,1,0:T(8,128)(2,1)S(1)}, bf16[2,2,512,128]{3,2,1,0:T(8,128)(2,1)S(1)}, u32[]{:S(2)}, u32[]{:S(2)}) %collective-permute-start.16) | collective-permute-done | bytes 524320 | tf_op jit(solution)/shard_map/ppermute | solution.py:864
  79.0 24.5 %ffn.1 = (bf16[512,512]{1,0:T(8,128)(2,1)S(1)}, bf16[512,512]{1,0:T(8,128)(2,1)S(1)}, f32[1024,512]{1,0:T(8,128)S(1)}, bf16[2,512,128]{2,1,0:T(8,128)(2,1)S(1)},...) custom-call(s32[3]{0:T(128)S(1)} %pad_add_fusion.meta, ...), custom_call_target="tpu_custom_call" | custom-call | flops 14495514624 | bytes 20971520 | tf_op jit(solution)/shard_map/ffn/pallas_call | solution.py:42
  104.4 4.4 %collective-permute-done.21.recv = bf16[4,4,576,128]{3,2,1,0:T(8,128)(2,1)S(1)} collective-permute-done((bf16[4,4,576,128]{3,2,1,0:T(8,128)(2,1)S(1)}, bf16[4,4,576,128]{3,2,1,0:T(8,128)(2,1)S(1)}, u32[]{:S(2)}, u32[]{:S(2)}) %collective-permute-start.21) | collective-permute-done | bytes 2359328 | tf_op jit(solution)/shard_map/ppermute | solution.py:864
  111.0 2.1 %collective-permute-start.24 = (bf16[4,576,128]{2,1,0:T(8,128)(2,1)S(1)}, bf16[4,576,128]{2,1,0:T(8,128)(2,1)S(1)}, u32[]{:S(2)}, u32[]{:S(2)}) collective-permute-start(bf16[4,576,128]{2,1,0:T(8,128)(2,1)S(1)} %get-tuple-element.150), channel_id=1, source_target_pairs={{0,24},{4,28},{8,16},{12,20},{16,8},{20,12},{24,0},{28,4},{1,25},{... | collective-permute-start | bytes 1769480 | tf_op jit(solution)/shard_map/ppermute | solution.py:870
  113.2 24.8 %attend_back.2 = (bf16[2048,384]{1,0:T(8,128)(2,1)S(1)}, bf16[2,512,384]{2,1,0:T(8,128)(2,1)S(1)}) custom-call(s32[3]{0:T(128)S(1)} %pad_add_fusion.meta, s32[2,8]{1,0:T(2,128)S(1)} %copy-done.6, s32[2048,128]{1,0:T(8,128)S(1)} %get-tuple-element.120.segk, s32[8,2048]{1,0:T(8,128)S(1)} %get-tuple-element.121.segq, ...), custom_call_target="tpu_custom_call" | custom-call | flops 10737418240 | bytes 5242880 | tf_op jit(solution)/shard_map/attend_back/pallas_call | solution.py:42
  138.8 1.7 collective-permute-start.28
  140.5 2.0 collective-permute-start.29
  142.5 2.8 %collective-permute-start.30 = (bf16[576,128]{1,0:T(8,128)(2,1)S(1)}, bf16[576,128]{1,0:T(8,128)(2,1)S(1)}, u32[]{:S(2)}, u32[]{:S(2)}) collective-permute-start(bf16[576,128]{1,0:T(8,128)(2,1)S(1)} %get-tuple-element.176), channel_id=1, source_target_pairs={{0,3},{1,0},{2,1},{3,2},{4,7},{5,4},{6,5},{7,6},{8,11},{9,8},{10,9... | collective-permute-start | bytes 442376 | tf_op jit(solution)/shard_map/ppermute | solution.py:873
  146.3 25.1 %attend_back.3 = (bf16[2048,384]{1,0:T(8,128)(2,1)S(1)}, bf16[2,512,384]{2,1,0:T(8,128)(2,1)S(1)}) custom-call(s32[3]{0:T(128)S(1)} %pad_add_fusion.meta, s32[2,8]{1,0:T(2,128)S(1)} %copy-done.6, s32[2048,128]{1,0:T(8,128)S(1)} %copy-done.8, s32[8,2048]{1,0:T(8,128)S(1)} %get-tuple-element.121.segq, bf16[2048,128]{1,0:T(8,128)(2,1)S(1)} %copy-done.10, ...), custom_call_target="tpu_custom_call" | custom-call | flops 10737418240 | bytes 5242880 | tf_op jit(solution)/shard_map/attend_back/pallas_call | solution.py:42
  171.4 5.1 %wgrad.1 = (bf16[1664,128]{1,0:T(8,128)(2,1)S(1)}, bf16[1664,128]{1,0:T(8,128)(2,1)S(1)}, bf16[576,128]{1,0:T(8,128)(2,1)}) custom-call(s32[3]{0:T(128)S(1)} %pad_add_fusion.meta, f32[16,512]{1,0:T(8,128)S(1)} %get-tuple-element.170.vec_in, f32[1,512]{1,0:T(1,128)S(1)} %bitcast.36, f32[1,512]{1,0:T(1,128)S(1)} %bitcast.39, ...), custom_call_target="tpu_custom_call" | custom-call | flops 1610612736 | bytes 8388608 | tf_op jit(solution)/shard_map/wgrad/pallas_call | solution.py:42
  176.6 1.8 collective-permute-done.31.recv
  178.8 1.5 arrange.1
  180.3 1.5 collective-permute-start.36
  181.8 1.9 collective-permute-start.37
  183.8 4.8 %token_back.1 = (bf16[2,512,512]{2,1,0:T(8,128)(2,1)}, bf16[512,512]{1,0:T(8,128)(2,1)}) custom-call(s32[3]{0:T(128)S(1)} %pad_add_fusion.meta, f32[1,512]{1,0:T(1,128)S(1)} %bitcast.37, f32[1024,512]{1,0:T(8,128)S(1)} %get-tuple-element.164.g_resid, bf16[512,512]{1,0:T(8,128)(2,1)S(1)} %get-tuple-element.118.refs_0_.x0, ...), custom_call_target="tpu_custom_call" | custom-call | flops 1610612736 | bytes 8388608 | tf_op jit(solution)/shard_map/token_back/pallas_call | solution.py:42
  188.6 1.5 collective-permute-start.41
  190.1 3.7 %collective-permute-done.36.c = bf16[896,128]{1,0:T(8,128)(2,1)} collective-permute-done((bf16[896,128]{1,0:T(8,128)(2,1)}, bf16[896,128]{1,0:T(8,128)(2,1)}, u32[]{:S(2)}, u32[]{:S(2)}) %collective-permute-start.36) | collective-permute-done | bytes 229408 | tf_op jit(solution)/shard_map/ppermute | solution.py:870
  193.8 1.2 plane_sum_qkv.1
  195.0 1.2 collective-permute-start.38
  196.7 2.6 %collective-permute-start.40 = (bf16[320,128]{1,0:T(8,128)(2,1)S(1)}, bf16[320,128]{1,0:T(8,128)(2,1)S(1)}, u32[]{:S(2)}, u32[]{:S(2)}) collective-permute-start(bf16[320,128]{1,0:T(8,128)(2,1)S(1)} %get-tuple-element.200), channel_id=1, source_target_pairs={{0,3},{1,0},{2,1},{3,2},{4,7},{5,4},{6,5},{7,6},{8,11},{9,8},{10,9... | collective-permute-start | bytes 245768 | tf_op jit(solution)/shard_map/ppermute | solution.py:873
  199.3 2.3 %maximum_select_fusion = bf16[2,512,512]{2,1,0:T(8,128)(2,1)} fusion(bf16[1,512,512]{2,1,0:T(8,128)(2,1)} %bitcast.45, bf16[1,512,512]{2,1,0:T(8,128)(2,1)S(1)} %bitcast.34, pred[]{:T(512)S(6)} %eq.3), kind=kLoop, calls=%fused_computation | loop fusion | flops 1572864 | bytes 2097153 | tf_op jit(solution)/shard_map/jit(_where)/select_n | solution.py:1116
  201.6 1.8 finish.1
  205.0 0.9 collective-permute-start.42
  206.0 1.1 bitcast_dynamic-update-slice_fusion
  207.1 2.0 collective-permute-done.42.o
  209.1 1.2 finish_qkv.1
  (136 shorter events, 13.0 us)
Async XLA Ops:
  3.1 16.1 %collective-permute-start = (bf16[512,512]{1,0:T(8,128)(2,1)S(1)}, bf16[512,512]{1,0:T(8,128)(2,1)S(1)}, u32[]{:S(2)}, u32[]{:S(2)}) collective-permute-start(bf16[512,512]{1,0:T(8,128)(2,1)S(1)} %get-tuple-element.214), channel_id=1, source_target_pairs={{0,8},{4,12},{8,0},{12,4},{1,9},{5,13},{9,1},{13,5},{2,10},{6,14},... | collective-permute-start | bytes 1572872 | tf_op jit(solution)/shard_map/ppermute | solution.py:861
  6.2 6.8 %collective-permute-start.4 = (bf16[128,384]{1,0:T(8,128)(2,1)S(1)}, bf16[128,384]{1,0:T(8,128)(2,1)S(1)}, u32[]{:S(2)}, u32[]{:S(2)}) collective-permute-start(bf16[128,384]{1,0:T(8,128)(2,1)S(1)} %convert_element_type.3), channel_id=1, source_target_pairs={{0,3},{1,0},{2,1},{3,2},{4,7},{5,4},{6,5},{7,6},{8,11},{9,8},{10,9... | collective-permute-start | bytes 294920 | tf_op jit(solution)/shard_map/ppermute | solution.py:873
  9.8 8.3 %collective-permute-start.3 = (bf16[128,384]{1,0:T(8,128)(2,1)S(1)}, bf16[128,384]{1,0:T(8,128)(2,1)S(1)}, u32[]{:S(2)}, u32[]{:S(2)}) collective-permute-start(bf16[128,384]{1,0:T(8,128)(2,1)S(1)} %convert_element_type.3), channel_id=1, source_target_pairs={{0,2},{1,3},{2,0},{3,1},{4,6},{5,7},{6,4},{7,5},{8,10},{9,11},{10,... | collective-permute-start | bytes 294920 | tf_op jit(solution)/shard_map/ppermute | solution.py:873
  9.8 8.3 %collective-permute-start.2 = (bf16[128,384]{1,0:T(8,128)(2,1)S(1)}, bf16[128,384]{1,0:T(8,128)(2,1)}, u32[]{:S(2)}, u32[]{:S(2)}) collective-permute-start(bf16[128,384]{1,0:T(8,128)(2,1)S(1)} %convert_element_type.3), channel_id=1, source_target_pairs={{0,1},{1,2},{2,3},{3,0},{4,5},{5,6},{6,7},{7,4},{8,9},{9,10},{10,1... | collective-permute-start | bytes 294920 | tf_op jit(solution)/shard_map/ppermute | solution.py:873
  11.4 26.5 %copy-start.29 = (f32[512]{0:T(512)S(1)}, f32[512]{0:T(512)}, u32[]{:S(2)}) copy-start(f32[512]{0:T(512)} %param.22) | copy-start | bytes 6148
  19.1 2.0 collective-permute-start.5
  19.2 2.6 %collective-permute-start.6 = (bf16[512,512]{1,0:T(8,128)(2,1)S(1)}, bf16[512,512]{1,0:T(8,128)(2,1)S(1)}, u32[]{:S(2)}, u32[]{:S(2)}) collective-permute-start(bf16[512,512]{1,0:T(8,128)(2,1)S(1)} %collective-permute-done.refs_2_.refs_1_.x1), channel_id=1, source_target_pairs={{0,4},{4,0},{8,12},{12,8},{1,5},{5,1},{9,13},{13,9},{2,6},{6,2},{1... | collective-permute-start | bytes 1572872 | tf_op jit(solution)/shard_map/ppermute | solution.py:864
  19.6 12.0 %collective-permute-start.8 = (bf16[4,128,384]{2,1,0:T(8,128)(2,1)S(1)}, bf16[4,128,384]{2,1,0:T(8,128)(2,1)S(1)}, u32[]{:S(2)}, u32[]{:S(2)}) collective-permute-start(bf16[4,128,384]{2,1,0:T(8,128)(2,1)S(1)} %pad_maximum_fusion.1.refs_0_), channel_id=1, source_target_pairs={{0,8},{4,12},{8,0},{12,4},{1,9},{5,13},{9,1},{13,5},{2,10},{6,14},... | collective-permute-start | bytes 1179656 | tf_op jit(solution)/shard_map/ppermute | solution.py:861
  21.8 9.8 %collective-permute-start.11 = (bf16[576,128]{1,0:T(8,128)(2,1)S(1)}, bf16[576,128]{1,0:T(8,128)(2,1)S(1)}, u32[]{:S(2)}, u32[]{:S(2)}) collective-permute-start(bf16[576,128]{1,0:T(8,128)(2,1)S(1)} %pack.1), channel_id=1, source_target_pairs={{0,3},{1,0},{2,1},{3,2},{4,7},{5,4},{6,5},{7,6},{8,11},{9,8},{10,9... | collective-permute-start | bytes 442376 | tf_op jit(solution)/shard_map/ppermute | solution.py:873
  23.8 14.1 %collective-permute-start.10 = (bf16[576,128]{1,0:T(8,128)(2,1)S(1)}, bf16[576,128]{1,0:T(8,128)(2,1)S(1)}, u32[]{:S(2)}, u32[]{:S(2)}) collective-permute-start(bf16[576,128]{1,0:T(8,128)(2,1)S(1)} %pack.1), channel_id=1, source_target_pairs={{0,2},{1,3},{2,0},{3,1},{4,6},{5,7},{6,4},{7,5},{8,10},{9,11},{10,... | collective-permute-start | bytes 442376 | tf_op jit(solution)/shard_map/ppermute | solution.py:873
  24.3 13.6 %collective-permute-start.9 = (bf16[576,128]{1,0:T(8,128)(2,1)S(1)}, bf16[576,128]{1,0:T(8,128)(2,1)S(1)}, u32[]{:S(2)}, u32[]{:S(2)}) collective-permute-start(bf16[576,128]{1,0:T(8,128)(2,1)S(1)} %pack.1), channel_id=1, source_target_pairs={{0,1},{1,2},{2,3},{3,0},{4,5},{5,6},{6,7},{7,4},{8,9},{9,10},{10,1... | collective-permute-start | bytes 442376 | tf_op jit(solution)/shard_map/ppermute | solution.py:873
  26.4 17.8 %collective-permute-start.1 = (bf16[512,512]{1,0:T(8,128)(2,1)S(1)}, bf16[512,512]{1,0:T(8,128)(2,1)S(1)}, u32[]{:S(2)}, u32[]{:S(2)}) collective-permute-start(bf16[512,512]{1,0:T(8,128)(2,1)S(1)} %dynamic-slice_bitcast_fusion), channel_id=1, source_target_pairs={{0,8},{4,12},{8,0},{12,4},{1,9},{5,13},{9,1},{13,5},{2,10},{6,14},... | collective-permute-start | bytes 1572872 | tf_op jit(solution)/shard_map/ppermute | solution.py:861
  30.5 82.6 %copy-start.7 = (s32[2048,128]{1,0:T(8,128)}, s32[2048,128]{1,0:T(8,128)S(1)}, u32[]{:S(2)}) copy-start(s32[2048,128]{1,0:T(8,128)S(1)} %get-tuple-element.120.segk) | copy-start | bytes 3145732
  31.6 6.3 %collective-permute-start.7 = (bf16[4,128,384]{2,1,0:T(8,128)(2,1)S(1)}, bf16[4,128,384]{2,1,0:T(8,128)(2,1)S(1)}, u32[]{:S(2)}, u32[]{:S(2)}) collective-permute-start(bf16[4,128,384]{2,1,0:T(8,128)(2,1)S(1)} %pad_maximum_fusion.1.refs_0_), channel_id=1, source_target_pairs={{0,4},{4,0},{8,12},{12,8},{1,5},{5,1},{9,13},{13,9},{2,6},{6,2},{1... | collective-permute-start | bytes 1179656 | tf_op jit(solution)/shard_map/ppermute | solution.py:864
  37.9 1.7 collective-permute-start.12
  44.3 13.1 %collective-permute-start.15 = (bf16[4,576,128]{2,1,0:T(8,128)(2,1)S(1)}, bf16[4,576,128]{2,1,0:T(8,128)(2,1)S(1)}, u32[]{:S(2)}, u32[]{:S(2)}) collective-permute-start(bf16[4,576,128]{2,1,0:T(8,128)(2,1)S(1)} %pad_maximum_fusion.refs_11_), channel_id=1, source_target_pairs={{0,4},{4,0},{8,12},{12,8},{1,5},{5,1},{9,13},{13,9},{2,6},{6,2},{1... | collective-permute-start | bytes 1769480 | tf_op jit(solution)/shard_map/ppermute | solution.py:864
  44.5 15.6 %collective-permute-start.14 = (bf16[4,576,128]{2,1,0:T(8,128)(2,1)S(1)}, bf16[4,576,128]{2,1,0:T(8,128)(2,1)S(1)}, u32[]{:S(2)}, u32[]{:S(2)}) collective-permute-start(bf16[4,576,128]{2,1,0:T(8,128)(2,1)S(1)} %pad_maximum_fusion.refs_11_), channel_id=1, source_target_pairs={{0,8},{4,12},{8,0},{12,4},{16,24},{20,28},{24,16},{28,20},{1,9},{5... | collective-permute-start | bytes 1769480 | tf_op jit(solution)/shard_map/ppermute | solution.py:870
  45.0 16.2 %collective-permute-start.13 = (bf16[4,576,128]{2,1,0:T(8,128)(2,1)S(1)}, bf16[4,576,128]{2,1,0:T(8,128)(2,1)S(1)}, u32[]{:S(2)}, u32[]{:S(2)}) collective-permute-start(bf16[4,576,128]{2,1,0:T(8,128)(2,1)S(1)} %pad_maximum_fusion.refs_11_), channel_id=1, source_target_pairs={{0,16},{4,20},{8,24},{12,28},{16,0},{20,4},{24,8},{28,12},{1,17},{... | collective-permute-start | bytes 1769480 | tf_op jit(solution)/shard_map/ppermute | solution.py:870
  46.5 28.0 %collective-permute-start.19 = (bf16[4,576,128]{2,1,0:T(8,128)(2,1)S(1)}, bf16[4,576,128]{2,1,0:T(8,128)(2,1)S(1)}, u32[]{:S(2)}, u32[]{:S(2)}) collective-permute-start(bf16[4,576,128]{2,1,0:T(8,128)(2,1)S(1)} %pad_maximum_fusion.refs_11_), channel_id=1, source_target_pairs={{0,24},{4,28},{8,16},{12,20},{16,8},{20,12},{24,0},{28,4},{1,25},{... | collective-permute-start | bytes 1769480 | tf_op jit(solution)/shard_map/ppermute | solution.py:870
  74.5 29.1 %copy-start.26 = (bf16[2,2,512,128]{3,2,1,0:T(8,128)(2,1)}, bf16[2,2,512,128]{3,2,1,0:T(8,128)(2,1)S(1)}, u32[]{:S(2)}) copy-start(bf16[2,2,512,128]{3,2,1,0:T(8,128)(2,1)S(1)} %get-tuple-element.141.refs_9_.refs_2_) | copy-start | bytes 1572868
  74.5 4.5 %collective-permute-start.20 = (bf16[4,576,128]{2,1,0:T(8,128)(2,1)S(1)}, bf16[4,576,128]{2,1,0:T(8,128)(2,1)S(1)}, u32[]{:S(2)}, u32[]{:S(2)}) collective-permute-start(bf16[4,576,128]{2,1,0:T(8,128)(2,1)S(1)} %collective-permute-done.19.refs_17_), channel_id=1, source_target_pairs={{0,4},{4,0},{8,12},{12,8},{1,5},{5,1},{9,13},{13,9},{2,6},{6,2},{1... | collective-permute-start | bytes 1769480 | tf_op jit(solution)/shard_map/ppermute | solution.py:864
  74.6 4.4 %collective-permute-start.17 = (bf16[4,576,128]{2,1,0:T(8,128)(2,1)S(1)}, bf16[4,576,128]{2,1,0:T(8,128)(2,1)S(1)}, u32[]{:S(2)}, u32[]{:S(2)}) collective-permute-start(bf16[4,576,128]{2,1,0:T(8,128)(2,1)S(1)} %collective-permute-done.13.refs_13_), channel_id=1, source_target_pairs={{0,4},{4,0},{8,12},{12,8},{1,5},{5,1},{9,13},{13,9},{2,6},{6,2},{1... | collective-permute-start | bytes 1769480 | tf_op jit(solution)/shard_map/ppermute | solution.py:864
  75.1 3.9 %collective-permute-start.18 = (bf16[4,576,128]{2,1,0:T(8,128)(2,1)S(1)}, bf16[4,576,128]{2,1,0:T(8,128)(2,1)S(1)}, u32[]{:S(2)}, u32[]{:S(2)}) collective-permute-start(bf16[4,576,128]{2,1,0:T(8,128)(2,1)S(1)} %collective-permute-done.14.refs_15_), channel_id=1, source_target_pairs={{0,4},{4,0},{8,12},{12,8},{1,5},{5,1},{9,13},{13,9},{2,6},{6,2},{1... | collective-permute-start | bytes 1769480 | tf_op jit(solution)/shard_map/ppermute | solution.py:864
  75.1 3.9 %collective-permute-start.16 = (bf16[2,2,512,128]{3,2,1,0:T(8,128)(2,1)S(1)}, bf16[2,2,512,128]{3,2,1,0:T(8,128)(2,1)S(1)}, u32[]{:S(2)}, u32[]{:S(2)}) collective-permute-start(bf16[2,2,512,128]{3,2,1,0:T(8,128)(2,1)S(1)} %get-tuple-element.132.refs_3_), channel_id=1, source_target_pairs={{0,4},{4,0},{8,12},{12,8},{1,5},{5,1},{9,13},{13,9},{2,6},{6,2},{1... | collective-permute-start | bytes 1572872 | tf_op jit(solution)/shard_map/ppermute | solution.py:864
  104.3 4.5 %collective-permute-start.21 = (bf16[4,4,576,128]{3,2,1,0:T(8,128)(2,1)S(1)}, bf16[4,4,576,128]{3,2,1,0:T(8,128)(2,1)S(1)}, u32[]{:S(2)}, u32[]{:S(2)}) collective-permute-start(bf16[4,4,576,128]{3,2,1,0:T(8,128)(2,1)S(1)} %get-tuple-element.146), channel_id=1, source_target_pairs={{0,4},{4,0},{8,12},{12,8},{1,5},{5,1},{9,13},{13,9},{2,6},{6,2},{1... | collective-permute-start | bytes 7077896 | tf_op jit(solution)/shard_map/ppermute | solution.py:864
  109.4 3.7 %collective-permute-start.25 = (bf16[2,512,128]{2,1,0:T(8,128)(2,1)S(1)}, bf16[2,512,128]{2,1,0:T(8,128)(2,1)S(1)}, u32[]{:S(2)}, u32[]{:S(2)}) collective-permute-start(bf16[2,512,128]{2,1,0:T(8,128)(2,1)S(1)} %get-tuple-element.156), channel_id=1, source_target_pairs={{0,4},{4,0},{8,12},{12,8},{1,5},{5,1},{9,13},{13,9},{2,6},{6,2},{1... | collective-permute-start | bytes 786440 | tf_op jit(solution)/shard_map/ppermute | solution.py:864
  109.6 28.4 %collective-permute-start.22 = (bf16[4,576,128]{2,1,0:T(8,128)(2,1)S(1)}, bf16[4,576,128]{2,1,0:T(8,128)(2,1)S(1)}, u32[]{:S(2)}, u32[]{:S(2)}) collective-permute-start(bf16[4,576,128]{2,1,0:T(8,128)(2,1)S(1)} %get-tuple-element.148), channel_id=1, source_target_pairs={{0,16},{4,20},{8,24},{12,28},{16,0},{20,4},{24,8},{28,12},{1,17},{... | collective-permute-start | bytes 1769480 | tf_op jit(solution)/shard_map/ppermute | solution.py:870
  110.5 28.0 %collective-permute-start.23 = (bf16[4,576,128]{2,1,0:T(8,128)(2,1)S(1)}, bf16[4,576,128]{2,1,0:T(8,128)(2,1)S(1)}, u32[]{:S(2)}, u32[]{:S(2)}) collective-permute-start(bf16[4,576,128]{2,1,0:T(8,128)(2,1)S(1)} %get-tuple-element.149), channel_id=1, source_target_pairs={{0,8},{4,12},{8,0},{12,4},{16,24},{20,28},{24,16},{28,20},{1,9},{5... | collective-permute-start | bytes 1769480 | tf_op jit(solution)/shard_map/ppermute | solution.py:870
  111.0 27.5 %collective-permute-start.24 = (bf16[4,576,128]{2,1,0:T(8,128)(2,1)S(1)}, bf16[4,576,128]{2,1,0:T(8,128)(2,1)S(1)}, u32[]{:S(2)}, u32[]{:S(2)}) collective-permute-start(bf16[4,576,128]{2,1,0:T(8,128)(2,1)S(1)} %get-tuple-element.150), channel_id=1, source_target_pairs={{0,24},{4,28},{8,16},{12,20},{16,8},{20,12},{24,0},{28,4},{1,25},{... | collective-permute-start | bytes 1769480 | tf_op jit(solution)/shard_map/ppermute | solution.py:870
  113.1 32.2 %copy-start.20 = (bf16[512,512]{1,0:T(8,128)(2,1)S(1)}, bf16[512,512]{1,0:T(8,128)(2,1)}, u32[]{:S(2)}) copy-start(bf16[512,512]{1,0:T(8,128)(2,1)} %copy-done.19) | copy-start | bytes 1572868
  113.1 33.1 %copy-start.14 = (bf16[2048,128]{1,0:T(8,128)(2,1)S(1)}, bf16[2048,128]{1,0:T(8,128)(2,1)}, u32[]{:S(2)}) copy-start(bf16[2048,128]{1,0:T(8,128)(2,1)} %copy-done.13) | copy-start | bytes 1572868
  138.7 7.5 %collective-permute-start.27 = (bf16[2,512,128]{2,1,0:T(8,128)(2,1)S(1)}, bf16[2,512,128]{2,1,0:T(8,128)(2,1)S(1)}, u32[]{:S(2)}, u32[]{:S(2)}) collective-permute-start(bf16[2,512,128]{2,1,0:T(8,128)(2,1)S(1)} %get-tuple-element.168), channel_id=1, source_target_pairs={{0,4},{4,0},{8,12},{12,8},{1,5},{5,1},{9,13},{13,9},{2,6},{6,2},{1... | collective-permute-start | bytes 786440 | tf_op jit(solution)/shard_map/ppermute | solution.py:864
  138.8 32.6 %collective-permute-start.28 = (bf16[576,128]{1,0:T(8,128)(2,1)S(1)}, bf16[576,128]{1,0:T(8,128)(2,1)S(1)}, u32[]{:S(2)}, u32[]{:S(2)}) collective-permute-start(bf16[576,128]{1,0:T(8,128)(2,1)S(1)} %get-tuple-element.174), channel_id=1, source_target_pairs={{0,1},{1,2},{2,3},{3,0},{4,5},{5,6},{6,7},{7,4},{8,9},{9,10},{10,1... | collective-permute-start | bytes 442376 | tf_op jit(solution)/shard_map/ppermute | solution.py:873
  140.5 30.8 %collective-permute-start.29 = (bf16[576,128]{1,0:T(8,128)(2,1)S(1)}, bf16[576,128]{1,0:T(8,128)(2,1)S(1)}, u32[]{:S(2)}, u32[]{:S(2)}) collective-permute-start(bf16[576,128]{1,0:T(8,128)(2,1)S(1)} %get-tuple-element.175), channel_id=1, source_target_pairs={{0,2},{1,3},{2,0},{3,1},{4,6},{5,7},{6,4},{7,5},{8,10},{9,11},{10,... | collective-permute-start | bytes 442376 | tf_op jit(solution)/shard_map/ppermute | solution.py:873
  142.5 28.9 %collective-permute-start.30 = (bf16[576,128]{1,0:T(8,128)(2,1)S(1)}, bf16[576,128]{1,0:T(8,128)(2,1)S(1)}, u32[]{:S(2)}, u32[]{:S(2)}) collective-permute-start(bf16[576,128]{1,0:T(8,128)(2,1)S(1)} %get-tuple-element.176), channel_id=1, source_target_pairs={{0,3},{1,0},{2,1},{3,2},{4,7},{5,4},{6,5},{7,6},{8,11},{9,8},{10,9... | collective-permute-start | bytes 442376 | tf_op jit(solution)/shard_map/ppermute | solution.py:873
  145.4 26.0 %collective-permute-start.26 = (bf16[512,512]{1,0:T(8,128)(2,1)S(1)}, bf16[512,512]{1,0:T(8,128)(2,1)S(1)}, u32[]{:S(2)}, u32[]{:S(2)}) collective-permute-start(bf16[512,512]{1,0:T(8,128)(2,1)S(1)} %copy-done.20), channel_id=1, source_target_pairs={{0,8},{4,12},{8,0},{12,4},{1,9},{5,13},{9,1},{13,5},{2,10},{6,14},... | collective-permute-start | bytes 1572872 | tf_op jit(solution)/shard_map/ppermute | solution.py:861
  176.6 1.8 collective-permute-start.31
  178.3 5.5 %collective-permute-start.32 = (bf16[2,512,384]{2,1,0:T(8,128)(2,1)S(1)}, bf16[2,512,384]{2,1,0:T(8,128)(2,1)S(1)}, u32[]{:S(2)}, u32[]{:S(2)}) collective-permute-start(bf16[2,512,384]{2,1,0:T(8,128)(2,1)S(1)} %get-tuple-element.183), channel_id=1, source_target_pairs={{0,4},{4,0},{8,12},{12,8},{1,5},{5,1},{9,13},{13,9},{2,6},{6,2},{1... | collective-permute-start | bytes 2359304 | tf_op jit(solution)/shard_map/ppermute | solution.py:864
  178.5 5.3 %collective-permute-start.33 = (bf16[2,512,384]{2,1,0:T(8,128)(2,1)S(1)}, bf16[2,512,384]{2,1,0:T(8,128)(2,1)S(1)}, u32[]{:S(2)}, u32[]{:S(2)}) collective-permute-start(bf16[2,512,384]{2,1,0:T(8,128)(2,1)S(1)} %get-tuple-element.185), channel_id=1, source_target_pairs={{0,4},{4,0},{8,12},{12,8},{1,5},{5,1},{9,13},{13,9},{2,6},{6,2},{1... | collective-permute-start | bytes 2359304 | tf_op jit(solution)/shard_map/ppermute | solution.py:864
  180.3 9.9 %collective-permute-start.35 = (bf16[896,128]{1,0:T(8,128)(2,1)}, bf16[896,128]{1,0:T(8,128)(2,1)S(1)}, u32[]{:S(2)}, u32[]{:S(2)}) collective-permute-start(bf16[896,128]{1,0:T(8,128)(2,1)} %get-tuple-element.190), channel_id=1, source_target_pairs={{0,16},{4,20},{8,24},{12,28},{16,0},{20,4},{24,8},{28,12},{1,17},{... | collective-permute-start | bytes 688136 | tf_op jit(solution)/shard_map/ppermute | solution.py:870
  180.3 13.5 %collective-permute-start.36 = (bf16[896,128]{1,0:T(8,128)(2,1)}, bf16[896,128]{1,0:T(8,128)(2,1)}, u32[]{:S(2)}, u32[]{:S(2)}) collective-permute-start(bf16[896,128]{1,0:T(8,128)(2,1)} %get-tuple-element.191), channel_id=1, source_target_pairs={{0,8},{4,12},{8,0},{12,4},{16,24},{20,28},{24,16},{28,20},{1,9},{5... | collective-permute-start | bytes 688136 | tf_op jit(solution)/shard_map/ppermute | solution.py:870
  181.8 12.0 %collective-permute-start.37 = (bf16[896,128]{1,0:T(8,128)(2,1)}, bf16[896,128]{1,0:T(8,128)(2,1)}, u32[]{:S(2)}, u32[]{:S(2)}) collective-permute-start(bf16[896,128]{1,0:T(8,128)(2,1)} %get-tuple-element.192), channel_id=1, source_target_pairs={{0,24},{4,28},{8,16},{12,20},{16,8},{20,12},{24,0},{28,4},{1,25},{... | collective-permute-start | bytes 688136 | tf_op jit(solution)/shard_map/ppermute | solution.py:870
  188.6 17.4 %collective-permute-start.34 = (bf16[512,512]{1,0:T(8,128)(2,1)}, bf16[512,512]{1,0:T(8,128)(2,1)}, u32[]{:S(2)}, u32[]{:S(2)}) collective-permute-start(bf16[512,512]{1,0:T(8,128)(2,1)} %get-tuple-element.189), channel_id=1, source_target_pairs={{0,8},{4,12},{8,0},{12,4},{1,9},{5,13},{9,1},{13,5},{2,10},{6,14},... | collective-permute-start | bytes 1572872 | tf_op jit(solution)/shard_map/ppermute | solution.py:861
  188.6 13.0 %collective-permute-start.41 = (bf16[576,128]{1,0:T(8,128)(2,1)}, bf16[576,128]{1,0:T(8,128)(2,1)S(1)}, u32[]{:S(2)}, u32[]{:S(2)}) collective-permute-start(bf16[576,128]{1,0:T(8,128)(2,1)} %get-tuple-element.203.r), channel_id=1, source_target_pairs={{0,16},{4,20},{8,24},{12,28},{16,0},{20,4},{24,8},{28,12},{1,17},{... | collective-permute-start | bytes 442376 | tf_op jit(solution)/shard_map/ppermute | solution.py:870
  195.0 8.4 %collective-permute-start.38 = (bf16[320,128]{1,0:T(8,128)(2,1)S(1)}, bf16[320,128]{1,0:T(8,128)(2,1)S(1)}, u32[]{:S(2)}, u32[]{:S(2)}) collective-permute-start(bf16[320,128]{1,0:T(8,128)(2,1)S(1)} %get-tuple-element.198), channel_id=1, source_target_pairs={{0,1},{1,2},{2,3},{3,0},{4,5},{5,6},{6,7},{7,4},{8,9},{9,10},{10,1... | collective-permute-start | bytes 245768 | tf_op jit(solution)/shard_map/ppermute | solution.py:873
  196.2 7.6 %collective-permute-start.39 = (bf16[320,128]{1,0:T(8,128)(2,1)S(1)}, bf16[320,128]{1,0:T(8,128)(2,1)S(1)}, u32[]{:S(2)}, u32[]{:S(2)}) collective-permute-start(bf16[320,128]{1,0:T(8,128)(2,1)S(1)} %get-tuple-element.199), channel_id=1, source_target_pairs={{0,2},{1,3},{2,0},{3,1},{4,6},{5,7},{6,4},{7,5},{8,10},{9,11},{10,... | collective-permute-start | bytes 245768 | tf_op jit(solution)/shard_map/ppermute | solution.py:873
  196.7 7.1 %collective-permute-start.40 = (bf16[320,128]{1,0:T(8,128)(2,1)S(1)}, bf16[320,128]{1,0:T(8,128)(2,1)S(1)}, u32[]{:S(2)}, u32[]{:S(2)}) collective-permute-start(bf16[320,128]{1,0:T(8,128)(2,1)S(1)} %get-tuple-element.200), channel_id=1, source_target_pairs={{0,3},{1,0},{2,1},{3,2},{4,7},{5,4},{6,5},{7,6},{8,11},{9,8},{10,9... | collective-permute-start | bytes 245768 | tf_op jit(solution)/shard_map/ppermute | solution.py:873
  205.0 4.1 %collective-permute-start.42 = (bf16[192,128]{1,0:T(8,128)(2,1)S(1)}, bf16[192,128]{1,0:T(8,128)(2,1)S(1)}, u32[]{:S(2)}, u32[]{:S(2)}) collective-permute-start(bf16[192,128]{1,0:T(8,128)(2,1)S(1)} %get-tuple-element.209.r), channel_id=1, source_target_pairs={{0,16},{4,20},{8,24},{12,28},{16,0},{20,4},{24,8},{28,12},{1,17},{... | collective-permute-start | bytes 147464 | tf_op jit(solution)/shard_map/ppermute | solution.py:870
  (28 other events, 395.0 us)

commit v7 on v6

--- a/solution.py
+++ b/solution.py
@@ -22,7 +22,7 @@
 TK = 256
 FC = 512
 FT = 1024
-RT = 256
+RT = 512
 KEEP_LB = ((0, 1, 4), (1, 4, 5))
 SEND_LB = ((2, 3, 5), (0, 2, 3))
 
@@ -87,7 +87,7 @@
         self.NP = self.HL // PW
         self.TQ = min(512, block_len)
         self.fast = (
-            dp == 2 and col == 4 and row == 4 and width == 512 and hidden == 2048 and block_len % 256 == 0
+            dp == 2 and col == 4 and row == 4 and width == 512 and hidden == 2048 and block_len % 512 == 0
         )
 
     def where(self, meta):
@@ -157,7 +157,7 @@
                 outs[(3 + d) * NP + p][:, part * PW : (part + 1) * PW] = wscr[:, at]
 
     def step(i, carry):
-        rows = pl.ds(al(i * 256, 256), 256)
+        rows = pl.ds(al(i * 512, 512), 512)
         a = h1[rows, :]
         for p in range(NP):
             res = nn(a, outs[3 * NP + p][...])
@@ -167,7 +167,7 @@
                 ).astype(BF)
         return carry
 
-    lax.fori_loop(0, geo.L // 256, step, 0)
+    lax.fori_loop(0, geo.L // 512, step, 0)
 
 
 def doc_ends(doc, s):

time: 211 us -> 208 us (0.986)
  Pallas kernels: 122 us -> 103 us
  waiting for transfers between devices: 37.3 us -> 48.8 us
  starting transfers between devices: 40.7 us -> 45.7 us
    pallas_call x17, Pallas kernels: 122 us -> 103 us  [call(): pl.pallas_call(kernel, name=name, out_shape=tuple((o for o in outs)), in_...]
    ppermute x11, waiting for transfers between devices: 9.97 us -> 20.9 us  [plane(): return lax.ppermute(v, ('dp', 'col'), pairs)]
    ppermute x11, starting transfers between devices: 13 us -> 17 us  [plane(): return lax.ppermute(v, ('dp', 'col'), pairs)]
    ppermute x5, starting transfers between devices: 5.02 us -> 7.76 us  [swap_half(): return lax.ppermute(v, 'col', [(i, (i + G) % C) for i in range(C)])]
  transfers between devices with their start and end apart: 43 -> 43, of which waited for: 16 -> 18; matrix products, arithmetic and copies ran while one was open for 3% -> 3% of each run, Pallas kernels for 43% -> 35%
where the time goes in v7:
time: 208 us
  Pallas kernels  103 us (50%)
  waiting for transfers between devices  48.8 us (23%)
  starting transfers between devices  45.7 us (22%)
  local copies, waits for them, and re-layouts  4.6 us (2%)
  other arithmetic  4.5 us (2%)
    pallas_call x17, Pallas kernels, call(): pl.pallas_call(kernel, name=name, out_shape=tuple((o for o in outs)), in_...  103 us
    ppermute x11, waiting for transfers between devices, plane(): return lax.ppermute(v, ('dp', 'col'), pairs)  20.9 us
    ppermute x12, starting transfers between devices, line(): return lax.ppermute(v, 'row', [(i, (i + d) % R) for i in range(R)])  18.2 us
    ppermute x11, starting transfers between devices, plane(): return lax.ppermute(v, ('dp', 'col'), pairs)  17 us
    ppermute x12, waiting for transfers between devices, line(): return lax.ppermute(v, 'row', [(i, (i + d) % R) for i in range(R)])  13.9 us
    ppermute x15, waiting for transfers between devices, turn(): lax.ppermute(v, 'col', [(i, i // G * G + (i % G + d) % G) for i in range(...  12.9 us
    ppermute x5, starting transfers between devices, swap_half(): return lax.ppermute(v, 'col', [(i, (i + G) % C) for i in range(C)])  7.76 us
  transfers between devices with their start and end apart: 43, of which 18 were waited for; matrix products, arithmetic and copies ran while one was open for 3% of the time, Pallas kernels for 35%

profile of v7, /device:TPU:0, one launch (start us, length us, event | category | flops | bytes accessed | tf_op | source)
XLA Modules:
  0.0 208.1 jit_solution(9000434178049100251)
XLA Ops:
  1.8 1.3 dynamic-slice_bitcast_fusion.2
  3.1 3.1 %collective-permute-start = (bf16[512,512]{1,0:T(8,128)(2,1)S(1)}, bf16[512,512]{1,0:T(8,128)(2,1)S(1)}, u32[]{:S(2)}, u32[]{:S(2)}) collective-permute-start(bf16[512,512]{1,0:T(8,128)(2,1)S(1)} %get-tuple-element.214), channel_id=1, source_target_pairs={{0,8},{4,12},{8,0},{12,4},{1,9},{5,13},{9,1},{13,5},{2,10},{6,14},... | collective-permute-start | bytes 1572872 | tf_op jit(solution)/shard_map/ppermute | solution.py:861
  6.2 3.6 %collective-permute-start.4 = (bf16[128,384]{1,0:T(8,128)(2,1)S(1)}, bf16[128,384]{1,0:T(8,128)(2,1)S(1)}, u32[]{:S(2)}, u32[]{:S(2)}) collective-permute-start(bf16[128,384]{1,0:T(8,128)(2,1)S(1)} %convert_element_type.3), channel_id=1, source_target_pairs={{0,3},{1,0},{2,1},{3,2},{4,7},{5,4},{6,5},{7,6},{8,11},{9,8},{10,9... | collective-permute-start | bytes 294920 | tf_op jit(solution)/shard_map/ppermute | solution.py:873
  11.4 1.5 collective-permute-done.4
  12.9 5.2 %collective-permute-done.3 = bf16[128,384]{1,0:T(8,128)(2,1)S(1)} collective-permute-done((bf16[128,384]{1,0:T(8,128)(2,1)S(1)}, bf16[128,384]{1,0:T(8,128)(2,1)S(1)}, u32[]{:S(2)}, u32[]{:S(2)}) %collective-permute-start.3) | collective-permute-done | bytes 98336 | tf_op jit(solution)/shard_map/ppermute | solution.py:873
  21.8 2.0 collective-permute-start.11
  24.3 2.0 collective-permute-start.9
  26.9 3.6 %norm_one.1 = (bf16[2048,512]{1,0:T(8,128)(2,1)S(1)}, s32[2048,128]{1,0:T(8,128)S(1)}, s32[8,2048]{1,0:T(8,128)S(1)}) custom-call(s32[3]{0:T(128)S(1)} %pad_add_fusion.meta, s32[2,8]{1,0:T(2,128)S(1)} %copy-done.6, f32[1,512]{1,0:T(1,128)S(1)} %bitcast.35, f32[1,512]{1,0:T(1,128)S(1)} %bitcast.38, bf16[512,512]{1,0:T(8,128)(2,1)S(1)} %get-tuple-element.118.refs_0_.x0, ...), custom_call_target="tpu_custom_call" | custom-call | flops 10485760 | bytes 4194304 | tf_op jit(solution)/shard_map/norm_one/pallas_call | solution.py:42
  30.6 1.1 collective-permute-done.8.refs_2_
  31.6 6.3 %collective-permute-done.10 = bf16[576,128]{1,0:T(8,128)(2,1)S(1)} collective-permute-done((bf16[576,128]{1,0:T(8,128)(2,1)S(1)}, bf16[576,128]{1,0:T(8,128)(2,1)S(1)}, u32[]{:S(2)}, u32[]{:S(2)}) %collective-permute-start.10) | collective-permute-done | bytes 147488 | tf_op jit(solution)/shard_map/ppermute | solution.py:873
  38.0 1.7 collective-permute-done.12.refs_3_
  39.6 3.9 %qkv.1 = (bf16[2048,128]{1,0:T(8,128)(2,1)S(1)}, bf16[2048,128]{1,0:T(8,128)(2,1)S(1)}, bf16[2048,128]{1,0:T(8,128)(2,1)S(1)}, bf16[2048,128]{1,0:T(8,128)(2,1)S...) custom-call(s32[3]{0:T(128)S(1)} %pad_add_fusion.meta, ...), custom_call_target="tpu_custom_call" | custom-call | tf_op jit(solution)/shard_map/qkv/pallas_call | solution.py:42
  44.4 1.5 collective-permute-start.13
  45.9 1.5 collective-permute-start.19
  47.4 8.4 %attend.2 = (bf16[2,2,512,128]{3,2,1,0:T(8,128)(2,1)S(1)}, f32[2,8,512]{2,1,0:T(8,128)S(1)}) custom-call(s32[3]{0:T(128)S(1)} %pad_add_fusion.meta, s32[2,8]{1,0:T(2,128)S(1)} %copy-done.6, s32[2048,128]{1,0:T(8,128)S(1)} %get-tuple-element.120.segk, s32[8,2048]{1,0:T(8,128)S(1)} %get-tuple-element.121.segq, ...), custom_call_target="tpu_custom_call" | custom-call | flops 4294967296 | bytes 4194304 | tf_op jit(solution)/shard_map/attend/pallas_call | solution.py:42
  55.8 3.7 %collective-permute-done.14.refs_15_ = bf16[4,576,128]{2,1,0:T(8,128)(2,1)S(1)} collective-permute-done((bf16[4,576,128]{2,1,0:T(8,128)(2,1)S(1)}, bf16[4,576,128]{2,1,0:T(8,128)(2,1)S(1)}, u32[]{:S(2)}, u32[]{:S(2)}) %collective-permute-start.14) | collective-permute-done | bytes 589856 | tf_op jit(solution)/shard_map/ppermute | solution.py:870
  59.5 1.1 collective-permute-done.13.refs_13_
  60.7 8.4 %attend.3 = (bf16[2,2,512,128]{3,2,1,0:T(8,128)(2,1)S(1)}, f32[2,8,512]{2,1,0:T(8,128)S(1)}) custom-call(s32[3]{0:T(128)S(1)} %pad_add_fusion.meta, s32[2,8]{1,0:T(2,128)S(1)} %copy-done.6, s32[2048,128]{1,0:T(8,128)S(1)} %get-tuple-element.120.segk, s32[8,2048]{1,0:T(8,128)S(1)} %get-tuple-element.121.segq, ...), custom_call_target="tpu_custom_call" | custom-call | flops 4294967296 | bytes 4194304 | tf_op jit(solution)/shard_map/attend/pallas_call | solution.py:42
  69.2 4.2 %collective-permute-done.19.refs_17_ = bf16[4,576,128]{2,1,0:T(8,128)(2,1)S(1)} collective-permute-done((bf16[4,576,128]{2,1,0:T(8,128)(2,1)S(1)}, bf16[4,576,128]{2,1,0:T(8,128)(2,1)S(1)}, u32[]{:S(2)}, u32[]{:S(2)}) %collective-permute-start.19) | collective-permute-done | bytes 589856 | tf_op jit(solution)/shard_map/ppermute | solution.py:870
  74.4 3.4 %collective-permute-done.16.refs_10_ = bf16[2,2,512,128]{3,2,1,0:T(8,128)(2,1)S(1)} collective-permute-done((bf16[2,2,512,128]{3,2,1,0:T(8,128)(2,1)S(1)}, bf16[2,2,512,128]{3,2,1,0:T(8,128)(2,1)S(1)}, u32[]{:S(2)}, u32[]{:S(2)}) %collective-permute-start.16) | collective-permute-done | bytes 524320 | tf_op jit(solution)/shard_map/ppermute | solution.py:864
  77.8 22.8 %ffn.1 = (bf16[512,512]{1,0:T(8,128)(2,1)S(1)}, bf16[512,512]{1,0:T(8,128)(2,1)S(1)}, f32[1024,512]{1,0:T(8,128)S(1)}, bf16[2,512,128]{2,1,0:T(8,128)(2,1)S(1)},...) custom-call(s32[3]{0:T(128)S(1)} %pad_add_fusion.meta, ...), custom_call_target="tpu_custom_call" | custom-call | flops 14495514624 | bytes 20971520 | tf_op jit(solution)/shard_map/ffn/pallas_call | solution.py:42
  101.6 4.4 %collective-permute-done.21.recv = bf16[4,4,576,128]{3,2,1,0:T(8,128)(2,1)S(1)} collective-permute-done((bf16[4,4,576,128]{3,2,1,0:T(8,128)(2,1)S(1)}, bf16[4,4,576,128]{3,2,1,0:T(8,128)(2,1)S(1)}, u32[]{:S(2)}, u32[]{:S(2)}) %collective-permute-start.21) | collective-permute-done | bytes 2359328 | tf_op jit(solution)/shard_map/ppermute | solution.py:864
  106.7 1.5 collective-permute-start.22
  108.2 2.1 %collective-permute-start.23 = (bf16[4,576,128]{2,1,0:T(8,128)(2,1)S(1)}, bf16[4,576,128]{2,1,0:T(8,128)(2,1)S(1)}, u32[]{:S(2)}, u32[]{:S(2)}) collective-permute-start(bf16[4,576,128]{2,1,0:T(8,128)(2,1)S(1)} %get-tuple-element.149), channel_id=1, source_target_pairs={{0,8},{4,12},{8,0},{12,4},{16,24},{20,28},{24,16},{28,20},{1,9},{5... | collective-permute-start | bytes 1769480 | tf_op jit(solution)/shard_map/ppermute | solution.py:870
  110.4 19.7 %attend_back.2 = (bf16[2048,384]{1,0:T(8,128)(2,1)S(1)}, bf16[2,512,384]{2,1,0:T(8,128)(2,1)S(1)}) custom-call(s32[3]{0:T(128)S(1)} %pad_add_fusion.meta, s32[2,8]{1,0:T(2,128)S(1)} %copy-done.6, s32[2048,128]{1,0:T(8,128)S(1)} %get-tuple-element.120.segk, s32[8,2048]{1,0:T(8,128)S(1)} %get-tuple-element.121.segq, ...), custom_call_target="tpu_custom_call" | custom-call | flops 10737418240 | bytes 5242880 | tf_op jit(solution)/shard_map/attend_back/pallas_call | solution.py:42
  130.1 6.4 %collective-permute-done.23.c = bf16[4,576,128]{2,1,0:T(8,128)(2,1)S(1)} collective-permute-done((bf16[4,576,128]{2,1,0:T(8,128)(2,1)S(1)}, bf16[4,576,128]{2,1,0:T(8,128)(2,1)S(1)}, u32[]{:S(2)}, u32[]{:S(2)}) %collective-permute-start.23) | collective-permute-done | bytes 589856 | tf_op jit(solution)/shard_map/ppermute | solution.py:870
  137.1 2.8 %collective-permute-start.29 = (bf16[576,128]{1,0:T(8,128)(2,1)S(1)}, bf16[576,128]{1,0:T(8,128)(2,1)S(1)}, u32[]{:S(2)}, u32[]{:S(2)}) collective-permute-start(bf16[576,128]{1,0:T(8,128)(2,1)S(1)} %get-tuple-element.175), channel_id=1, source_target_pairs={{0,2},{1,3},{2,0},{3,1},{4,6},{5,7},{6,4},{7,5},{8,10},{9,11},{10,... | collective-permute-start | bytes 442376 | tf_op jit(solution)/shard_map/ppermute | solution.py:873
  139.9 2.2 %collective-permute-start.30 = (bf16[576,128]{1,0:T(8,128)(2,1)S(1)}, bf16[576,128]{1,0:T(8,128)(2,1)S(1)}, u32[]{:S(2)}, u32[]{:S(2)}) collective-permute-start(bf16[576,128]{1,0:T(8,128)(2,1)S(1)} %get-tuple-element.176), channel_id=1, source_target_pairs={{0,3},{1,0},{2,1},{3,2},{4,7},{5,4},{6,5},{7,6},{8,11},{9,8},{10,9... | collective-permute-start | bytes 442376 | tf_op jit(solution)/shard_map/ppermute | solution.py:873
  142.1 1.7 collective-permute-start.26
  143.9 19.9 %attend_back.3 = (bf16[2048,384]{1,0:T(8,128)(2,1)S(1)}, bf16[2,512,384]{2,1,0:T(8,128)(2,1)S(1)}) custom-call(s32[3]{0:T(128)S(1)} %pad_add_fusion.meta, s32[2,8]{1,0:T(2,128)S(1)} %copy-done.6, s32[2048,128]{1,0:T(8,128)S(1)} %copy-done.8, s32[8,2048]{1,0:T(8,128)S(1)} %get-tuple-element.121.segq, bf16[2048,128]{1,0:T(8,128)(2,1)S(1)} %copy-done.10, ...), custom_call_target="tpu_custom_call" | custom-call | flops 10737418240 | bytes 5242880 | tf_op jit(solution)/shard_map/attend_back/pallas_call | solution.py:42
  163.9 5.1 %wgrad.1 = (bf16[1664,128]{1,0:T(8,128)(2,1)S(1)}, bf16[1664,128]{1,0:T(8,128)(2,1)S(1)}, bf16[576,128]{1,0:T(8,128)(2,1)}) custom-call(s32[3]{0:T(128)S(1)} %pad_add_fusion.meta, f32[16,512]{1,0:T(8,128)S(1)} %get-tuple-element.170.vec_in, f32[1,512]{1,0:T(1,128)S(1)} %bitcast.36, f32[1,512]{1,0:T(1,128)S(1)} %bitcast.39, ...), custom_call_target="tpu_custom_call" | custom-call | flops 1610612736 | bytes 8388608 | tf_op jit(solution)/shard_map/wgrad/pallas_call | solution.py:42
  169.0 1.8 collective-permute-done.31.recv
  171.3 1.5 arrange.1
  172.8 5.5 %collective-permute-start.35 = (bf16[896,128]{1,0:T(8,128)(2,1)}, bf16[896,128]{1,0:T(8,128)(2,1)S(1)}, u32[]{:S(2)}, u32[]{:S(2)}) collective-permute-start(bf16[896,128]{1,0:T(8,128)(2,1)} %get-tuple-element.190), channel_id=1, source_target_pairs={{0,16},{4,20},{8,24},{12,28},{16,0},{20,4},{24,8},{28,12},{1,17},{... | collective-permute-start | bytes 688136 | tf_op jit(solution)/shard_map/ppermute | solution.py:870
  178.3 1.3 collective-permute-start.36
  179.7 4.2 %token_back.1 = (bf16[2,512,512]{2,1,0:T(8,128)(2,1)}, bf16[512,512]{1,0:T(8,128)(2,1)}) custom-call(s32[3]{0:T(128)S(1)} %pad_add_fusion.meta, f32[1,512]{1,0:T(1,128)S(1)} %bitcast.37, f32[1024,512]{1,0:T(8,128)S(1)} %get-tuple-element.164.g_resid, bf16[512,512]{1,0:T(8,128)(2,1)S(1)} %get-tuple-element.118.refs_0_.x0, ...), custom_call_target="tpu_custom_call" | custom-call | flops 1610612736 | bytes 8388608 | tf_op jit(solution)/shard_map/token_back/pallas_call | solution.py:42
  184.0 1.9 collective-permute-start.34
  185.8 1.4 collective-permute-start.41
  187.3 3.8 %collective-permute-done.36.c = bf16[896,128]{1,0:T(8,128)(2,1)} collective-permute-done((bf16[896,128]{1,0:T(8,128)(2,1)}, bf16[896,128]{1,0:T(8,128)(2,1)}, u32[]{:S(2)}, u32[]{:S(2)}) %collective-permute-start.36) | collective-permute-done | bytes 229408 | tf_op jit(solution)/shard_map/ppermute | solution.py:870
  191.3 1.2 plane_sum_qkv.1
  192.5 1.2 collective-permute-start.38
  194.4 2.0 collective-permute-start.40
  196.4 2.3 %maximum_select_fusion = bf16[2,512,512]{2,1,0:T(8,128)(2,1)} fusion(bf16[1,512,512]{2,1,0:T(8,128)(2,1)} %bitcast.45, bf16[1,512,512]{2,1,0:T(8,128)(2,1)S(1)} %bitcast.34, pred[]{:T(512)S(6)} %eq.3), kind=kLoop, calls=%fused_computation | loop fusion | flops 1572864 | bytes 2097153 | tf_op jit(solution)/shard_map/jit(_where)/select_n | solution.py:1116
  198.7 1.8 finish.1
  202.7 1.5 collective-permute-start.42
  204.2 1.1 bitcast_dynamic-update-slice_fusion
  205.3 1.5 collective-permute-done.42.o
  206.8 1.2 finish_qkv.1
  (136 shorter events, 15.6 us)
Async XLA Ops:
  3.1 16.1 %collective-permute-start = (bf16[512,512]{1,0:T(8,128)(2,1)S(1)}, bf16[512,512]{1,0:T(8,128)(2,1)S(1)}, u32[]{:S(2)}, u32[]{:S(2)}) collective-permute-start(bf16[512,512]{1,0:T(8,128)(2,1)S(1)} %get-tuple-element.214), channel_id=1, source_target_pairs={{0,8},{4,12},{8,0},{12,4},{1,9},{5,13},{9,1},{13,5},{2,10},{6,14},... | collective-permute-start | bytes 1572872 | tf_op jit(solution)/shard_map/ppermute | solution.py:861
  6.2 6.8 %collective-permute-start.4 = (bf16[128,384]{1,0:T(8,128)(2,1)S(1)}, bf16[128,384]{1,0:T(8,128)(2,1)S(1)}, u32[]{:S(2)}, u32[]{:S(2)}) collective-permute-start(bf16[128,384]{1,0:T(8,128)(2,1)S(1)} %convert_element_type.3), channel_id=1, source_target_pairs={{0,3},{1,0},{2,1},{3,2},{4,7},{5,4},{6,5},{7,6},{8,11},{9,8},{10,9... | collective-permute-start | bytes 294920 | tf_op jit(solution)/shard_map/ppermute | solution.py:873
  9.8 8.3 %collective-permute-start.3 = (bf16[128,384]{1,0:T(8,128)(2,1)S(1)}, bf16[128,384]{1,0:T(8,128)(2,1)S(1)}, u32[]{:S(2)}, u32[]{:S(2)}) collective-permute-start(bf16[128,384]{1,0:T(8,128)(2,1)S(1)} %convert_element_type.3), channel_id=1, source_target_pairs={{0,2},{1,3},{2,0},{3,1},{4,6},{5,7},{6,4},{7,5},{8,10},{9,11},{10,... | collective-permute-start | bytes 294920 | tf_op jit(solution)/shard_map/ppermute | solution.py:873
  9.8 8.3 %collective-permute-start.2 = (bf16[128,384]{1,0:T(8,128)(2,1)S(1)}, bf16[128,384]{1,0:T(8,128)(2,1)}, u32[]{:S(2)}, u32[]{:S(2)}) collective-permute-start(bf16[128,384]{1,0:T(8,128)(2,1)S(1)} %convert_element_type.3), channel_id=1, source_target_pairs={{0,1},{1,2},{2,3},{3,0},{4,5},{5,6},{6,7},{7,4},{8,9},{9,10},{10,1... | collective-permute-start | bytes 294920 | tf_op jit(solution)/shard_map/ppermute | solution.py:873
  11.4 26.5 %copy-start.29 = (f32[512]{0:T(512)S(1)}, f32[512]{0:T(512)}, u32[]{:S(2)}) copy-start(f32[512]{0:T(512)} %param.22) | copy-start | bytes 6148
  19.1 2.0 collective-permute-start.5
  19.2 2.6 %collective-permute-start.6 = (bf16[512,512]{1,0:T(8,128)(2,1)S(1)}, bf16[512,512]{1,0:T(8,128)(2,1)S(1)}, u32[]{:S(2)}, u32[]{:S(2)}) collective-permute-start(bf16[512,512]{1,0:T(8,128)(2,1)S(1)} %collective-permute-done.refs_2_.refs_1_.x1), channel_id=1, source_target_pairs={{0,4},{4,0},{8,12},{12,8},{1,5},{5,1},{9,13},{13,9},{2,6},{6,2},{1... | collective-permute-start | bytes 1572872 | tf_op jit(solution)/shard_map/ppermute | solution.py:864
  19.6 12.0 %collective-permute-start.8 = (bf16[4,128,384]{2,1,0:T(8,128)(2,1)S(1)}, bf16[4,128,384]{2,1,0:T(8,128)(2,1)S(1)}, u32[]{:S(2)}, u32[]{:S(2)}) collective-permute-start(bf16[4,128,384]{2,1,0:T(8,128)(2,1)S(1)} %pad_maximum_fusion.1.refs_0_), channel_id=1, source_target_pairs={{0,8},{4,12},{8,0},{12,4},{1,9},{5,13},{9,1},{13,5},{2,10},{6,14},... | collective-permute-start | bytes 1179656 | tf_op jit(solution)/shard_map/ppermute | solution.py:861
  21.8 9.8 %collective-permute-start.11 = (bf16[576,128]{1,0:T(8,128)(2,1)S(1)}, bf16[576,128]{1,0:T(8,128)(2,1)S(1)}, u32[]{:S(2)}, u32[]{:S(2)}) collective-permute-start(bf16[576,128]{1,0:T(8,128)(2,1)S(1)} %pack.1), channel_id=1, source_target_pairs={{0,3},{1,0},{2,1},{3,2},{4,7},{5,4},{6,5},{7,6},{8,11},{9,8},{10,9... | collective-permute-start | bytes 442376 | tf_op jit(solution)/shard_map/ppermute | solution.py:873
  23.8 14.1 %collective-permute-start.10 = (bf16[576,128]{1,0:T(8,128)(2,1)S(1)}, bf16[576,128]{1,0:T(8,128)(2,1)S(1)}, u32[]{:S(2)}, u32[]{:S(2)}) collective-permute-start(bf16[576,128]{1,0:T(8,128)(2,1)S(1)} %pack.1), channel_id=1, source_target_pairs={{0,2},{1,3},{2,0},{3,1},{4,6},{5,7},{6,4},{7,5},{8,10},{9,11},{10,... | collective-permute-start | bytes 442376 | tf_op jit(solution)/shard_map/ppermute | solution.py:873
  24.3 13.6 %collective-permute-start.9 = (bf16[576,128]{1,0:T(8,128)(2,1)S(1)}, bf16[576,128]{1,0:T(8,128)(2,1)S(1)}, u32[]{:S(2)}, u32[]{:S(2)}) collective-permute-start(bf16[576,128]{1,0:T(8,128)(2,1)S(1)} %pack.1), channel_id=1, source_target_pairs={{0,1},{1,2},{2,3},{3,0},{4,5},{5,6},{6,7},{7,4},{8,9},{9,10},{10,1... | collective-permute-start | bytes 442376 | tf_op jit(solution)/shard_map/ppermute | solution.py:873
  26.4 17.3 %collective-permute-start.1 = (bf16[512,512]{1,0:T(8,128)(2,1)S(1)}, bf16[512,512]{1,0:T(8,128)(2,1)S(1)}, u32[]{:S(2)}, u32[]{:S(2)}) collective-permute-start(bf16[512,512]{1,0:T(8,128)(2,1)S(1)} %dynamic-slice_bitcast_fusion), channel_id=1, source_target_pairs={{0,8},{4,12},{8,0},{12,4},{1,9},{5,13},{9,1},{13,5},{2,10},{6,14},... | collective-permute-start | bytes 1572872 | tf_op jit(solution)/shard_map/ppermute | solution.py:861
  30.5 79.8 %copy-start.7 = (s32[2048,128]{1,0:T(8,128)}, s32[2048,128]{1,0:T(8,128)S(1)}, u32[]{:S(2)}) copy-start(s32[2048,128]{1,0:T(8,128)S(1)} %get-tuple-element.120.segk) | copy-start | bytes 3145732
  31.6 6.3 %collective-permute-start.7 = (bf16[4,128,384]{2,1,0:T(8,128)(2,1)S(1)}, bf16[4,128,384]{2,1,0:T(8,128)(2,1)S(1)}, u32[]{:S(2)}, u32[]{:S(2)}) collective-permute-start(bf16[4,128,384]{2,1,0:T(8,128)(2,1)S(1)} %pad_maximum_fusion.1.refs_0_), channel_id=1, source_target_pairs={{0,4},{4,0},{8,12},{12,8},{1,5},{5,1},{9,13},{13,9},{2,6},{6,2},{1... | collective-permute-start | bytes 1179656 | tf_op jit(solution)/shard_map/ppermute | solution.py:864
  37.9 1.7 collective-permute-start.12
  43.7 12.1 %collective-permute-start.15 = (bf16[4,576,128]{2,1,0:T(8,128)(2,1)S(1)}, bf16[4,576,128]{2,1,0:T(8,128)(2,1)S(1)}, u32[]{:S(2)}, u32[]{:S(2)}) collective-permute-start(bf16[4,576,128]{2,1,0:T(8,128)(2,1)S(1)} %pad_maximum_fusion.refs_11_), channel_id=1, source_target_pairs={{0,4},{4,0},{8,12},{12,8},{1,5},{5,1},{9,13},{13,9},{2,6},{6,2},{1... | collective-permute-start | bytes 1769480 | tf_op jit(solution)/shard_map/ppermute | solution.py:864
  43.9 15.6 %collective-permute-start.14 = (bf16[4,576,128]{2,1,0:T(8,128)(2,1)S(1)}, bf16[4,576,128]{2,1,0:T(8,128)(2,1)S(1)}, u32[]{:S(2)}, u32[]{:S(2)}) collective-permute-start(bf16[4,576,128]{2,1,0:T(8,128)(2,1)S(1)} %pad_maximum_fusion.refs_11_), channel_id=1, source_target_pairs={{0,8},{4,12},{8,0},{12,4},{16,24},{20,28},{24,16},{28,20},{1,9},{5... | collective-permute-start | bytes 1769480 | tf_op jit(solution)/shard_map/ppermute | solution.py:870
  44.4 16.2 %collective-permute-start.13 = (bf16[4,576,128]{2,1,0:T(8,128)(2,1)S(1)}, bf16[4,576,128]{2,1,0:T(8,128)(2,1)S(1)}, u32[]{:S(2)}, u32[]{:S(2)}) collective-permute-start(bf16[4,576,128]{2,1,0:T(8,128)(2,1)S(1)} %pad_maximum_fusion.refs_11_), channel_id=1, source_target_pairs={{0,16},{4,20},{8,24},{12,28},{16,0},{20,4},{24,8},{28,12},{1,17},{... | collective-permute-start | bytes 1769480 | tf_op jit(solution)/shard_map/ppermute | solution.py:870
  45.9 27.4 %collective-permute-start.19 = (bf16[4,576,128]{2,1,0:T(8,128)(2,1)S(1)}, bf16[4,576,128]{2,1,0:T(8,128)(2,1)S(1)}, u32[]{:S(2)}, u32[]{:S(2)}) collective-permute-start(bf16[4,576,128]{2,1,0:T(8,128)(2,1)S(1)} %pad_maximum_fusion.refs_11_), channel_id=1, source_target_pairs={{0,24},{4,28},{8,16},{12,20},{16,8},{20,12},{24,0},{28,4},{1,25},{... | collective-permute-start | bytes 1769480 | tf_op jit(solution)/shard_map/ppermute | solution.py:870
  69.2 31.5 %copy-start.26 = (bf16[2,2,512,128]{3,2,1,0:T(8,128)(2,1)}, bf16[2,2,512,128]{3,2,1,0:T(8,128)(2,1)S(1)}, u32[]{:S(2)}) copy-start(bf16[2,2,512,128]{3,2,1,0:T(8,128)(2,1)S(1)} %get-tuple-element.141.refs_9_.refs_2_) | copy-start | bytes 1572868
  73.3 4.4 %collective-permute-start.20 = (bf16[4,576,128]{2,1,0:T(8,128)(2,1)S(1)}, bf16[4,576,128]{2,1,0:T(8,128)(2,1)S(1)}, u32[]{:S(2)}, u32[]{:S(2)}) collective-permute-start(bf16[4,576,128]{2,1,0:T(8,128)(2,1)S(1)} %collective-permute-done.19.refs_17_), channel_id=1, source_target_pairs={{0,4},{4,0},{8,12},{12,8},{1,5},{5,1},{9,13},{13,9},{2,6},{6,2},{1... | collective-permute-start | bytes 1769480 | tf_op jit(solution)/shard_map/ppermute | solution.py:864
  73.3 4.4 %collective-permute-start.17 = (bf16[4,576,128]{2,1,0:T(8,128)(2,1)S(1)}, bf16[4,576,128]{2,1,0:T(8,128)(2,1)S(1)}, u32[]{:S(2)}, u32[]{:S(2)}) collective-permute-start(bf16[4,576,128]{2,1,0:T(8,128)(2,1)S(1)} %collective-permute-done.13.refs_13_), channel_id=1, source_target_pairs={{0,4},{4,0},{8,12},{12,8},{1,5},{5,1},{9,13},{13,9},{2,6},{6,2},{1... | collective-permute-start | bytes 1769480 | tf_op jit(solution)/shard_map/ppermute | solution.py:864
  73.8 3.9 %collective-permute-start.18 = (bf16[4,576,128]{2,1,0:T(8,128)(2,1)S(1)}, bf16[4,576,128]{2,1,0:T(8,128)(2,1)S(1)}, u32[]{:S(2)}, u32[]{:S(2)}) collective-permute-start(bf16[4,576,128]{2,1,0:T(8,128)(2,1)S(1)} %collective-permute-done.14.refs_15_), channel_id=1, source_target_pairs={{0,4},{4,0},{8,12},{12,8},{1,5},{5,1},{9,13},{13,9},{2,6},{6,2},{1... | collective-permute-start | bytes 1769480 | tf_op jit(solution)/shard_map/ppermute | solution.py:864
  73.9 3.9 %collective-permute-start.16 = (bf16[2,2,512,128]{3,2,1,0:T(8,128)(2,1)S(1)}, bf16[2,2,512,128]{3,2,1,0:T(8,128)(2,1)S(1)}, u32[]{:S(2)}, u32[]{:S(2)}) collective-permute-start(bf16[2,2,512,128]{3,2,1,0:T(8,128)(2,1)S(1)} %get-tuple-element.132.refs_3_), channel_id=1, source_target_pairs={{0,4},{4,0},{8,12},{12,8},{1,5},{5,1},{9,13},{13,9},{2,6},{6,2},{1... | collective-permute-start | bytes 1572872 | tf_op jit(solution)/shard_map/ppermute | solution.py:864
  101.4 4.5 %collective-permute-start.21 = (bf16[4,4,576,128]{3,2,1,0:T(8,128)(2,1)S(1)}, bf16[4,4,576,128]{3,2,1,0:T(8,128)(2,1)S(1)}, u32[]{:S(2)}, u32[]{:S(2)}) collective-permute-start(bf16[4,4,576,128]{3,2,1,0:T(8,128)(2,1)S(1)} %get-tuple-element.146), channel_id=1, source_target_pairs={{0,4},{4,0},{8,12},{12,8},{1,5},{5,1},{9,13},{13,9},{2,6},{6,2},{1... | collective-permute-start | bytes 7077896 | tf_op jit(solution)/shard_map/ppermute | solution.py:864
  106.5 3.8 %collective-permute-start.25 = (bf16[2,512,128]{2,1,0:T(8,128)(2,1)S(1)}, bf16[2,512,128]{2,1,0:T(8,128)(2,1)S(1)}, u32[]{:S(2)}, u32[]{:S(2)}) collective-permute-start(bf16[2,512,128]{2,1,0:T(8,128)(2,1)S(1)} %get-tuple-element.156), channel_id=1, source_target_pairs={{0,4},{4,0},{8,12},{12,8},{1,5},{5,1},{9,13},{13,9},{2,6},{6,2},{1... | collective-permute-start | bytes 786440 | tf_op jit(solution)/shard_map/ppermute | solution.py:864
  106.7 23.4 %collective-permute-start.22 = (bf16[4,576,128]{2,1,0:T(8,128)(2,1)S(1)}, bf16[4,576,128]{2,1,0:T(8,128)(2,1)S(1)}, u32[]{:S(2)}, u32[]{:S(2)}) collective-permute-start(bf16[4,576,128]{2,1,0:T(8,128)(2,1)S(1)} %get-tuple-element.148), channel_id=1, source_target_pairs={{0,16},{4,20},{8,24},{12,28},{16,0},{20,4},{24,8},{28,12},{1,17},{... | collective-permute-start | bytes 1769480 | tf_op jit(solution)/shard_map/ppermute | solution.py:870
  108.2 28.3 %collective-permute-start.23 = (bf16[4,576,128]{2,1,0:T(8,128)(2,1)S(1)}, bf16[4,576,128]{2,1,0:T(8,128)(2,1)S(1)}, u32[]{:S(2)}, u32[]{:S(2)}) collective-permute-start(bf16[4,576,128]{2,1,0:T(8,128)(2,1)S(1)} %get-tuple-element.149), channel_id=1, source_target_pairs={{0,8},{4,12},{8,0},{12,4},{16,24},{20,28},{24,16},{28,20},{1,9},{5... | collective-permute-start | bytes 1769480 | tf_op jit(solution)/shard_map/ppermute | solution.py:870
  110.3 26.2 %collective-permute-start.24 = (bf16[4,576,128]{2,1,0:T(8,128)(2,1)S(1)}, bf16[4,576,128]{2,1,0:T(8,128)(2,1)S(1)}, u32[]{:S(2)}, u32[]{:S(2)}) collective-permute-start(bf16[4,576,128]{2,1,0:T(8,128)(2,1)S(1)} %get-tuple-element.150), channel_id=1, source_target_pairs={{0,24},{4,28},{8,16},{12,20},{16,8},{20,12},{24,0},{28,4},{1,25},{... | collective-permute-start | bytes 1769480 | tf_op jit(solution)/shard_map/ppermute | solution.py:870
  110.4 31.7 %copy-start.20 = (bf16[512,512]{1,0:T(8,128)(2,1)S(1)}, bf16[512,512]{1,0:T(8,128)(2,1)}, u32[]{:S(2)}) copy-start(bf16[512,512]{1,0:T(8,128)(2,1)} %copy-done.19) | copy-start | bytes 1572868
  110.4 33.5 %copy-start.14 = (bf16[2048,128]{1,0:T(8,128)(2,1)S(1)}, bf16[2048,128]{1,0:T(8,128)(2,1)}, u32[]{:S(2)}) copy-start(bf16[2048,128]{1,0:T(8,128)(2,1)} %copy-done.13) | copy-start | bytes 1572868
  136.8 7.0 %collective-permute-start.27 = (bf16[2,512,128]{2,1,0:T(8,128)(2,1)S(1)}, bf16[2,512,128]{2,1,0:T(8,128)(2,1)S(1)}, u32[]{:S(2)}, u32[]{:S(2)}) collective-permute-start(bf16[2,512,128]{2,1,0:T(8,128)(2,1)S(1)} %get-tuple-element.168), channel_id=1, source_target_pairs={{0,4},{4,0},{8,12},{12,8},{1,5},{5,1},{9,13},{13,9},{2,6},{6,2},{1... | collective-permute-start | bytes 786440 | tf_op jit(solution)/shard_map/ppermute | solution.py:864
  136.9 26.9 %collective-permute-start.28 = (bf16[576,128]{1,0:T(8,128)(2,1)S(1)}, bf16[576,128]{1,0:T(8,128)(2,1)S(1)}, u32[]{:S(2)}, u32[]{:S(2)}) collective-permute-start(bf16[576,128]{1,0:T(8,128)(2,1)S(1)} %get-tuple-element.174), channel_id=1, source_target_pairs={{0,1},{1,2},{2,3},{3,0},{4,5},{5,6},{6,7},{7,4},{8,9},{9,10},{10,1... | collective-permute-start | bytes 442376 | tf_op jit(solution)/shard_map/ppermute | solution.py:873
  137.1 26.8 %collective-permute-start.29 = (bf16[576,128]{1,0:T(8,128)(2,1)S(1)}, bf16[576,128]{1,0:T(8,128)(2,1)S(1)}, u32[]{:S(2)}, u32[]{:S(2)}) collective-permute-start(bf16[576,128]{1,0:T(8,128)(2,1)S(1)} %get-tuple-element.175), channel_id=1, source_target_pairs={{0,2},{1,3},{2,0},{3,1},{4,6},{5,7},{6,4},{7,5},{8,10},{9,11},{10,... | collective-permute-start | bytes 442376 | tf_op jit(solution)/shard_map/ppermute | solution.py:873
  139.9 23.9 %collective-permute-start.30 = (bf16[576,128]{1,0:T(8,128)(2,1)S(1)}, bf16[576,128]{1,0:T(8,128)(2,1)S(1)}, u32[]{:S(2)}, u32[]{:S(2)}) collective-permute-start(bf16[576,128]{1,0:T(8,128)(2,1)S(1)} %get-tuple-element.176), channel_id=1, source_target_pairs={{0,3},{1,0},{2,1},{3,2},{4,7},{5,4},{6,5},{7,6},{8,11},{9,8},{10,9... | collective-permute-start | bytes 442376 | tf_op jit(solution)/shard_map/ppermute | solution.py:873
  142.1 21.7 %collective-permute-start.26 = (bf16[512,512]{1,0:T(8,128)(2,1)S(1)}, bf16[512,512]{1,0:T(8,128)(2,1)S(1)}, u32[]{:S(2)}, u32[]{:S(2)}) collective-permute-start(bf16[512,512]{1,0:T(8,128)(2,1)S(1)} %copy-done.20), channel_id=1, source_target_pairs={{0,8},{4,12},{8,0},{12,4},{1,9},{5,13},{9,1},{13,5},{2,10},{6,14},... | collective-permute-start | bytes 1572872 | tf_op jit(solution)/shard_map/ppermute | solution.py:861
  169.0 1.8 collective-permute-start.31
  170.8 9.0 %collective-permute-start.32 = (bf16[2,512,384]{2,1,0:T(8,128)(2,1)S(1)}, bf16[2,512,384]{2,1,0:T(8,128)(2,1)S(1)}, u32[]{:S(2)}, u32[]{:S(2)}) collective-permute-start(bf16[2,512,384]{2,1,0:T(8,128)(2,1)S(1)} %get-tuple-element.183), channel_id=1, source_target_pairs={{0,4},{4,0},{8,12},{12,8},{1,5},{5,1},{9,13},{13,9},{2,6},{6,2},{1... | collective-permute-start | bytes 2359304 | tf_op jit(solution)/shard_map/ppermute | solution.py:864
  170.9 8.8 %collective-permute-start.33 = (bf16[2,512,384]{2,1,0:T(8,128)(2,1)S(1)}, bf16[2,512,384]{2,1,0:T(8,128)(2,1)S(1)}, u32[]{:S(2)}, u32[]{:S(2)}) collective-permute-start(bf16[2,512,384]{2,1,0:T(8,128)(2,1)S(1)} %get-tuple-element.185), channel_id=1, source_target_pairs={{0,4},{4,0},{8,12},{12,8},{1,5},{5,1},{9,13},{13,9},{2,6},{6,2},{1... | collective-permute-start | bytes 2359304 | tf_op jit(solution)/shard_map/ppermute | solution.py:864
  172.8 14.5 %collective-permute-start.35 = (bf16[896,128]{1,0:T(8,128)(2,1)}, bf16[896,128]{1,0:T(8,128)(2,1)S(1)}, u32[]{:S(2)}, u32[]{:S(2)}) collective-permute-start(bf16[896,128]{1,0:T(8,128)(2,1)} %get-tuple-element.190), channel_id=1, source_target_pairs={{0,16},{4,20},{8,24},{12,28},{16,0},{20,4},{24,8},{28,12},{1,17},{... | collective-permute-start | bytes 688136 | tf_op jit(solution)/shard_map/ppermute | solution.py:870
  178.3 12.8 %collective-permute-start.36 = (bf16[896,128]{1,0:T(8,128)(2,1)}, bf16[896,128]{1,0:T(8,128)(2,1)}, u32[]{:S(2)}, u32[]{:S(2)}) collective-permute-start(bf16[896,128]{1,0:T(8,128)(2,1)} %get-tuple-element.191), channel_id=1, source_target_pairs={{0,8},{4,12},{8,0},{12,4},{16,24},{20,28},{24,16},{28,20},{1,9},{5... | collective-permute-start | bytes 688136 | tf_op jit(solution)/shard_map/ppermute | solution.py:870
  179.6 11.8 %collective-permute-start.37 = (bf16[896,128]{1,0:T(8,128)(2,1)}, bf16[896,128]{1,0:T(8,128)(2,1)}, u32[]{:S(2)}, u32[]{:S(2)}) collective-permute-start(bf16[896,128]{1,0:T(8,128)(2,1)} %get-tuple-element.192), channel_id=1, source_target_pairs={{0,24},{4,28},{8,16},{12,20},{16,8},{20,12},{24,0},{28,4},{1,25},{... | collective-permute-start | bytes 688136 | tf_op jit(solution)/shard_map/ppermute | solution.py:870
  184.0 20.3 %collective-permute-start.34 = (bf16[512,512]{1,0:T(8,128)(2,1)}, bf16[512,512]{1,0:T(8,128)(2,1)}, u32[]{:S(2)}, u32[]{:S(2)}) collective-permute-start(bf16[512,512]{1,0:T(8,128)(2,1)} %get-tuple-element.189), channel_id=1, source_target_pairs={{0,8},{4,12},{8,0},{12,4},{1,9},{5,13},{9,1},{13,5},{2,10},{6,14},... | collective-permute-start | bytes 1572872 | tf_op jit(solution)/shard_map/ppermute | solution.py:861
  185.8 12.9 %collective-permute-start.41 = (bf16[576,128]{1,0:T(8,128)(2,1)}, bf16[576,128]{1,0:T(8,128)(2,1)S(1)}, u32[]{:S(2)}, u32[]{:S(2)}) collective-permute-start(bf16[576,128]{1,0:T(8,128)(2,1)} %get-tuple-element.203.r), channel_id=1, source_target_pairs={{0,16},{4,20},{8,24},{12,28},{16,0},{20,4},{24,8},{28,12},{1,17},{... | collective-permute-start | bytes 442376 | tf_op jit(solution)/shard_map/ppermute | solution.py:870
  192.5 8.0 %collective-permute-start.38 = (bf16[320,128]{1,0:T(8,128)(2,1)S(1)}, bf16[320,128]{1,0:T(8,128)(2,1)S(1)}, u32[]{:S(2)}, u32[]{:S(2)}) collective-permute-start(bf16[320,128]{1,0:T(8,128)(2,1)S(1)} %get-tuple-element.198), channel_id=1, source_target_pairs={{0,1},{1,2},{2,3},{3,0},{4,5},{5,6},{6,7},{7,4},{8,9},{9,10},{10,1... | collective-permute-start | bytes 245768 | tf_op jit(solution)/shard_map/ppermute | solution.py:873
  193.7 7.8 %collective-permute-start.39 = (bf16[320,128]{1,0:T(8,128)(2,1)S(1)}, bf16[320,128]{1,0:T(8,128)(2,1)S(1)}, u32[]{:S(2)}, u32[]{:S(2)}) collective-permute-start(bf16[320,128]{1,0:T(8,128)(2,1)S(1)} %get-tuple-element.199), channel_id=1, source_target_pairs={{0,2},{1,3},{2,0},{3,1},{4,6},{5,7},{6,4},{7,5},{8,10},{9,11},{10,... | collective-permute-start | bytes 245768 | tf_op jit(solution)/shard_map/ppermute | solution.py:873
  194.4 7.1 %collective-permute-start.40 = (bf16[320,128]{1,0:T(8,128)(2,1)S(1)}, bf16[320,128]{1,0:T(8,128)(2,1)S(1)}, u32[]{:S(2)}, u32[]{:S(2)}) collective-permute-start(bf16[320,128]{1,0:T(8,128)(2,1)S(1)} %get-tuple-element.200), channel_id=1, source_target_pairs={{0,3},{1,0},{2,1},{3,2},{4,7},{5,4},{6,5},{7,6},{8,11},{9,8},{10,9... | collective-permute-start | bytes 245768 | tf_op jit(solution)/shard_map/ppermute | solution.py:873
  202.7 4.1 %collective-permute-start.42 = (bf16[192,128]{1,0:T(8,128)(2,1)S(1)}, bf16[192,128]{1,0:T(8,128)(2,1)S(1)}, u32[]{:S(2)}, u32[]{:S(2)}) collective-permute-start(bf16[192,128]{1,0:T(8,128)(2,1)S(1)} %get-tuple-element.209.r), channel_id=1, source_target_pairs={{0,16},{4,20},{8,24},{12,28},{16,0},{20,4},{24,8},{28,12},{1,17},{... | collective-permute-start | bytes 147464 | tf_op jit(solution)/shard_map/ppermute | solution.py:870
  (28 other events, 409.3 us)
